TPU v7x, 32 devices: a whole 2x2x4 slice. The times are simulated.
32 devices in a mesh: groups: 2 (over y), view: 4 (over z), row: 4 (over x, core).
Axes of the slice: x: 2, y: 2, z: 4, core: 2. Of those that a mesh axis runs over, the one named last changes fastest.
Arguments:
- inputs: bfloat16 [64, 292, 16, 16], P(None, 'view', ('groups', 'row')), parts along dimension 2, may hold values from -24 to 24
- cotangent: bfloat16 [64, 292, 16, 16], P(None, None, ('groups', 'row'), 'view'), parts along dimension 2, may hold values from -6 to 6
- keep: int32 [584], P('groups'), parts along dimension 0, may hold values from 0 to 1, as said below
- w_conv: bfloat16 [64, 64, 3, 3], replicated, may hold values from -0.25 to 0.25
- gain: float32 [64], replicated, may hold values from 0.5 to 1.5
- w_query: bfloat16 [64, 64], replicated, may hold values from -3 to 3
- w_key: bfloat16 [64, 64], replicated, may hold values from -3 to 3
- w_value: bfloat16 [64, 64], replicated, may hold values from -0.75 to 0.75
- w_out: bfloat16 [64, 64], replicated, may hold values from -0.75 to 0.75
Outputs:
- output: bfloat16 [64, 292, 16, 16], P(None, None, ('groups', 'row'), 'view'), parts along dimension 2
- d_input: bfloat16 [64, 292, 16, 16], P(None, 'view', ('groups', 'row')), parts along dimension 2
- g_conv: float32 [128, 64, 3, 3], P('groups'), parts along dimension 0
- g_gain: float32 [128], P('groups'), parts along dimension 0
- g_query: float32 [128, 64], P('groups'), parts along dimension 0
- g_key: float32 [128, 64], P('groups'), parts along dimension 0
- g_value: float32 [128, 64], P('groups'), parts along dimension 0
- g_out: float32 [128, 64], P('groups'), parts along dimension 0
There are 2 independent parts, one for each index of `groups`. A program takes and returns all parts, laid end to end along the dimension named above; an argument that names none is the same for every part. Nothing has to cross between parts.
Inputs may be any that keep to these rules, and one draw needn't show every extreme that they name: `keep`: zero at every view from 289 on, one at view 289 // 2.
All inputs are finite; a program needn't handle non-finite values.
Results may differ from a plain program's by a relative error of at most 0.012.
The roundings to bfloat16 on the way count: a program that leaves them out, or rounds other values in their place, can miss the bound.
Values may be sent and summed in bfloat16 or wider, within the bound.
No kernel may reach another device: no remote copies, remote signals or barrier semaphores. Data moves between devices by JAX's collectives and lax.ppermute only.
A program may use at most 64 MiB of HBM per device.

v0:
```python
import math

import jax
import jax.numpy as jnp
from jax import lax
from jax.sharding import PartitionSpec as P


def with_halo(cells, sides, width):
    for axis, dim in sides:
        count = lax.axis_size(axis)
        ends = count - 1
        head = lax.slice_in_dim(cells, 0, width, axis=dim)
        tail = lax.slice_in_dim(cells, cells.shape[dim] - width, cells.shape[dim], axis=dim)
        cells = jnp.concatenate(
            [
                lax.ppermute(tail, axis, [(i, (i + 1) % count) for i in range(ends)]),
                cells,
                lax.ppermute(head, axis, [((i + 1) % count, i) for i in range(ends)]),
            ],
            axis=dim,
        )
    return cells


def product(form, left, right):
    return jnp.einsum(form, left, right, preferred_element_type=jnp.float32)


def convolve(padded, w_conv):
    height = padded.shape[2] - 2
    breadth = padded.shape[3] - 2
    total = jnp.zeros((w_conv.shape[0], padded.shape[1], height, breadth), jnp.float32)
    for row_tap in range(3):
        for col_tap in range(3):
            window = padded[:, :, row_tap : row_tap + height, col_tap : col_tap + breadth]
            total = total + product("oc,cvrw->ovrw", w_conv[:, :, row_tap, col_tap], window)
    return total


def input_grad(grad_pad, w_conv):
    height = grad_pad.shape[2] - 2
    breadth = grad_pad.shape[3] - 2
    total = jnp.zeros((w_conv.shape[1], grad_pad.shape[1], height, breadth), jnp.float32)
    for row_tap in range(3):
        for col_tap in range(3):
            window = grad_pad[
                :, :, 2 - row_tap : 2 - row_tap + height, 2 - col_tap : 2 - col_tap + breadth
            ]
            total = total + product("oc,ovrw->cvrw", w_conv[:, :, row_tap, col_tap], window)
    return total


def weight_grad(grad, padded):
    height = grad.shape[2]
    breadth = grad.shape[3]
    taps = []
    for row_tap in range(3):
        for col_tap in range(3):
            window = padded[:, :, row_tap : row_tap + height, col_tap : col_tap + breadth]
            taps.append(product("ovrw,cvrw->oc", grad, window))
    stacked = jnp.stack(taps, axis=2)
    return stacked.reshape(grad.shape[0], padded.shape[0], 3, 3)


def angular(mixed_in, grad_out, keep, gain, w_query, w_key, w_value, w_out, used):
    pixels, all_views, channels = mixed_in.shape
    scale = 1.0 / math.sqrt(channels)
    values = mixed_in.astype(jnp.float32)
    centred = values - jnp.mean(values, axis=2, keepdims=True)
    rstd = lax.rsqrt(jnp.mean(centred * centred, axis=2, keepdims=True) + 1e-05)
    normed = centred * rstd
    normal_in = (normed * gain[None, None, :]).astype(jnp.bfloat16)
    query = product("cd,pvc->pvd", w_query, normal_in).astype(jnp.bfloat16)
    key_proj = product("cd,pvc->pvd", w_key, normal_in).astype(jnp.bfloat16)
    value_proj = product("cd,pvc->pvd", w_value, normal_in).astype(jnp.bfloat16)
    scores = product("pvd,pud->pvu", query, key_proj) * scale
    scores = jnp.where(keep[None, None, :used] > 0, scores, -1e30)
    highest = jnp.max(scores, axis=2, keepdims=True)
    expo = jnp.exp(scores - highest)
    probs = expo / jnp.sum(expo, axis=2, keepdims=True)
    probs_b = probs.astype(jnp.bfloat16)
    attended = product("pvu,pud->pvd", probs_b, value_proj).astype(jnp.bfloat16)
    output = (values + product("dc,pvd->pvc", w_out, attended)).astype(jnp.bfloat16)
    d_attended = product("dc,pvc->pvd", w_out, grad_out).astype(jnp.bfloat16)
    g_out = product("pvd,pvc->dc", attended, grad_out)
    d_probs = product("pvd,pud->pvu", d_attended, value_proj)
    d_value = product("pvu,pvd->pud", probs_b, d_attended).astype(jnp.bfloat16)
    inner = jnp.sum(probs * d_probs, axis=2, keepdims=True)
    d_scores = (probs * (d_probs - inner) * scale).astype(jnp.bfloat16)
    d_query = product("pvu,pud->pvd", d_scores, key_proj).astype(jnp.bfloat16)
    d_key = product("pvu,pvd->pud", d_scores, query).astype(jnp.bfloat16)
    g_query = product("pvc,pvd->cd", normal_in, d_query)
    g_key = product("pvc,pvd->cd", normal_in, d_key)
    g_value = product("pvc,pvd->cd", normal_in, d_value)
    d_normal = (
        product("cd,pvd->pvc", w_query, d_query)
        + product("cd,pvd->pvc", w_key, d_key)
        + product("cd,pvd->pvc", w_value, d_value)
    )
    g_gain = jnp.sum(d_normal * normed, axis=(0, 1))
    scaled = d_normal * gain[None, None, :]
    back = (
        scaled
        - jnp.mean(scaled, axis=2, keepdims=True)
        - normed * jnp.mean(scaled * normed, axis=2, keepdims=True)
    )
    d_spatial = (grad_out.astype(jnp.float32) + back * rstd).astype(jnp.bfloat16)
    return (output, d_spatial, (g_gain, g_query, g_key, g_value, g_out))


def angular_rows(spatial, cotangent, keep, gain, w_query, w_key, w_value, w_out, used):

    def row_pass(pair):
        return angular(pair[0], pair[1], keep, gain, w_query, w_key, w_value, w_out, used)

    spatial_last = jnp.transpose(spatial, (2, 3, 1, 0))
    cotangent_last = jnp.transpose(cotangent, (2, 3, 1, 0))
    out_rows, grad_rows, grads = lax.map(row_pass, (spatial_last, cotangent_last))
    summed = tuple((jnp.sum(item, axis=0) for item in grads))
    return (jnp.transpose(out_rows, (3, 2, 0, 1)), jnp.transpose(grad_rows, (3, 2, 0, 1)), summed)


def body(inputs, cotangent, keep, w_conv, gain, w_query, w_key, w_value, w_out):
    channels, view_dev, row_dev, width = inputs.shape
    blocks = lax.axis_size("view")
    breadth = width // blocks
    all_views = view_dev * blocks
    padded = with_halo(inputs, (("row", 2),), 1)
    padded = jnp.pad(padded, ((0, 0), (0, 0), (0, 0), (1, 1)))
    spatial = (inputs.astype(jnp.float32) + convolve(padded, w_conv)).astype(jnp.bfloat16)
    moved = lax.all_to_all(
        spatial.reshape(channels, view_dev, row_dev, blocks, breadth),
        "view",
        split_axis=3,
        concat_axis=1,
        tiled=True,
    )
    moved = moved.reshape(channels, all_views, row_dev, breadth)
    output, d_spatial, grads = angular_rows(
        moved, cotangent, keep, gain, w_query, w_key, w_value, w_out, all_views
    )
    returned = lax.all_to_all(
        d_spatial.reshape(channels, all_views, row_dev, 1, breadth),
        "view",
        split_axis=1,
        concat_axis=3,
        tiled=True,
    )
    returned = returned.reshape(channels, view_dev, row_dev, width)
    grad_pad = with_halo(returned, (("row", 2),), 1)
    grad_pad = jnp.pad(grad_pad, ((0, 0), (0, 0), (0, 0), (1, 1)))
    d_input = (returned.astype(jnp.float32) + input_grad(grad_pad, w_conv)).astype(jnp.bfloat16)
    g_conv = weight_grad(returned, padded)
    g_gain, g_query, g_key, g_value, g_out = grads
    g_conv, g_gain, g_query, g_key, g_value, g_out = lax.psum(
        (g_conv, g_gain, g_query, g_key, g_value, g_out), ("view", "row")
    )
    return (output, d_input, g_conv, g_gain, g_query, g_key, g_value, g_out)


def solution(mesh):
    placed = (
        P(None, "view", ("groups", "row"), None),
        P(None, None, ("groups", "row"), "view"),
        P("groups"),
        P(),
        P(),
        P(),
        P(),
        P(),
        P(),
    )
    return jax.shard_map(
        body,
        mesh=mesh,
        in_specs=placed,
        out_specs=(
            P(None, None, ("groups", "row"), "view"),
            P(None, "view", ("groups", "row"), None),
            P("groups", None, None, None),
            P("groups"),
            P("groups", None),
            P("groups", None),
            P("groups", None),
            P("groups", None),
        ),
        check_vma=False,
    )
```

profile of v0, /device:TPU:1, one launch (start us, length us, event | category | flops | bytes accessed | tf_op | source)
XLA Modules:
  0.0 309.8 jit_solution(1073874773569292355)
XLA Ops:
  8.4 4.5 %collective-permute-start = (bf16[64,73,1,16]{1,0,3,2:T(8,128)(2,1)S(1)}, bf16[64,73,1,16]{1,0,3,2:T(8,128)(2,1)S(1)}, u32[]{:S(2)}, u32[]{:S(2)}) collective-permute-start(bf16[64,73,1,16]{1,0,3,2:T(8,128)(2,1)S(1)} %copy.172), channel_id=1, source_target_pairs={{0,1},{1,2},{2,3},{4,5},{5,6},{6,7},{8,9},{9,10},{10,11},{12,13},{... | collective-permute-start | bytes 448520 | tf_op jit(solution)/shard_map/ppermute | solution.py:17
  13.0 1.9 collective-permute-start.1
  16.9 3.8 %collective-permute-done.1 = bf16[64,73,1,16]{1,0,3,2:T(8,128)(2,1)S(1)} collective-permute-done((bf16[64,73,1,16]{1,0,3,2:T(8,128)(2,1)S(1)}, bf16[64,73,1,16]{1,0,3,2:T(8,128)(2,1)S(1)}, u32[]{:S(2)}, u32[]{:S(2)}) %collective-permute-start.1) | collective-permute-done | bytes 149536 | tf_op jit(solution)/shard_map/ppermute | solution.py:19
  24.2 4.7 %all-to-all-start = ((bf16[64,73,2,4,4]{1,0,4,2,3:T(8,128)(2,1)}), bf16[64,73,2,4,4]{1,0,4,2,3:T(8,128)(2,1)S(1)}, u32[]{:S(2)}, u32[]{:S(2)}) async-start(bf16[64,73,2,4,4]{1,0,4,2,3:T(8,128)(2,1)} %copy.93), calls=%async_computation | async-start | bytes 1048576 | tf_op jit(solution)/shard_map/all_to_all | solution.py:132
  29.0 11.2 %all-to-all-done = bf16[64,73,2,4,4]{1,0,4,2,3:T(8,128)(2,1)S(1)} async-done(((bf16[64,73,2,4,4]{1,0,4,2,3:T(8,128)(2,1)}), bf16[64,73,2,4,4]{1,0,4,2,3:T(8,128)(2,1)S(1)}, u32[]{:S(2)}, u32[]{:S(2)}) %all-to-all-start) | async-done | bytes 299040 | tf_op jit(solution)/shard_map/all_to_all | solution.py:132
  41.0 56.6 %while.22 = (s32[]{:T(128)}, bf16[2,4,292,64]{2,1,0,3:T(4,128)(2,1)}, bf16[2,4,292,64]{2,3,1,0:T(8,128)(2,1)}, f32[2,64]{1,0:T(2,128)}, f32[2,64,64]{2,1,0:T(8,1...) while((s32[]{:T(128)}, ...), condition=%wide.region_9.10_spmd, body=%wide.region_0.9_spmd.sunk | while | flops 399432576 | bytes 35407752 | solution.py:119
  45.7 3.1 %fusion.288 = (f32[4,292]{1,0:T(4,128)S(1)}, f32[4,292,292]{1,2,0:T(8,128)}) fusion(pred[292]{0:T(512)(128)(4,1)S(1)} %broadcast_compare_fusion.2, bf16[4,292,64]{1,2,0:T(8,128)(2,1)} %convolution_convert_fusion.12, bf16[64,64]{1,0:T(8,128)(2,1)S(1)} %copy-done.17, f32[64]{0:T(128)} %get-tuple-element.425, f32[4,292]{1,0:T(4,128)S(1)} %add_rsqrt_fusion.2, ...), kind=kOutput, calls=%fused_computation.193.clone.1 | convolution fusion | flops 55036452 | bytes 1744452 | tf_op jit(solution)/shard_map/while/body/eval_jaxpr/sub | solution.py:80
  48.9 3.5 %fusion.293 = bf16[4,292,64]{1,2,0:T(8,128)(2,1)} fusion(f32[4,292,292]{1,2,0:T(8,128)S(1)} %fusion.290, f32[4,292,292]{1,2,0:T(8,128)} %get-tuple-element.288, f32[4,292]{1,0:T(4,128)S(1)} %get-tuple-element.289, bf16[64,64]{1,0:T(8,128)(2,1)S(1)} %copy-done.17, f32[64]{0:T(128)} %get-tuple-element.425, f32[4,292]{1,0:T(4,128)S(1)} %add_rsqrt_fusion.2, ...), kind=kOutput, calls=%fused_computation.14.clone.1 | convolution fusion | flops 56135540 | bytes 7662592 | tf_op jit(solution)/shard_map/while/body/eval_jaxpr/pvu,pvd->pud/dot_general | solution.py:27
  52.4 3.5 %fusion.291 = bf16[4,292,64]{1,2,0:T(8,128)(2,1)} fusion(bf16[4,292,64]{1,2,0:T(8,128)(2,1)} %convolution_convert_fusion.12, f32[4,292,292]{1,2,0:T(8,128)S(1)} %fusion.290, f32[4,292,292]{1,2,0:T(8,128)} %get-tuple-element.288, f32[4,292]{1,0:T(4,128)S(1)} %get-tuple-element.289), kind=kOutput, calls=%fused_computation.13.clone.1 | convolution fusion | flops 46118772 | bytes 3032128 | tf_op jit(solution)/shard_map/while/body/eval_jaxpr/pvu,pud->pvd/dot_general | solution.py:27
  58.1 2.0 convolution_convert_fusion.15
  65.3 1.9 convolution_convert_fusion.13
  74.0 3.1 %fusion.288 = (f32[4,292]{1,0:T(4,128)S(1)}, f32[4,292,292]{1,2,0:T(8,128)}) fusion(pred[292]{0:T(512)(128)(4,1)S(1)} %broadcast_compare_fusion.2, bf16[4,292,64]{1,2,0:T(8,128)(2,1)} %convolution_convert_fusion.12, bf16[64,64]{1,0:T(8,128)(2,1)S(1)} %copy-done.17, f32[64]{0:T(128)} %get-tuple-element.425, f32[4,292]{1,0:T(4,128)S(1)} %add_rsqrt_fusion.2, ...), kind=kOutput, calls=%fused_computation.193.clone.1 | convolution fusion | flops 55036452 | bytes 1744452 | tf_op jit(solution)/shard_map/while/body/eval_jaxpr/sub | solution.py:80
  77.2 3.5 %fusion.293 = bf16[4,292,64]{1,2,0:T(8,128)(2,1)} fusion(f32[4,292,292]{1,2,0:T(8,128)S(1)} %fusion.290, f32[4,292,292]{1,2,0:T(8,128)} %get-tuple-element.288, f32[4,292]{1,0:T(4,128)S(1)} %get-tuple-element.289, bf16[64,64]{1,0:T(8,128)(2,1)S(1)} %copy-done.17, f32[64]{0:T(128)} %get-tuple-element.425, f32[4,292]{1,0:T(4,128)S(1)} %add_rsqrt_fusion.2, ...), kind=kOutput, calls=%fused_computation.14.clone.1 | convolution fusion | flops 56135540 | bytes 7662592 | tf_op jit(solution)/shard_map/while/body/eval_jaxpr/pvu,pvd->pud/dot_general | solution.py:27
  80.7 3.5 %fusion.291 = bf16[4,292,64]{1,2,0:T(8,128)(2,1)} fusion(bf16[4,292,64]{1,2,0:T(8,128)(2,1)} %convolution_convert_fusion.12, f32[4,292,292]{1,2,0:T(8,128)S(1)} %fusion.290, f32[4,292,292]{1,2,0:T(8,128)} %get-tuple-element.288, f32[4,292]{1,0:T(4,128)S(1)} %get-tuple-element.289), kind=kOutput, calls=%fused_computation.13.clone.1 | convolution fusion | flops 46118772 | bytes 3032128 | tf_op jit(solution)/shard_map/while/body/eval_jaxpr/pvu,pud->pvd/dot_general | solution.py:27
  86.4 2.0 convolution_convert_fusion.15
  93.7 1.9 convolution_convert_fusion.13
  100.6 3.5 %all-to-all-start.1 = ((bf16[4,2,18688]{2,1,0:T(2,128)(2,1)}), bf16[4,2,18688]{2,1,0:T(2,128)(2,1)S(1)}, u32[]{:S(2)}, u32[]{:S(2)}) async-start(bf16[4,2,18688]{2,1,0:T(2,128)(2,1)} %reshape.106), calls=%async_computation.1 | async-start | bytes 598016 | tf_op jit(solution)/shard_map/all_to_all | solution.py:143
  107.4 6.0 %all-to-all-done.1 = bf16[4,2,18688]{2,1,0:T(2,128)(2,1)S(1)} async-done(((bf16[4,2,18688]{2,1,0:T(2,128)(2,1)}), bf16[4,2,18688]{2,1,0:T(2,128)(2,1)S(1)}, u32[]{:S(2)}, u32[]{:S(2)}) %all-to-all-start.1) | async-done | bytes 299040 | tf_op jit(solution)/shard_map/all_to_all | solution.py:143
  118.3 1.9 collective-permute-start.3
  120.3 3.6 %collective-permute-start.2 = (bf16[64,73,1,16]{1,0,3,2:T(8,128)(2,1)S(1)}, bf16[64,73,1,16]{1,0,3,2:T(8,128)(2,1)S(1)}, u32[]{:S(2)}, u32[]{:S(2)}) collective-permute-start(bf16[64,73,1,16]{1,0,3,2:T(8,128)(2,1)S(1)} %get-tuple-element.172), channel_id=1, source_target_pairs={{0,1},{1,2},{2,3},{4,5},{5,6},{6,7},{8,9},{9,10},{10,11},{12,13},{... | collective-permute-start | bytes 448520 | tf_op jit(solution)/shard_map/ppermute | solution.py:17
  124.3 1.8 collective-permute-done.3
  131.1 67.6 %all-reduce.8.cloned.1.call-done = (f32[64]{0:T(128)}, f32[64,64]{1,0:T(8,128)}, f32[64,64]{1,0:T(8,128)}, f32[64,64]{1,0:T(8,128)}, f32[64,64]{1,0:T(8,128)}) async-done(((f32[64]{0:T(128)}, f32[64,64]{1,0:T(8,128)}, f32[64,64]{1,0:T(8,128)}, f32[64,64]{1,0:T(8,128)}, f32[64,64]{1,0:T(8,128)}), (f32[64]{0:T(128)}, f32[64,64]{1,0:T(8,128)}, f32[64,64]{1,0:T(8,128)}, f32[64,64]{1,0:T(8,128)}, ...) | async-done | bytes 65808 | tf_op jit(solution)/shard_map/psum | solution.py:156
  198.7 95.8 %all-reduce.6.cloned.1.call-done = f32[64,64,3,3]{1,0,3,2:T(8,128)} async-done(((f32[64,64,3,3]{1,0,3,2:T(8,128)}), f32[64,64,3,3]{1,0,3,2:T(8,128)}) %all-reduce.6.cloned.1.call-update) | async-done | bytes 147472 | tf_op jit(solution)/shard_map/psum | solution.py:156
  294.5 1.7 copy.226
  (251 shorter events, 58.2 us)
Async XLA Ops:
  7.2 7.7 %copy-start.2 = (bf16[64,73,2,16]{1,3,2,0:T(8,128)(2,1)S(1)}, bf16[64,73,2,16]{1,3,2,0:T(8,128)(2,1)}, u32[]{:S(2)}) copy-start(bf16[64,73,2,16]{1,3,2,0:T(8,128)(2,1)} %param.11) | copy-start | bytes 897028
  7.2 7.7 %copy-start.13 = (bf16[64,64,3,3]{1,0,3,2:T(8,128)(2,1)S(1)}, bf16[64,64,3,3]{1,0,3,2:T(8,128)(2,1)}, u32[]{:S(2)}) copy-start(bf16[64,64,3,3]{1,0,3,2:T(8,128)(2,1)} %param.14) | copy-start | bytes 221188
  8.4 7.8 %collective-permute-start = (bf16[64,73,1,16]{1,0,3,2:T(8,128)(2,1)S(1)}, bf16[64,73,1,16]{1,0,3,2:T(8,128)(2,1)S(1)}, u32[]{:S(2)}, u32[]{:S(2)}) collective-permute-start(bf16[64,73,1,16]{1,0,3,2:T(8,128)(2,1)S(1)} %copy.172), channel_id=1, source_target_pairs={{0,1},{1,2},{2,3},{4,5},{5,6},{6,7},{8,9},{9,10},{10,11},{12,13},{... | collective-permute-start | bytes 448520 | tf_op jit(solution)/shard_map/ppermute | solution.py:17
  13.0 7.7 %collective-permute-start.1 = (bf16[64,73,1,16]{1,0,3,2:T(8,128)(2,1)S(1)}, bf16[64,73,1,16]{1,0,3,2:T(8,128)(2,1)S(1)}, u32[]{:S(2)}, u32[]{:S(2)}) collective-permute-start(bf16[64,73,1,16]{1,0,3,2:T(8,128)(2,1)S(1)} %copy.173), channel_id=1, source_target_pairs={{1,0},{2,1},{3,2},{5,4},{6,5},{7,6},{9,8},{10,9},{11,10},{13,12},{... | collective-permute-start | bytes 448520 | tf_op jit(solution)/shard_map/ppermute | solution.py:19
  23.4 5.6 %copy-start.18 = (bf16[64,292,2,4]{1,3,2,0:T(4,128)(2,1)S(1)}, bf16[64,292,2,4]{1,3,2,0:T(4,128)(2,1)}, u32[]{:S(2)}) copy-start(bf16[64,292,2,4]{1,3,2,0:T(4,128)(2,1)} %param.12) | copy-start | bytes 897028
  24.2 16.7 %copy-start.12 = (bf16[64,64]{1,0:T(8,128)(2,1)S(1)}, bf16[64,64]{1,0:T(8,128)(2,1)}, u32[]{:S(2)}) copy-start(bf16[64,64]{1,0:T(8,128)(2,1)} %param.19) | copy-start | bytes 24580
  24.2 16.7 %copy-start.15 = (bf16[64,64]{1,0:T(8,128)(2,1)S(1)}, bf16[64,64]{1,0:T(8,128)(2,1)}, u32[]{:S(2)}) copy-start(bf16[64,64]{1,0:T(8,128)(2,1)} %param.18) | copy-start | bytes 24580
  24.2 16.8 %copy-start.34 = (f32[64]{0:T(128)S(1)}, f32[64]{0:T(128)}, u32[]{:S(2)}) copy-start(f32[64]{0:T(128)} %param.15) | copy-start | bytes 772
  24.2 16.0 %all-to-all-start = ((bf16[64,73,2,4,4]{1,0,4,2,3:T(8,128)(2,1)}), bf16[64,73,2,4,4]{1,0,4,2,3:T(8,128)(2,1)S(1)}, u32[]{:S(2)}, u32[]{:S(2)}) async-start(bf16[64,73,2,4,4]{1,0,4,2,3:T(8,128)(2,1)} %copy.93), calls=%async_computation | async-start | bytes 1048576 | tf_op jit(solution)/shard_map/all_to_all | solution.py:132
  48.9 9.2 %copy-start.42 = (f32[4,292]{1,0:T(4,128)}, f32[4,292]{1,0:T(4,128)S(1)}, u32[]{:S(2)}) copy-start(f32[4,292]{1,0:T(4,128)S(1)} %get-tuple-element.289) | copy-start | bytes 14020 | tf_op jit(solution)/shard_map/while
  60.2 5.1 %copy-start.5 = (bf16[4,292,64]{1,2,0:T(8,128)(2,1)S(1)}, bf16[4,292,64]{1,2,0:T(8,128)(2,1)}, u32[]{:S(2)}) copy-start(bf16[4,292,64]{1,2,0:T(8,128)(2,1)} %copy-done.4) | copy-start | bytes 448516 | tf_op jit(solution)/shard_map/while
  60.2 5.1 %copy-start.43 = (f32[4,292]{1,0:T(4,128)S(1)}, f32[4,292]{1,0:T(4,128)}, u32[]{:S(2)}) copy-start(f32[4,292]{1,0:T(4,128)} %copy-done.42) | copy-start | bytes 14020 | tf_op jit(solution)/shard_map/while
  77.2 9.2 %copy-start.42 = (f32[4,292]{1,0:T(4,128)}, f32[4,292]{1,0:T(4,128)S(1)}, u32[]{:S(2)}) copy-start(f32[4,292]{1,0:T(4,128)S(1)} %get-tuple-element.289) | copy-start | bytes 14020 | tf_op jit(solution)/shard_map/while
  97.6 6.5 %copy-start.27 = (f32[2,64,64]{2,1,0:T(8,128)S(1)}, f32[2,64,64]{2,1,0:T(8,128)}, u32[]{:S(2)}) copy-start(f32[2,64,64]{2,1,0:T(8,128)} %get-tuple-element.410) | copy-start | bytes 98308
  97.6 7.1 %copy-start.30 = (f32[2,64,64]{2,1,0:T(8,128)S(1)}, f32[2,64,64]{2,1,0:T(8,128)}, u32[]{:S(2)}) copy-start(f32[2,64,64]{2,1,0:T(8,128)} %get-tuple-element.411) | copy-start | bytes 98308
  97.6 7.7 %copy-start.33 = (f32[2,64,64]{2,1,0:T(8,128)S(1)}, f32[2,64,64]{2,1,0:T(8,128)}, u32[]{:S(2)}) copy-start(f32[2,64,64]{2,1,0:T(8,128)} %get-tuple-element.412) | copy-start | bytes 98308
  97.6 8.4 %copy-start.24 = (f32[2,64,64]{2,1,0:T(8,128)S(1)}, f32[2,64,64]{2,1,0:T(8,128)}, u32[]{:S(2)}) copy-start(f32[2,64,64]{2,1,0:T(8,128)} %get-tuple-element.413) | copy-start | bytes 98308
  97.7 9.0 %copy-start.39 = (f32[2,64]{1,0:T(2,128)S(1)}, f32[2,64]{1,0:T(2,128)}, u32[]{:S(2)}) copy-start(f32[2,64]{1,0:T(2,128)} %get-tuple-element.409) | copy-start | bytes 1540
  100.6 12.8 %all-to-all-start.1 = ((bf16[4,2,18688]{2,1,0:T(2,128)(2,1)}), bf16[4,2,18688]{2,1,0:T(2,128)(2,1)S(1)}, u32[]{:S(2)}, u32[]{:S(2)}) async-start(bf16[4,2,18688]{2,1,0:T(2,128)(2,1)} %reshape.106), calls=%async_computation.1 | async-start | bytes 598016 | tf_op jit(solution)/shard_map/all_to_all | solution.py:143
  104.1 94.6 %all-reduce.8.cloned.1.call-start = ((), (), s32[]{:S(2)}) async-start(), calls=%async_computation.3 | async-start | bytes 263168 | tf_op jit(solution)/shard_map/psum | solution.py:156
  107.2 187.4 %all-reduce.6.cloned.1.call-start = ((), (), s32[]{:S(2)}) async-start(), calls=%async_computation.2 | async-start | bytes 589824 | tf_op jit(solution)/shard_map/psum | solution.py:156
  118.3 5.6 %copy-start.21 = (f32[64,64,9]{1,0,2:T(8,128)}, f32[64,64,9]{1,0,2:T(8,128)S(1)}, u32[]{:S(2)}) copy-start(f32[64,64,9]{1,0,2:T(8,128)S(1)} %fusion.104) | copy-start | bytes 442372
  118.3 7.8 %collective-permute-start.3 = (bf16[64,73,1,16]{1,0,3,2:T(8,128)(2,1)S(1)}, bf16[64,73,1,16]{1,0,3,2:T(8,128)(2,1)S(1)}, u32[]{:S(2)}, u32[]{:S(2)}) collective-permute-start(bf16[64,73,1,16]{1,0,3,2:T(8,128)(2,1)S(1)} %get-tuple-element.173), channel_id=1, source_target_pairs={{1,0},{2,1},{3,2},{5,4},{6,5},{7,6},{9,8},{10,9},{11,10},{13,12},{... | collective-permute-start | bytes 448520 | tf_op jit(solution)/shard_map/ppermute | solution.py:19
  120.3 7.0 %collective-permute-start.2 = (bf16[64,73,1,16]{1,0,3,2:T(8,128)(2,1)S(1)}, bf16[64,73,1,16]{1,0,3,2:T(8,128)(2,1)S(1)}, u32[]{:S(2)}, u32[]{:S(2)}) collective-permute-start(bf16[64,73,1,16]{1,0,3,2:T(8,128)(2,1)S(1)} %get-tuple-element.172), channel_id=1, source_target_pairs={{0,1},{1,2},{2,3},{4,5},{5,6},{6,7},{8,9},{9,10},{10,11},{12,13},{... | collective-permute-start | bytes 448520 | tf_op jit(solution)/shard_map/ppermute | solution.py:17
  (55 other events, 162.5 us)
Sparse Core Ops, SparseCore 0:
  109.5 89.1 all-reduce.7
  202.6 91.8 all-reduce.5
where the time goes:
time: 313 us; the launch traced here: 310 us
  waiting for transfers between devices  188 us (60%)
  matrix products  58.5 us (19%)
  local copies, waits for them, and re-layouts  22.2 us (7%)
  starting transfers between devices  20.4 us (7%)
  between operations  14.6 us (5%)
  other arithmetic  5.08 us (2%)
    psum x2, waiting for transfers between devices, body(): lax.psum((g_conv, g_gain, g_query, g_key, g_value, g_out), ('view', 'row'))  163 us
    dot_general x59, matrix products, product(): return jnp.einsum(form, left, right, preferred_element_type=jnp.float32)  52.2 us
    unnamed x48, local copies, waits for them, and re-layouts  12.5 us
    all_to_all x1, waiting for transfers between devices, body(): lax.all_to_all(spatial.reshape(channels, view_dev, row_dev, blocks, bread...  11.2 us
    ppermute x2, starting transfers between devices, with_halo(): lax.ppermute(tail, axis, [(i, (i + 1) % count) for i in range(ends)])  8.14 us
  transfers between devices with their start and end apart: 8, of which 8 were waited for; matrix products, arithmetic and copies ran while one was open for 4% of the time, Pallas kernels for 0%

commit v1 on v0

v1 whole, which is shorter than its diff:
```python
import functools
import math

import jax
import jax.numpy as jnp
from jax import lax
from jax.experimental import pallas as pl
from jax.experimental.pallas import tpu as pltpu
from jax.sharding import PartitionSpec as P

F32 = jnp.float32
BF16 = jnp.bfloat16


def round_up(value, unit):
    return -(-value // unit) * unit


def swap(cells, axis, step):
    count = lax.axis_size(axis)
    return lax.ppermute(cells, axis, [(i, i ^ step) for i in range(count)])


def row_halo(first, last):
    count = lax.axis_size("row")
    index = lax.axis_index("row")
    even = lax.rem(index, 2) == 0
    if count % 2:
        above = lax.ppermute(last, "row", [(i, i + 1) for i in range(count - 1)])
        below = lax.ppermute(first, "row", [(i + 1, i) for i in range(count - 1)])
        return above, below
    near = lax.ppermute(
        jnp.where(even, last, first), "row", [(i, i ^ 1) for i in range(count)]
    )
    pairs = []
    for i in range(1, count - 1, 2):
        pairs += [(i, i + 1), (i + 1, i)]
    if pairs:
        far = lax.ppermute(jnp.where(even, first, last), "row", pairs)
    else:
        far = jnp.zeros_like(near)
    return jnp.where(even, far, near), jnp.where(even, near, far)


def dot(left, right, contract=(1, 0)):
    return lax.dot_general(
        left, right, (((contract[0],), (contract[1],)), ((), ())), preferred_element_type=F32
    )


def angular_kernel(
    scale,
    x_ref,
    cot_ref,
    bias_ref,
    gain_ref,
    wqkv_ref,
    wk_ref,
    wv_ref,
    wo_ref,
    wot_ref,
    wcat_ref,
    out_ref,
    ds_ref,
    g_ref,
    ggain_ref,
    e_s,
    g_s,
    gain_s,
):
    pixels, chan, lanes = x_ref.shape
    rows = bias_ref.shape[0]
    e_s[...] = jnp.zeros_like(e_s)
    g_s[...] = jnp.zeros_like(g_s)
    g_ref[...] = jnp.zeros_like(g_ref)
    gain_s[...] = jnp.zeros_like(gain_s)
    inv_chan = 1.0 / chan

    def pixel(p, carry):
        gain = gain_ref[...]
        s = x_ref[p].astype(F32)
        cen = s - jnp.sum(s, axis=0, keepdims=True) * inv_chan
        rstd = lax.rsqrt(jnp.sum(cen * cen, axis=0, keepdims=True) * inv_chan + 1e-05)
        normed = cen * rstd
        nin32 = normed * gain
        nin = nin32.astype(BF16)
        qkv = dot(wqkv_ref[...], nin)
        q = (qkv[:chan].astype(BF16).astype(F32) * scale).astype(BF16)
        k = qkv[chan : 2 * chan].astype(BF16)
        v = qkv[2 * chan :].astype(BF16)
        nin_t = jnp.transpose(nin32)[:rows].astype(BF16)
        k_t = dot(nin_t, wk_ref[...]).astype(BF16)
        v_t = dot(nin_t, wv_ref[...]).astype(BF16)
        sc = dot(k_t, q) + bias_ref[...]
        e = jnp.exp(sc - jnp.max(sc, axis=0, keepdims=True))
        e_s[:rows] = e.astype(BF16)
        v_aug = jnp.concatenate([v, jnp.ones((16, lanes), BF16)], axis=0)
        att_aug = dot(v_aug, e_s[...])
        inv = 1.0 / att_aug[chan : chan + 1]
        att = att_aug[:chan] * inv
        att_b = att.astype(BF16)
        cot = cot_ref[p]
        out_ref[p] = (s + dot(wot_ref[...], att_b)).astype(BF16)
        d_att = dot(wo_ref[...], cot).astype(BF16).astype(F32)
        d_att = (d_att * inv).astype(BF16)
        inner = jnp.sum(att * d_att.astype(F32), axis=0, keepdims=True)
        dp = dot(v_t, d_att)
        g_s[:rows] = (e * (dp - inner)).astype(BF16)
        d_v = dot(d_att, e_s[...], (1, 1)).astype(BF16)
        d_q = (dot(k, g_s[...]) * scale).astype(BF16)
        d_k = dot(q, g_s[...], (1, 1)).astype(BF16)
        d_qkv = jnp.concatenate([d_q, d_k, d_v], axis=0)
        dn = dot(wcat_ref[...], d_qkv)
        g_ref[:chan] += dot(nin, d_qkv[: 2 * chan], (1, 1))
        both = dot(
            jnp.concatenate([nin, att_b], axis=0), jnp.concatenate([d_v, cot], axis=0), (1, 1)
        )
        lane = lax.broadcasted_iota(jnp.int32, (chan, 2 * chan), 1)
        g_ref[chan:] += jnp.where(lane < chan, both[:chan], both[chan:])
        gain_s[...] += dn * normed
        scaled = dn * gain
        back = (
            scaled
            - jnp.sum(scaled, axis=0, keepdims=True) * inv_chan
            - normed * (jnp.sum(scaled * normed, axis=0, keepdims=True) * inv_chan)
        )
        ds_ref[p] = (cot.astype(F32) + back * rstd).astype(BF16)
        return carry

    lax.fori_loop(0, pixels, pixel, 0)
    ggain_ref[...] = jnp.sum(gain_s[...], axis=1, keepdims=True)


def angular(moved, cotangent, keep, gain, w_query, w_key, w_value, w_out):
    pixels, chan, lanes = moved.shape
    used = keep.shape[0]
    rows = round_up(used, 16)
    bias = jnp.where(keep > 0, 0.0, -1e30).astype(F32)
    bias = jnp.pad(bias, (0, rows - used), constant_values=-1e30)[:, None]
    vmem = pl.BlockSpec(memory_space=pltpu.VMEM)
    scale = 1.0 / math.sqrt(chan)
    return pl.pallas_call(
        functools.partial(angular_kernel, scale),
        out_shape=(
            jax.ShapeDtypeStruct((pixels, chan, lanes), BF16),
            jax.ShapeDtypeStruct((pixels, chan, lanes), BF16),
            jax.ShapeDtypeStruct((2 * chan, 2 * chan), F32),
            jax.ShapeDtypeStruct((chan, 1), F32),
        ),
        in_specs=[vmem] * 10,
        out_specs=(vmem,) * 4,
        scratch_shapes=[
            pltpu.VMEM((lanes, lanes), BF16),
            pltpu.VMEM((lanes, lanes), BF16),
            pltpu.VMEM((chan, lanes), F32),
        ],
        name="angular",
    )(
        moved,
        cotangent,
        bias,
        gain[:, None],
        jnp.concatenate([w_query, w_key, w_value], axis=1).T,
        w_key,
        w_value,
        w_out,
        w_out.T,
        jnp.concatenate([w_query, w_key, w_value], axis=1),
    )


def product(form, left, right):
    return jnp.einsum(form, left, right, preferred_element_type=F32)


def convolve(padded, w_conv):
    height = padded.shape[2] - 2
    breadth = padded.shape[3] - 2
    total = jnp.zeros((w_conv.shape[0], padded.shape[1], height, breadth), F32)
    for row_tap in range(3):
        for col_tap in range(3):
            window = padded[:, :, row_tap : row_tap + height, col_tap : col_tap + breadth]
            total = total + product("oc,cvrw->ovrw", w_conv[:, :, row_tap, col_tap], window)
    return total


def input_grad(grad_pad, w_conv):
    height = grad_pad.shape[2] - 2
    breadth = grad_pad.shape[3] - 2
    total = jnp.zeros((w_conv.shape[1], grad_pad.shape[1], height, breadth), F32)
    for row_tap in range(3):
        for col_tap in range(3):
            window = grad_pad[
                :, :, 2 - row_tap : 2 - row_tap + height, 2 - col_tap : 2 - col_tap + breadth
            ]
            total = total + product("oc,ovrw->cvrw", w_conv[:, :, row_tap, col_tap], window)
    return total


def weight_grad(grad, padded):
    height = grad.shape[2]
    breadth = grad.shape[3]
    taps = []
    for row_tap in range(3):
        for col_tap in range(3):
            window = padded[:, :, row_tap : row_tap + height, col_tap : col_tap + breadth]
            taps.append(product("ovrw,cvrw->oc", grad, window))
    return jnp.stack(taps, axis=0)


def exchange(blocks, axis):
    count = blocks.shape[0]
    if count > 8 or count & (count - 1):
        return lax.all_to_all(blocks, axis, split_axis=0, concat_axis=0, tiled=True)
    index = lax.axis_index(axis)
    got = []
    for step in range(count):
        block = lax.dynamic_index_in_dim(blocks, index ^ step, keepdims=False)
        got.append(block if step == 0 else swap(block, axis, step))
    level = 1
    while level < count:
        odd = (index & level) > 0
        got = [jnp.where(odd, got[i ^ level], got[i]) for i in range(count)]
        level *= 2
    return jnp.stack(got)


def reduce_all(part):
    rows_axis, views_axis = lax.axis_size("row"), lax.axis_size("view")
    if rows_axis != 4 or views_axis > 8 or views_axis & (views_axis - 1):
        return lax.psum(part, ("view", "row"))
    half = part.shape[0] // 2
    odd = (lax.axis_index("row") & 1) > 0
    low, high = part[:half], part[half:]
    own = jnp.where(odd, high, low) + swap(jnp.where(odd, low, high), "row", 1)
    own = own + swap(own, "row", 2)
    total = own
    for step in range(1, views_axis):
        total = total + swap(own, "view", step)
    other = swap(total, "row", 1)
    return jnp.concatenate([jnp.where(odd, other, total), jnp.where(odd, total, other)])


def body(inputs, cotangent, keep, w_conv, gain, w_query, w_key, w_value, w_out):
    chan, view_dev, row_dev, width = inputs.shape
    blocks = lax.axis_size("view")
    breadth = width // blocks
    views = view_dev * blocks
    lanes = round_up(views, 128)
    pixels = row_dev * breadth
    above, below = row_halo(inputs[:, :, :1], inputs[:, :, row_dev - 1 :])
    padded = jnp.concatenate([above, inputs, below], axis=2)
    padded = jnp.pad(padded, ((0, 0), (0, 0), (0, 0), (1, 1)))
    spatial = (inputs.astype(F32) + convolve(padded, w_conv)).astype(BF16)
    out_blocks = spatial.reshape(chan, view_dev, row_dev, blocks, breadth)
    out_blocks = jnp.transpose(out_blocks, (3, 2, 4, 0, 1))
    got = exchange(out_blocks.reshape(blocks, pixels, chan, view_dev), "view")
    moved = jnp.transpose(got, (1, 2, 0, 3)).reshape(pixels, chan, views)
    moved = jnp.pad(moved, ((0, 0), (0, 0), (0, lanes - views)))
    cot = jnp.transpose(cotangent, (2, 3, 0, 1)).reshape(pixels, chan, views)
    cot = jnp.pad(cot, ((0, 0), (0, 0), (0, lanes - views)))
    output, d_spatial, g_weights, g_gain = angular(
        moved, cot, keep, gain, w_query, w_key, w_value, w_out
    )
    output = output[:, :, :views].reshape(row_dev, breadth, chan, views)
    output = jnp.transpose(output, (2, 3, 0, 1))
    back = d_spatial[:, :, :views].reshape(pixels, chan, blocks, view_dev)
    back = exchange(jnp.transpose(back, (2, 0, 1, 3)), "view")
    back = back.reshape(blocks, row_dev, breadth, chan, view_dev)
    returned = jnp.transpose(back, (3, 4, 1, 0, 2)).reshape(chan, view_dev, row_dev, width)
    above, below = row_halo(returned[:, :, :1], returned[:, :, row_dev - 1 :])
    grad_pad = jnp.concatenate([above, returned, below], axis=2)
    grad_pad = jnp.pad(grad_pad, ((0, 0), (0, 0), (0, 0), (1, 1)))
    d_input = (returned.astype(F32) + input_grad(grad_pad, w_conv)).astype(BF16)
    packed = jnp.concatenate(
        [g_weights, jnp.pad(g_gain.reshape(1, chan), ((0, 15), (0, chan)))], axis=0
    )
    packed = reduce_all(packed)
    g_conv = weight_grad(returned, padded)
    g_conv = reduce_all(g_conv.reshape(-1, 2 * chan)).reshape(3, 3, chan, chan)
    g_conv = jnp.transpose(g_conv, (2, 3, 0, 1))
    return (
        output,
        d_input,
        g_conv,
        packed[2 * chan, :chan],
        packed[:chan, :chan],
        packed[:chan, chan:],
        packed[chan : 2 * chan, :chan],
        packed[chan : 2 * chan, chan:],
    )


def solution(mesh):
    placed = (
        P(None, "view", ("groups", "row"), None),
        P(None, None, ("groups", "row"), "view"),
        P("groups"),
        P(),
        P(),
        P(),
        P(),
        P(),
        P(),
    )
    return jax.shard_map(
        body,
        mesh=mesh,
        in_specs=placed,
        out_specs=(
            P(None, None, ("groups", "row"), "view"),
            P(None, "view", ("groups", "row"), None),
            P("groups", None, None, None),
            P("groups"),
            P("groups", None),
            P("groups", None),
            P("groups", None),
            P("groups", None),
        ),
        check_vma=False,
    )
```

time: 313 us -> 98.1 us (0.31)
  waiting for transfers between devices: 188 us -> 15.9 us
  matrix products: 58.5 us -> 14.4 us
  Pallas kernels: 0 us -> 15.1 us
  between operations: 14.6 us -> 1.19 us
  starting transfers between devices: 20.4 us -> 30.2 us
  local copies, waits for them, and re-layouts: 22.2 us -> 14.5 us
    psum x2 -> x0, waiting for transfers between devices: 163 us -> none  [body(): lax.psum((g_conv, g_gain, g_query, g_key, g_value, g_out), ('view', 'row'))]
    dot_general x59 -> x27, matrix products: 52.2 us -> 14.4 us  [product(): return jnp.einsum(form, left, right, preferred_element_type=F32)]
    ppermute x4 -> x22, starting transfers between devices: 12 us -> 30.2 us  [the longest x18 23 us: swap(): return lax.ppermute(cells, axis, [(i, i ^ step) for i in range(count)])]
    all_to_all x2 -> x0, waiting for transfers between devices: 17.1 us -> none  [the longest x1 11.2 us: body(): lax.all_to_all(spatial.reshape(channels, view_dev, row_dev, blocks, bread...]
    pallas_call x0 -> x1, Pallas kernels: none -> 15.1 us  [angular(): pl.pallas_call(functools.partial(angular_kernel, scale), out_shape=(jax.S...]
    unnamed x48 -> x30, local copies, waits for them, and re-layouts: 12.5 us -> 3.85 us
    ppermute x4 -> x22, waiting for transfers between devices: 7.42 us -> 15.9 us  [the longest x18 15.9 us: swap(): return lax.ppermute(cells, axis, [(i, i ^ step) for i in range(count)])]
    all_to_all x2 -> x0, starting transfers between devices: 8.17 us -> none  [the longest x1 4.71 us: body(): lax.all_to_all(spatial.reshape(channels, view_dev, row_dev, blocks, bread...]
  transfers between devices with their start and end apart: 8 -> 22, of which waited for: 8 -> 6; matrix products, arithmetic and copies ran while one was open for 4% -> 26% of each run, Pallas kernels for 0% -> 0%
where the time goes in v1:
time: 98.1 us; the launch traced here: 97.6 us
  starting transfers between devices  30.2 us (31%)
  waiting for transfers between devices  15.9 us (16%)
  Pallas kernels  15.1 us (15%)
  local copies, waits for them, and re-layouts  14.5 us (15%)
  matrix products  14.4 us (15%)
  other arithmetic  6.23 us (6%)
  between operations  1.19 us (1%)
    ppermute x18, starting transfers between devices, swap(): return lax.ppermute(cells, axis, [(i, i ^ step) for i in range(count)])  23 us
    ppermute x18, waiting for transfers between devices, swap(): return lax.ppermute(cells, axis, [(i, i ^ step) for i in range(count)])  15.9 us
    pallas_call x1, Pallas kernels, angular(): pl.pallas_call(functools.partial(angular_kernel, scale), out_shape=(jax.S...  15.1 us
    dot_general x27, matrix products, product(): return jnp.einsum(form, left, right, preferred_element_type=F32)  14.4 us
    ppermute x2, starting transfers between devices, row_halo(): far = lax.ppermute(jnp.where(even, first, last), 'row', pairs)  7.08 us
    unnamed x30, local copies, waits for them, and re-layouts  3.85 us
  transfers between devices with their start and end apart: 22, of which 6 were waited for; matrix products, arithmetic and copies ran while one was open for 26% of the time, Pallas kernels for 0%

profile of v1, /device:TPU:1, one launch (start us, length us, event | category | flops | bytes accessed | tf_op | source)
XLA Modules:
  0.0 97.6 jit_solution(174755023544619257)
XLA Ops:
  0.6 1.3 %copy.47 = bf16[64,73,2,16]{1,0,3,2:T(8,128)(2,1)S(1)} copy(bf16[64,73,2,16]{1,3,2,0:T(8,128)(2,1)} %param.9) | data formatting | bytes 598016 | tf_op args[0]
  2.1 4.6 %collective-permute-start = (bf16[64,73,1,16]{1,0,3,2:T(8,128)(2,1)S(1)}, bf16[64,73,1,16]{1,0,3,2:T(8,128)(2,1)S(1)}, u32[]{:S(2)}, u32[]{:S(2)}) collective-permute-start(bf16[64,73,1,16]{1,0,3,2:T(8,128)(2,1)S(1)} %get-tuple-element.55), channel_id=1, source_target_pairs={{1,2},{2,1},{5,6},{6,5},{9,10},{10,9},{13,14},{14,13},{17,18},{18,... | collective-permute-start | bytes 448520 | tf_op jit(solution)/shard_map/ppermute | solution.py:39
  13.7 3.4 %collective-permute-start.2 = (bf16[8,64,73]{2,1,0:T(8,128)(2,1)S(1)}, bf16[8,64,73]{2,1,0:T(8,128)(2,1)S(1)}, u32[]{:S(2)}, u32[]{:S(2)}) collective-permute-start(bf16[8,64,73]{2,1,0:T(8,128)(2,1)S(1)} %get-tuple-element.52), channel_id=1, source_target_pairs={{0,12},{4,8},{8,4},{12,0},{1,13},{5,9},{9,5},{13,1},{2,14},{6,10},... | collective-permute-start | bytes 224264 | tf_op jit(solution)/shard_map/ppermute | solution.py:21
  18.1 2.2 %collective-permute-done.2 = bf16[8,64,73]{2,1,0:T(8,128)(2,1)S(1)} collective-permute-done((bf16[8,64,73]{2,1,0:T(8,128)(2,1)S(1)}, bf16[8,64,73]{2,1,0:T(8,128)(2,1)S(1)}, u32[]{:S(2)}, u32[]{:S(2)}) %collective-permute-start.2) | collective-permute-done | bytes 74784 | tf_op jit(solution)/shard_map/ppermute | solution.py:21
  20.3 7.5 %collective-permute-done.3 = bf16[8,64,73]{2,1,0:T(8,128)(2,1)S(1)} collective-permute-done((bf16[8,64,73]{2,1,0:T(8,128)(2,1)S(1)}, bf16[8,64,73]{2,1,0:T(8,128)(2,1)S(1)}, u32[]{:S(2)}, u32[]{:S(2)}) %collective-permute-start.3) | collective-permute-done | bytes 74784 | tf_op jit(solution)/shard_map/ppermute | solution.py:21
  29.6 15.1 %angular.1 = (bf16[8,64,384]{2,1,0:T(8,128)(2,1)}, bf16[8,64,384]{2,1,0:T(8,128)(2,1)}, f32[128,128]{1,0:T(8,128)}, f32[64,1]{1,0:T(8,128)}) custom-call(bf16[8,64,384]{2,1,0:T(8,128)(2,1)} %pad.23.x_ref, bf16[8,64,384]{2,1,0:T(8,128)(2,1)} %pad.24.cot_ref, f32[304,1]{1,0:T(8,128)} %broadcast_in_dim.18.bias_ref, f32[64,1]{1,0:T(8,128)} %copy.59.gain_ref, ...), custom_call_target="tpu_custom_call" | custom-call | tf_op jit(solution)/shard_map/angular/pallas_call | solution.py:142
  46.3 1.3 %collective-permute-start.16 = (f32[72,128]{1,0:T(8,128)S(1)}, f32[72,128]{1,0:T(8,128)S(1)}, u32[]{:S(2)}, u32[]{:S(2)}) collective-permute-start(f32[72,128]{1,0:T(8,128)S(1)} %slice_select_fusion.1), channel_id=1, source_target_pairs={{0,1},{1,0},{2,3},{3,2},{4,5},{5,4},{6,7},{7,6},{8,9},{9,8},{10,11... | collective-permute-start | bytes 110600 | tf_op jit(solution)/shard_map/ppermute | solution.py:21
  47.7 1.3 %reshape.68 = bf16[8,64,4,73]{3,2,1,0:T(4,128)(2,1)S(1)} reshape(bf16[8,64,292]{2,1,0:T(8,128)(2,1)} %bitcast.281) | data formatting | bytes 598016 | tf_op jit(solution)/shard_map/reshape | solution.py:267
  49.0 1.2 %constant_dynamic-slice_fusion = (bf16[8,64,1,73]{3,2,1,0:T(2,128)(2,1)S(1)}, bf16[8,64,1,73]{3,2,1,0:T(2,128)(2,1)S(1)}, bf16[8,64,1,73]{3,2,1,0:T(2,128)(2,1)S(1)}, bf16[8,64,1,73]{3,2,1,0:T(2,128)(2,1)S(1)}) fusion(bf16[8,64,4,73]{3,2,1,0:T(4,128)(2,1)S(1)} %reshape.68, s32[]{:T(128)S(6)} %select_n.178, s32[]{:T(128)S(6)} %select_n.177, ...), kind=kLoop, calls=%fused_computation.150 | loop fusion | bytes 598032 | tf_op jit(solution)/shard_map/dynamic-slice.3
  50.3 2.3 %collective-permute-start.5 = (bf16[8,64,73]{2,1,0:T(8,128)(2,1)S(1)}, bf16[8,64,73]{2,1,0:T(8,128)(2,1)S(1)}, u32[]{:S(2)}, u32[]{:S(2)}) collective-permute-start(bf16[8,64,73]{2,1,0:T(8,128)(2,1)S(1)} %bitcast.287), channel_id=1, source_target_pairs={{0,12},{4,8},{8,4},{12,0},{1,13},{5,9},{9,5},{13,1},{2,14},{6,10},... | collective-permute-start | bytes 224264 | tf_op jit(solution)/shard_map/ppermute | solution.py:21
  52.7 1.4 %collective-permute-start.7 = (bf16[8,64,73]{2,1,0:T(8,128)(2,1)S(1)}, bf16[8,64,73]{2,1,0:T(8,128)(2,1)S(1)}, u32[]{:S(2)}, u32[]{:S(2)}) collective-permute-start(bf16[8,64,73]{2,1,0:T(8,128)(2,1)S(1)} %bitcast.288), channel_id=1, source_target_pairs={{0,4},{4,0},{8,12},{12,8},{1,5},{5,1},{9,13},{13,9},{2,6},{6,2},{1... | collective-permute-start | bytes 224264 | tf_op jit(solution)/shard_map/ppermute | solution.py:21
  55.1 1.1 %copy.137 = bf16[2,4,64,292]{3,1,0,2:T(4,128)(2,1)} copy(bf16[2,4,64,292]{3,2,1,0:T(8,128)(2,1)S(1)} %bitcast.284) | data formatting | bytes 598016 | tf_op jit(solution)/shard_map/reshape | solution.py:265
  56.1 1.1 %collective-permute-done.17 = f32[72,128]{1,0:T(8,128)S(1)} collective-permute-done((f32[72,128]{1,0:T(8,128)S(1)}, f32[72,128]{1,0:T(8,128)S(1)}, u32[]{:S(2)}, u32[]{:S(2)}) %collective-permute-start.17) | collective-permute-done | bytes 36896 | tf_op jit(solution)/shard_map/ppermute | solution.py:21
  58.0 2.3 %collective-permute-start.19 = (f32[72,128]{1,0:T(8,128)}, f32[72,128]{1,0:T(8,128)}, u32[]{:S(2)}, u32[]{:S(2)}) collective-permute-start(f32[72,128]{1,0:T(8,128)} %add.154), channel_id=1, source_target_pairs={{0,8},{4,12},{8,0},{12,4},{1,9},{5,13},{9,1},{13,5},{2,10},{6,14},... | collective-permute-start | bytes 110600 | tf_op jit(solution)/shard_map/ppermute | solution.py:21
  60.4 1.1 %collective-permute-start.20 = (f32[72,128]{1,0:T(8,128)}, f32[72,128]{1,0:T(8,128)}, u32[]{:S(2)}, u32[]{:S(2)}) collective-permute-start(f32[72,128]{1,0:T(8,128)} %add.154), channel_id=1, source_target_pairs={{0,12},{4,8},{8,4},{12,0},{1,13},{5,9},{9,5},{13,1},{2,14},{6,10},... | collective-permute-start | bytes 110600 | tf_op jit(solution)/shard_map/ppermute | solution.py:21
  61.4 2.0 %collective-permute-done.6 = bf16[8,64,73]{2,1,0:T(8,128)(2,1)S(1)} collective-permute-done((bf16[8,64,73]{2,1,0:T(8,128)(2,1)S(1)}, bf16[8,64,73]{2,1,0:T(8,128)(2,1)S(1)}, u32[]{:S(2)}, u32[]{:S(2)}) %collective-permute-start.6) | collective-permute-done | bytes 74784 | tf_op jit(solution)/shard_map/ppermute | solution.py:21
  73.0 1.1 %reshape.70 = f32[288,128]{1,0:T(8,128)S(1)} reshape(f32[9,64,64]{2,1,0:T(8,128)} %fusion.19) | data formatting | bytes 294912 | tf_op jit(solution)/shard_map/reshape | solution.py:280
  76.0 2.5 %collective-permute-start.8 = (bf16[64,73,1,16]{1,0,3,2:T(8,128)(2,1)S(1)}, bf16[64,73,1,16]{1,0,3,2:T(8,128)(2,1)S(1)}, u32[]{:S(2)}, u32[]{:S(2)}) collective-permute-start(bf16[64,73,1,16]{1,0,3,2:T(8,128)(2,1)S(1)} %copy-done.5), channel_id=1, source_target_pairs={{1,2},{2,1},{5,6},{6,5},{9,10},{10,9},{13,14},{14,13},{17,18},{18,... | collective-permute-start | bytes 448520 | tf_op jit(solution)/shard_map/ppermute | solution.py:39
  79.3 1.5 %collective-permute-start.11 = (f32[144,128]{1,0:T(8,128)S(1)}, f32[144,128]{1,0:T(8,128)S(1)}, u32[]{:S(2)}, u32[]{:S(2)}) collective-permute-start(f32[144,128]{1,0:T(8,128)S(1)} %select_add_fusion), channel_id=1, source_target_pairs={{0,2},{1,3},{2,0},{3,1},{4,6},{5,7},{6,4},{7,5},{8,10},{9,11},{10,... | collective-permute-start | bytes 221192 | tf_op jit(solution)/shard_map/ppermute | solution.py:21
  81.4 2.0 %collective-permute-done.11 = f32[144,128]{1,0:T(8,128)S(1)} collective-permute-done((f32[144,128]{1,0:T(8,128)S(1)}, f32[144,128]{1,0:T(8,128)S(1)}, u32[]{:S(2)}, u32[]{:S(2)}) %collective-permute-start.11) | collective-permute-done | bytes 73760 | tf_op jit(solution)/shard_map/ppermute | solution.py:21
  83.8 1.9 %collective-permute-start.13 = (f32[144,128]{1,0:T(8,128)S(1)}, f32[144,128]{1,0:T(8,128)S(1)}, u32[]{:S(2)}, u32[]{:S(2)}) collective-permute-start(f32[144,128]{1,0:T(8,128)S(1)} %add.149), channel_id=1, source_target_pairs={{0,8},{4,12},{8,0},{12,4},{1,9},{5,13},{9,1},{13,5},{2,10},{6,14},... | collective-permute-start | bytes 221192 | tf_op jit(solution)/shard_map/ppermute | solution.py:21
  85.7 1.4 %collective-permute-start.14 = (f32[144,128]{1,0:T(8,128)S(1)}, f32[144,128]{1,0:T(8,128)S(1)}, u32[]{:S(2)}, u32[]{:S(2)}) collective-permute-start(f32[144,128]{1,0:T(8,128)S(1)} %add.149), channel_id=1, source_target_pairs={{0,12},{4,8},{8,4},{12,0},{1,13},{5,9},{9,5},{13,1},{2,14},{6,10},... | collective-permute-start | bytes 221192 | tf_op jit(solution)/shard_map/ppermute | solution.py:21
  90.7 4.3 %collective-permute-start.15 = (f32[144,128]{1,0:T(8,128)S(1)}, f32[144,128]{1,0:T(8,128)S(1)}, u32[]{:S(2)}, u32[]{:S(2)}) collective-permute-start(f32[144,128]{1,0:T(8,128)S(1)} %add_add_fusion), channel_id=1, source_target_pairs={{0,1},{1,0},{2,3},{3,2},{4,5},{5,4},{6,7},{7,6},{8,9},{9,8},{10,11... | collective-permute-start | bytes 221192 | tf_op jit(solution)/shard_map/ppermute | solution.py:21
  95.6 1.1 %copy.80 = bf16[64,73,2,16]{1,3,2,0:T(8,128)(2,1)} copy(bf16[64,73,2,16]{1,0,3,2:T(8,128)(2,1)S(1)} %fusion.18) | data formatting | bytes 598016
  (121 shorter events, 31.5 us)
Async XLA Ops:
  2.1 8.6 %copy-start = (bf16[64,73,2,16]{1,3,2,0:T(8,128)(2,1)S(1)}, bf16[64,73,2,16]{1,3,2,0:T(8,128)(2,1)}, u32[]{:S(2)}) copy-start(bf16[64,73,2,16]{1,3,2,0:T(8,128)(2,1)} %param.9) | copy-start | bytes 897028
  2.1 8.6 %copy-start.2 = (bf16[64,64,3,3]{1,0,3,2:T(8,128)(2,1)S(1)}, bf16[64,64,3,3]{1,0,3,2:T(8,128)(2,1)}, u32[]{:S(2)}) copy-start(bf16[64,64,3,3]{1,0,3,2:T(8,128)(2,1)} %param.12) | copy-start | bytes 221188
  2.1 8.9 %collective-permute-start = (bf16[64,73,1,16]{1,0,3,2:T(8,128)(2,1)S(1)}, bf16[64,73,1,16]{1,0,3,2:T(8,128)(2,1)S(1)}, u32[]{:S(2)}, u32[]{:S(2)}) collective-permute-start(bf16[64,73,1,16]{1,0,3,2:T(8,128)(2,1)S(1)} %get-tuple-element.55), channel_id=1, source_target_pairs={{1,2},{2,1},{5,6},{6,5},{9,10},{10,9},{13,14},{14,13},{17,18},{18,... | collective-permute-start | bytes 448520 | tf_op jit(solution)/shard_map/ppermute | solution.py:39
  6.7 4.3 %collective-permute-start.1 = (bf16[64,73,1,16]{1,0,3,2:T(8,128)(2,1)S(1)}, bf16[64,73,1,16]{1,0,3,2:T(8,128)(2,1)S(1)}, u32[]{:S(2)}, u32[]{:S(2)}) collective-permute-start(bf16[64,73,1,16]{1,0,3,2:T(8,128)(2,1)S(1)} %get-tuple-element.56), channel_id=1, source_target_pairs={{0,1},{1,0},{2,3},{3,2},{4,5},{5,4},{6,7},{7,6},{8,9},{9,8},{10,11... | collective-permute-start | bytes 448520 | tf_op jit(solution)/shard_map/ppermute | solution.py:32
  13.7 6.6 %collective-permute-start.2 = (bf16[8,64,73]{2,1,0:T(8,128)(2,1)S(1)}, bf16[8,64,73]{2,1,0:T(8,128)(2,1)S(1)}, u32[]{:S(2)}, u32[]{:S(2)}) collective-permute-start(bf16[8,64,73]{2,1,0:T(8,128)(2,1)S(1)} %get-tuple-element.52), channel_id=1, source_target_pairs={{0,12},{4,8},{8,4},{12,0},{1,13},{5,9},{9,5},{13,1},{2,14},{6,10},... | collective-permute-start | bytes 224264 | tf_op jit(solution)/shard_map/ppermute | solution.py:21
  17.1 10.7 %collective-permute-start.3 = (bf16[8,64,73]{2,1,0:T(8,128)(2,1)S(1)}, bf16[8,64,73]{2,1,0:T(8,128)(2,1)S(1)}, u32[]{:S(2)}, u32[]{:S(2)}) collective-permute-start(bf16[8,64,73]{2,1,0:T(8,128)(2,1)S(1)} %get-tuple-element.51), channel_id=1, source_target_pairs={{0,8},{4,12},{8,0},{12,4},{1,9},{5,13},{9,1},{13,5},{2,10},{6,14},... | collective-permute-start | bytes 224264 | tf_op jit(solution)/shard_map/ppermute | solution.py:21
  17.1 10.7 %collective-permute-start.4 = (bf16[8,64,73]{2,1,0:T(8,128)(2,1)S(1)}, bf16[8,64,73]{2,1,0:T(8,128)(2,1)S(1)}, u32[]{:S(2)}, u32[]{:S(2)}) collective-permute-start(bf16[8,64,73]{2,1,0:T(8,128)(2,1)S(1)} %get-tuple-element.50), channel_id=1, source_target_pairs={{0,4},{4,0},{8,12},{12,8},{1,5},{5,1},{9,13},{13,9},{2,6},{6,2},{1... | collective-permute-start | bytes 224264 | tf_op jit(solution)/shard_map/ppermute | solution.py:21
  46.3 7.7 %collective-permute-start.16 = (f32[72,128]{1,0:T(8,128)S(1)}, f32[72,128]{1,0:T(8,128)S(1)}, u32[]{:S(2)}, u32[]{:S(2)}) collective-permute-start(f32[72,128]{1,0:T(8,128)S(1)} %slice_select_fusion.1), channel_id=1, source_target_pairs={{0,1},{1,0},{2,3},{3,2},{4,5},{5,4},{6,7},{7,6},{8,9},{9,8},{10,11... | collective-permute-start | bytes 110600 | tf_op jit(solution)/shard_map/ppermute | solution.py:21
  50.3 10.1 %collective-permute-start.5 = (bf16[8,64,73]{2,1,0:T(8,128)(2,1)S(1)}, bf16[8,64,73]{2,1,0:T(8,128)(2,1)S(1)}, u32[]{:S(2)}, u32[]{:S(2)}) collective-permute-start(bf16[8,64,73]{2,1,0:T(8,128)(2,1)S(1)} %bitcast.287), channel_id=1, source_target_pairs={{0,12},{4,8},{8,4},{12,0},{1,13},{5,9},{9,5},{13,1},{2,14},{6,10},... | collective-permute-start | bytes 224264 | tf_op jit(solution)/shard_map/ppermute | solution.py:21
  52.6 10.9 %collective-permute-start.6 = (bf16[8,64,73]{2,1,0:T(8,128)(2,1)S(1)}, bf16[8,64,73]{2,1,0:T(8,128)(2,1)S(1)}, u32[]{:S(2)}, u32[]{:S(2)}) collective-permute-start(bf16[8,64,73]{2,1,0:T(8,128)(2,1)S(1)} %bitcast.286), channel_id=1, source_target_pairs={{0,8},{4,12},{8,0},{12,4},{1,9},{5,13},{9,1},{13,5},{2,10},{6,14},... | collective-permute-start | bytes 224264 | tf_op jit(solution)/shard_map/ppermute | solution.py:21
  52.7 10.8 %collective-permute-start.7 = (bf16[8,64,73]{2,1,0:T(8,128)(2,1)S(1)}, bf16[8,64,73]{2,1,0:T(8,128)(2,1)S(1)}, u32[]{:S(2)}, u32[]{:S(2)}) collective-permute-start(bf16[8,64,73]{2,1,0:T(8,128)(2,1)S(1)} %bitcast.288), channel_id=1, source_target_pairs={{0,4},{4,0},{8,12},{12,8},{1,5},{5,1},{9,13},{13,9},{2,6},{6,2},{1... | collective-permute-start | bytes 224264 | tf_op jit(solution)/shard_map/ppermute | solution.py:21
  54.1 3.2 %collective-permute-start.17 = (f32[72,128]{1,0:T(8,128)S(1)}, f32[72,128]{1,0:T(8,128)S(1)}, u32[]{:S(2)}, u32[]{:S(2)}) collective-permute-start(f32[72,128]{1,0:T(8,128)S(1)} %select_add_fusion.1), channel_id=1, source_target_pairs={{0,2},{1,3},{2,0},{3,1},{4,6},{5,7},{6,4},{7,5},{8,10},{9,11},{10,... | collective-permute-start | bytes 110600 | tf_op jit(solution)/shard_map/ppermute | solution.py:21
  57.9 16.2 %collective-permute-start.18 = (f32[72,128]{1,0:T(8,128)}, f32[72,128]{1,0:T(8,128)}, u32[]{:S(2)}, u32[]{:S(2)}) collective-permute-start(f32[72,128]{1,0:T(8,128)} %add.154), channel_id=1, source_target_pairs={{0,4},{4,0},{8,12},{12,8},{1,5},{5,1},{9,13},{13,9},{2,6},{6,2},{1... | collective-permute-start | bytes 110600 | tf_op jit(solution)/shard_map/ppermute | solution.py:21
  58.0 16.1 %collective-permute-start.19 = (f32[72,128]{1,0:T(8,128)}, f32[72,128]{1,0:T(8,128)}, u32[]{:S(2)}, u32[]{:S(2)}) collective-permute-start(f32[72,128]{1,0:T(8,128)} %add.154), channel_id=1, source_target_pairs={{0,8},{4,12},{8,0},{12,4},{1,9},{5,13},{9,1},{13,5},{2,10},{6,14},... | collective-permute-start | bytes 110600 | tf_op jit(solution)/shard_map/ppermute | solution.py:21
  60.4 13.7 %collective-permute-start.20 = (f32[72,128]{1,0:T(8,128)}, f32[72,128]{1,0:T(8,128)}, u32[]{:S(2)}, u32[]{:S(2)}) collective-permute-start(f32[72,128]{1,0:T(8,128)} %add.154), channel_id=1, source_target_pairs={{0,12},{4,8},{8,4},{12,0},{1,13},{5,9},{9,5},{13,1},{2,14},{6,10},... | collective-permute-start | bytes 110600 | tf_op jit(solution)/shard_map/ppermute | solution.py:21
  75.0 3.6 %collective-permute-start.21 = (f32[72,128]{1,0:T(8,128)S(1)}, f32[72,128]{1,0:T(8,128)S(1)}, u32[]{:S(2)}, u32[]{:S(2)}) collective-permute-start(f32[72,128]{1,0:T(8,128)S(1)} %add_add_fusion.1), channel_id=1, source_target_pairs={{0,1},{1,0},{2,3},{3,2},{4,5},{5,4},{6,7},{7,6},{8,9},{9,8},{10,11... | collective-permute-start | bytes 110600 | tf_op jit(solution)/shard_map/ppermute | solution.py:21
  75.9 3.4 %collective-permute-start.10 = (f32[144,128]{1,0:T(8,128)S(1)}, f32[144,128]{1,0:T(8,128)S(1)}, u32[]{:S(2)}, u32[]{:S(2)}) collective-permute-start(f32[144,128]{1,0:T(8,128)S(1)} %slice_select_fusion), channel_id=1, source_target_pairs={{0,1},{1,0},{2,3},{3,2},{4,5},{5,4},{6,7},{7,6},{8,9},{9,8},{10,11... | collective-permute-start | bytes 221192 | tf_op jit(solution)/shard_map/ppermute | solution.py:21
  76.0 11.0 %collective-permute-start.8 = (bf16[64,73,1,16]{1,0,3,2:T(8,128)(2,1)S(1)}, bf16[64,73,1,16]{1,0,3,2:T(8,128)(2,1)S(1)}, u32[]{:S(2)}, u32[]{:S(2)}) collective-permute-start(bf16[64,73,1,16]{1,0,3,2:T(8,128)(2,1)S(1)} %copy-done.5), channel_id=1, source_target_pairs={{1,2},{2,1},{5,6},{6,5},{9,10},{10,9},{13,14},{14,13},{17,18},{18,... | collective-permute-start | bytes 448520 | tf_op jit(solution)/shard_map/ppermute | solution.py:39
  78.5 8.5 %collective-permute-start.9 = (bf16[64,73,1,16]{1,0,3,2:T(8,128)(2,1)S(1)}, bf16[64,73,1,16]{1,0,3,2:T(8,128)(2,1)S(1)}, u32[]{:S(2)}, u32[]{:S(2)}) collective-permute-start(bf16[64,73,1,16]{1,0,3,2:T(8,128)(2,1)S(1)} %get-tuple-element.45), channel_id=1, source_target_pairs={{0,1},{1,0},{2,3},{3,2},{4,5},{5,4},{6,7},{7,6},{8,9},{9,8},{10,11... | collective-permute-start | bytes 448520 | tf_op jit(solution)/shard_map/ppermute | solution.py:32
  79.3 4.1 %collective-permute-start.11 = (f32[144,128]{1,0:T(8,128)S(1)}, f32[144,128]{1,0:T(8,128)S(1)}, u32[]{:S(2)}, u32[]{:S(2)}) collective-permute-start(f32[144,128]{1,0:T(8,128)S(1)} %select_add_fusion), channel_id=1, source_target_pairs={{0,2},{1,3},{2,0},{3,1},{4,6},{5,7},{6,4},{7,5},{8,10},{9,11},{10,... | collective-permute-start | bytes 221192 | tf_op jit(solution)/shard_map/ppermute | solution.py:21
  83.4 6.3 %collective-permute-start.12 = (f32[144,128]{1,0:T(8,128)S(1)}, f32[144,128]{1,0:T(8,128)S(1)}, u32[]{:S(2)}, u32[]{:S(2)}) collective-permute-start(f32[144,128]{1,0:T(8,128)S(1)} %add.149), channel_id=1, source_target_pairs={{0,4},{4,0},{8,12},{12,8},{1,5},{5,1},{9,13},{13,9},{2,6},{6,2},{1... | collective-permute-start | bytes 221192 | tf_op jit(solution)/shard_map/ppermute | solution.py:21
  83.8 5.9 %collective-permute-start.13 = (f32[144,128]{1,0:T(8,128)S(1)}, f32[144,128]{1,0:T(8,128)S(1)}, u32[]{:S(2)}, u32[]{:S(2)}) collective-permute-start(f32[144,128]{1,0:T(8,128)S(1)} %add.149), channel_id=1, source_target_pairs={{0,8},{4,12},{8,0},{12,4},{1,9},{5,13},{9,1},{13,5},{2,10},{6,14},... | collective-permute-start | bytes 221192 | tf_op jit(solution)/shard_map/ppermute | solution.py:21
  85.7 5.0 %collective-permute-start.14 = (f32[144,128]{1,0:T(8,128)S(1)}, f32[144,128]{1,0:T(8,128)S(1)}, u32[]{:S(2)}, u32[]{:S(2)}) collective-permute-start(f32[144,128]{1,0:T(8,128)S(1)} %add.149), channel_id=1, source_target_pairs={{0,12},{4,8},{8,4},{12,0},{1,13},{5,9},{9,5},{13,1},{2,14},{6,10},... | collective-permute-start | bytes 221192 | tf_op jit(solution)/shard_map/ppermute | solution.py:21
  90.7 6.0 %collective-permute-start.15 = (f32[144,128]{1,0:T(8,128)S(1)}, f32[144,128]{1,0:T(8,128)S(1)}, u32[]{:S(2)}, u32[]{:S(2)}) collective-permute-start(f32[144,128]{1,0:T(8,128)S(1)} %add_add_fusion), channel_id=1, source_target_pairs={{0,1},{1,0},{2,3},{3,2},{4,5},{5,4},{6,7},{7,6},{8,9},{9,8},{10,11... | collective-permute-start | bytes 221192 | tf_op jit(solution)/shard_map/ppermute | solution.py:21
  (10 other events, 50.9 us)

commit v2 on v0

v2 whole, which is shorter than its diff:
```python
import functools
import math

import jax
import jax.numpy as jnp
from jax import lax
from jax.experimental import pallas as pl
from jax.experimental.pallas import tpu as pltpu
from jax.sharding import PartitionSpec as P

F32 = jnp.float32
BF16 = jnp.bfloat16


def round_up(value, unit):
    return -(-value // unit) * unit


def dot(left, right, contract=(1, 0)):
    return lax.dot_general(
        left, right, (((contract[0],), (contract[1],)), ((), ())), preferred_element_type=F32
    )


def pairwise(count):
    return count <= 8 and count & (count - 1) == 0


def swap(cells, axis, step):
    count = lax.axis_size(axis)
    return lax.ppermute(cells, axis, [(i, i ^ step) for i in range(count)])


def halo_swap(near, far):
    count = lax.axis_size("row")
    pairs = []
    for i in range(1, count - 1, 2):
        pairs += [(i, i + 1), (i + 1, i)]
    got_near = lax.ppermute(near, "row", [(i, i ^ 1) for i in range(count)])
    got_far = lax.ppermute(far, "row", pairs) if pairs else jnp.zeros_like(far)
    return got_near, got_far


def row_is_odd():
    return lax.rem(lax.axis_index("row"), 2)


def give(refs, held):
    if len(refs) == 1:
        refs[0][...] = held[...].astype(refs[0].dtype)
        return
    me = lax.axis_index("view")
    for step, ref in enumerate(refs):
        ref[...] = held[me ^ step].astype(ref.dtype)


def take(refs, held):
    if len(refs) == 1:
        held[...] = refs[0][...].astype(held.dtype)
        return
    me = lax.axis_index("view")
    for step, ref in enumerate(refs):
        held[me ^ step] = ref[...].astype(held.dtype)


def wire_shapes(blocks, chan, lanes):
    if pairwise(blocks):
        return [jax.ShapeDtypeStruct((chan, lanes), BF16)] * blocks
    return [jax.ShapeDtypeStruct((blocks, chan, lanes), BF16)]


def exchange(wires):
    if len(wires) == 1:
        return [lax.all_to_all(wires[0], "view", split_axis=0, concat_axis=0, tiled=True)]
    return [wires[0]] + [swap(wires[step], "view", step) for step in range(1, len(wires))]


def taps(w_ref, rows, forward):
    chan = w_ref.shape[2]
    blank = jnp.zeros((chan, chan), F32)
    found = {}
    for i in range(3):
        for j in range(3):
            tap = w_ref[i, j].astype(F32)
            found[i, j] = tap if forward else jnp.transpose(tap)
    bands = []
    for j in range(3):
        for r in range(rows):
            row = []
            for place in range(rows + 2):
                i = place - r if forward else r + 2 - place
                row.append(found[i, j] if 0 <= i < 3 else blank)
            bands.append(jnp.concatenate(row, axis=1))
    return jnp.concatenate(bands, axis=0).astype(BF16)


def spread(frame_ref, acc_ref, weights, rows, forward):
    width, deep, lanes = frame_ref.shape
    chan = deep // (rows + 2)
    size = rows * chan
    acc_ref[...] = jnp.zeros_like(acc_ref)

    def pair(q, carry):
        two = jnp.concatenate([frame_ref[2 * q], frame_ref[2 * q + 1]], axis=1)
        part = dot(weights, two)
        for j in range(3):
            move = 1 - j if forward else j - 1
            for side in range(2):
                acc_ref[2 * q + side + move + 1] += part[
                    j * size : (j + 1) * size, side * lanes : (side + 1) * lanes
                ]
        return carry

    lax.fori_loop(0, width // 2, pair, 0, unroll=width <= 16)


def conv_kernel(blocks, x_ref, near_ref, far_ref, w_ref, *refs):
    *wires, frame_ref, acc_s, held_s = refs
    width, own, views = x_ref.shape
    chan = near_ref.shape[1]
    rows = own // chan
    lanes = frame_ref.shape[2]
    odd = row_is_odd() > 0
    frame_ref[...] = jnp.zeros_like(frame_ref)

    def fill(w, carry):
        near, far = near_ref[w], far_ref[w]
        frame_ref[w, :chan, :views] = jnp.where(odd, near, far)
        frame_ref[w, chan : chan + own, :views] = x_ref[w]
        frame_ref[w, chan + own :, :views] = jnp.where(odd, far, near)
        return carry

    lax.fori_loop(0, width, fill, 0, unroll=width <= 16)
    weights = taps(w_ref, rows, True)
    spread(frame_ref, acc_s, weights, rows, True)
    breadth = width // blocks

    def block(b, carry):
        cells = []
        for r in range(rows):
            for k in range(breadth):
                w = b * breadth + k
                value = acc_s[w + 1, r * chan : (r + 1) * chan]
                value = value + frame_ref[w, (r + 1) * chan : (r + 2) * chan].astype(F32)
                cells.append(value[:, :views])
        cells = jnp.concatenate(cells, axis=1)
        held_s[b, :, : cells.shape[1]] = cells
        return carry

    lax.fori_loop(0, blocks, block, 0, unroll=blocks <= 4)
    give(wires, held_s)


def convolve(x, near, far, w_conv, blocks):
    width, own, views = x.shape
    chan = w_conv.shape[2]
    rows = own // chan
    lanes = round_up(views, 128)
    wire = round_up(rows * (width // blocks) * views, 128)
    vmem = pl.BlockSpec(memory_space=pltpu.VMEM)
    shapes = wire_shapes(blocks, chan, wire)
    shapes = shapes + [jax.ShapeDtypeStruct((width, own + 2 * chan, lanes), BF16)]
    *wires, frame = pl.pallas_call(
        functools.partial(conv_kernel, blocks),
        out_shape=shapes,
        in_specs=[vmem] * 4,
        out_specs=[vmem] * len(shapes),
        scratch_shapes=[
            pltpu.VMEM((width + 2, own, lanes), F32),
            pltpu.VMEM((blocks, chan, wire), F32),
        ],
        name="conv",
    )(x, near, far, w_conv)
    return wires, frame


def weight_kernel(count, pieces, *refs):
    wires = refs[:pieces]
    frame_ref, g_ref, gain_ref = refs[pieces : pieces + 3]
    near_ref, far_ref, own_ref, keep_ref, send_ref, held_s, col_s, pack_s = refs[pieces + 3 :]
    width, own, lanes = own_ref.shape
    blocks, chan, wire = held_s.shape
    rows = own // chan
    breadth = width // blocks
    views = count
    odd = row_is_odd()
    take(wires, held_s)
    col_s[0] = jnp.zeros((own, lanes), BF16)
    col_s[width + 1] = jnp.zeros((own, lanes), BF16)

    def block(b, carry):
        cells = held_s[b]
        for r in range(rows):
            for k in range(breadth):
                at = (r * breadth + k) * views
                value = cells[:, at : at + views]
                if lanes > views:
                    value = jnp.concatenate(
                        [value, jnp.zeros((chan, lanes - views), F32)], axis=1
                    )
                col_s[b * breadth + k + 1, r * chan : (r + 1) * chan] = value.astype(BF16)
        return carry

    lax.fori_loop(0, blocks, block, 0, unroll=blocks <= 4)

    def copy(w, carry):
        cells = col_s[w + 1]
        own_ref[w] = cells
        first, last = cells[:chan], cells[own - chan :]
        near_ref[w] = jnp.where(odd > 0, first, last)
        far_ref[w] = jnp.where(odd > 0, last, first)
        return carry

    lax.fori_loop(0, width, copy, 0, unroll=width <= 16)

    def pair(q, total):
        left, right = [], []
        for side in range(2):
            w = 2 * q + side
            left.append(jnp.concatenate([col_s[w], col_s[w + 1], col_s[w + 2]], axis=0))
            right.append(frame_ref[w])
        return total + dot(
            jnp.concatenate(left, axis=1), jnp.concatenate(right, axis=1), (1, 1)
        )

    total = lax.fori_loop(
        0,
        width // 2,
        pair,
        jnp.zeros((3 * own, own + 2 * chan), F32),
        unroll=width <= 16,
    )
    bands = []
    for shift in range(3):
        band = 0.0
        for r in range(rows):
            top = (shift * rows + r) * chan
            band = band + total[top : top + chan, r * chan : (r + 3) * chan]
        bands.append(band)
    g_conv = jnp.concatenate(bands, axis=0)
    edge = 2 * chan
    pack_s[...] = jnp.zeros_like(pack_s)
    pack_s[: 2 * chan] = g_ref[...]
    pack_s[2 * chan : 2 * chan + 8] = gain_ref[...]
    at = 2 * chan + 8
    pack_s[at : at + 3 * chan] = g_conv[:, :edge]
    half = 3 * chan // 2
    rest = g_conv[:, edge:]
    pack_s[at + 3 * chan : at + 3 * chan + half] = jnp.concatenate(
        [rest[:half], rest[half:]], axis=1
    )
    size = keep_ref.shape[0]
    keep_ref[...] = pack_s[pl.ds(pl.multiple_of(odd * size, 8), size)]
    send_ref[...] = pack_s[pl.ds(pl.multiple_of((1 - odd) * size, 8), size)]


def weight_grads(wires, frame, g_weights, g_gain, views, blocks):
    width, deep, lanes = frame.shape
    chan, wire = wires[0].shape[-2:]
    own = deep - 2 * chan
    size = round_up(2 * chan + 8 + 9 * chan // 2, 32) // 2
    vmem = pl.BlockSpec(memory_space=pltpu.VMEM)
    return pl.pallas_call(
        functools.partial(weight_kernel, views, len(wires)),
        out_shape=(
            jax.ShapeDtypeStruct((width, chan, lanes), BF16),
            jax.ShapeDtypeStruct((width, chan, lanes), BF16),
            jax.ShapeDtypeStruct((width, own, lanes), BF16),
            jax.ShapeDtypeStruct((size, 2 * chan), F32),
            jax.ShapeDtypeStruct((size, 2 * chan), F32),
        ),
        in_specs=[vmem] * (len(wires) + 3),
        out_specs=(vmem,) * 5,
        scratch_shapes=[
            pltpu.VMEM((blocks, chan, wire), F32),
            pltpu.VMEM((width + 2, own, lanes), BF16),
            pltpu.VMEM((2 * size, 2 * chan), F32),
        ],
        name="weights",
    )(*wires, frame, g_weights, g_gain)


def input_kernel(own_ref, near_ref, far_ref, w_ref, out_ref, frame_s, acc_s):
    width, own, lanes = own_ref.shape
    chan = near_ref.shape[1]
    rows = own // chan
    views = out_ref.shape[3]
    odd = row_is_odd() > 0

    def fill(w, carry):
        near, far = near_ref[w], far_ref[w]
        frame_s[w, :chan] = jnp.where(odd, near, far)
        frame_s[w, chan : chan + own] = own_ref[w]
        frame_s[w, chan + own :] = jnp.where(odd, far, near)
        return carry

    lax.fori_loop(0, width, fill, 0, unroll=width <= 16)
    spread(frame_s, acc_s, taps(w_ref, rows, False), rows, False)

    def column(w, carry):
        value = acc_s[w + 1] + own_ref[w].astype(F32)
        for r in range(rows):
            out_ref[r, w] = value[r * chan : (r + 1) * chan, :views].astype(BF16)
        return carry

    lax.fori_loop(0, width, column, 0, unroll=width <= 16)


def input_grad(own, near, far, w_conv, views):
    width, size, lanes = own.shape
    chan = near.shape[1]
    vmem = pl.BlockSpec(memory_space=pltpu.VMEM)
    return pl.pallas_call(
        input_kernel,
        out_shape=jax.ShapeDtypeStruct((size // chan, width, chan, views), BF16),
        in_specs=[vmem] * 4,
        out_specs=vmem,
        scratch_shapes=[
            pltpu.VMEM((width, size + 2 * chan, lanes), BF16),
            pltpu.VMEM((width + 2, size, lanes), F32),
        ],
        name="input",
    )(own, near, far, w_conv)


def unpack_kernel(mine_ref, other_ref, conv_ref, q_ref, k_ref, v_ref, o_ref, gain_ref, pack_s):
    size = mine_ref.shape[0]
    chan = q_ref.shape[0]
    odd = row_is_odd()
    pack_s[pl.ds(pl.multiple_of(odd * size, 8), size)] = mine_ref[...]
    pack_s[pl.ds(pl.multiple_of((1 - odd) * size, 8), size)] = other_ref[...]
    q_ref[...] = pack_s[:chan, :chan]
    k_ref[...] = pack_s[:chan, chan:]
    v_ref[...] = pack_s[chan : 2 * chan, :chan]
    o_ref[...] = pack_s[chan : 2 * chan, chan:]
    gain_ref[...] = pack_s[2 * chan : 2 * chan + 1, :chan]
    at = 2 * chan + 8
    half = 3 * chan // 2
    for j in range(3):
        top = (2 - j) * chan
        for i in range(2):
            conv_ref[i, j] = pack_s[at + top : at + top + chan, i * chan : (i + 1) * chan]
        for low in range(0, chan, chan // 2):
            row = top + low
            side = row // half
            start = at + 3 * chan + row - side * half
            conv_ref[2, j, low : low + chan // 2] = pack_s[
                start : start + chan // 2, side * chan : (side + 1) * chan
            ]


def unpack(mine, other, chan):
    vmem = pl.BlockSpec(memory_space=pltpu.VMEM)
    square = jax.ShapeDtypeStruct((chan, chan), F32)
    return pl.pallas_call(
        unpack_kernel,
        out_shape=(
            jax.ShapeDtypeStruct((3, 3, chan, chan), F32),
            square,
            square,
            square,
            square,
            jax.ShapeDtypeStruct((1, chan), F32),
        ),
        in_specs=[vmem] * 2,
        out_specs=(vmem,) * 6,
        scratch_shapes=[pltpu.VMEM((2 * mine.shape[0], 2 * chan), F32)],
        name="unpack",
    )(mine, other)


def angular_kernel(
    scale,
    lag,
    pieces,
    *refs,
):
    wires_in = refs[:pieces]
    cot_ref, keep_ref, gain_row, wq_ref, wkey_ref, wv_ref, wo_ref = refs[pieces : pieces + 7]
    refs = refs[pieces + 7 :]
    wires_out = refs[:pieces]
    out_ref, g_ref, ggain_ref, held_s, bias_ref, gain_ref, wqkv_ref, wk_ref, wot_ref, wcat_ref = (
        refs[pieces : pieces + 10]
    )
    give_s = refs[pieces + 10]
    scratch = refs[pieces + 11 :]
    blocks = held_s.shape[0]
    pixels, chan, lanes = cot_ref.shape
    used = keep_ref.shape[1]
    each = used // blocks
    rows = bias_ref.shape[0]
    slots = len(scratch) // 6
    inv_chan = 1.0 / chan
    take(wires_in, held_s)
    live = jnp.where(keep_ref[...] > 0, 0.0, -1e30).astype(F32)
    live = jnp.concatenate([live, jnp.full((1, lanes - used), -1e30, F32)], axis=1)
    live = jnp.transpose(jnp.broadcast_to(live, (128, lanes)))[:rows]
    lane = lax.broadcasted_iota(jnp.int32, (rows, 128), 1)
    bias_ref[...] = jnp.where(lane == chan, live, 0.0)[:, : 2 * chan]
    eye = lax.broadcasted_iota(jnp.int32, (chan, chan), 0) == lax.broadcasted_iota(
        jnp.int32, (chan, chan), 1
    )
    gain_ref[...] = jnp.sum(jnp.where(eye, gain_row[...], 0.0), axis=1, keepdims=True)
    w_q, w_k, w_v = (ref[...].astype(F32) for ref in (wq_ref, wkey_ref, wv_ref))
    wqkv_ref[...] = jnp.concatenate(
        [jnp.transpose(w_q), jnp.transpose(w_k), jnp.transpose(w_v)], axis=0
    ).astype(BF16)
    wcat_ref[...] = jnp.concatenate([w_q, w_k, w_v], axis=1).astype(BF16)
    wk_ref[...] = jnp.concatenate([w_k, jnp.zeros((chan, chan), F32)], axis=1).astype(BF16)
    wot_ref[...] = jnp.transpose(wo_ref[...].astype(F32)).astype(BF16)
    for slot in range(slots):
        s_s, e_s, g_s, n_s, t_s, x_s = scratch[6 * slot : 6 * slot + 6]
        e_s[rows:] = jnp.zeros((lanes - rows, lanes), BF16)
        g_s[rows:] = jnp.zeros((lanes - rows, lanes), BF16)
    chunks = []
    at = 0
    while at < rows:
        size = min(80, rows - at)
        chunks.append((at, size))
        at += size
    sums = {}

    def add(name, value):
        sums[name] = value if name not in sums else sums[name] + value

    def pixel(p):
        s_s, e_s, g_s, n_s, t_s, x_s = scratch[6 * (p % slots) : 6 * (p % slots) + 6]
        cells = [held_s[b, :, p * each : (p + 1) * each] for b in range(blocks)]
        if lanes > used:
            cells.append(jnp.zeros((chan, lanes - used), F32))
        s = jnp.concatenate(cells, axis=1)
        x_s[...] = s
        cen = s - jnp.sum(s, axis=0, keepdims=True) * inv_chan
        rstd = lax.rsqrt(jnp.sum(cen * cen, axis=0, keepdims=True) * inv_chan + 1e-05)
        normed = cen * rstd
        n_s[...] = normed
        nin32 = normed * gain_ref[...]
        nin = nin32.astype(BF16)
        t_s[...] = jnp.transpose(nin32).astype(BF16)
        yield
        qkv = dot(wqkv_ref[...], nin)
        q = (qkv[:chan].astype(BF16).astype(F32) * scale).astype(BF16)
        q_aug = jnp.concatenate([q, jnp.ones((16, lanes), BF16), jnp.zeros((chan - 16, lanes), BF16)], axis=0)
        k = qkv[chan : 2 * chan].astype(BF16)
        v = qkv[2 * chan :].astype(BF16)
        yield
        high = None
        for at, size in chunks:
            k_t = (dot(t_s[at : at + size], wk_ref[...]) + bias_ref[at : at + size]).astype(BF16)
            sc = dot(k_t, q_aug)
            s_s[at : at + size] = sc
            top = jnp.max(sc.reshape(size // 8, 8, lanes), axis=0)
            high = top if high is None else jnp.maximum(high, top)
            yield
        high = jnp.max(high, axis=0, keepdims=True)
        cot = cot_ref[p]
        d_att32 = dot(wo_ref[...], cot).astype(BF16).astype(F32)
        for at, size in chunks:
            e_s[at : at + size] = jnp.exp(s_s[at : at + size] - high).astype(BF16)
            yield
        v_aug = jnp.concatenate([v, jnp.ones((16, lanes), BF16)], axis=0)
        att_aug = dot(v_aug, e_s[...])
        inv = 1.0 / att_aug[chan : chan + 1]
        att = att_aug[:chan] * inv
        att_b = att.astype(BF16)
        d_att = (d_att32 * inv).astype(BF16)
        inner = jnp.sum(att * d_att.astype(F32), axis=0, keepdims=True)
        yield
        for at, size in chunks:
            v_t = dot(t_s[at : at + size], wv_ref[...]).astype(BF16)
            dp = dot(v_t, d_att)
            g_s[at : at + size] = e_s[at : at + size] * (dp - inner).astype(BF16)
            yield
        out_ref[p] = (x_s[...] + dot(wot_ref[...], att_b)).astype(BF16)[:, :used]
        d_v = dot(d_att, e_s[...], (1, 1)).astype(BF16)
        yield
        d_q = (dot(k, g_s[...]) * scale).astype(BF16)
        yield
        d_k = dot(q, g_s[...], (1, 1)).astype(BF16)
        d_qkv = jnp.concatenate([d_q, d_k, d_v], axis=0)
        yield
        dn = dot(wcat_ref[...], d_qkv)
        normed = n_s[...]
        nin = (normed * gain_ref[...]).astype(BF16)
        both = dot(
            jnp.concatenate([nin, att_b], axis=0),
            jnp.concatenate([d_q, d_k, d_v, cot], axis=0),
            (1, 1),
        )
        add("qkv", both[:chan, : 2 * chan])
        lane = lax.broadcasted_iota(jnp.int32, (chan, 2 * chan), 1)
        add("vo", jnp.where(lane < chan, both[:chan, 2 * chan :], both[chan:, 2 * chan :]))
        yield
        dnn = dn * normed
        add("gain", dnn)
        scaled = dn * gain_ref[...]
        back = (
            scaled
            - jnp.sum(scaled, axis=0, keepdims=True) * inv_chan
            - normed * (jnp.sum(dnn * gain_ref[...], axis=0, keepdims=True) * inv_chan)
        )
        done = cot.astype(F32) + back * rstd
        for b in range(blocks):
            give_s[b, :, p * each : (p + 1) * each] = done[:, b * each : (b + 1) * each]
        yield

    waiting = [pixel(p) for p in range(pixels)]
    active = []
    step = 0
    while waiting or active:
        if waiting and step % lag == 0:
            active.append(waiting.pop(0))
        for run in list(active):
            try:
                next(run)
            except StopIteration:
                active.remove(run)
        step += 1
    g_ref[:chan] = sums["qkv"]
    g_ref[chan:] = sums["vo"]
    g_gain = jnp.sum(sums["gain"], axis=1, keepdims=True)
    g_gain = jnp.sum(jnp.where(eye, g_gain, 0.0), axis=0, keepdims=True)
    g_gain = jnp.concatenate([g_gain, jnp.zeros((1, chan), F32)], axis=1)
    ggain_ref[...] = jnp.broadcast_to(g_gain, ggain_ref.shape)
    give(wires_out, give_s)


def angular(wires, cotangent, keep, gain, w_query, w_key, w_value, w_out, blocks):
    pixels, chan, lanes = cotangent.shape
    used = keep.shape[0]
    rows = round_up(used, 16)
    wire = wires[0].shape[-1]
    vmem = pl.BlockSpec(memory_space=pltpu.VMEM)
    scale = 1.0 / math.sqrt(chan)
    shapes = wire_shapes(blocks, chan, wire) + [
        jax.ShapeDtypeStruct((pixels, chan, used), BF16),
        jax.ShapeDtypeStruct((2 * chan, 2 * chan), F32),
        jax.ShapeDtypeStruct((8, 2 * chan), F32),
    ]
    *out, output, g_weights, g_gain = pl.pallas_call(
        functools.partial(angular_kernel, scale, 10, len(wires)),
        out_shape=shapes,
        in_specs=[vmem] * (len(wires) + 7),
        out_specs=[vmem] * len(shapes),
        scratch_shapes=[
            pltpu.VMEM((blocks, chan, wire), F32),
            pltpu.VMEM((rows, 2 * chan), F32),
            pltpu.VMEM((chan, 1), F32),
            pltpu.VMEM((3 * chan, chan), BF16),
            pltpu.VMEM((chan, 2 * chan), BF16),
            pltpu.VMEM((chan, chan), BF16),
            pltpu.VMEM((chan, 3 * chan), BF16),
            pltpu.VMEM((blocks, chan, wire), F32),
        ]
        + [
            pltpu.VMEM((rows, lanes), F32),
            pltpu.VMEM((lanes, lanes), BF16),
            pltpu.VMEM((lanes, lanes), BF16),
            pltpu.VMEM((chan, lanes), F32),
            pltpu.VMEM((lanes, chan), BF16),
            pltpu.VMEM((chan, lanes), F32),
        ]
        * 2,
        name="angular",
    )(*wires, cotangent, keep[None, :], gain[None, :], w_query, w_key, w_value, w_out)
    return out, output, g_weights, g_gain


def reduce_views(own):
    count = lax.axis_size("view")
    if not pairwise(count):
        return lax.psum(own, "view")
    own = own.astype(BF16)
    parts = [own] + [swap(own, "view", step) for step in range(1, count)]
    total = 0.0
    for part in parts:
        total = total + part.astype(F32)
    return total


def reduce_rows(own):
    count = lax.axis_size("row")
    step = 2
    while step < count:
        own = own + swap(own, "row", step)
        step *= 2
    return own


def body(inputs, cotangent, keep, w_conv, gain, w_query, w_key, w_value, w_out):
    chan, view_dev, row_dev, width = inputs.shape
    blocks = lax.axis_size("view")
    breadth = width // blocks
    views = view_dev * blocks
    lanes = round_up(views, 128)
    pixels = row_dev * breadth
    odd = row_is_odd() > 0
    x = jnp.transpose(inputs, (3, 2, 0, 1))
    first, last = x[:, 0], x[:, row_dev - 1]
    near, far = halo_swap(jnp.where(odd, first, last), jnp.where(odd, last, first))
    w_conv = jnp.transpose(w_conv, (2, 3, 0, 1))
    x = x.reshape(width, row_dev * chan, view_dev)
    wires, frame = convolve(x, near, far, w_conv, blocks)
    wires = exchange(wires)
    cot = jnp.transpose(cotangent, (2, 3, 0, 1)).reshape(pixels, chan, views)
    cot = jnp.pad(cot, ((0, 0), (0, 0), (0, lanes - views)))
    wires, output, g_weights, g_gain = angular(
        wires, cot, keep, gain, w_query, w_key, w_value, w_out, blocks
    )
    wires = exchange(wires)
    output = jnp.transpose(output.reshape(row_dev, breadth, chan, views), (2, 3, 0, 1))
    near, far, own, kept, sent = weight_grads(wires, frame, g_weights, g_gain, view_dev, blocks)
    near, far = halo_swap(near, far)
    part = reduce_rows(kept + swap(sent, "row", 1))
    part = reduce_views(part)
    g_conv, g_query, g_key, g_value, g_out, g_gain = unpack(part, swap(part, "row", 1), chan)
    d_input = input_grad(own, near, far, w_conv, view_dev)
    d_input = jnp.transpose(d_input, (2, 3, 0, 1))
    g_conv = jnp.transpose(g_conv, (2, 3, 0, 1))
    return (output, d_input, g_conv, g_gain[0], g_query, g_key, g_value, g_out)


def solution(mesh):
    placed = (
        P(None, "view", ("groups", "row"), None),
        P(None, None, ("groups", "row"), "view"),
        P("groups"),
        P(),
        P(),
        P(),
        P(),
        P(),
        P(),
    )
    return jax.shard_map(
        body,
        mesh=mesh,
        in_specs=placed,
        out_specs=(
            P(None, None, ("groups", "row"), "view"),
            P(None, "view", ("groups", "row"), None),
            P("groups", None, None, None),
            P("groups"),
            P("groups", None),
            P("groups", None),
            P("groups", None),
            P("groups", None),
        ),
        check_vma=False,
    )
```

time: 313 us -> 84.7 us (0.27)
  waiting for transfers between devices: 188 us -> 21.6 us
  matrix products: 58.5 us -> 0 us
  Pallas kernels: 0 us -> 27.6 us
  between operations: 14.6 us -> 0.79 us
  local copies, waits for them, and re-layouts: 22.2 us -> 10.3 us
  other arithmetic: 5.08 us -> 1.07 us
    psum x2 -> x0, waiting for transfers between devices: 163 us -> none  [body(): lax.psum((g_conv, g_gain, g_query, g_key, g_value, g_out), ('view', 'row'))]
    dot_general x59 -> x0, matrix products: 52.2 us -> none  [product(): return jnp.einsum(form, left, right, preferred_element_type=jnp.float32)]
    pallas_call x0 -> x5, Pallas kernels: none -> 27.6 us  [the longest x1 16.6 us: angular(): pl.pallas_call(functools.partial(angular_kernel, scale, 10, len(wires)),...]
    all_to_all x2 -> x0, waiting for transfers between devices: 17.1 us -> none  [the longest x1 11.2 us: body(): lax.all_to_all(spatial.reshape(channels, view_dev, row_dev, blocks, bread...]
    ppermute x4 -> x16, waiting for transfers between devices: 7.42 us -> 21.6 us  [the longest x12 16 us: swap(): return lax.ppermute(cells, axis, [(i, i ^ step) for i in range(count)])]
    ppermute x4 -> x16, starting transfers between devices: 12 us -> 22.9 us  [the longest x12 14.2 us: swap(): return lax.ppermute(cells, axis, [(i, i ^ step) for i in range(count)])]
    all_to_all x2 -> x0, starting transfers between devices: 8.17 us -> none  [the longest x1 4.71 us: body(): lax.all_to_all(spatial.reshape(channels, view_dev, row_dev, blocks, bread...]
    sub x2 -> x0, matrix products: 6.25 us -> none  [angular(): expo = jnp.exp(scores - highest)]
  transfers between devices with their start and end apart: 8 -> 16, of which waited for: 8 -> 8; matrix products, arithmetic and copies ran while one was open for 4% -> 7% of each run, Pallas kernels for 0% -> 3%
where the time goes in v2:
time: 84.7 us; the launch traced here: 84.3 us
  Pallas kernels  27.6 us (33%)
  starting transfers between devices  22.9 us (27%)
  waiting for transfers between devices  21.6 us (26%)
  local copies, waits for them, and re-layouts  10.3 us (12%)
  other arithmetic  1.07 us (1%)
    pallas_call x1, Pallas kernels, angular(): pl.pallas_call(functools.partial(angular_kernel, scale, 10, len(wires)),...  16.6 us
    ppermute x12, waiting for transfers between devices, swap(): return lax.ppermute(cells, axis, [(i, i ^ step) for i in range(count)])  16 us
    ppermute x12, starting transfers between devices, swap(): return lax.ppermute(cells, axis, [(i, i ^ step) for i in range(count)])  14.2 us
    unnamed x38, local copies, waits for them, and re-layouts  6.87 us
    ppermute x2, starting transfers between devices, halo_swap(): got_far = lax.ppermute(far, 'row', pairs) if pairs else jnp.zeros_like(far)  6.54 us
    ppermute x2, waiting for transfers between devices, halo_swap(): got_far = lax.ppermute(far, 'row', pairs) if pairs else jnp.zeros_like(far)  5.58 us
    pallas_call x1, Pallas kernels, convolve(): pl.pallas_call(functools.partial(conv_kernel, blocks), out_shape=shapes,...  3.3 us
    pallas_call x1, Pallas kernels, weight_grads(): pl.pallas_call(functools.partial(weight_kernel, views, len(wires)), out_s...  3.1 us
  transfers between devices with their start and end apart: 16, of which 8 were waited for; matrix products, arithmetic and copies ran while one was open for 7% of the time, Pallas kernels for 3%

profile of v2, /device:TPU:1, one launch (start us, length us, event | category | flops | bytes accessed | tf_op | source)
XLA Modules:
  0.0 84.3 jit_solution(11609519317098291976)
XLA Ops:
  0.6 1.2 %copy.32 = bf16[64,73,2,16]{1,0,3,2:T(8,128)(2,1)S(1)} copy(bf16[64,73,2,16]{1,3,2,0:T(8,128)(2,1)} %param.9) | data formatting | bytes 598016 | tf_op args[0]
  2.0 4.6 %collective-permute-start.1 = (bf16[16,64,73]{2,1,0:T(8,128)(2,1)S(1)}, bf16[16,64,73]{2,1,0:T(8,128)(2,1)S(1)}, u32[]{:S(2)}, u32[]{:S(2)}) collective-permute-start(bf16[16,64,73]{2,1,0:T(8,128)(2,1)S(1)} %get-tuple-element.70), channel_id=1, source_target_pairs={{1,2},{2,1},{5,6},{6,5},{9,10},{10,9},{13,14},{14,13},{17,18},{18,... | collective-permute-start | bytes 448520 | tf_op jit(solution)/shard_map/ppermute | solution.py:40
  7.7 3.0 %collective-permute-done.1.far_ref = bf16[16,64,73]{2,1,0:T(8,128)(2,1)S(1)} collective-permute-done((bf16[16,64,73]{2,1,0:T(8,128)(2,1)S(1)}, bf16[16,64,73]{2,1,0:T(8,128)(2,1)S(1)}, u32[]{:S(2)}, u32[]{:S(2)}) %collective-permute-start.1) | collective-permute-done | bytes 149536 | tf_op jit(solution)/shard_map/ppermute | solution.py:40
  11.4 3.3 %conv.1 = (bf16[64,640]{1,0:T(8,128)(2,1)}, bf16[64,640]{1,0:T(8,128)(2,1)}, bf16[64,640]{1,0:T(8,128)(2,1)}, bf16[64,640]{1,0:T(8,128)(2,1)}, bf16[16,256,128]{2,1,0:T(8,128)(2,1)}) custom-call(bf16[16,128,73]{2,1,0:T(8,128)(2,1)} %bitcast.20, bf16[16,64,73]{2,1,0:T(8,128)(2,1)} %copy-done.7, bf16[16,64,73]{2,1,0:T(8,128)(2,1)} %copy-done.6, ...), custom_call_target="tpu_custom_call" | custom-call | tf_op jit(solution)/shard_map/conv/pallas_call | solution.py:163
  14.7 1.3 %collective-permute-start.2 = (bf16[64,640]{1,0:T(8,128)(2,1)}, bf16[64,640]{1,0:T(8,128)(2,1)S(1)}, u32[]{:S(2)}, u32[]{:S(2)}) collective-permute-start(bf16[64,640]{1,0:T(8,128)(2,1)} %get-tuple-element.32), channel_id=1, source_target_pairs={{0,4},{4,0},{8,12},{12,8},{1,5},{5,1},{9,13},{13,9},{2,6},{6,2},{1... | collective-permute-start | bytes 245768 | tf_op jit(solution)/shard_map/ppermute | solution.py:31
  16.0 2.3 %collective-permute-start.3 = (bf16[64,640]{1,0:T(8,128)(2,1)}, bf16[64,640]{1,0:T(8,128)(2,1)S(1)}, u32[]{:S(2)}, u32[]{:S(2)}) collective-permute-start(bf16[64,640]{1,0:T(8,128)(2,1)} %get-tuple-element.33), channel_id=1, source_target_pairs={{0,8},{4,12},{8,0},{12,4},{1,9},{5,13},{9,1},{13,5},{2,10},{6,14},... | collective-permute-start | bytes 245768 | tf_op jit(solution)/shard_map/ppermute | solution.py:31
  19.8 4.2 %collective-permute-done.3.refs_2_ = bf16[64,640]{1,0:T(8,128)(2,1)S(1)} collective-permute-done((bf16[64,640]{1,0:T(8,128)(2,1)}, bf16[64,640]{1,0:T(8,128)(2,1)S(1)}, u32[]{:S(2)}, u32[]{:S(2)}) %collective-permute-start.3) | collective-permute-done | bytes 81952 | tf_op jit(solution)/shard_map/ppermute | solution.py:31
  24.6 16.6 %angular.1 = (bf16[64,640]{1,0:T(8,128)(2,1)}, bf16[64,640]{1,0:T(8,128)(2,1)}, bf16[64,640]{1,0:T(8,128)(2,1)}, bf16[64,640]{1,0:T(8,128)(2,1)}, bf16[8,64,292]...) custom-call(bf16[64,640]{1,0:T(8,128)(2,1)} %get-tuple-element.31.refs_0_, bf16[64,640]{1,0:T(8,128)(2,1)} %copy-done.12, ...), custom_call_target="tpu_custom_call" | custom-call | tf_op jit(solution)/shard_map/angular/pallas_call | solution.py:540
  41.2 1.2 %collective-permute-start.5 = (bf16[64,640]{1,0:T(8,128)(2,1)}, bf16[64,640]{1,0:T(8,128)(2,1)S(1)}, u32[]{:S(2)}, u32[]{:S(2)}) collective-permute-start(bf16[64,640]{1,0:T(8,128)(2,1)} %get-tuple-element.37), channel_id=1, source_target_pairs={{0,4},{4,0},{8,12},{12,8},{1,5},{5,1},{9,13},{13,9},{2,6},{6,2},{1... | collective-permute-start | bytes 245768 | tf_op jit(solution)/shard_map/ppermute | solution.py:31
  42.4 1.3 %collective-permute-start.6 = (bf16[64,640]{1,0:T(8,128)(2,1)}, bf16[64,640]{1,0:T(8,128)(2,1)S(1)}, u32[]{:S(2)}, u32[]{:S(2)}) collective-permute-start(bf16[64,640]{1,0:T(8,128)(2,1)} %get-tuple-element.38), channel_id=1, source_target_pairs={{0,8},{4,12},{8,0},{12,4},{1,9},{5,13},{9,1},{13,5},{2,10},{6,14},... | collective-permute-start | bytes 245768 | tf_op jit(solution)/shard_map/ppermute | solution.py:31
  45.6 1.7 %collective-permute-done.6.refs_2_ = bf16[64,640]{1,0:T(8,128)(2,1)S(1)} collective-permute-done((bf16[64,640]{1,0:T(8,128)(2,1)}, bf16[64,640]{1,0:T(8,128)(2,1)S(1)}, u32[]{:S(2)}, u32[]{:S(2)}) %collective-permute-start.6) | collective-permute-done | bytes 81952 | tf_op jit(solution)/shard_map/ppermute | solution.py:31
  47.3 3.7 %collective-permute-done.7.refs_3_ = bf16[64,640]{1,0:T(8,128)(2,1)S(1)} collective-permute-done((bf16[64,640]{1,0:T(8,128)(2,1)}, bf16[64,640]{1,0:T(8,128)(2,1)S(1)}, u32[]{:S(2)}, u32[]{:S(2)}) %collective-permute-start.7) | collective-permute-done | bytes 81952 | tf_op jit(solution)/shard_map/ppermute | solution.py:31
  51.6 3.1 %weights.1 = (bf16[16,64,128]{2,1,0:T(8,128)(2,1)}, bf16[16,64,128]{2,1,0:T(8,128)(2,1)}, bf16[16,128,128]{2,1,0:T(8,128)(2,1)}, f32[224,128]{1,0:T(8,128)}, f32[224,128]{1,0:T(8,128)}) custom-call(bf16[64,640]{1,0:T(8,128)(2,1)} %get-tuple-element.36.refs_0_, bf16[64,640]{1,0:T(8,128)(2,1)} %copy-done.9, bf16[64,640]{1,0:T(8,128)(2,1)} %copy-done.10, ...), custom_call_target="tpu_custom_call" | custom-call | tf_op jit(solution)/shard_map/weights/pallas_call | solution.py:263
  54.7 1.4 %collective-permute-start.10 = (f32[224,128]{1,0:T(8,128)}, f32[224,128]{1,0:T(8,128)S(1)}, u32[]{:S(2)}, u32[]{:S(2)}) collective-permute-start(f32[224,128]{1,0:T(8,128)} %get-tuple-element.47), channel_id=1, source_target_pairs={{0,1},{1,0},{2,3},{3,2},{4,5},{5,4},{6,7},{7,6},{8,9},{9,8},{10,11... | collective-permute-start | bytes 344072 | tf_op jit(solution)/shard_map/ppermute | solution.py:31
  56.1 1.2 %collective-permute-done.10 = f32[224,128]{1,0:T(8,128)S(1)} collective-permute-done((f32[224,128]{1,0:T(8,128)}, f32[224,128]{1,0:T(8,128)S(1)}, u32[]{:S(2)}, u32[]{:S(2)}) %collective-permute-start.10) | collective-permute-done | bytes 114720 | tf_op jit(solution)/shard_map/ppermute | solution.py:31
  58.4 4.3 %collective-permute-done.11 = f32[224,128]{1,0:T(8,128)S(1)} collective-permute-done((f32[224,128]{1,0:T(8,128)S(1)}, f32[224,128]{1,0:T(8,128)S(1)}, u32[]{:S(2)}, u32[]{:S(2)}) %collective-permute-start.11) | collective-permute-done | bytes 114720 | tf_op jit(solution)/shard_map/ppermute | solution.py:31
  62.7 1.9 %collective-permute-start.14 = (bf16[224,128]{1,0:T(8,128)(2,1)S(1)}, bf16[224,128]{1,0:T(8,128)(2,1)S(1)}, u32[]{:S(2)}, u32[]{:S(2)}) collective-permute-start(bf16[224,128]{1,0:T(8,128)(2,1)S(1)} %add_convert_fusion), channel_id=1, source_target_pairs={{0,12},{4,8},{8,4},{12,0},{1,13},{5,9},{9,5},{13,1},{2,14},{6,10},... | collective-permute-start | bytes 172040 | tf_op jit(solution)/shard_map/ppermute | solution.py:31
  66.3 2.1 %collective-permute-start.8 = (bf16[16,64,128]{2,1,0:T(8,128)(2,1)S(1)}, bf16[16,64,128]{2,1,0:T(8,128)(2,1)S(1)}, u32[]{:S(2)}, u32[]{:S(2)}) collective-permute-start(bf16[16,64,128]{2,1,0:T(8,128)(2,1)S(1)} %copy-done.17), channel_id=1, source_target_pairs={{0,1},{1,0},{2,3},{3,2},{4,5},{5,4},{6,7},{7,6},{8,9},{9,8},{10,11... | collective-permute-start | bytes 786440 | tf_op jit(solution)/shard_map/ppermute | solution.py:39
  68.4 1.9 %collective-permute-start.9 = (bf16[16,64,128]{2,1,0:T(8,128)(2,1)S(1)}, bf16[16,64,128]{2,1,0:T(8,128)(2,1)S(1)}, u32[]{:S(2)}, u32[]{:S(2)}) collective-permute-start(bf16[16,64,128]{2,1,0:T(8,128)(2,1)S(1)} %copy-done.16), channel_id=1, source_target_pairs={{1,2},{2,1},{5,6},{6,5},{9,10},{10,9},{13,14},{14,13},{17,18},{18,... | collective-permute-start | bytes 786440 | tf_op jit(solution)/shard_map/ppermute | solution.py:40
  70.4 2.0 %collective-permute-start.15 = (f32[224,128]{1,0:T(8,128)S(1)}, f32[224,128]{1,0:T(8,128)S(1)}, u32[]{:S(2)}, u32[]{:S(2)}) collective-permute-start(f32[224,128]{1,0:T(8,128)S(1)} %convert_add_fusion.mine_ref), channel_id=1, source_target_pairs={{0,1},{1,0},{2,3},{3,2},{4,5},{5,4},{6,7},{7,6},{8,9},{9,8},{10,11... | collective-permute-start | bytes 344072 | tf_op jit(solution)/shard_map/ppermute | solution.py:31
  73.5 2.6 %collective-permute-done.9.far_ref = bf16[16,64,128]{2,1,0:T(8,128)(2,1)S(1)} collective-permute-done((bf16[16,64,128]{2,1,0:T(8,128)(2,1)S(1)}, bf16[16,64,128]{2,1,0:T(8,128)(2,1)S(1)}, u32[]{:S(2)}, u32[]{:S(2)}) %collective-permute-start.9) | collective-permute-done | bytes 262176 | tf_op jit(solution)/shard_map/ppermute | solution.py:40
  76.8 2.8 %input.1 = bf16[2,16,64,73]{3,2,1,0:T(8,128)(2,1)} custom-call(bf16[16,128,128]{2,1,0:T(8,128)(2,1)} %get-tuple-element.43.own_ref, bf16[16,64,128]{2,1,0:T(8,128)(2,1)} %copy-done.4, bf16[16,64,128]{2,1,0:T(8,128)(2,1)} %copy-done.5, bf16[3,3,64,64]{3,2,1,0:T(8,128)(2,1)} %bitcast.26), custom_call_target="tpu_custom_call" | custom-call | tf_op jit(solution)/shard_map/input/pallas_call | solution.py:313
  79.6 2.2 %copy.26 = bf16[64,73,2,16]{1,3,2,0:T(8,128)(2,1)} copy(bf16[64,73,2,16]{1,0,3,2:T(8,128)(2,1)} %bitcast.23) | data formatting | bytes 598016
  82.5 1.8 %unpack.1 = (f32[3,3,64,64]{3,2,1,0:T(8,128)}, f32[64,64]{1,0:T(8,128)}, f32[64,64]{1,0:T(8,128)}, f32[64,64]{1,0:T(8,128)}, f32[64,64]{1,0:T(8,128)}, /*index=5*/f32[1,64]{1,0:T(1,128)}) custom-call(f32[224,128]{1,0:T(8,128)} %copy-done.1, f32[224,128]{1,0:T(8,128)} %copy-done.8), custom_call_target="tpu_custom_call" | custom-call | tf_op jit(solution)/shard_map/unpack/pallas_call | solution.py:355
  (60 shorter events, 11.7 us)
Async XLA Ops:
  1.9 4.8 %copy-start = (bf16[64,73,2,16]{1,3,2,0:T(8,128)(2,1)S(1)}, bf16[64,73,2,16]{1,3,2,0:T(8,128)(2,1)}, u32[]{:S(2)}) copy-start(bf16[64,73,2,16]{1,3,2,0:T(8,128)(2,1)} %param.9) | copy-start | bytes 897028
  2.0 8.7 %collective-permute-start.1 = (bf16[16,64,73]{2,1,0:T(8,128)(2,1)S(1)}, bf16[16,64,73]{2,1,0:T(8,128)(2,1)S(1)}, u32[]{:S(2)}, u32[]{:S(2)}) collective-permute-start(bf16[16,64,73]{2,1,0:T(8,128)(2,1)S(1)} %get-tuple-element.70), channel_id=1, source_target_pairs={{1,2},{2,1},{5,6},{6,5},{9,10},{10,9},{13,14},{14,13},{17,18},{18,... | collective-permute-start | bytes 448520 | tf_op jit(solution)/shard_map/ppermute | solution.py:40
  6.6 4.0 %collective-permute-start = (bf16[16,64,73]{2,1,0:T(8,128)(2,1)S(1)}, bf16[16,64,73]{2,1,0:T(8,128)(2,1)S(1)}, u32[]{:S(2)}, u32[]{:S(2)}) collective-permute-start(bf16[16,64,73]{2,1,0:T(8,128)(2,1)S(1)} %get-tuple-element.71), channel_id=1, source_target_pairs={{0,1},{1,0},{2,3},{3,2},{4,5},{5,4},{6,7},{7,6},{8,9},{9,8},{10,11... | collective-permute-start | bytes 448520 | tf_op jit(solution)/shard_map/ppermute | solution.py:39
  11.4 7.5 %copy-start.2 = (bf16[64,292,2,4]{1,3,2,0:T(4,128)(2,1)S(1)}, bf16[64,292,2,4]{1,3,2,0:T(4,128)(2,1)}, u32[]{:S(2)}) copy-start(bf16[64,292,2,4]{1,3,2,0:T(4,128)(2,1)} %param.10) | copy-start | bytes 897028
  14.7 5.0 %collective-permute-start.2 = (bf16[64,640]{1,0:T(8,128)(2,1)}, bf16[64,640]{1,0:T(8,128)(2,1)S(1)}, u32[]{:S(2)}, u32[]{:S(2)}) collective-permute-start(bf16[64,640]{1,0:T(8,128)(2,1)} %get-tuple-element.32), channel_id=1, source_target_pairs={{0,4},{4,0},{8,12},{12,8},{1,5},{5,1},{9,13},{13,9},{2,6},{6,2},{1... | collective-permute-start | bytes 245768 | tf_op jit(solution)/shard_map/ppermute | solution.py:31
  16.0 7.9 %collective-permute-start.3 = (bf16[64,640]{1,0:T(8,128)(2,1)}, bf16[64,640]{1,0:T(8,128)(2,1)S(1)}, u32[]{:S(2)}, u32[]{:S(2)}) collective-permute-start(bf16[64,640]{1,0:T(8,128)(2,1)} %get-tuple-element.33), channel_id=1, source_target_pairs={{0,8},{4,12},{8,0},{12,4},{1,9},{5,13},{9,1},{13,5},{2,10},{6,14},... | collective-permute-start | bytes 245768 | tf_op jit(solution)/shard_map/ppermute | solution.py:31
  18.3 5.6 %collective-permute-start.4 = (bf16[64,640]{1,0:T(8,128)(2,1)}, bf16[64,640]{1,0:T(8,128)(2,1)S(1)}, u32[]{:S(2)}, u32[]{:S(2)}) collective-permute-start(bf16[64,640]{1,0:T(8,128)(2,1)} %get-tuple-element.34), channel_id=1, source_target_pairs={{0,12},{4,8},{8,4},{12,0},{1,13},{5,9},{9,5},{13,1},{2,14},{6,10},... | collective-permute-start | bytes 245768 | tf_op jit(solution)/shard_map/ppermute | solution.py:31
  19.8 4.2 %copy-start.12 = (bf16[64,640]{1,0:T(8,128)(2,1)}, bf16[64,640]{1,0:T(8,128)(2,1)S(1)}, u32[]{:S(2)}) copy-start(bf16[64,640]{1,0:T(8,128)(2,1)S(1)} %collective-permute-done.2.refs_1_) | copy-start | bytes 245764
  41.2 4.4 %collective-permute-start.5 = (bf16[64,640]{1,0:T(8,128)(2,1)}, bf16[64,640]{1,0:T(8,128)(2,1)S(1)}, u32[]{:S(2)}, u32[]{:S(2)}) collective-permute-start(bf16[64,640]{1,0:T(8,128)(2,1)} %get-tuple-element.37), channel_id=1, source_target_pairs={{0,4},{4,0},{8,12},{12,8},{1,5},{5,1},{9,13},{13,9},{2,6},{6,2},{1... | collective-permute-start | bytes 245768 | tf_op jit(solution)/shard_map/ppermute | solution.py:31
  42.4 4.9 %collective-permute-start.6 = (bf16[64,640]{1,0:T(8,128)(2,1)}, bf16[64,640]{1,0:T(8,128)(2,1)S(1)}, u32[]{:S(2)}, u32[]{:S(2)}) collective-permute-start(bf16[64,640]{1,0:T(8,128)(2,1)} %get-tuple-element.38), channel_id=1, source_target_pairs={{0,8},{4,12},{8,0},{12,4},{1,9},{5,13},{9,1},{13,5},{2,10},{6,14},... | collective-permute-start | bytes 245768 | tf_op jit(solution)/shard_map/ppermute | solution.py:31
  43.7 7.3 %collective-permute-start.7 = (bf16[64,640]{1,0:T(8,128)(2,1)}, bf16[64,640]{1,0:T(8,128)(2,1)S(1)}, u32[]{:S(2)}, u32[]{:S(2)}) collective-permute-start(bf16[64,640]{1,0:T(8,128)(2,1)} %get-tuple-element.39), channel_id=1, source_target_pairs={{0,12},{4,8},{8,4},{12,0},{1,13},{5,9},{9,5},{13,1},{2,14},{6,10},... | collective-permute-start | bytes 245768 | tf_op jit(solution)/shard_map/ppermute | solution.py:31
  45.6 5.4 %copy-start.9 = (bf16[64,640]{1,0:T(8,128)(2,1)}, bf16[64,640]{1,0:T(8,128)(2,1)S(1)}, u32[]{:S(2)}) copy-start(bf16[64,640]{1,0:T(8,128)(2,1)S(1)} %collective-permute-done.5.refs_1_) | copy-start | bytes 245764
  47.3 3.7 %copy-start.10 = (bf16[64,640]{1,0:T(8,128)(2,1)}, bf16[64,640]{1,0:T(8,128)(2,1)S(1)}, u32[]{:S(2)}) copy-start(bf16[64,640]{1,0:T(8,128)(2,1)S(1)} %collective-permute-done.6.refs_2_) | copy-start | bytes 245764
  54.7 2.6 %collective-permute-start.10 = (f32[224,128]{1,0:T(8,128)}, f32[224,128]{1,0:T(8,128)S(1)}, u32[]{:S(2)}, u32[]{:S(2)}) collective-permute-start(f32[224,128]{1,0:T(8,128)} %get-tuple-element.47), channel_id=1, source_target_pairs={{0,1},{1,0},{2,3},{3,2},{4,5},{5,4},{6,7},{7,6},{8,9},{9,8},{10,11... | collective-permute-start | bytes 344072 | tf_op jit(solution)/shard_map/ppermute | solution.py:31
  57.3 9.0 %copy-start.17 = (bf16[16,64,128]{2,1,0:T(8,128)(2,1)S(1)}, bf16[16,64,128]{2,1,0:T(8,128)(2,1)}, u32[]{:S(2)}) copy-start(bf16[16,64,128]{2,1,0:T(8,128)(2,1)} %get-tuple-element.44) | copy-start | bytes 786436
  57.3 11.1 %copy-start.16 = (bf16[16,64,128]{2,1,0:T(8,128)(2,1)S(1)}, bf16[16,64,128]{2,1,0:T(8,128)(2,1)}, u32[]{:S(2)}) copy-start(bf16[16,64,128]{2,1,0:T(8,128)(2,1)} %get-tuple-element.45) | copy-start | bytes 786436
  58.3 14.1 %copy-start.3 = (bf16[8,64,292]{2,1,0:T(8,128)(2,1)S(1)}, bf16[8,64,292]{2,1,0:T(8,128)(2,1)}, u32[]{:S(2)}) copy-start(bf16[8,64,292]{2,1,0:T(8,128)(2,1)} %get-tuple-element.35) | copy-start | bytes 897028
  58.3 4.4 %collective-permute-start.11 = (f32[224,128]{1,0:T(8,128)S(1)}, f32[224,128]{1,0:T(8,128)S(1)}, u32[]{:S(2)}, u32[]{:S(2)}) collective-permute-start(f32[224,128]{1,0:T(8,128)S(1)} %add.17), channel_id=1, source_target_pairs={{0,2},{1,3},{2,0},{3,1},{4,6},{5,7},{6,4},{7,5},{8,10},{9,11},{10,... | collective-permute-start | bytes 344072 | tf_op jit(solution)/shard_map/ppermute | solution.py:31
  62.7 7.6 %collective-permute-start.14 = (bf16[224,128]{1,0:T(8,128)(2,1)S(1)}, bf16[224,128]{1,0:T(8,128)(2,1)S(1)}, u32[]{:S(2)}, u32[]{:S(2)}) collective-permute-start(bf16[224,128]{1,0:T(8,128)(2,1)S(1)} %add_convert_fusion), channel_id=1, source_target_pairs={{0,12},{4,8},{8,4},{12,0},{1,13},{5,9},{9,5},{13,1},{2,14},{6,10},... | collective-permute-start | bytes 172040 | tf_op jit(solution)/shard_map/ppermute | solution.py:31
  64.6 5.7 %collective-permute-start.13 = (bf16[224,128]{1,0:T(8,128)(2,1)S(1)}, bf16[224,128]{1,0:T(8,128)(2,1)S(1)}, u32[]{:S(2)}, u32[]{:S(2)}) collective-permute-start(bf16[224,128]{1,0:T(8,128)(2,1)S(1)} %add_convert_fusion), channel_id=1, source_target_pairs={{0,8},{4,12},{8,0},{12,4},{1,9},{5,13},{9,1},{13,5},{2,10},{6,14},... | collective-permute-start | bytes 172040 | tf_op jit(solution)/shard_map/ppermute | solution.py:31
  65.5 4.9 %collective-permute-start.12 = (bf16[224,128]{1,0:T(8,128)(2,1)S(1)}, bf16[224,128]{1,0:T(8,128)(2,1)S(1)}, u32[]{:S(2)}, u32[]{:S(2)}) collective-permute-start(bf16[224,128]{1,0:T(8,128)(2,1)S(1)} %add_convert_fusion), channel_id=1, source_target_pairs={{0,4},{4,0},{8,12},{12,8},{1,5},{5,1},{9,13},{13,9},{2,6},{6,2},{1... | collective-permute-start | bytes 172040 | tf_op jit(solution)/shard_map/ppermute | solution.py:31
  66.3 7.1 %collective-permute-start.8 = (bf16[16,64,128]{2,1,0:T(8,128)(2,1)S(1)}, bf16[16,64,128]{2,1,0:T(8,128)(2,1)S(1)}, u32[]{:S(2)}, u32[]{:S(2)}) collective-permute-start(bf16[16,64,128]{2,1,0:T(8,128)(2,1)S(1)} %copy-done.17), channel_id=1, source_target_pairs={{0,1},{1,0},{2,3},{3,2},{4,5},{5,4},{6,7},{7,6},{8,9},{9,8},{10,11... | collective-permute-start | bytes 786440 | tf_op jit(solution)/shard_map/ppermute | solution.py:39
  68.4 7.7 %collective-permute-start.9 = (bf16[16,64,128]{2,1,0:T(8,128)(2,1)S(1)}, bf16[16,64,128]{2,1,0:T(8,128)(2,1)S(1)}, u32[]{:S(2)}, u32[]{:S(2)}) collective-permute-start(bf16[16,64,128]{2,1,0:T(8,128)(2,1)S(1)} %copy-done.16), channel_id=1, source_target_pairs={{1,2},{2,1},{5,6},{6,5},{9,10},{10,9},{13,14},{14,13},{17,18},{18,... | collective-permute-start | bytes 786440 | tf_op jit(solution)/shard_map/ppermute | solution.py:40
  70.4 11.4 %collective-permute-start.15 = (f32[224,128]{1,0:T(8,128)S(1)}, f32[224,128]{1,0:T(8,128)S(1)}, u32[]{:S(2)}, u32[]{:S(2)}) collective-permute-start(f32[224,128]{1,0:T(8,128)S(1)} %convert_add_fusion.mine_ref), channel_id=1, source_target_pairs={{0,1},{1,0},{2,3},{3,2},{4,5},{5,4},{6,7},{7,6},{8,9},{9,8},{10,11... | collective-permute-start | bytes 344072 | tf_op jit(solution)/shard_map/ppermute | solution.py:31
  (10 other events, 14.1 us)

commit v3 on v2

--- a/solution.py
+++ b/solution.py
@@ -63,10 +63,24 @@
         held[me ^ step] = ref[...].astype(held.dtype)
 
 
+def here(blocks, *arrays):
+    if not pairwise(blocks):
+        return arrays
+    return [pltpu.with_memory_space_constraint(array, pltpu.VMEM) for array in arrays]
+
+
+def grant(blocks):
+    return pltpu.CompilerParams(vmem_limit_bytes=(24 << 20) if pairwise(blocks) else None)
+
+
+def held(blocks, shape, dtype):
+    return (pltpu.VMEM if pairwise(blocks) else jax.ShapeDtypeStruct)(shape, dtype)
+
+
 def wire_shapes(blocks, chan, lanes):
     if pairwise(blocks):
-        return [jax.ShapeDtypeStruct((chan, lanes), BF16)] * blocks
-    return [jax.ShapeDtypeStruct((blocks, chan, lanes), BF16)]
+        return [held(blocks, (chan, lanes), BF16)] * blocks
+    return [held(blocks, (blocks, chan, lanes), BF16)]
 
 
 def exchange(wires):
@@ -116,9 +130,8 @@
 
 def conv_kernel(blocks, x_ref, near_ref, far_ref, w_ref, *refs):
     *wires, frame_ref, acc_s, held_s = refs
-    width, own, views = x_ref.shape
-    chan = near_ref.shape[1]
-    rows = own // chan
+    rows, width, chan, views = x_ref.shape
+    own = rows * chan
     lanes = frame_ref.shape[2]
     odd = row_is_odd() > 0
     frame_ref[...] = jnp.zeros_like(frame_ref)
@@ -126,7 +139,8 @@
     def fill(w, carry):
         near, far = near_ref[w], far_ref[w]
         frame_ref[w, :chan, :views] = jnp.where(odd, near, far)
-        frame_ref[w, chan : chan + own, :views] = x_ref[w]
+        for r in range(rows):
+            frame_ref[w, (r + 1) * chan : (r + 2) * chan, :views] = x_ref[r, w]
         frame_ref[w, chan + own :, :views] = jnp.where(odd, far, near)
         return carry
 
@@ -152,14 +166,13 @@
 
 
 def convolve(x, near, far, w_conv, blocks):
-    width, own, views = x.shape
-    chan = w_conv.shape[2]
-    rows = own // chan
+    rows, width, chan, views = x.shape
+    own = rows * chan
     lanes = round_up(views, 128)
     wire = round_up(rows * (width // blocks) * views, 128)
     vmem = pl.BlockSpec(memory_space=pltpu.VMEM)
     shapes = wire_shapes(blocks, chan, wire)
-    shapes = shapes + [jax.ShapeDtypeStruct((width, own + 2 * chan, lanes), BF16)]
+    shapes = shapes + [held(blocks, (width, own + 2 * chan, lanes), BF16)]
     *wires, frame = pl.pallas_call(
         functools.partial(conv_kernel, blocks),
         out_shape=shapes,
@@ -170,7 +183,8 @@
             pltpu.VMEM((blocks, chan, wire), F32),
         ],
         name="conv",
-    )(x, near, far, w_conv)
+        compiler_params=grant(blocks),
+    )(*here(blocks, x, near, far), w_conv)
     return wires, frame
 
 
@@ -263,11 +277,11 @@
     return pl.pallas_call(
         functools.partial(weight_kernel, views, len(wires)),
         out_shape=(
-            jax.ShapeDtypeStruct((width, chan, lanes), BF16),
-            jax.ShapeDtypeStruct((width, chan, lanes), BF16),
-            jax.ShapeDtypeStruct((width, own, lanes), BF16),
-            jax.ShapeDtypeStruct((size, 2 * chan), F32),
-            jax.ShapeDtypeStruct((size, 2 * chan), F32),
+            held(blocks, (width, chan, lanes), BF16),
+            held(blocks, (width, chan, lanes), BF16),
+            held(blocks, (width, own, lanes), BF16),
+            held(blocks, (size, 2 * chan), F32),
+            held(blocks, (size, 2 * chan), F32),
         ),
         in_specs=[vmem] * (len(wires) + 3),
         out_specs=(vmem,) * 5,
@@ -277,7 +291,8 @@
             pltpu.VMEM((2 * size, 2 * chan), F32),
         ],
         name="weights",
-    )(*wires, frame, g_weights, g_gain)
+        compiler_params=grant(blocks),
+    )(*here(blocks, *wires, frame, g_weights, g_gain))
 
 
 def input_kernel(own_ref, near_ref, far_ref, w_ref, out_ref, frame_s, acc_s):
@@ -297,22 +312,26 @@
     lax.fori_loop(0, width, fill, 0, unroll=width <= 16)
     spread(frame_s, acc_s, taps(w_ref, rows, False), rows, False)
 
-    def column(w, carry):
-        value = acc_s[w + 1] + own_ref[w].astype(F32)
+    def columns(q, carry):
+        at = pl.multiple_of(16 * q, 16)
+        cells = []
+        for k in range(16):
+            cells.append(acc_s[at + k + 1] + own_ref[at + k].astype(F32))
+        cells = jnp.swapaxes(jnp.stack(cells), 0, 1).astype(BF16)
         for r in range(rows):
-            out_ref[r, w] = value[r * chan : (r + 1) * chan, :views].astype(BF16)
+            out_ref[:, r, pl.ds(at, 16), :] = cells[r * chan : (r + 1) * chan, :, :views]
         return carry
 
-    lax.fori_loop(0, width, column, 0, unroll=width <= 16)
-
-
-def input_grad(own, near, far, w_conv, views):
+    lax.fori_loop(0, width // 16, columns, 0)
+
+
+def input_grad(own, near, far, w_conv, views, blocks):
     width, size, lanes = own.shape
     chan = near.shape[1]
     vmem = pl.BlockSpec(memory_space=pltpu.VMEM)
     return pl.pallas_call(
         input_kernel,
-        out_shape=jax.ShapeDtypeStruct((size // chan, width, chan, views), BF16),
+        out_shape=jax.ShapeDtypeStruct((chan, size // chan, width, views), BF16),
         in_specs=[vmem] * 4,
         out_specs=vmem,
         scratch_shapes=[
@@ -320,7 +339,8 @@
             pltpu.VMEM((width + 2, size, lanes), F32),
         ],
         name="input",
-    )(own, near, far, w_conv)
+        compiler_params=grant(blocks),
+    )(*here(blocks, own, near, far), w_conv)
 
 
 def unpack_kernel(mine_ref, other_ref, conv_ref, q_ref, k_ref, v_ref, o_ref, gain_ref, pack_s):
@@ -349,7 +369,7 @@
             ]
 
 
-def unpack(mine, other, chan):
+def unpack(mine, other, chan, blocks):
     vmem = pl.BlockSpec(memory_space=pltpu.VMEM)
     square = jax.ShapeDtypeStruct((chan, chan), F32)
     return pl.pallas_call(
@@ -366,7 +386,8 @@
         out_specs=(vmem,) * 6,
         scratch_shapes=[pltpu.VMEM((2 * mine.shape[0], 2 * chan), F32)],
         name="unpack",
-    )(mine, other)
+        compiler_params=grant(blocks),
+    )(*here(blocks, mine, other))
 
 
 def angular_kernel(
@@ -534,8 +555,8 @@
     scale = 1.0 / math.sqrt(chan)
     shapes = wire_shapes(blocks, chan, wire) + [
         jax.ShapeDtypeStruct((pixels, chan, used), BF16),
-        jax.ShapeDtypeStruct((2 * chan, 2 * chan), F32),
-        jax.ShapeDtypeStruct((8, 2 * chan), F32),
+        held(blocks, (2 * chan, 2 * chan), F32),
+        held(blocks, (8, 2 * chan), F32),
     ]
     *out, output, g_weights, g_gain = pl.pallas_call(
         functools.partial(angular_kernel, scale, 10, len(wires)),
@@ -562,7 +583,8 @@
         ]
         * 2,
         name="angular",
-    )(*wires, cotangent, keep[None, :], gain[None, :], w_query, w_key, w_value, w_out)
+        compiler_params=grant(blocks),
+    )(*here(blocks, *wires, cotangent), keep[None, :], gain[None, :], w_query, w_key, w_value, w_out)
     return out, output, g_weights, g_gain
 
 
@@ -578,13 +600,16 @@
     return total
 
 
-def reduce_rows(own):
+def reduce_rows(own, beside):
     count = lax.axis_size("row")
     step = 2
     while step < count:
-        own = own + swap(own, "row", step)
+        other = swap(own, "row", step)
+        if step == 2:
+            other, beside = lax.optimization_barrier((other, beside))
+        own = own + other
         step *= 2
-    return own
+    return own, beside
 
 
 def body(inputs, cotangent, keep, w_conv, gain, w_query, w_key, w_value, w_out):
@@ -595,11 +620,10 @@
     lanes = round_up(views, 128)
     pixels = row_dev * breadth
     odd = row_is_odd() > 0
-    x = jnp.transpose(inputs, (3, 2, 0, 1))
-    first, last = x[:, 0], x[:, row_dev - 1]
+    x = jnp.transpose(inputs, (2, 3, 0, 1))
+    first, last = x[0], x[row_dev - 1]
     near, far = halo_swap(jnp.where(odd, first, last), jnp.where(odd, last, first))
     w_conv = jnp.transpose(w_conv, (2, 3, 0, 1))
-    x = x.reshape(width, row_dev * chan, view_dev)
     wires, frame = convolve(x, near, far, w_conv, blocks)
     wires = exchange(wires)
     cot = jnp.transpose(cotangent, (2, 3, 0, 1)).reshape(pixels, chan, views)
@@ -610,12 +634,15 @@
     wires = exchange(wires)
     output = jnp.transpose(output.reshape(row_dev, breadth, chan, views), (2, 3, 0, 1))
     near, far, own, kept, sent = weight_grads(wires, frame, g_weights, g_gain, view_dev, blocks)
+    other = swap(sent, "row", 1)
     near, far = halo_swap(near, far)
-    part = reduce_rows(kept + swap(sent, "row", 1))
+    part = kept + other
+    d_input = input_grad(own, near, far, w_conv, view_dev, blocks)
+    part, d_input = reduce_rows(part, d_input)
     part = reduce_views(part)
-    g_conv, g_query, g_key, g_value, g_out, g_gain = unpack(part, swap(part, "row", 1), chan)
-    d_input = input_grad(own, near, far, w_conv, view_dev)
-    d_input = jnp.transpose(d_input, (2, 3, 0, 1))
+    other = swap(part, "row", 1)
+    g_conv, g_query, g_key, g_value, g_out, g_gain = unpack(part, other, chan, blocks)
+    d_input = jnp.transpose(d_input, (0, 3, 1, 2))
     g_conv = jnp.transpose(g_conv, (2, 3, 0, 1))
     return (output, d_input, g_conv, g_gain[0], g_query, g_key, g_value, g_out)
 

time: 84.7 us -> 70.4 us (0.83)
  Pallas kernels: 27.6 us -> 19 us
  local copies, waits for them, and re-layouts: 10.3 us -> 3.06 us
  waiting for transfers between devices: 21.6 us -> 25.6 us
  starting transfers between devices: 22.9 us -> 21.3 us
  other arithmetic: 1.07 us -> 0.11 us
    unnamed x38 -> x17, local copies, waits for them, and re-layouts: 6.87 us -> 1.91 us
    ppermute x2, waiting for transfers between devices: 5.58 us -> 7.99 us  [halo_swap(): got_far = lax.ppermute(far, 'row', pairs) if pairs else jnp.zeros_like(far)]
    pallas_call x1, Pallas kernels: 3.3 us -> 0.94 us  [convolve(): pl.pallas_call(functools.partial(conv_kernel, blocks), out_shape=shapes,...]
    pallas_call x1, Pallas kernels: 3.1 us -> 0.97 us  [weight_grads(): pl.pallas_call(functools.partial(weight_kernel, views, len(wires)), out_s...]
    pallas_call x1, Pallas kernels: 16.6 us -> 14.5 us  [angular(): pl.pallas_call(functools.partial(angular_kernel, scale, 10, len(wires)),...]
    ppermute x12, waiting for transfers between devices: 16 us -> 17.7 us  [swap(): return lax.ppermute(cells, axis, [(i, i ^ step) for i in range(count)])]
    pallas_call x1, Pallas kernels: 2.83 us -> 1.74 us  [input_grad(): pl.pallas_call(input_kernel, out_shape=jax.ShapeDtypeStruct((chan, size /...]
    reshape x1 -> x0, local copies, waits for them, and re-layouts: 1 us -> none  [body(): x = x.reshape(width, row_dev * chan, view_dev)]
  transfers between devices with their start and end apart: 16 -> 16, of which waited for: 8 -> 10; matrix products, arithmetic and copies ran while one was open for 7% -> 2% of each run, Pallas kernels for 3% -> 2%
where the time goes in v3:
time: 70.4 us; the launch traced here: 70 us
  waiting for transfers between devices  25.6 us (36%)
  starting transfers between devices  21.3 us (30%)
  Pallas kernels  19 us (27%)
  local copies, waits for them, and re-layouts  3.06 us (4%)
  between operations  0.83 us (1%)
    ppermute x12, waiting for transfers between devices, swap(): return lax.ppermute(cells, axis, [(i, i ^ step) for i in range(count)])  17.7 us
    pallas_call x1, Pallas kernels, angular(): pl.pallas_call(functools.partial(angular_kernel, scale, 10, len(wires)),...  14.5 us
    ppermute x12, starting transfers between devices, swap(): return lax.ppermute(cells, axis, [(i, i ^ step) for i in range(count)])  13.6 us
    ppermute x2, waiting for transfers between devices, halo_swap(): got_far = lax.ppermute(far, 'row', pairs) if pairs else jnp.zeros_like(far)  7.99 us
    ppermute x2, starting transfers between devices, halo_swap(): got_far = lax.ppermute(far, 'row', pairs) if pairs else jnp.zeros_like(far)  6.41 us
    unnamed x17, local copies, waits for them, and re-layouts  1.91 us
    pallas_call x1, Pallas kernels, input_grad(): pl.pallas_call(input_kernel, out_shape=jax.ShapeDtypeStruct((chan, size /...  1.74 us
  transfers between devices with their start and end apart: 16, of which 10 were waited for; matrix products, arithmetic and copies ran while one was open for 2% of the time, Pallas kernels for 2%

profile of v3, /device:TPU:1, one launch (start us, length us, event | category | flops | bytes accessed | tf_op | source)
XLA Modules:
  0.0 70.0 jit_solution(1084768006029657135)
XLA Ops:
  0.6 1.2 %copy.22 = bf16[64,73,2,16]{1,0,3,2:T(8,128)(2,1)S(1)} copy(bf16[64,73,2,16]{1,3,2,0:T(8,128)(2,1)} %param.9) | data formatting | bytes 598016 | tf_op args[0]
  2.0 4.5 %collective-permute-start.1 = (bf16[16,64,73]{2,1,0:T(8,128)(2,1)S(1)}, bf16[16,64,73]{2,1,0:T(8,128)(2,1)S(1)}, u32[]{:S(2)}, u32[]{:S(2)}) collective-permute-start(bf16[16,64,73]{2,1,0:T(8,128)(2,1)S(1)} %get-tuple-element.58), channel_id=1, source_target_pairs={{1,2},{2,1},{5,6},{6,5},{9,10},{10,9},{13,14},{14,13},{17,18},{18,... | collective-permute-start | bytes 448520 | tf_op jit(solution)/shard_map/ppermute | solution.py:40
  6.5 4.0 %collective-permute-done.1.far_ref = bf16[16,64,73]{2,1,0:T(8,128)(2,1)S(1)} collective-permute-done((bf16[16,64,73]{2,1,0:T(8,128)(2,1)S(1)}, bf16[16,64,73]{2,1,0:T(8,128)(2,1)S(1)}, u32[]{:S(2)}, u32[]{:S(2)}) %collective-permute-start.1) | collective-permute-done | bytes 149536 | tf_op jit(solution)/shard_map/ppermute | solution.py:40
  10.5 0.9 %conv.1 = (bf16[64,640]{1,0:T(8,128)(2,1)S(1)}, bf16[64,640]{1,0:T(8,128)(2,1)S(1)}, bf16[64,640]{1,0:T(8,128)(2,1)S(1)}, bf16[64,640]{1,0:T(8,128)(2,1)S(1)}, bf16[16,256,128]{2,1,0:T(8,128)(2,1)S(1)}) custom-call(bf16[2,16,64,73]{3,2,1,0:T(8,128)(2,1)S(1)} %bitcast.19, bf16[16,64,73]{2,1,0:T(8,128)(2,1)S(1)} %collective-permute-done.near_ref, ...), custom_call_target="tpu_custom_call" | custom-call | tf_op jit(solution)/shard_map/conv/pallas_call | solution.py:176
  11.5 1.4 %collective-permute-start.2 = (bf16[64,640]{1,0:T(8,128)(2,1)S(1)}, bf16[64,640]{1,0:T(8,128)(2,1)S(1)}, u32[]{:S(2)}, u32[]{:S(2)}) collective-permute-start(bf16[64,640]{1,0:T(8,128)(2,1)S(1)} %get-tuple-element.34), channel_id=1, source_target_pairs={{0,4},{4,0},{8,12},{12,8},{1,5},{5,1},{9,13},{13,9},{2,6},{6,2},{1... | collective-permute-start | bytes 245768 | tf_op jit(solution)/shard_map/ppermute | solution.py:31
  12.8 2.3 %collective-permute-start.3 = (bf16[64,640]{1,0:T(8,128)(2,1)S(1)}, bf16[64,640]{1,0:T(8,128)(2,1)S(1)}, u32[]{:S(2)}, u32[]{:S(2)}) collective-permute-start(bf16[64,640]{1,0:T(8,128)(2,1)S(1)} %get-tuple-element.35), channel_id=1, source_target_pairs={{0,8},{4,12},{8,0},{12,4},{1,9},{5,13},{9,1},{13,5},{2,10},{6,14},... | collective-permute-start | bytes 245768 | tf_op jit(solution)/shard_map/ppermute | solution.py:31
  15.6 4.9 %collective-permute-done.3.refs_2_ = bf16[64,640]{1,0:T(8,128)(2,1)S(1)} collective-permute-done((bf16[64,640]{1,0:T(8,128)(2,1)S(1)}, bf16[64,640]{1,0:T(8,128)(2,1)S(1)}, u32[]{:S(2)}, u32[]{:S(2)}) %collective-permute-start.3) | collective-permute-done | bytes 81952 | tf_op jit(solution)/shard_map/ppermute | solution.py:31
  21.2 14.5 %angular.1 = (bf16[64,640]{1,0:T(8,128)(2,1)S(1)}, bf16[64,640]{1,0:T(8,128)(2,1)S(1)}, bf16[64,640]{1,0:T(8,128)(2,1)S(1)}, bf16[64,640]{1,0:T(8,128)(2,1)S(1)}...) custom-call(bf16[64,640]{1,0:T(8,128)(2,1)S(1)} %get-tuple-element.33.refs_0_, ...), custom_call_target="tpu_custom_call" | custom-call | tf_op jit(solution)/shard_map/angular/pallas_call | solution.py:561
  35.7 1.4 %collective-permute-start.5 = (bf16[64,640]{1,0:T(8,128)(2,1)S(1)}, bf16[64,640]{1,0:T(8,128)(2,1)S(1)}, u32[]{:S(2)}, u32[]{:S(2)}) collective-permute-start(bf16[64,640]{1,0:T(8,128)(2,1)S(1)} %get-tuple-element.39), channel_id=1, source_target_pairs={{0,4},{4,0},{8,12},{12,8},{1,5},{5,1},{9,13},{13,9},{2,6},{6,2},{1... | collective-permute-start | bytes 245768 | tf_op jit(solution)/shard_map/ppermute | solution.py:31
  37.1 1.3 %collective-permute-start.6 = (bf16[64,640]{1,0:T(8,128)(2,1)S(1)}, bf16[64,640]{1,0:T(8,128)(2,1)S(1)}, u32[]{:S(2)}, u32[]{:S(2)}) collective-permute-start(bf16[64,640]{1,0:T(8,128)(2,1)S(1)} %get-tuple-element.40), channel_id=1, source_target_pairs={{0,8},{4,12},{8,0},{12,4},{1,9},{5,13},{9,1},{13,5},{2,10},{6,14},... | collective-permute-start | bytes 245768 | tf_op jit(solution)/shard_map/ppermute | solution.py:31
  40.2 1.6 %collective-permute-done.6.refs_2_ = bf16[64,640]{1,0:T(8,128)(2,1)S(1)} collective-permute-done((bf16[64,640]{1,0:T(8,128)(2,1)S(1)}, bf16[64,640]{1,0:T(8,128)(2,1)S(1)}, u32[]{:S(2)}, u32[]{:S(2)}) %collective-permute-start.6) | collective-permute-done | bytes 81952 | tf_op jit(solution)/shard_map/ppermute | solution.py:31
  41.8 3.9 %collective-permute-done.7.refs_3_ = bf16[64,640]{1,0:T(8,128)(2,1)S(1)} collective-permute-done((bf16[64,640]{1,0:T(8,128)(2,1)S(1)}, bf16[64,640]{1,0:T(8,128)(2,1)S(1)}, u32[]{:S(2)}, u32[]{:S(2)}) %collective-permute-start.7) | collective-permute-done | bytes 81952 | tf_op jit(solution)/shard_map/ppermute | solution.py:31
  45.7 1.0 %weights.1 = (bf16[16,64,128]{2,1,0:T(8,128)(2,1)S(1)}, bf16[16,64,128]{2,1,0:T(8,128)(2,1)S(1)}, bf16[16,128,128]{2,1,0:T(8,128)(2,1)S(1)}, f32[224,128]{1,0:T(8,128)S(1)}, f32[224,128]{1,0:T(8,128)S(1)}) custom-call(bf16[64,640]{1,0:T(8,128)(2,1)S(1)} %get-tuple-element.38.refs_0_, bf16[64,640]{1,0:T(8,128)(2,1)S(1)} %collective-permute-done.5.refs_1_, ...), custom_call_target="tpu_custom_call" | custom-call | tf_op jit(solution)/shard_map/weights/pallas_call | solution.py:277
  46.7 1.2 %collective-permute-start.10 = (bf16[16,64,128]{2,1,0:T(8,128)(2,1)S(1)}, bf16[16,64,128]{2,1,0:T(8,128)(2,1)S(1)}, u32[]{:S(2)}, u32[]{:S(2)}) collective-permute-start(bf16[16,64,128]{2,1,0:T(8,128)(2,1)S(1)} %get-tuple-element.48), channel_id=1, source_target_pairs={{0,1},{1,0},{2,3},{3,2},{4,5},{5,4},{6,7},{7,6},{8,9},{9,8},{10,11... | collective-permute-start | bytes 786440 | tf_op jit(solution)/shard_map/ppermute | solution.py:39
  47.9 1.9 %collective-permute-start.11 = (bf16[16,64,128]{2,1,0:T(8,128)(2,1)S(1)}, bf16[16,64,128]{2,1,0:T(8,128)(2,1)S(1)}, u32[]{:S(2)}, u32[]{:S(2)}) collective-permute-start(bf16[16,64,128]{2,1,0:T(8,128)(2,1)S(1)} %get-tuple-element.49), channel_id=1, source_target_pairs={{1,2},{2,1},{5,6},{6,5},{9,10},{10,9},{13,14},{14,13},{17,18},{18,... | collective-permute-start | bytes 786440 | tf_op jit(solution)/shard_map/ppermute | solution.py:40
  49.9 1.3 %collective-permute-done.8 = f32[224,128]{1,0:T(8,128)S(1)} collective-permute-done((f32[224,128]{1,0:T(8,128)S(1)}, f32[224,128]{1,0:T(8,128)S(1)}, u32[]{:S(2)}, u32[]{:S(2)}) %collective-permute-start.8) | collective-permute-done | bytes 114720 | tf_op jit(solution)/shard_map/ppermute | solution.py:31
  51.2 1.6 %collective-permute-start.9 = (f32[224,128]{1,0:T(8,128)S(1)}, f32[224,128]{1,0:T(8,128)S(1)}, u32[]{:S(2)}, u32[]{:S(2)}) collective-permute-start(f32[224,128]{1,0:T(8,128)S(1)} %add.17), channel_id=1, source_target_pairs={{0,2},{1,3},{2,0},{3,1},{4,6},{5,7},{6,4},{7,5},{8,10},{9,11},{10,... | collective-permute-start | bytes 344072 | tf_op jit(solution)/shard_map/ppermute | solution.py:31
  52.8 4.0 %collective-permute-done.11.far_ref = bf16[16,64,128]{2,1,0:T(8,128)(2,1)S(1)} collective-permute-done((bf16[16,64,128]{2,1,0:T(8,128)(2,1)S(1)}, bf16[16,64,128]{2,1,0:T(8,128)(2,1)S(1)}, u32[]{:S(2)}, u32[]{:S(2)}) %collective-permute-start.11) | collective-permute-done | bytes 262176 | tf_op jit(solution)/shard_map/ppermute | solution.py:40
  56.8 1.7 %input.1 = bf16[64,2,16,73]{3,2,1,0:T(8,128)(2,1)} custom-call(bf16[16,128,128]{2,1,0:T(8,128)(2,1)S(1)} %get-tuple-element.47.own_ref, bf16[16,64,128]{2,1,0:T(8,128)(2,1)S(1)} %collective-permute-done.10.near_ref, bf16[16,64,128]{2,1,0:T(8,128)(2,1)S(1)} %collective-permute-done.11.far_ref, bf16[3,3,64,64]{3,2,1,0:T(8,128)(2,1)S(1)} %bitcast.21), custom_call_target="tpu_custom_call" | custom-call | tf_op jit(solution)/shard_map/input/pallas_call | solution.py:332
  58.6 1.9 %collective-permute-start.14 = (bf16[224,128]{1,0:T(8,128)(2,1)S(1)}, bf16[224,128]{1,0:T(8,128)(2,1)S(1)}, u32[]{:S(2)}, u32[]{:S(2)}) collective-permute-start(bf16[224,128]{1,0:T(8,128)(2,1)S(1)} %add_convert_fusion), channel_id=1, source_target_pairs={{0,12},{4,8},{8,4},{12,0},{1,13},{5,9},{9,5},{13,1},{2,14},{6,10},... | collective-permute-start | bytes 172040 | tf_op jit(solution)/shard_map/ppermute | solution.py:31
  62.2 1.4 %collective-permute-done.14 = bf16[224,128]{1,0:T(8,128)(2,1)S(1)} collective-permute-done((bf16[224,128]{1,0:T(8,128)(2,1)S(1)}, bf16[224,128]{1,0:T(8,128)(2,1)S(1)}, u32[]{:S(2)}, u32[]{:S(2)}) %collective-permute-start.14) | collective-permute-done | bytes 57376 | tf_op jit(solution)/shard_map/ppermute | solution.py:31
  63.6 3.4 %collective-permute-done.13 = bf16[224,128]{1,0:T(8,128)(2,1)S(1)} collective-permute-done((bf16[224,128]{1,0:T(8,128)(2,1)S(1)}, bf16[224,128]{1,0:T(8,128)(2,1)S(1)}, u32[]{:S(2)}, u32[]{:S(2)}) %collective-permute-start.13) | collective-permute-done | bytes 57376 | tf_op jit(solution)/shard_map/ppermute | solution.py:31
  67.0 1.1 %collective-permute-start.15 = (f32[224,128]{1,0:T(8,128)S(1)}, f32[224,128]{1,0:T(8,128)S(1)}, u32[]{:S(2)}, u32[]{:S(2)}) collective-permute-start(f32[224,128]{1,0:T(8,128)S(1)} %convert_add_fusion.mine_ref), channel_id=1, source_target_pairs={{0,1},{1,0},{2,3},{3,2},{4,5},{5,4},{6,7},{7,6},{8,9},{9,8},{10,11... | collective-permute-start | bytes 344072 | tf_op jit(solution)/shard_map/ppermute | solution.py:31
  68.1 1.1 %copy.23 = bf16[2,4,64,292]{3,1,0,2:T(4,128)(2,1)} copy(bf16[2,4,64,292]{3,2,1,0:T(8,128)(2,1)S(1)} %bitcast.22) | data formatting | bytes 598016 | tf_op jit(solution)/shard_map/reshape | solution.py:635
  (38 shorter events, 5.6 us)
Async XLA Ops:
  1.9 8.6 %copy-start = (bf16[64,64,3,3]{1,0,3,2:T(8,128)(2,1)S(1)}, bf16[64,64,3,3]{1,0,3,2:T(8,128)(2,1)}, u32[]{:S(2)}) copy-start(bf16[64,64,3,3]{1,0,3,2:T(8,128)(2,1)} %param.12) | copy-start | bytes 221188
  2.0 8.5 %collective-permute-start.1 = (bf16[16,64,73]{2,1,0:T(8,128)(2,1)S(1)}, bf16[16,64,73]{2,1,0:T(8,128)(2,1)S(1)}, u32[]{:S(2)}, u32[]{:S(2)}) collective-permute-start(bf16[16,64,73]{2,1,0:T(8,128)(2,1)S(1)} %get-tuple-element.58), channel_id=1, source_target_pairs={{1,2},{2,1},{5,6},{6,5},{9,10},{10,9},{13,14},{14,13},{17,18},{18,... | collective-permute-start | bytes 448520 | tf_op jit(solution)/shard_map/ppermute | solution.py:40
  6.5 4.0 %collective-permute-start = (bf16[16,64,73]{2,1,0:T(8,128)(2,1)S(1)}, bf16[16,64,73]{2,1,0:T(8,128)(2,1)S(1)}, u32[]{:S(2)}, u32[]{:S(2)}) collective-permute-start(bf16[16,64,73]{2,1,0:T(8,128)(2,1)S(1)} %get-tuple-element.59), channel_id=1, source_target_pairs={{0,1},{1,0},{2,3},{3,2},{4,5},{5,4},{6,7},{7,6},{8,9},{9,8},{10,11... | collective-permute-start | bytes 448520 | tf_op jit(solution)/shard_map/ppermute | solution.py:39
  10.5 4.7 %copy-start.6 = (bf16[64,292,2,4]{1,3,2,0:T(4,128)(2,1)S(1)}, bf16[64,292,2,4]{1,3,2,0:T(4,128)(2,1)}, u32[]{:S(2)}) copy-start(bf16[64,292,2,4]{1,3,2,0:T(4,128)(2,1)} %param.10) | copy-start | bytes 897028
  11.5 3.7 %copy-start.7 = (s32[292]{0:T(512)S(1)}, s32[292]{0:T(512)}, u32[]{:S(2)}) copy-start(s32[292]{0:T(512)} %param.11) | copy-start | bytes 3508
  11.5 4.2 %collective-permute-start.2 = (bf16[64,640]{1,0:T(8,128)(2,1)S(1)}, bf16[64,640]{1,0:T(8,128)(2,1)S(1)}, u32[]{:S(2)}, u32[]{:S(2)}) collective-permute-start(bf16[64,640]{1,0:T(8,128)(2,1)S(1)} %get-tuple-element.34), channel_id=1, source_target_pairs={{0,4},{4,0},{8,12},{12,8},{1,5},{5,1},{9,13},{13,9},{2,6},{6,2},{1... | collective-permute-start | bytes 245768 | tf_op jit(solution)/shard_map/ppermute | solution.py:31
  12.8 7.7 %collective-permute-start.3 = (bf16[64,640]{1,0:T(8,128)(2,1)S(1)}, bf16[64,640]{1,0:T(8,128)(2,1)S(1)}, u32[]{:S(2)}, u32[]{:S(2)}) collective-permute-start(bf16[64,640]{1,0:T(8,128)(2,1)S(1)} %get-tuple-element.35), channel_id=1, source_target_pairs={{0,8},{4,12},{8,0},{12,4},{1,9},{5,13},{9,1},{13,5},{2,10},{6,14},... | collective-permute-start | bytes 245768 | tf_op jit(solution)/shard_map/ppermute | solution.py:31
  15.2 5.4 %collective-permute-start.4 = (bf16[64,640]{1,0:T(8,128)(2,1)S(1)}, bf16[64,640]{1,0:T(8,128)(2,1)S(1)}, u32[]{:S(2)}, u32[]{:S(2)}) collective-permute-start(bf16[64,640]{1,0:T(8,128)(2,1)S(1)} %get-tuple-element.36), channel_id=1, source_target_pairs={{0,12},{4,8},{8,4},{12,0},{1,13},{5,9},{9,5},{13,1},{2,14},{6,10},... | collective-permute-start | bytes 245768 | tf_op jit(solution)/shard_map/ppermute | solution.py:31
  15.2 5.3 %copy-start.1 = (bf16[64,64]{1,0:T(8,128)(2,1)S(1)}, bf16[64,64]{1,0:T(8,128)(2,1)}, u32[]{:S(2)}) copy-start(bf16[64,64]{1,0:T(8,128)(2,1)} %refs_7_.1) | copy-start | bytes 24580
  15.2 5.3 %copy-start.2 = (bf16[64,64]{1,0:T(8,128)(2,1)S(1)}, bf16[64,64]{1,0:T(8,128)(2,1)}, u32[]{:S(2)}) copy-start(bf16[64,64]{1,0:T(8,128)(2,1)} %refs_8_.1) | copy-start | bytes 24580
  15.3 5.3 %copy-start.3 = (bf16[64,64]{1,0:T(8,128)(2,1)S(1)}, bf16[64,64]{1,0:T(8,128)(2,1)}, u32[]{:S(2)}) copy-start(bf16[64,64]{1,0:T(8,128)(2,1)} %refs_9_.1) | copy-start | bytes 24580
  15.3 5.3 %copy-start.4 = (bf16[64,64]{1,0:T(8,128)(2,1)S(1)}, bf16[64,64]{1,0:T(8,128)(2,1)}, u32[]{:S(2)}) copy-start(bf16[64,64]{1,0:T(8,128)(2,1)} %refs_10_.1) | copy-start | bytes 24580
  20.5 0.7 copy-start.5
  35.7 4.5 %collective-permute-start.5 = (bf16[64,640]{1,0:T(8,128)(2,1)S(1)}, bf16[64,640]{1,0:T(8,128)(2,1)S(1)}, u32[]{:S(2)}, u32[]{:S(2)}) collective-permute-start(bf16[64,640]{1,0:T(8,128)(2,1)S(1)} %get-tuple-element.39), channel_id=1, source_target_pairs={{0,4},{4,0},{8,12},{12,8},{1,5},{5,1},{9,13},{13,9},{2,6},{6,2},{1... | collective-permute-start | bytes 245768 | tf_op jit(solution)/shard_map/ppermute | solution.py:31
  37.1 4.6 %collective-permute-start.6 = (bf16[64,640]{1,0:T(8,128)(2,1)S(1)}, bf16[64,640]{1,0:T(8,128)(2,1)S(1)}, u32[]{:S(2)}, u32[]{:S(2)}) collective-permute-start(bf16[64,640]{1,0:T(8,128)(2,1)S(1)} %get-tuple-element.40), channel_id=1, source_target_pairs={{0,8},{4,12},{8,0},{12,4},{1,9},{5,13},{9,1},{13,5},{2,10},{6,14},... | collective-permute-start | bytes 245768 | tf_op jit(solution)/shard_map/ppermute | solution.py:31
  38.5 7.2 %collective-permute-start.7 = (bf16[64,640]{1,0:T(8,128)(2,1)S(1)}, bf16[64,640]{1,0:T(8,128)(2,1)S(1)}, u32[]{:S(2)}, u32[]{:S(2)}) collective-permute-start(bf16[64,640]{1,0:T(8,128)(2,1)S(1)} %get-tuple-element.41), channel_id=1, source_target_pairs={{0,12},{4,8},{8,4},{12,0},{1,13},{5,9},{9,5},{13,1},{2,14},{6,10},... | collective-permute-start | bytes 245768 | tf_op jit(solution)/shard_map/ppermute | solution.py:31
  46.7 6.1 %collective-permute-start.10 = (bf16[16,64,128]{2,1,0:T(8,128)(2,1)S(1)}, bf16[16,64,128]{2,1,0:T(8,128)(2,1)S(1)}, u32[]{:S(2)}, u32[]{:S(2)}) collective-permute-start(bf16[16,64,128]{2,1,0:T(8,128)(2,1)S(1)} %get-tuple-element.48), channel_id=1, source_target_pairs={{0,1},{1,0},{2,3},{3,2},{4,5},{5,4},{6,7},{7,6},{8,9},{9,8},{10,11... | collective-permute-start | bytes 786440 | tf_op jit(solution)/shard_map/ppermute | solution.py:39
  47.9 8.9 %collective-permute-start.11 = (bf16[16,64,128]{2,1,0:T(8,128)(2,1)S(1)}, bf16[16,64,128]{2,1,0:T(8,128)(2,1)S(1)}, u32[]{:S(2)}, u32[]{:S(2)}) collective-permute-start(bf16[16,64,128]{2,1,0:T(8,128)(2,1)S(1)} %get-tuple-element.49), channel_id=1, source_target_pairs={{1,2},{2,1},{5,6},{6,5},{9,10},{10,9},{13,14},{14,13},{17,18},{18,... | collective-permute-start | bytes 786440 | tf_op jit(solution)/shard_map/ppermute | solution.py:40
  49.8 1.4 %collective-permute-start.8 = (f32[224,128]{1,0:T(8,128)S(1)}, f32[224,128]{1,0:T(8,128)S(1)}, u32[]{:S(2)}, u32[]{:S(2)}) collective-permute-start(f32[224,128]{1,0:T(8,128)S(1)} %get-tuple-element.46), channel_id=1, source_target_pairs={{0,1},{1,0},{2,3},{3,2},{4,5},{5,4},{6,7},{7,6},{8,9},{9,8},{10,11... | collective-permute-start | bytes 344072 | tf_op jit(solution)/shard_map/ppermute | solution.py:31
  51.2 7.3 %collective-permute-start.9 = (f32[224,128]{1,0:T(8,128)S(1)}, f32[224,128]{1,0:T(8,128)S(1)}, u32[]{:S(2)}, u32[]{:S(2)}) collective-permute-start(f32[224,128]{1,0:T(8,128)S(1)} %add.17), channel_id=1, source_target_pairs={{0,2},{1,3},{2,0},{3,1},{4,6},{5,7},{6,4},{7,5},{8,10},{9,11},{10,... | collective-permute-start | bytes 344072 | tf_op jit(solution)/shard_map/ppermute | solution.py:31
  58.6 5.0 %collective-permute-start.14 = (bf16[224,128]{1,0:T(8,128)(2,1)S(1)}, bf16[224,128]{1,0:T(8,128)(2,1)S(1)}, u32[]{:S(2)}, u32[]{:S(2)}) collective-permute-start(bf16[224,128]{1,0:T(8,128)(2,1)S(1)} %add_convert_fusion), channel_id=1, source_target_pairs={{0,12},{4,8},{8,4},{12,0},{1,13},{5,9},{9,5},{13,1},{2,14},{6,10},... | collective-permute-start | bytes 172040 | tf_op jit(solution)/shard_map/ppermute | solution.py:31
  60.5 6.5 %collective-permute-start.13 = (bf16[224,128]{1,0:T(8,128)(2,1)S(1)}, bf16[224,128]{1,0:T(8,128)(2,1)S(1)}, u32[]{:S(2)}, u32[]{:S(2)}) collective-permute-start(bf16[224,128]{1,0:T(8,128)(2,1)S(1)} %add_convert_fusion), channel_id=1, source_target_pairs={{0,8},{4,12},{8,0},{12,4},{1,9},{5,13},{9,1},{13,5},{2,10},{6,14},... | collective-permute-start | bytes 172040 | tf_op jit(solution)/shard_map/ppermute | solution.py:31
  61.4 5.6 %collective-permute-start.12 = (bf16[224,128]{1,0:T(8,128)(2,1)S(1)}, bf16[224,128]{1,0:T(8,128)(2,1)S(1)}, u32[]{:S(2)}, u32[]{:S(2)}) collective-permute-start(bf16[224,128]{1,0:T(8,128)(2,1)S(1)} %add_convert_fusion), channel_id=1, source_target_pairs={{0,4},{4,0},{8,12},{12,8},{1,5},{5,1},{9,13},{13,9},{2,6},{6,2},{1... | collective-permute-start | bytes 172040 | tf_op jit(solution)/shard_map/ppermute | solution.py:31
  67.0 2.1 %collective-permute-start.15 = (f32[224,128]{1,0:T(8,128)S(1)}, f32[224,128]{1,0:T(8,128)S(1)}, u32[]{:S(2)}, u32[]{:S(2)}) collective-permute-start(f32[224,128]{1,0:T(8,128)S(1)} %convert_add_fusion.mine_ref), channel_id=1, source_target_pairs={{0,1},{1,0},{2,3},{3,2},{4,5},{5,4},{6,7},{7,6},{8,9},{9,8},{10,11... | collective-permute-start | bytes 344072 | tf_op jit(solution)/shard_map/ppermute | solution.py:31

commit v4 on v3

--- a/solution.py
+++ b/solution.py
@@ -588,28 +588,27 @@
     return out, output, g_weights, g_gain
 
 
-def reduce_views(own):
+def reduce_views(own, beside):
     count = lax.axis_size("view")
     if not pairwise(count):
-        return lax.psum(own, "view")
+        return lax.psum(own, "view"), beside
     own = own.astype(BF16)
-    parts = [own] + [swap(own, "view", step) for step in range(1, count)]
-    total = 0.0
+    parts = [swap(own, "view", step) for step in range(1, count)]
+    parts, beside = lax.optimization_barrier((parts, beside))
+    total = own.astype(F32)
     for part in parts:
         total = total + part.astype(F32)
-    return total
-
-
-def reduce_rows(own, beside):
+    return total, beside
+
+
+def reduce_rows(own):
     count = lax.axis_size("row")
     step = 2
     while step < count:
-        other = swap(own, "row", step)
-        if step == 2:
-            other, beside = lax.optimization_barrier((other, beside))
-        own = own + other
+        own = own.astype(BF16)
+        own = own.astype(F32) + swap(own, "row", step).astype(F32)
         step *= 2
-    return own, beside
+    return own
 
 
 def body(inputs, cotangent, keep, w_conv, gain, w_query, w_key, w_value, w_out):
@@ -631,15 +630,15 @@
     wires, output, g_weights, g_gain = angular(
         wires, cot, keep, gain, w_query, w_key, w_value, w_out, blocks
     )
-    wires = exchange(wires)
     output = jnp.transpose(output.reshape(row_dev, breadth, chan, views), (2, 3, 0, 1))
+    wires, output = lax.optimization_barrier((exchange(wires), output))
     near, far, own, kept, sent = weight_grads(wires, frame, g_weights, g_gain, view_dev, blocks)
     other = swap(sent, "row", 1)
+    other, near, far = lax.optimization_barrier((other, near, far))
+    part = reduce_rows(kept + other)
     near, far = halo_swap(near, far)
-    part = kept + other
     d_input = input_grad(own, near, far, w_conv, view_dev, blocks)
-    part, d_input = reduce_rows(part, d_input)
-    part = reduce_views(part)
+    part, d_input = reduce_views(part, d_input)
     other = swap(part, "row", 1)
     g_conv, g_query, g_key, g_value, g_out, g_gain = unpack(part, other, chan, blocks)
     d_input = jnp.transpose(d_input, (0, 3, 1, 2))

time: 70.4 us -> 64.7 us (0.919)
  waiting for transfers between devices: 25.6 us -> 19.6 us
    ppermute x2, waiting for transfers between devices: 7.99 us -> 4.7 us  [halo_swap(): got_far = lax.ppermute(far, 'row', pairs) if pairs else jnp.zeros_like(far)]
    ppermute x12, waiting for transfers between devices: 17.7 us -> 14.9 us  [swap(): return lax.ppermute(cells, axis, [(i, i ^ step) for i in range(count)])]
    ppermute x2, starting transfers between devices: 6.41 us -> 7.78 us  [halo_swap(): got_far = lax.ppermute(far, 'row', pairs) if pairs else jnp.zeros_like(far)]
  transfers between devices with their start and end apart: 16 -> 16, of which waited for: 10 -> 9; matrix products, arithmetic and copies ran while one was open for 2% -> 2% of each run, Pallas kernels for 2% -> 3%
where the time goes in v4:
time: 64.7 us; the launch traced here: 64.2 us
  starting transfers between devices  21.5 us (33%)
  waiting for transfers between devices  19.6 us (30%)
  Pallas kernels  19 us (29%)
  local copies, waits for them, and re-layouts  3.06 us (5%)
  between operations  0.84 us (1%)
    ppermute x12, waiting for transfers between devices, swap(): return lax.ppermute(cells, axis, [(i, i ^ step) for i in range(count)])  14.9 us
    pallas_call x1, Pallas kernels, angular(): pl.pallas_call(functools.partial(angular_kernel, scale, 10, len(wires)),...  14.5 us
    ppermute x12, starting transfers between devices, swap(): return lax.ppermute(cells, axis, [(i, i ^ step) for i in range(count)])  13.1 us
    ppermute x2, starting transfers between devices, halo_swap(): got_far = lax.ppermute(far, 'row', pairs) if pairs else jnp.zeros_like(far)  7.78 us
    ppermute x2, waiting for transfers between devices, halo_swap(): got_far = lax.ppermute(far, 'row', pairs) if pairs else jnp.zeros_like(far)  4.7 us
    unnamed x17, local copies, waits for them, and re-layouts  1.91 us
    pallas_call x1, Pallas kernels, input_grad(): pl.pallas_call(input_kernel, out_shape=jax.ShapeDtypeStruct((chan, size /...  1.74 us
  transfers between devices with their start and end apart: 16, of which 9 were waited for; matrix products, arithmetic and copies ran while one was open for 2% of the time, Pallas kernels for 3%

profile of v4, /device:TPU:1, one launch (start us, length us, event | category | flops | bytes accessed | tf_op | source)
XLA Modules:
  0.0 64.2 jit_solution(14819613299929500265)
XLA Ops:
  0.6 1.2 %copy.22 = bf16[64,73,2,16]{1,0,3,2:T(8,128)(2,1)S(1)} copy(bf16[64,73,2,16]{1,3,2,0:T(8,128)(2,1)} %param.9) | data formatting | bytes 598016 | tf_op args[0]
  2.0 4.5 %collective-permute-start.1 = (bf16[16,64,73]{2,1,0:T(8,128)(2,1)S(1)}, bf16[16,64,73]{2,1,0:T(8,128)(2,1)S(1)}, u32[]{:S(2)}, u32[]{:S(2)}) collective-permute-start(bf16[16,64,73]{2,1,0:T(8,128)(2,1)S(1)} %get-tuple-element.78), channel_id=1, source_target_pairs={{1,2},{2,1},{5,6},{6,5},{9,10},{10,9},{13,14},{14,13},{17,18},{18,... | collective-permute-start | bytes 448520 | tf_op jit(solution)/shard_map/ppermute | solution.py:40
  6.5 4.0 %collective-permute-done.1.far_ref = bf16[16,64,73]{2,1,0:T(8,128)(2,1)S(1)} collective-permute-done((bf16[16,64,73]{2,1,0:T(8,128)(2,1)S(1)}, bf16[16,64,73]{2,1,0:T(8,128)(2,1)S(1)}, u32[]{:S(2)}, u32[]{:S(2)}) %collective-permute-start.1) | collective-permute-done | bytes 149536 | tf_op jit(solution)/shard_map/ppermute | solution.py:40
  10.5 0.9 %conv.1 = (bf16[64,640]{1,0:T(8,128)(2,1)S(1)}, bf16[64,640]{1,0:T(8,128)(2,1)S(1)}, bf16[64,640]{1,0:T(8,128)(2,1)S(1)}, bf16[64,640]{1,0:T(8,128)(2,1)S(1)}, bf16[16,256,128]{2,1,0:T(8,128)(2,1)S(1)}) custom-call(bf16[2,16,64,73]{3,2,1,0:T(8,128)(2,1)S(1)} %bitcast.19, bf16[16,64,73]{2,1,0:T(8,128)(2,1)S(1)} %collective-permute-done.near_ref, ...), custom_call_target="tpu_custom_call" | custom-call | tf_op jit(solution)/shard_map/conv/pallas_call | solution.py:176
  11.5 1.4 %collective-permute-start.2 = (bf16[64,640]{1,0:T(8,128)(2,1)S(1)}, bf16[64,640]{1,0:T(8,128)(2,1)S(1)}, u32[]{:S(2)}, u32[]{:S(2)}) collective-permute-start(bf16[64,640]{1,0:T(8,128)(2,1)S(1)} %get-tuple-element.44), channel_id=1, source_target_pairs={{0,4},{4,0},{8,12},{12,8},{1,5},{5,1},{9,13},{13,9},{2,6},{6,2},{1... | collective-permute-start | bytes 245768 | tf_op jit(solution)/shard_map/ppermute | solution.py:31
  12.8 2.3 %collective-permute-start.3 = (bf16[64,640]{1,0:T(8,128)(2,1)S(1)}, bf16[64,640]{1,0:T(8,128)(2,1)S(1)}, u32[]{:S(2)}, u32[]{:S(2)}) collective-permute-start(bf16[64,640]{1,0:T(8,128)(2,1)S(1)} %get-tuple-element.45), channel_id=1, source_target_pairs={{0,8},{4,12},{8,0},{12,4},{1,9},{5,13},{9,1},{13,5},{2,10},{6,14},... | collective-permute-start | bytes 245768 | tf_op jit(solution)/shard_map/ppermute | solution.py:31
  15.6 4.9 %collective-permute-done.3.refs_2_ = bf16[64,640]{1,0:T(8,128)(2,1)S(1)} collective-permute-done((bf16[64,640]{1,0:T(8,128)(2,1)S(1)}, bf16[64,640]{1,0:T(8,128)(2,1)S(1)}, u32[]{:S(2)}, u32[]{:S(2)}) %collective-permute-start.3) | collective-permute-done | bytes 81952 | tf_op jit(solution)/shard_map/ppermute | solution.py:31
  21.2 14.5 %angular.1 = (bf16[64,640]{1,0:T(8,128)(2,1)S(1)}, bf16[64,640]{1,0:T(8,128)(2,1)S(1)}, bf16[64,640]{1,0:T(8,128)(2,1)S(1)}, bf16[64,640]{1,0:T(8,128)(2,1)S(1)}...) custom-call(bf16[64,640]{1,0:T(8,128)(2,1)S(1)} %get-tuple-element.43.refs_0_, ...), custom_call_target="tpu_custom_call" | custom-call | tf_op jit(solution)/shard_map/angular/pallas_call | solution.py:561
  35.7 1.4 %collective-permute-start.5 = (bf16[64,640]{1,0:T(8,128)(2,1)S(1)}, bf16[64,640]{1,0:T(8,128)(2,1)S(1)}, u32[]{:S(2)}, u32[]{:S(2)}) collective-permute-start(bf16[64,640]{1,0:T(8,128)(2,1)S(1)} %get-tuple-element.48), channel_id=1, source_target_pairs={{0,4},{4,0},{8,12},{12,8},{1,5},{5,1},{9,13},{13,9},{2,6},{6,2},{1... | collective-permute-start | bytes 245768 | tf_op jit(solution)/shard_map/ppermute | solution.py:31
  37.1 1.3 %collective-permute-start.6 = (bf16[64,640]{1,0:T(8,128)(2,1)S(1)}, bf16[64,640]{1,0:T(8,128)(2,1)S(1)}, u32[]{:S(2)}, u32[]{:S(2)}) collective-permute-start(bf16[64,640]{1,0:T(8,128)(2,1)S(1)} %get-tuple-element.49), channel_id=1, source_target_pairs={{0,8},{4,12},{8,0},{12,4},{1,9},{5,13},{9,1},{13,5},{2,10},{6,14},... | collective-permute-start | bytes 245768 | tf_op jit(solution)/shard_map/ppermute | solution.py:31
  38.5 0.9 %collective-permute-start.7 = (bf16[64,640]{1,0:T(8,128)(2,1)S(1)}, bf16[64,640]{1,0:T(8,128)(2,1)S(1)}, u32[]{:S(2)}, u32[]{:S(2)}) collective-permute-start(bf16[64,640]{1,0:T(8,128)(2,1)S(1)} %get-tuple-element.50), channel_id=1, source_target_pairs={{0,12},{4,8},{8,4},{12,0},{1,13},{5,9},{9,5},{13,1},{2,14},{6,10},... | collective-permute-start | bytes 245768 | tf_op jit(solution)/shard_map/ppermute | solution.py:31
  39.3 1.1 %copy.23 = bf16[2,4,64,292]{3,1,0,2:T(4,128)(2,1)} copy(bf16[2,4,64,292]{3,2,1,0:T(8,128)(2,1)S(1)} %bitcast.22) | data formatting | bytes 598016 | tf_op jit(solution)/shard_map/reshape | solution.py:633
  40.4 1.4 %collective-permute-done.6.refs_2_ = bf16[64,640]{1,0:T(8,128)(2,1)S(1)} collective-permute-done((bf16[64,640]{1,0:T(8,128)(2,1)S(1)}, bf16[64,640]{1,0:T(8,128)(2,1)S(1)}, u32[]{:S(2)}, u32[]{:S(2)}) %collective-permute-start.6) | collective-permute-done | bytes 81952 | tf_op jit(solution)/shard_map/ppermute | solution.py:31
  41.8 3.9 %collective-permute-done.7.refs_3_ = bf16[64,640]{1,0:T(8,128)(2,1)S(1)} collective-permute-done((bf16[64,640]{1,0:T(8,128)(2,1)S(1)}, bf16[64,640]{1,0:T(8,128)(2,1)S(1)}, u32[]{:S(2)}, u32[]{:S(2)}) %collective-permute-start.7) | collective-permute-done | bytes 81952 | tf_op jit(solution)/shard_map/ppermute | solution.py:31
  45.7 1.0 %weights.1 = (bf16[16,64,128]{2,1,0:T(8,128)(2,1)S(1)}, bf16[16,64,128]{2,1,0:T(8,128)(2,1)S(1)}, bf16[16,128,128]{2,1,0:T(8,128)(2,1)S(1)}, f32[224,128]{1,0:T(8,128)S(1)}, f32[224,128]{1,0:T(8,128)S(1)}) custom-call(bf16[64,640]{1,0:T(8,128)(2,1)S(1)} %get-tuple-element.53.refs_0_, bf16[64,640]{1,0:T(8,128)(2,1)S(1)} %collective-permute-done.5.refs_1_, ...), custom_call_target="tpu_custom_call" | custom-call | tf_op jit(solution)/shard_map/weights/pallas_call | solution.py:277
  46.7 1.2 %collective-permute-start.8 = (f32[224,128]{1,0:T(8,128)S(1)}, f32[224,128]{1,0:T(8,128)S(1)}, u32[]{:S(2)}, u32[]{:S(2)}) collective-permute-start(f32[224,128]{1,0:T(8,128)S(1)} %get-tuple-element.61), channel_id=1, source_target_pairs={{0,1},{1,0},{2,3},{3,2},{4,5},{5,4},{6,7},{7,6},{8,9},{9,8},{10,11... | collective-permute-start | bytes 344072 | tf_op jit(solution)/shard_map/ppermute | solution.py:31
  47.9 1.0 %collective-permute-done.8 = f32[224,128]{1,0:T(8,128)S(1)} collective-permute-done((f32[224,128]{1,0:T(8,128)S(1)}, f32[224,128]{1,0:T(8,128)S(1)}, u32[]{:S(2)}, u32[]{:S(2)}) %collective-permute-start.8) | collective-permute-done | bytes 114720 | tf_op jit(solution)/shard_map/ppermute | solution.py:31
  49.6 3.3 %collective-permute-start.14 = (bf16[16,64,128]{2,1,0:T(8,128)(2,1)S(1)}, bf16[16,64,128]{2,1,0:T(8,128)(2,1)S(1)}, u32[]{:S(2)}, u32[]{:S(2)}) collective-permute-start(bf16[16,64,128]{2,1,0:T(8,128)(2,1)S(1)} %get-tuple-element.67), channel_id=1, source_target_pairs={{1,2},{2,1},{5,6},{6,5},{9,10},{10,9},{13,14},{14,13},{17,18},{18,... | collective-permute-start | bytes 786440 | tf_op jit(solution)/shard_map/ppermute | solution.py:40
  52.9 1.9 %collective-permute-start.12 = (bf16[224,128]{1,0:T(8,128)(2,1)S(1)}, bf16[224,128]{1,0:T(8,128)(2,1)S(1)}, u32[]{:S(2)}, u32[]{:S(2)}) collective-permute-start(bf16[224,128]{1,0:T(8,128)(2,1)S(1)} %add_convert_fusion), channel_id=1, source_target_pairs={{0,12},{4,8},{8,4},{12,0},{1,13},{5,9},{9,5},{13,1},{2,14},{6,10},... | collective-permute-start | bytes 172040 | tf_op jit(solution)/shard_map/ppermute | solution.py:31
  54.8 0.9 %collective-permute-start.11 = (bf16[224,128]{1,0:T(8,128)(2,1)S(1)}, bf16[224,128]{1,0:T(8,128)(2,1)S(1)}, u32[]{:S(2)}, u32[]{:S(2)}) collective-permute-start(bf16[224,128]{1,0:T(8,128)(2,1)S(1)} %add_convert_fusion), channel_id=1, source_target_pairs={{0,8},{4,12},{8,0},{12,4},{1,9},{5,13},{9,1},{13,5},{2,10},{6,14},... | collective-permute-start | bytes 172040 | tf_op jit(solution)/shard_map/ppermute | solution.py:31
  57.2 1.7 %input.1 = bf16[64,2,16,73]{3,2,1,0:T(8,128)(2,1)} custom-call(bf16[16,128,128]{2,1,0:T(8,128)(2,1)S(1)} %get-tuple-element.65.own_ref, bf16[16,64,128]{2,1,0:T(8,128)(2,1)S(1)} %collective-permute-done.13.near_ref, bf16[16,64,128]{2,1,0:T(8,128)(2,1)S(1)} %collective-permute-done.14.far_ref, bf16[3,3,64,64]{3,2,1,0:T(8,128)(2,1)S(1)} %bitcast.21), custom_call_target="tpu_custom_call" | custom-call | tf_op jit(solution)/shard_map/input/pallas_call | solution.py:332
  59.0 2.5 %collective-permute-done.11 = bf16[224,128]{1,0:T(8,128)(2,1)S(1)} collective-permute-done((bf16[224,128]{1,0:T(8,128)(2,1)S(1)}, bf16[224,128]{1,0:T(8,128)(2,1)S(1)}, u32[]{:S(2)}, u32[]{:S(2)}) %collective-permute-start.11) | collective-permute-done | bytes 57376 | tf_op jit(solution)/shard_map/ppermute | solution.py:31
  62.4 1.0 %collective-permute-done.15.other_ref = f32[224,128]{1,0:T(8,128)S(1)} collective-permute-done((f32[224,128]{1,0:T(8,128)S(1)}, f32[224,128]{1,0:T(8,128)S(1)}, u32[]{:S(2)}, u32[]{:S(2)}) %collective-permute-start.15) | collective-permute-done | bytes 114720 | tf_op jit(solution)/shard_map/ppermute | solution.py:31
  63.3 0.9 %unpack.1 = (f32[3,3,64,64]{3,2,1,0:T(8,128)}, f32[64,64]{1,0:T(8,128)}, f32[64,64]{1,0:T(8,128)}, f32[64,64]{1,0:T(8,128)}, f32[64,64]{1,0:T(8,128)}, /*index=5*/f32[1,64]{1,0:T(1,128)}) custom-call(f32[224,128]{1,0:T(8,128)S(1)} %convert_add_fusion.mine_ref, f32[224,128]{1,0:T(8,128)S(1)} %collective-permute-done.15.other_ref), custom_call_target="tpu_custom_call" | custom-call | tf_op jit(solution)/shard_map/unpack/pallas_call | solution.py:375
  (38 shorter events, 4.3 us)
Async XLA Ops:
  1.9 8.6 %copy-start = (bf16[64,64,3,3]{1,0,3,2:T(8,128)(2,1)S(1)}, bf16[64,64,3,3]{1,0,3,2:T(8,128)(2,1)}, u32[]{:S(2)}) copy-start(bf16[64,64,3,3]{1,0,3,2:T(8,128)(2,1)} %param.12) | copy-start | bytes 221188
  2.0 8.5 %collective-permute-start.1 = (bf16[16,64,73]{2,1,0:T(8,128)(2,1)S(1)}, bf16[16,64,73]{2,1,0:T(8,128)(2,1)S(1)}, u32[]{:S(2)}, u32[]{:S(2)}) collective-permute-start(bf16[16,64,73]{2,1,0:T(8,128)(2,1)S(1)} %get-tuple-element.78), channel_id=1, source_target_pairs={{1,2},{2,1},{5,6},{6,5},{9,10},{10,9},{13,14},{14,13},{17,18},{18,... | collective-permute-start | bytes 448520 | tf_op jit(solution)/shard_map/ppermute | solution.py:40
  6.5 4.0 %collective-permute-start = (bf16[16,64,73]{2,1,0:T(8,128)(2,1)S(1)}, bf16[16,64,73]{2,1,0:T(8,128)(2,1)S(1)}, u32[]{:S(2)}, u32[]{:S(2)}) collective-permute-start(bf16[16,64,73]{2,1,0:T(8,128)(2,1)S(1)} %get-tuple-element.79), channel_id=1, source_target_pairs={{0,1},{1,0},{2,3},{3,2},{4,5},{5,4},{6,7},{7,6},{8,9},{9,8},{10,11... | collective-permute-start | bytes 448520 | tf_op jit(solution)/shard_map/ppermute | solution.py:39
  10.5 4.7 %copy-start.6 = (bf16[64,292,2,4]{1,3,2,0:T(4,128)(2,1)S(1)}, bf16[64,292,2,4]{1,3,2,0:T(4,128)(2,1)}, u32[]{:S(2)}) copy-start(bf16[64,292,2,4]{1,3,2,0:T(4,128)(2,1)} %param.10) | copy-start | bytes 897028
  11.5 3.7 %copy-start.7 = (s32[292]{0:T(512)S(1)}, s32[292]{0:T(512)}, u32[]{:S(2)}) copy-start(s32[292]{0:T(512)} %param.11) | copy-start | bytes 3508
  11.5 4.2 %collective-permute-start.2 = (bf16[64,640]{1,0:T(8,128)(2,1)S(1)}, bf16[64,640]{1,0:T(8,128)(2,1)S(1)}, u32[]{:S(2)}, u32[]{:S(2)}) collective-permute-start(bf16[64,640]{1,0:T(8,128)(2,1)S(1)} %get-tuple-element.44), channel_id=1, source_target_pairs={{0,4},{4,0},{8,12},{12,8},{1,5},{5,1},{9,13},{13,9},{2,6},{6,2},{1... | collective-permute-start | bytes 245768 | tf_op jit(solution)/shard_map/ppermute | solution.py:31
  12.8 7.7 %collective-permute-start.3 = (bf16[64,640]{1,0:T(8,128)(2,1)S(1)}, bf16[64,640]{1,0:T(8,128)(2,1)S(1)}, u32[]{:S(2)}, u32[]{:S(2)}) collective-permute-start(bf16[64,640]{1,0:T(8,128)(2,1)S(1)} %get-tuple-element.45), channel_id=1, source_target_pairs={{0,8},{4,12},{8,0},{12,4},{1,9},{5,13},{9,1},{13,5},{2,10},{6,14},... | collective-permute-start | bytes 245768 | tf_op jit(solution)/shard_map/ppermute | solution.py:31
  15.2 5.4 %collective-permute-start.4 = (bf16[64,640]{1,0:T(8,128)(2,1)S(1)}, bf16[64,640]{1,0:T(8,128)(2,1)S(1)}, u32[]{:S(2)}, u32[]{:S(2)}) collective-permute-start(bf16[64,640]{1,0:T(8,128)(2,1)S(1)} %get-tuple-element.46), channel_id=1, source_target_pairs={{0,12},{4,8},{8,4},{12,0},{1,13},{5,9},{9,5},{13,1},{2,14},{6,10},... | collective-permute-start | bytes 245768 | tf_op jit(solution)/shard_map/ppermute | solution.py:31
  15.2 5.3 %copy-start.1 = (bf16[64,64]{1,0:T(8,128)(2,1)S(1)}, bf16[64,64]{1,0:T(8,128)(2,1)}, u32[]{:S(2)}) copy-start(bf16[64,64]{1,0:T(8,128)(2,1)} %refs_7_.1) | copy-start | bytes 24580
  15.2 5.3 %copy-start.2 = (bf16[64,64]{1,0:T(8,128)(2,1)S(1)}, bf16[64,64]{1,0:T(8,128)(2,1)}, u32[]{:S(2)}) copy-start(bf16[64,64]{1,0:T(8,128)(2,1)} %refs_8_.1) | copy-start | bytes 24580
  15.3 5.3 %copy-start.3 = (bf16[64,64]{1,0:T(8,128)(2,1)S(1)}, bf16[64,64]{1,0:T(8,128)(2,1)}, u32[]{:S(2)}) copy-start(bf16[64,64]{1,0:T(8,128)(2,1)} %refs_9_.1) | copy-start | bytes 24580
  15.3 5.3 %copy-start.4 = (bf16[64,64]{1,0:T(8,128)(2,1)S(1)}, bf16[64,64]{1,0:T(8,128)(2,1)}, u32[]{:S(2)}) copy-start(bf16[64,64]{1,0:T(8,128)(2,1)} %refs_10_.1) | copy-start | bytes 24580
  20.5 0.7 %copy-start.5 = (f32[64]{0:T(128)S(1)}, f32[64]{0:T(128)}, u32[]{:S(2)}) copy-start(f32[64]{0:T(128)} %param.13) | copy-start | bytes 772
  35.7 4.7 %collective-permute-start.5 = (bf16[64,640]{1,0:T(8,128)(2,1)S(1)}, bf16[64,640]{1,0:T(8,128)(2,1)S(1)}, u32[]{:S(2)}, u32[]{:S(2)}) collective-permute-start(bf16[64,640]{1,0:T(8,128)(2,1)S(1)} %get-tuple-element.48), channel_id=1, source_target_pairs={{0,4},{4,0},{8,12},{12,8},{1,5},{5,1},{9,13},{13,9},{2,6},{6,2},{1... | collective-permute-start | bytes 245768 | tf_op jit(solution)/shard_map/ppermute | solution.py:31
  37.1 4.6 %collective-permute-start.6 = (bf16[64,640]{1,0:T(8,128)(2,1)S(1)}, bf16[64,640]{1,0:T(8,128)(2,1)S(1)}, u32[]{:S(2)}, u32[]{:S(2)}) collective-permute-start(bf16[64,640]{1,0:T(8,128)(2,1)S(1)} %get-tuple-element.49), channel_id=1, source_target_pairs={{0,8},{4,12},{8,0},{12,4},{1,9},{5,13},{9,1},{13,5},{2,10},{6,14},... | collective-permute-start | bytes 245768 | tf_op jit(solution)/shard_map/ppermute | solution.py:31
  38.5 7.2 %collective-permute-start.7 = (bf16[64,640]{1,0:T(8,128)(2,1)S(1)}, bf16[64,640]{1,0:T(8,128)(2,1)S(1)}, u32[]{:S(2)}, u32[]{:S(2)}) collective-permute-start(bf16[64,640]{1,0:T(8,128)(2,1)S(1)} %get-tuple-element.50), channel_id=1, source_target_pairs={{0,12},{4,8},{8,4},{12,0},{1,13},{5,9},{9,5},{13,1},{2,14},{6,10},... | collective-permute-start | bytes 245768 | tf_op jit(solution)/shard_map/ppermute | solution.py:31
  46.7 2.2 %collective-permute-start.8 = (f32[224,128]{1,0:T(8,128)S(1)}, f32[224,128]{1,0:T(8,128)S(1)}, u32[]{:S(2)}, u32[]{:S(2)}) collective-permute-start(f32[224,128]{1,0:T(8,128)S(1)} %get-tuple-element.61), channel_id=1, source_target_pairs={{0,1},{1,0},{2,3},{3,2},{4,5},{5,4},{6,7},{7,6},{8,9},{9,8},{10,11... | collective-permute-start | bytes 344072 | tf_op jit(solution)/shard_map/ppermute | solution.py:31
  48.9 4.0 %collective-permute-start.9 = (bf16[224,128]{1,0:T(8,128)(2,1)S(1)}, bf16[224,128]{1,0:T(8,128)(2,1)S(1)}, u32[]{:S(2)}, u32[]{:S(2)}) collective-permute-start(bf16[224,128]{1,0:T(8,128)(2,1)S(1)} %add_convert_fusion.1), channel_id=1, source_target_pairs={{0,2},{1,3},{2,0},{3,1},{4,6},{5,7},{6,4},{7,5},{8,10},{9,11},{10,... | collective-permute-start | bytes 172040 | tf_op jit(solution)/shard_map/ppermute | solution.py:31
  49.0 7.5 %collective-permute-start.13 = (bf16[16,64,128]{2,1,0:T(8,128)(2,1)S(1)}, bf16[16,64,128]{2,1,0:T(8,128)(2,1)S(1)}, u32[]{:S(2)}, u32[]{:S(2)}) collective-permute-start(bf16[16,64,128]{2,1,0:T(8,128)(2,1)S(1)} %get-tuple-element.66), channel_id=1, source_target_pairs={{0,1},{1,0},{2,3},{3,2},{4,5},{5,4},{6,7},{7,6},{8,9},{9,8},{10,11... | collective-permute-start | bytes 786440 | tf_op jit(solution)/shard_map/ppermute | solution.py:39
  49.6 7.7 %collective-permute-start.14 = (bf16[16,64,128]{2,1,0:T(8,128)(2,1)S(1)}, bf16[16,64,128]{2,1,0:T(8,128)(2,1)S(1)}, u32[]{:S(2)}, u32[]{:S(2)}) collective-permute-start(bf16[16,64,128]{2,1,0:T(8,128)(2,1)S(1)} %get-tuple-element.67), channel_id=1, source_target_pairs={{1,2},{2,1},{5,6},{6,5},{9,10},{10,9},{13,14},{14,13},{17,18},{18,... | collective-permute-start | bytes 786440 | tf_op jit(solution)/shard_map/ppermute | solution.py:40
  52.9 6.1 %collective-permute-start.12 = (bf16[224,128]{1,0:T(8,128)(2,1)S(1)}, bf16[224,128]{1,0:T(8,128)(2,1)S(1)}, u32[]{:S(2)}, u32[]{:S(2)}) collective-permute-start(bf16[224,128]{1,0:T(8,128)(2,1)S(1)} %add_convert_fusion), channel_id=1, source_target_pairs={{0,12},{4,8},{8,4},{12,0},{1,13},{5,9},{9,5},{13,1},{2,14},{6,10},... | collective-permute-start | bytes 172040 | tf_op jit(solution)/shard_map/ppermute | solution.py:31
  54.8 6.7 %collective-permute-start.11 = (bf16[224,128]{1,0:T(8,128)(2,1)S(1)}, bf16[224,128]{1,0:T(8,128)(2,1)S(1)}, u32[]{:S(2)}, u32[]{:S(2)}) collective-permute-start(bf16[224,128]{1,0:T(8,128)(2,1)S(1)} %add_convert_fusion), channel_id=1, source_target_pairs={{0,8},{4,12},{8,0},{12,4},{1,9},{5,13},{9,1},{13,5},{2,10},{6,14},... | collective-permute-start | bytes 172040 | tf_op jit(solution)/shard_map/ppermute | solution.py:31
  55.7 5.8 %collective-permute-start.10 = (bf16[224,128]{1,0:T(8,128)(2,1)S(1)}, bf16[224,128]{1,0:T(8,128)(2,1)S(1)}, u32[]{:S(2)}, u32[]{:S(2)}) collective-permute-start(bf16[224,128]{1,0:T(8,128)(2,1)S(1)} %add_convert_fusion), channel_id=1, source_target_pairs={{0,4},{4,0},{8,12},{12,8},{1,5},{5,1},{9,13},{13,9},{2,6},{6,2},{1... | collective-permute-start | bytes 172040 | tf_op jit(solution)/shard_map/ppermute | solution.py:31
  61.5 1.8 %collective-permute-start.15 = (f32[224,128]{1,0:T(8,128)S(1)}, f32[224,128]{1,0:T(8,128)S(1)}, u32[]{:S(2)}, u32[]{:S(2)}) collective-permute-start(f32[224,128]{1,0:T(8,128)S(1)} %convert_add_fusion.mine_ref), channel_id=1, source_target_pairs={{0,1},{1,0},{2,3},{3,2},{4,5},{5,4},{6,7},{7,6},{8,9},{9,8},{10,11... | collective-permute-start | bytes 344072 | tf_op jit(solution)/shard_map/ppermute | solution.py:31

commit v5 on v4

--- a/solution.py
+++ b/solution.py
@@ -349,9 +349,9 @@
     odd = row_is_odd()
     pack_s[pl.ds(pl.multiple_of(odd * size, 8), size)] = mine_ref[...]
     pack_s[pl.ds(pl.multiple_of((1 - odd) * size, 8), size)] = other_ref[...]
-    q_ref[...] = pack_s[:chan, :chan]
-    k_ref[...] = pack_s[:chan, chan:]
-    v_ref[...] = pack_s[chan : 2 * chan, :chan]
+    k_ref[...] = pack_s[:chan, :chan]
+    v_ref[...] = pack_s[:chan, chan:]
+    q_ref[...] = pack_s[chan : 2 * chan, :chan]
     o_ref[...] = pack_s[chan : 2 * chan, chan:]
     gain_ref[...] = pack_s[2 * chan : 2 * chan + 1, :chan]
     at = 2 * chan + 8
@@ -400,17 +400,17 @@
     cot_ref, keep_ref, gain_row, wq_ref, wkey_ref, wv_ref, wo_ref = refs[pieces : pieces + 7]
     refs = refs[pieces + 7 :]
     wires_out = refs[:pieces]
-    out_ref, g_ref, ggain_ref, held_s, bias_ref, gain_ref, wqkv_ref, wk_ref, wot_ref, wcat_ref = (
-        refs[pieces : pieces + 10]
-    )
-    give_s = refs[pieces + 10]
-    scratch = refs[pieces + 11 :]
+    out_ref, g_ref, ggain_ref = refs[pieces : pieces + 3]
+    refs = refs[pieces + 3 :]
+    held_s, give_s, bias_ref, gain_ref, wqkv_ref, wkv_ref, wot_ref, wkv2_ref, gain_s = refs[:9]
+    scratch = refs[9:]
     blocks = held_s.shape[0]
     pixels, chan, lanes = cot_ref.shape
     used = keep_ref.shape[1]
     each = used // blocks
     rows = bias_ref.shape[0]
-    slots = len(scratch) // 6
+    per = 7
+    slots = len(scratch) // per
     inv_chan = 1.0 / chan
     take(wires_in, held_s)
     live = jnp.where(keep_ref[...] > 0, 0.0, -1e30).astype(F32)
@@ -426,30 +426,30 @@
     wqkv_ref[...] = jnp.concatenate(
         [jnp.transpose(w_q), jnp.transpose(w_k), jnp.transpose(w_v)], axis=0
     ).astype(BF16)
-    wcat_ref[...] = jnp.concatenate([w_q, w_k, w_v], axis=1).astype(BF16)
-    wk_ref[...] = jnp.concatenate([w_k, jnp.zeros((chan, chan), F32)], axis=1).astype(BF16)
+    blank = jnp.zeros((chan, chan), F32)
+    wkv_ref[...] = jnp.concatenate([w_k, blank, w_v, blank], axis=1).astype(BF16)
+    wkv2_ref[...] = jnp.concatenate([w_k, w_v], axis=1).astype(BF16)
     wot_ref[...] = jnp.transpose(wo_ref[...].astype(F32)).astype(BF16)
+    g_ref[...] = jnp.zeros_like(g_ref)
+    gain_s[...] = jnp.zeros_like(gain_s)
     for slot in range(slots):
-        s_s, e_s, g_s, n_s, t_s, x_s = scratch[6 * slot : 6 * slot + 6]
-        e_s[rows:] = jnp.zeros((lanes - rows, lanes), BF16)
-        g_s[rows:] = jnp.zeros((lanes - rows, lanes), BF16)
+        d_s = scratch[per * slot + 5]
+        d_s[rows:] = jnp.zeros((lanes - rows, 2 * chan), BF16)
     chunks = []
     at = 0
     while at < rows:
         size = min(80, rows - at)
         chunks.append((at, size))
         at += size
-    sums = {}
-
-    def add(name, value):
-        sums[name] = value if name not in sums else sums[name] + value
+    half_lane = lax.broadcasted_iota(jnp.int32, (chan, 2 * chan), 1) < chan
 
     def pixel(p):
-        s_s, e_s, g_s, n_s, t_s, x_s = scratch[6 * (p % slots) : 6 * (p % slots) + 6]
+        start = per * (p % slots)
+        s_s, e_s, n_s, x_s, kv_s, d_s, nb_s = scratch[start : start + per]
         cells = [held_s[b, :, p * each : (p + 1) * each] for b in range(blocks)]
         if lanes > used:
-            cells.append(jnp.zeros((chan, lanes - used), F32))
-        s = jnp.concatenate(cells, axis=1)
+            cells.append(jnp.zeros((chan, lanes - used), held_s.dtype))
+        s = jnp.concatenate(cells, axis=1).astype(F32)
         x_s[...] = s
         cen = s - jnp.sum(s, axis=0, keepdims=True) * inv_chan
         rstd = lax.rsqrt(jnp.sum(cen * cen, axis=0, keepdims=True) * inv_chan + 1e-05)
@@ -457,70 +457,75 @@
         n_s[...] = normed
         nin32 = normed * gain_ref[...]
         nin = nin32.astype(BF16)
-        t_s[...] = jnp.transpose(nin32).astype(BF16)
+        nb_s[...] = nin
+        nin_t = jnp.transpose(nin32)[:rows].astype(BF16)
+        yield
+        kv = dot(nin_t, wkv_ref[...])
+        kv_s[:, : 2 * chan] = (kv[:, : 2 * chan] + bias_ref[...]).astype(BF16)
+        kv_s[:, 2 * chan :] = kv[:, 2 * chan :].astype(BF16)
         yield
         qkv = dot(wqkv_ref[...], nin)
         q = (qkv[:chan].astype(BF16).astype(F32) * scale).astype(BF16)
-        q_aug = jnp.concatenate([q, jnp.ones((16, lanes), BF16), jnp.zeros((chan - 16, lanes), BF16)], axis=0)
-        k = qkv[chan : 2 * chan].astype(BF16)
-        v = qkv[2 * chan :].astype(BF16)
+        k = qkv[chan : 2 * chan, :rows].astype(BF16)
+        v = qkv[2 * chan :, :rows].astype(BF16)
+        zero = jnp.zeros((chan, lanes), BF16)
+        q_aug = jnp.concatenate([q, jnp.ones((16, lanes), BF16), zero[16:]], axis=0)
+        yield
+        s_s[...] = dot(kv_s[:, : 2 * chan], q_aug)
         yield
         high = None
         for at, size in chunks:
-            k_t = (dot(t_s[at : at + size], wk_ref[...]) + bias_ref[at : at + size]).astype(BF16)
-            sc = dot(k_t, q_aug)
-            s_s[at : at + size] = sc
-            top = jnp.max(sc.reshape(size // 8, 8, lanes), axis=0)
+            top = jnp.max(s_s[at : at + size].reshape(size // 8, 8, lanes), axis=0)
             high = top if high is None else jnp.maximum(high, top)
+        high = jnp.max(high, axis=0, keepdims=True)
+        yield
+        for at, size in chunks:
+            e_s[at : at + size, :lanes] = jnp.exp(s_s[at : at + size] - high).astype(BF16)
             yield
-        high = jnp.max(high, axis=0, keepdims=True)
+        v_aug = jnp.concatenate([v, jnp.ones((16, rows), BF16)], axis=0)
+        att_aug = dot(v_aug, e_s[:, :lanes])
+        yield
         cot = cot_ref[p]
         d_att32 = dot(wo_ref[...], cot).astype(BF16).astype(F32)
-        for at, size in chunks:
-            e_s[at : at + size] = jnp.exp(s_s[at : at + size] - high).astype(BF16)
-            yield
-        v_aug = jnp.concatenate([v, jnp.ones((16, lanes), BF16)], axis=0)
-        att_aug = dot(v_aug, e_s[...])
         inv = 1.0 / att_aug[chan : chan + 1]
         att = att_aug[:chan] * inv
         att_b = att.astype(BF16)
         d_att = (d_att32 * inv).astype(BF16)
         inner = jnp.sum(att * d_att.astype(F32), axis=0, keepdims=True)
         yield
+        d_aug = jnp.concatenate([d_att, zero], axis=0)
+        s_s[...] = dot(kv_s[:, 2 * chan :], d_aug)
+        yield
         for at, size in chunks:
-            v_t = dot(t_s[at : at + size], wv_ref[...]).astype(BF16)
-            dp = dot(v_t, d_att)
-            g_s[at : at + size] = e_s[at : at + size] * (dp - inner).astype(BF16)
+            e_s[at : at + size, lanes:] = e_s[at : at + size, :lanes] * (s_s[at : at + size] - inner).astype(BF16)
             yield
+        low = jnp.concatenate(
+            [jnp.concatenate([zero, d_att], axis=0), jnp.concatenate([q, zero], axis=0)], axis=1
+        )
+        d_s[:rows] = dot(e_s[...], low, (1, 1)).astype(BF16)
+        yield
+        d_q = (dot(k, e_s[:, lanes:]) * scale).astype(BF16)
+        yield
         out_ref[p] = (x_s[...] + dot(wot_ref[...], att_b)).astype(BF16)[:, :used]
-        d_v = dot(d_att, e_s[...], (1, 1)).astype(BF16)
-        yield
-        d_q = (dot(k, g_s[...]) * scale).astype(BF16)
-        yield
-        d_k = dot(q, g_s[...], (1, 1)).astype(BF16)
-        d_qkv = jnp.concatenate([d_q, d_k, d_v], axis=0)
-        yield
-        dn = dot(wcat_ref[...], d_qkv)
+        yield
+        dn = dot(wq_ref[...], d_q) + dot(wkv2_ref[...], d_s[...], (1, 1))
+        nin = nb_s[...]
+        g_ref[:chan] += dot(nin, d_s[...])
+        both = dot(
+            jnp.concatenate([nin, att_b], axis=0), jnp.concatenate([d_q, cot], axis=0), (1, 1)
+        )
+        g_ref[chan:] += jnp.where(half_lane, both[:chan], both[chan:])
+        yield
         normed = n_s[...]
-        nin = (normed * gain_ref[...]).astype(BF16)
-        both = dot(
-            jnp.concatenate([nin, att_b], axis=0),
-            jnp.concatenate([d_q, d_k, d_v, cot], axis=0),
-            (1, 1),
-        )
-        add("qkv", both[:chan, : 2 * chan])
-        lane = lax.broadcasted_iota(jnp.int32, (chan, 2 * chan), 1)
-        add("vo", jnp.where(lane < chan, both[:chan, 2 * chan :], both[chan:, 2 * chan :]))
-        yield
         dnn = dn * normed
-        add("gain", dnn)
+        gain_s[...] += dnn
         scaled = dn * gain_ref[...]
         back = (
             scaled
             - jnp.sum(scaled, axis=0, keepdims=True) * inv_chan
             - normed * (jnp.sum(dnn * gain_ref[...], axis=0, keepdims=True) * inv_chan)
         )
-        done = cot.astype(F32) + back * rstd
+        done = (cot.astype(F32) + back * rstd).astype(give_s.dtype)
         for b in range(blocks):
             give_s[b, :, p * each : (p + 1) * each] = done[:, b * each : (b + 1) * each]
         yield
@@ -530,16 +535,15 @@
     step = 0
     while waiting or active:
         if waiting and step % lag == 0:
-            active.append(waiting.pop(0))
+            active += waiting[:2]
+            waiting = waiting[2:]
         for run in list(active):
             try:
                 next(run)
             except StopIteration:
                 active.remove(run)
         step += 1
-    g_ref[:chan] = sums["qkv"]
-    g_ref[chan:] = sums["vo"]
-    g_gain = jnp.sum(sums["gain"], axis=1, keepdims=True)
+    g_gain = jnp.sum(gain_s[...], axis=1, keepdims=True)
     g_gain = jnp.sum(jnp.where(eye, g_gain, 0.0), axis=0, keepdims=True)
     g_gain = jnp.concatenate([g_gain, jnp.zeros((1, chan), F32)], axis=1)
     ggain_ref[...] = jnp.broadcast_to(g_gain, ggain_ref.shape)
@@ -559,29 +563,31 @@
         held(blocks, (8, 2 * chan), F32),
     ]
     *out, output, g_weights, g_gain = pl.pallas_call(
-        functools.partial(angular_kernel, scale, 10, len(wires)),
+        functools.partial(angular_kernel, scale, 8, len(wires)),
         out_shape=shapes,
         in_specs=[vmem] * (len(wires) + 7),
         out_specs=[vmem] * len(shapes),
         scratch_shapes=[
-            pltpu.VMEM((blocks, chan, wire), F32),
+            pltpu.VMEM((blocks, chan, wire), BF16),
+            pltpu.VMEM((blocks, chan, wire), BF16),
             pltpu.VMEM((rows, 2 * chan), F32),
             pltpu.VMEM((chan, 1), F32),
             pltpu.VMEM((3 * chan, chan), BF16),
+            pltpu.VMEM((chan, 4 * chan), BF16),
+            pltpu.VMEM((chan, chan), BF16),
             pltpu.VMEM((chan, 2 * chan), BF16),
-            pltpu.VMEM((chan, chan), BF16),
-            pltpu.VMEM((chan, 3 * chan), BF16),
-            pltpu.VMEM((blocks, chan, wire), F32),
+            pltpu.VMEM((chan, lanes), F32),
         ]
         + [
             pltpu.VMEM((rows, lanes), F32),
-            pltpu.VMEM((lanes, lanes), BF16),
-            pltpu.VMEM((lanes, lanes), BF16),
+            pltpu.VMEM((rows, 2 * lanes), BF16),
             pltpu.VMEM((chan, lanes), F32),
-            pltpu.VMEM((lanes, chan), BF16),
             pltpu.VMEM((chan, lanes), F32),
+            pltpu.VMEM((rows, 4 * chan), BF16),
+            pltpu.VMEM((lanes, 2 * chan), BF16),
+            pltpu.VMEM((chan, lanes), BF16),
         ]
-        * 2,
+        * 6,
         name="angular",
         compiler_params=grant(blocks),
     )(*here(blocks, *wires, cotangent), keep[None, :], gain[None, :], w_query, w_key, w_value, w_out)

time: 64.7 us -> 56.1 us (0.87)
  Pallas kernels: 19 us -> 10.4 us
    pallas_call x1, Pallas kernels: 14.5 us -> 5.92 us  [angular(): pl.pallas_call(functools.partial(angular_kernel, scale, 8, len(wires)), o...]
where the time goes in v5:
time: 56.1 us; the launch traced here: 55.6 us
  starting transfers between devices  21.5 us (38%)
  waiting for transfers between devices  19.6 us (35%)
  Pallas kernels  10.4 us (19%)
  local copies, waits for them, and re-layouts  3.06 us (5%)
  between operations  0.83 us (1%)
    ppermute x12, waiting for transfers between devices, swap(): return lax.ppermute(cells, axis, [(i, i ^ step) for i in range(count)])  14.9 us
    ppermute x12, starting transfers between devices, swap(): return lax.ppermute(cells, axis, [(i, i ^ step) for i in range(count)])  13.1 us
    ppermute x2, starting transfers between devices, halo_swap(): got_far = lax.ppermute(far, 'row', pairs) if pairs else jnp.zeros_like(far)  7.79 us
    pallas_call x1, Pallas kernels, angular(): pl.pallas_call(functools.partial(angular_kernel, scale, 8, len(wires)), o...  5.92 us
    ppermute x2, waiting for transfers between devices, halo_swap(): got_far = lax.ppermute(far, 'row', pairs) if pairs else jnp.zeros_like(far)  4.69 us
    unnamed x17, local copies, waits for them, and re-layouts  1.91 us
    pallas_call x1, Pallas kernels, input_grad(): pl.pallas_call(input_kernel, out_shape=jax.ShapeDtypeStruct((chan, size /...  1.74 us
  transfers between devices with their start and end apart: 16, of which 9 were waited for; matrix products, arithmetic and copies ran while one was open for 2% of the time, Pallas kernels for 3%

profile of v5, /device:TPU:1, one launch (start us, length us, event | category | flops | bytes accessed | tf_op | source)
XLA Modules:
  0.0 55.6 jit_solution(16897550922692134203)
XLA Ops:
  0.6 1.2 %copy.22 = bf16[64,73,2,16]{1,0,3,2:T(8,128)(2,1)S(1)} copy(bf16[64,73,2,16]{1,3,2,0:T(8,128)(2,1)} %param.9) | data formatting | bytes 598016 | tf_op args[0]
  2.0 4.5 %collective-permute-start.1 = (bf16[16,64,73]{2,1,0:T(8,128)(2,1)S(1)}, bf16[16,64,73]{2,1,0:T(8,128)(2,1)S(1)}, u32[]{:S(2)}, u32[]{:S(2)}) collective-permute-start(bf16[16,64,73]{2,1,0:T(8,128)(2,1)S(1)} %get-tuple-element.78), channel_id=1, source_target_pairs={{1,2},{2,1},{5,6},{6,5},{9,10},{10,9},{13,14},{14,13},{17,18},{18,... | collective-permute-start | bytes 448520 | tf_op jit(solution)/shard_map/ppermute | solution.py:40
  6.5 4.0 %collective-permute-done.1.far_ref = bf16[16,64,73]{2,1,0:T(8,128)(2,1)S(1)} collective-permute-done((bf16[16,64,73]{2,1,0:T(8,128)(2,1)S(1)}, bf16[16,64,73]{2,1,0:T(8,128)(2,1)S(1)}, u32[]{:S(2)}, u32[]{:S(2)}) %collective-permute-start.1) | collective-permute-done | bytes 149536 | tf_op jit(solution)/shard_map/ppermute | solution.py:40
  10.5 0.9 %conv.1 = (bf16[64,640]{1,0:T(8,128)(2,1)S(1)}, bf16[64,640]{1,0:T(8,128)(2,1)S(1)}, bf16[64,640]{1,0:T(8,128)(2,1)S(1)}, bf16[64,640]{1,0:T(8,128)(2,1)S(1)}, bf16[16,256,128]{2,1,0:T(8,128)(2,1)S(1)}) custom-call(bf16[2,16,64,73]{3,2,1,0:T(8,128)(2,1)S(1)} %bitcast.19, bf16[16,64,73]{2,1,0:T(8,128)(2,1)S(1)} %collective-permute-done.near_ref, ...), custom_call_target="tpu_custom_call" | custom-call | tf_op jit(solution)/shard_map/conv/pallas_call | solution.py:176
  11.5 1.4 %collective-permute-start.2 = (bf16[64,640]{1,0:T(8,128)(2,1)S(1)}, bf16[64,640]{1,0:T(8,128)(2,1)S(1)}, u32[]{:S(2)}, u32[]{:S(2)}) collective-permute-start(bf16[64,640]{1,0:T(8,128)(2,1)S(1)} %get-tuple-element.44), channel_id=1, source_target_pairs={{0,4},{4,0},{8,12},{12,8},{1,5},{5,1},{9,13},{13,9},{2,6},{6,2},{1... | collective-permute-start | bytes 245768 | tf_op jit(solution)/shard_map/ppermute | solution.py:31
  12.8 2.3 %collective-permute-start.3 = (bf16[64,640]{1,0:T(8,128)(2,1)S(1)}, bf16[64,640]{1,0:T(8,128)(2,1)S(1)}, u32[]{:S(2)}, u32[]{:S(2)}) collective-permute-start(bf16[64,640]{1,0:T(8,128)(2,1)S(1)} %get-tuple-element.45), channel_id=1, source_target_pairs={{0,8},{4,12},{8,0},{12,4},{1,9},{5,13},{9,1},{13,5},{2,10},{6,14},... | collective-permute-start | bytes 245768 | tf_op jit(solution)/shard_map/ppermute | solution.py:31
  15.6 4.9 %collective-permute-done.3.refs_2_ = bf16[64,640]{1,0:T(8,128)(2,1)S(1)} collective-permute-done((bf16[64,640]{1,0:T(8,128)(2,1)S(1)}, bf16[64,640]{1,0:T(8,128)(2,1)S(1)}, u32[]{:S(2)}, u32[]{:S(2)}) %collective-permute-start.3) | collective-permute-done | bytes 81952 | tf_op jit(solution)/shard_map/ppermute | solution.py:31
  21.2 5.9 %angular.1 = (bf16[64,640]{1,0:T(8,128)(2,1)S(1)}, bf16[64,640]{1,0:T(8,128)(2,1)S(1)}, bf16[64,640]{1,0:T(8,128)(2,1)S(1)}, bf16[64,640]{1,0:T(8,128)(2,1)S(1)}...) custom-call(bf16[64,640]{1,0:T(8,128)(2,1)S(1)} %get-tuple-element.43.refs_0_, ...), custom_call_target="tpu_custom_call" | custom-call | tf_op jit(solution)/shard_map/angular/pallas_call | solution.py:565
  27.1 1.4 %collective-permute-start.5 = (bf16[64,640]{1,0:T(8,128)(2,1)S(1)}, bf16[64,640]{1,0:T(8,128)(2,1)S(1)}, u32[]{:S(2)}, u32[]{:S(2)}) collective-permute-start(bf16[64,640]{1,0:T(8,128)(2,1)S(1)} %get-tuple-element.48), channel_id=1, source_target_pairs={{0,4},{4,0},{8,12},{12,8},{1,5},{5,1},{9,13},{13,9},{2,6},{6,2},{1... | collective-permute-start | bytes 245768 | tf_op jit(solution)/shard_map/ppermute | solution.py:31
  28.5 1.3 %collective-permute-start.6 = (bf16[64,640]{1,0:T(8,128)(2,1)S(1)}, bf16[64,640]{1,0:T(8,128)(2,1)S(1)}, u32[]{:S(2)}, u32[]{:S(2)}) collective-permute-start(bf16[64,640]{1,0:T(8,128)(2,1)S(1)} %get-tuple-element.49), channel_id=1, source_target_pairs={{0,8},{4,12},{8,0},{12,4},{1,9},{5,13},{9,1},{13,5},{2,10},{6,14},... | collective-permute-start | bytes 245768 | tf_op jit(solution)/shard_map/ppermute | solution.py:31
  29.9 0.9 %collective-permute-start.7 = (bf16[64,640]{1,0:T(8,128)(2,1)S(1)}, bf16[64,640]{1,0:T(8,128)(2,1)S(1)}, u32[]{:S(2)}, u32[]{:S(2)}) collective-permute-start(bf16[64,640]{1,0:T(8,128)(2,1)S(1)} %get-tuple-element.50), channel_id=1, source_target_pairs={{0,12},{4,8},{8,4},{12,0},{1,13},{5,9},{9,5},{13,1},{2,14},{6,10},... | collective-permute-start | bytes 245768 | tf_op jit(solution)/shard_map/ppermute | solution.py:31
  30.7 1.1 %copy.23 = bf16[2,4,64,292]{3,1,0,2:T(4,128)(2,1)} copy(bf16[2,4,64,292]{3,2,1,0:T(8,128)(2,1)S(1)} %bitcast.22) | data formatting | bytes 598016 | tf_op jit(solution)/shard_map/reshape | solution.py:639
  31.8 1.4 %collective-permute-done.6.refs_2_ = bf16[64,640]{1,0:T(8,128)(2,1)S(1)} collective-permute-done((bf16[64,640]{1,0:T(8,128)(2,1)S(1)}, bf16[64,640]{1,0:T(8,128)(2,1)S(1)}, u32[]{:S(2)}, u32[]{:S(2)}) %collective-permute-start.6) | collective-permute-done | bytes 81952 | tf_op jit(solution)/shard_map/ppermute | solution.py:31
  33.2 3.9 %collective-permute-done.7.refs_3_ = bf16[64,640]{1,0:T(8,128)(2,1)S(1)} collective-permute-done((bf16[64,640]{1,0:T(8,128)(2,1)S(1)}, bf16[64,640]{1,0:T(8,128)(2,1)S(1)}, u32[]{:S(2)}, u32[]{:S(2)}) %collective-permute-start.7) | collective-permute-done | bytes 81952 | tf_op jit(solution)/shard_map/ppermute | solution.py:31
  37.1 1.0 %weights.1 = (bf16[16,64,128]{2,1,0:T(8,128)(2,1)S(1)}, bf16[16,64,128]{2,1,0:T(8,128)(2,1)S(1)}, bf16[16,128,128]{2,1,0:T(8,128)(2,1)S(1)}, f32[224,128]{1,0:T(8,128)S(1)}, f32[224,128]{1,0:T(8,128)S(1)}) custom-call(bf16[64,640]{1,0:T(8,128)(2,1)S(1)} %get-tuple-element.53.refs_0_, bf16[64,640]{1,0:T(8,128)(2,1)S(1)} %collective-permute-done.5.refs_1_, ...), custom_call_target="tpu_custom_call" | custom-call | tf_op jit(solution)/shard_map/weights/pallas_call | solution.py:277
  38.1 1.2 %collective-permute-start.8 = (f32[224,128]{1,0:T(8,128)S(1)}, f32[224,128]{1,0:T(8,128)S(1)}, u32[]{:S(2)}, u32[]{:S(2)}) collective-permute-start(f32[224,128]{1,0:T(8,128)S(1)} %get-tuple-element.61), channel_id=1, source_target_pairs={{0,1},{1,0},{2,3},{3,2},{4,5},{5,4},{6,7},{7,6},{8,9},{9,8},{10,11... | collective-permute-start | bytes 344072 | tf_op jit(solution)/shard_map/ppermute | solution.py:31
  39.3 1.0 %collective-permute-done.8 = f32[224,128]{1,0:T(8,128)S(1)} collective-permute-done((f32[224,128]{1,0:T(8,128)S(1)}, f32[224,128]{1,0:T(8,128)S(1)}, u32[]{:S(2)}, u32[]{:S(2)}) %collective-permute-start.8) | collective-permute-done | bytes 114720 | tf_op jit(solution)/shard_map/ppermute | solution.py:31
  40.9 3.3 %collective-permute-start.14 = (bf16[16,64,128]{2,1,0:T(8,128)(2,1)S(1)}, bf16[16,64,128]{2,1,0:T(8,128)(2,1)S(1)}, u32[]{:S(2)}, u32[]{:S(2)}) collective-permute-start(bf16[16,64,128]{2,1,0:T(8,128)(2,1)S(1)} %get-tuple-element.67), channel_id=1, source_target_pairs={{1,2},{2,1},{5,6},{6,5},{9,10},{10,9},{13,14},{14,13},{17,18},{18,... | collective-permute-start | bytes 786440 | tf_op jit(solution)/shard_map/ppermute | solution.py:40
  44.3 1.9 %collective-permute-start.12 = (bf16[224,128]{1,0:T(8,128)(2,1)S(1)}, bf16[224,128]{1,0:T(8,128)(2,1)S(1)}, u32[]{:S(2)}, u32[]{:S(2)}) collective-permute-start(bf16[224,128]{1,0:T(8,128)(2,1)S(1)} %add_convert_fusion), channel_id=1, source_target_pairs={{0,12},{4,8},{8,4},{12,0},{1,13},{5,9},{9,5},{13,1},{2,14},{6,10},... | collective-permute-start | bytes 172040 | tf_op jit(solution)/shard_map/ppermute | solution.py:31
  46.2 0.9 %collective-permute-start.11 = (bf16[224,128]{1,0:T(8,128)(2,1)S(1)}, bf16[224,128]{1,0:T(8,128)(2,1)S(1)}, u32[]{:S(2)}, u32[]{:S(2)}) collective-permute-start(bf16[224,128]{1,0:T(8,128)(2,1)S(1)} %add_convert_fusion), channel_id=1, source_target_pairs={{0,8},{4,12},{8,0},{12,4},{1,9},{5,13},{9,1},{13,5},{2,10},{6,14},... | collective-permute-start | bytes 172040 | tf_op jit(solution)/shard_map/ppermute | solution.py:31
  48.6 1.7 %input.1 = bf16[64,2,16,73]{3,2,1,0:T(8,128)(2,1)} custom-call(bf16[16,128,128]{2,1,0:T(8,128)(2,1)S(1)} %get-tuple-element.65.own_ref, bf16[16,64,128]{2,1,0:T(8,128)(2,1)S(1)} %collective-permute-done.13.near_ref, bf16[16,64,128]{2,1,0:T(8,128)(2,1)S(1)} %collective-permute-done.14.far_ref, bf16[3,3,64,64]{3,2,1,0:T(8,128)(2,1)S(1)} %bitcast.21), custom_call_target="tpu_custom_call" | custom-call | tf_op jit(solution)/shard_map/input/pallas_call | solution.py:332
  50.4 2.5 %collective-permute-done.11 = bf16[224,128]{1,0:T(8,128)(2,1)S(1)} collective-permute-done((bf16[224,128]{1,0:T(8,128)(2,1)S(1)}, bf16[224,128]{1,0:T(8,128)(2,1)S(1)}, u32[]{:S(2)}, u32[]{:S(2)}) %collective-permute-start.11) | collective-permute-done | bytes 57376 | tf_op jit(solution)/shard_map/ppermute | solution.py:31
  53.8 1.0 %collective-permute-done.15.other_ref = f32[224,128]{1,0:T(8,128)S(1)} collective-permute-done((f32[224,128]{1,0:T(8,128)S(1)}, f32[224,128]{1,0:T(8,128)S(1)}, u32[]{:S(2)}, u32[]{:S(2)}) %collective-permute-start.15) | collective-permute-done | bytes 114720 | tf_op jit(solution)/shard_map/ppermute | solution.py:31
  54.7 0.9 %unpack.1 = (f32[3,3,64,64]{3,2,1,0:T(8,128)}, f32[64,64]{1,0:T(8,128)}, f32[64,64]{1,0:T(8,128)}, f32[64,64]{1,0:T(8,128)}, f32[64,64]{1,0:T(8,128)}, /*index=5*/f32[1,64]{1,0:T(1,128)}) custom-call(f32[224,128]{1,0:T(8,128)S(1)} %convert_add_fusion.mine_ref, f32[224,128]{1,0:T(8,128)S(1)} %collective-permute-done.15.other_ref), custom_call_target="tpu_custom_call" | custom-call | tf_op jit(solution)/shard_map/unpack/pallas_call | solution.py:375
  (38 shorter events, 4.3 us)
Async XLA Ops:
  1.9 8.6 %copy-start = (bf16[64,64,3,3]{1,0,3,2:T(8,128)(2,1)S(1)}, bf16[64,64,3,3]{1,0,3,2:T(8,128)(2,1)}, u32[]{:S(2)}) copy-start(bf16[64,64,3,3]{1,0,3,2:T(8,128)(2,1)} %param.12) | copy-start | bytes 221188
  2.0 8.5 %collective-permute-start.1 = (bf16[16,64,73]{2,1,0:T(8,128)(2,1)S(1)}, bf16[16,64,73]{2,1,0:T(8,128)(2,1)S(1)}, u32[]{:S(2)}, u32[]{:S(2)}) collective-permute-start(bf16[16,64,73]{2,1,0:T(8,128)(2,1)S(1)} %get-tuple-element.78), channel_id=1, source_target_pairs={{1,2},{2,1},{5,6},{6,5},{9,10},{10,9},{13,14},{14,13},{17,18},{18,... | collective-permute-start | bytes 448520 | tf_op jit(solution)/shard_map/ppermute | solution.py:40
  6.5 4.0 %collective-permute-start = (bf16[16,64,73]{2,1,0:T(8,128)(2,1)S(1)}, bf16[16,64,73]{2,1,0:T(8,128)(2,1)S(1)}, u32[]{:S(2)}, u32[]{:S(2)}) collective-permute-start(bf16[16,64,73]{2,1,0:T(8,128)(2,1)S(1)} %get-tuple-element.79), channel_id=1, source_target_pairs={{0,1},{1,0},{2,3},{3,2},{4,5},{5,4},{6,7},{7,6},{8,9},{9,8},{10,11... | collective-permute-start | bytes 448520 | tf_op jit(solution)/shard_map/ppermute | solution.py:39
  10.5 4.7 %copy-start.6 = (bf16[64,292,2,4]{1,3,2,0:T(4,128)(2,1)S(1)}, bf16[64,292,2,4]{1,3,2,0:T(4,128)(2,1)}, u32[]{:S(2)}) copy-start(bf16[64,292,2,4]{1,3,2,0:T(4,128)(2,1)} %param.10) | copy-start | bytes 897028
  11.5 3.7 %copy-start.7 = (s32[292]{0:T(512)S(1)}, s32[292]{0:T(512)}, u32[]{:S(2)}) copy-start(s32[292]{0:T(512)} %param.11) | copy-start | bytes 3508
  11.5 4.2 %collective-permute-start.2 = (bf16[64,640]{1,0:T(8,128)(2,1)S(1)}, bf16[64,640]{1,0:T(8,128)(2,1)S(1)}, u32[]{:S(2)}, u32[]{:S(2)}) collective-permute-start(bf16[64,640]{1,0:T(8,128)(2,1)S(1)} %get-tuple-element.44), channel_id=1, source_target_pairs={{0,4},{4,0},{8,12},{12,8},{1,5},{5,1},{9,13},{13,9},{2,6},{6,2},{1... | collective-permute-start | bytes 245768 | tf_op jit(solution)/shard_map/ppermute | solution.py:31
  12.8 7.7 %collective-permute-start.3 = (bf16[64,640]{1,0:T(8,128)(2,1)S(1)}, bf16[64,640]{1,0:T(8,128)(2,1)S(1)}, u32[]{:S(2)}, u32[]{:S(2)}) collective-permute-start(bf16[64,640]{1,0:T(8,128)(2,1)S(1)} %get-tuple-element.45), channel_id=1, source_target_pairs={{0,8},{4,12},{8,0},{12,4},{1,9},{5,13},{9,1},{13,5},{2,10},{6,14},... | collective-permute-start | bytes 245768 | tf_op jit(solution)/shard_map/ppermute | solution.py:31
  15.2 5.4 %collective-permute-start.4 = (bf16[64,640]{1,0:T(8,128)(2,1)S(1)}, bf16[64,640]{1,0:T(8,128)(2,1)S(1)}, u32[]{:S(2)}, u32[]{:S(2)}) collective-permute-start(bf16[64,640]{1,0:T(8,128)(2,1)S(1)} %get-tuple-element.46), channel_id=1, source_target_pairs={{0,12},{4,8},{8,4},{12,0},{1,13},{5,9},{9,5},{13,1},{2,14},{6,10},... | collective-permute-start | bytes 245768 | tf_op jit(solution)/shard_map/ppermute | solution.py:31
  15.2 5.3 %copy-start.1 = (bf16[64,64]{1,0:T(8,128)(2,1)S(1)}, bf16[64,64]{1,0:T(8,128)(2,1)}, u32[]{:S(2)}) copy-start(bf16[64,64]{1,0:T(8,128)(2,1)} %refs_7_.1) | copy-start | bytes 24580
  15.2 5.3 %copy-start.2 = (bf16[64,64]{1,0:T(8,128)(2,1)S(1)}, bf16[64,64]{1,0:T(8,128)(2,1)}, u32[]{:S(2)}) copy-start(bf16[64,64]{1,0:T(8,128)(2,1)} %refs_8_.1) | copy-start | bytes 24580
  15.3 5.3 %copy-start.3 = (bf16[64,64]{1,0:T(8,128)(2,1)S(1)}, bf16[64,64]{1,0:T(8,128)(2,1)}, u32[]{:S(2)}) copy-start(bf16[64,64]{1,0:T(8,128)(2,1)} %refs_9_.1) | copy-start | bytes 24580
  15.3 5.3 %copy-start.4 = (bf16[64,64]{1,0:T(8,128)(2,1)S(1)}, bf16[64,64]{1,0:T(8,128)(2,1)}, u32[]{:S(2)}) copy-start(bf16[64,64]{1,0:T(8,128)(2,1)} %refs_10_.1) | copy-start | bytes 24580
  20.5 0.7 %copy-start.5 = (f32[64]{0:T(128)S(1)}, f32[64]{0:T(128)}, u32[]{:S(2)}) copy-start(f32[64]{0:T(128)} %param.13) | copy-start | bytes 772
  27.1 4.7 %collective-permute-start.5 = (bf16[64,640]{1,0:T(8,128)(2,1)S(1)}, bf16[64,640]{1,0:T(8,128)(2,1)S(1)}, u32[]{:S(2)}, u32[]{:S(2)}) collective-permute-start(bf16[64,640]{1,0:T(8,128)(2,1)S(1)} %get-tuple-element.48), channel_id=1, source_target_pairs={{0,4},{4,0},{8,12},{12,8},{1,5},{5,1},{9,13},{13,9},{2,6},{6,2},{1... | collective-permute-start | bytes 245768 | tf_op jit(solution)/shard_map/ppermute | solution.py:31
  28.5 4.6 %collective-permute-start.6 = (bf16[64,640]{1,0:T(8,128)(2,1)S(1)}, bf16[64,640]{1,0:T(8,128)(2,1)S(1)}, u32[]{:S(2)}, u32[]{:S(2)}) collective-permute-start(bf16[64,640]{1,0:T(8,128)(2,1)S(1)} %get-tuple-element.49), channel_id=1, source_target_pairs={{0,8},{4,12},{8,0},{12,4},{1,9},{5,13},{9,1},{13,5},{2,10},{6,14},... | collective-permute-start | bytes 245768 | tf_op jit(solution)/shard_map/ppermute | solution.py:31
  29.9 7.2 %collective-permute-start.7 = (bf16[64,640]{1,0:T(8,128)(2,1)S(1)}, bf16[64,640]{1,0:T(8,128)(2,1)S(1)}, u32[]{:S(2)}, u32[]{:S(2)}) collective-permute-start(bf16[64,640]{1,0:T(8,128)(2,1)S(1)} %get-tuple-element.50), channel_id=1, source_target_pairs={{0,12},{4,8},{8,4},{12,0},{1,13},{5,9},{9,5},{13,1},{2,14},{6,10},... | collective-permute-start | bytes 245768 | tf_op jit(solution)/shard_map/ppermute | solution.py:31
  38.1 2.2 %collective-permute-start.8 = (f32[224,128]{1,0:T(8,128)S(1)}, f32[224,128]{1,0:T(8,128)S(1)}, u32[]{:S(2)}, u32[]{:S(2)}) collective-permute-start(f32[224,128]{1,0:T(8,128)S(1)} %get-tuple-element.61), channel_id=1, source_target_pairs={{0,1},{1,0},{2,3},{3,2},{4,5},{5,4},{6,7},{7,6},{8,9},{9,8},{10,11... | collective-permute-start | bytes 344072 | tf_op jit(solution)/shard_map/ppermute | solution.py:31
  40.3 4.0 %collective-permute-start.9 = (bf16[224,128]{1,0:T(8,128)(2,1)S(1)}, bf16[224,128]{1,0:T(8,128)(2,1)S(1)}, u32[]{:S(2)}, u32[]{:S(2)}) collective-permute-start(bf16[224,128]{1,0:T(8,128)(2,1)S(1)} %add_convert_fusion.1), channel_id=1, source_target_pairs={{0,2},{1,3},{2,0},{3,1},{4,6},{5,7},{6,4},{7,5},{8,10},{9,11},{10,... | collective-permute-start | bytes 172040 | tf_op jit(solution)/shard_map/ppermute | solution.py:31
  40.4 7.5 %collective-permute-start.13 = (bf16[16,64,128]{2,1,0:T(8,128)(2,1)S(1)}, bf16[16,64,128]{2,1,0:T(8,128)(2,1)S(1)}, u32[]{:S(2)}, u32[]{:S(2)}) collective-permute-start(bf16[16,64,128]{2,1,0:T(8,128)(2,1)S(1)} %get-tuple-element.66), channel_id=1, source_target_pairs={{0,1},{1,0},{2,3},{3,2},{4,5},{5,4},{6,7},{7,6},{8,9},{9,8},{10,11... | collective-permute-start | bytes 786440 | tf_op jit(solution)/shard_map/ppermute | solution.py:39
  40.9 7.7 %collective-permute-start.14 = (bf16[16,64,128]{2,1,0:T(8,128)(2,1)S(1)}, bf16[16,64,128]{2,1,0:T(8,128)(2,1)S(1)}, u32[]{:S(2)}, u32[]{:S(2)}) collective-permute-start(bf16[16,64,128]{2,1,0:T(8,128)(2,1)S(1)} %get-tuple-element.67), channel_id=1, source_target_pairs={{1,2},{2,1},{5,6},{6,5},{9,10},{10,9},{13,14},{14,13},{17,18},{18,... | collective-permute-start | bytes 786440 | tf_op jit(solution)/shard_map/ppermute | solution.py:40
  44.3 6.1 %collective-permute-start.12 = (bf16[224,128]{1,0:T(8,128)(2,1)S(1)}, bf16[224,128]{1,0:T(8,128)(2,1)S(1)}, u32[]{:S(2)}, u32[]{:S(2)}) collective-permute-start(bf16[224,128]{1,0:T(8,128)(2,1)S(1)} %add_convert_fusion), channel_id=1, source_target_pairs={{0,12},{4,8},{8,4},{12,0},{1,13},{5,9},{9,5},{13,1},{2,14},{6,10},... | collective-permute-start | bytes 172040 | tf_op jit(solution)/shard_map/ppermute | solution.py:31
  46.2 6.7 %collective-permute-start.11 = (bf16[224,128]{1,0:T(8,128)(2,1)S(1)}, bf16[224,128]{1,0:T(8,128)(2,1)S(1)}, u32[]{:S(2)}, u32[]{:S(2)}) collective-permute-start(bf16[224,128]{1,0:T(8,128)(2,1)S(1)} %add_convert_fusion), channel_id=1, source_target_pairs={{0,8},{4,12},{8,0},{12,4},{1,9},{5,13},{9,1},{13,5},{2,10},{6,14},... | collective-permute-start | bytes 172040 | tf_op jit(solution)/shard_map/ppermute | solution.py:31
  47.1 5.8 %collective-permute-start.10 = (bf16[224,128]{1,0:T(8,128)(2,1)S(1)}, bf16[224,128]{1,0:T(8,128)(2,1)S(1)}, u32[]{:S(2)}, u32[]{:S(2)}) collective-permute-start(bf16[224,128]{1,0:T(8,128)(2,1)S(1)} %add_convert_fusion), channel_id=1, source_target_pairs={{0,4},{4,0},{8,12},{12,8},{1,5},{5,1},{9,13},{13,9},{2,6},{6,2},{1... | collective-permute-start | bytes 172040 | tf_op jit(solution)/shard_map/ppermute | solution.py:31
  52.9 1.8 %collective-permute-start.15 = (f32[224,128]{1,0:T(8,128)S(1)}, f32[224,128]{1,0:T(8,128)S(1)}, u32[]{:S(2)}, u32[]{:S(2)}) collective-permute-start(f32[224,128]{1,0:T(8,128)S(1)} %convert_add_fusion.mine_ref), channel_id=1, source_target_pairs={{0,1},{1,0},{2,3},{3,2},{4,5},{5,4},{6,7},{7,6},{8,9},{9,8},{10,11... | collective-permute-start | bytes 344072 | tf_op jit(solution)/shard_map/ppermute | solution.py:31

commit v6 on v5

--- a/solution.py
+++ b/solution.py
@@ -45,22 +45,34 @@
     return lax.rem(lax.axis_index("row"), 2)
 
 
-def give(refs, held):
+def plan(pixels, views, blocks):
+    tiles = round_up(pixels * views, 128) // 128
+    early = (tiles + 1) // 2
+    count = min(early * 128 // views, pixels)
+    late = pixels - count
+    if not pairwise(blocks) or late == 0 or late * views > (tiles - early) * 128:
+        return [(0, pixels, 0, 128 * tiles)]
+    return [(0, count, 0, 128 * early), (count, late, 128 * early, 128 * (tiles - early))]
+
+
+def give(refs, held, start=0):
+    lanes = refs[0].shape[-1]
     if len(refs) == 1:
-        refs[0][...] = held[...].astype(refs[0].dtype)
+        refs[0][...] = held[:, :, start : start + lanes].astype(refs[0].dtype)
         return
     me = lax.axis_index("view")
     for step, ref in enumerate(refs):
-        ref[...] = held[me ^ step].astype(ref.dtype)
-
-
-def take(refs, held):
+        ref[...] = held[me ^ step, :, start : start + lanes].astype(ref.dtype)
+
+
+def take(refs, held, start=0):
+    lanes = refs[0].shape[-1]
     if len(refs) == 1:
-        held[...] = refs[0][...].astype(held.dtype)
+        held[:, :, start : start + lanes] = refs[0][...].astype(held.dtype)
         return
     me = lax.axis_index("view")
     for step, ref in enumerate(refs):
-        held[me ^ step] = ref[...].astype(held.dtype)
+        held[me ^ step, :, start : start + lanes] = ref[...].astype(held.dtype)
 
 
 def here(blocks, *arrays):
@@ -148,6 +160,7 @@
     weights = taps(w_ref, rows, True)
     spread(frame_ref, acc_s, weights, rows, True)
     breadth = width // blocks
+    chunks = plan(rows * breadth, views, blocks)
 
     def block(b, carry):
         cells = []
@@ -157,12 +170,15 @@
                 value = acc_s[w + 1, r * chan : (r + 1) * chan]
                 value = value + frame_ref[w, (r + 1) * chan : (r + 2) * chan].astype(F32)
                 cells.append(value[:, :views])
-        cells = jnp.concatenate(cells, axis=1)
-        held_s[b, :, : cells.shape[1]] = cells
+        for first, count, at, _ in chunks:
+            some = jnp.concatenate(cells[first : first + count], axis=1)
+            held_s[b, :, at : at + count * views] = some
         return carry
 
     lax.fori_loop(0, blocks, block, 0, unroll=blocks <= 4)
-    give(wires, held_s)
+    pieces = len(wires) // len(chunks)
+    for c, (_, _, at, _) in enumerate(chunks):
+        give(wires[c * pieces : (c + 1) * pieces], held_s, at)
 
 
 def convolve(x, near, far, w_conv, blocks):
@@ -171,7 +187,9 @@
     lanes = round_up(views, 128)
     wire = round_up(rows * (width // blocks) * views, 128)
     vmem = pl.BlockSpec(memory_space=pltpu.VMEM)
-    shapes = wire_shapes(blocks, chan, wire)
+    shapes = []
+    for _, _, _, size in plan(rows * (width // blocks), views, blocks):
+        shapes += wire_shapes(blocks, chan, size)
     shapes = shapes + [held(blocks, (width, own + 2 * chan, lanes), BF16)]
     *wires, frame = pl.pallas_call(
         functools.partial(conv_kernel, blocks),
@@ -188,17 +206,27 @@
     return wires, frame
 
 
-def weight_kernel(count, pieces, *refs):
+def weight_kernel(count, pieces, parts, *refs):
     wires = refs[:pieces]
-    frame_ref, g_ref, gain_ref = refs[pieces : pieces + 3]
-    near_ref, far_ref, own_ref, keep_ref, send_ref, held_s, col_s, pack_s = refs[pieces + 3 :]
+    frame_ref = refs[pieces]
+    g_refs = refs[pieces + 1 : pieces + 1 + parts]
+    gain_refs = refs[pieces + 1 + parts : pieces + 1 + 2 * parts]
+    near_ref, far_ref, own_ref, keep_ref, send_ref, held_s, col_s, pack_s = refs[
+        pieces + 1 + 2 * parts :
+    ]
     width, own, lanes = own_ref.shape
     blocks, chan, wire = held_s.shape
     rows = own // chan
     breadth = width // blocks
     views = count
     odd = row_is_odd()
-    take(wires, held_s)
+    chunks = plan(rows * breadth, views, blocks)
+    each = pieces // len(chunks)
+    places = {}
+    for c, (first, pixels, start, _) in enumerate(chunks):
+        take(wires[c * each : (c + 1) * each], held_s, start)
+        for p in range(pixels):
+            places[first + p] = start + p * views
     col_s[0] = jnp.zeros((own, lanes), BF16)
     col_s[width + 1] = jnp.zeros((own, lanes), BF16)
 
@@ -206,7 +234,7 @@
         cells = held_s[b]
         for r in range(rows):
             for k in range(breadth):
-                at = (r * breadth + k) * views
+                at = places[r * breadth + k]
                 value = cells[:, at : at + views]
                 if lanes > views:
                     value = jnp.concatenate(
@@ -254,8 +282,8 @@
     g_conv = jnp.concatenate(bands, axis=0)
     edge = 2 * chan
     pack_s[...] = jnp.zeros_like(pack_s)
-    pack_s[: 2 * chan] = g_ref[...]
-    pack_s[2 * chan : 2 * chan + 8] = gain_ref[...]
+    pack_s[: 2 * chan] = sum(ref[...] for ref in g_refs)
+    pack_s[2 * chan : 2 * chan + 8] = sum(ref[...] for ref in gain_refs)
     at = 2 * chan + 8
     pack_s[at : at + 3 * chan] = g_conv[:, :edge]
     half = 3 * chan // 2
@@ -270,12 +298,14 @@
 
 def weight_grads(wires, frame, g_weights, g_gain, views, blocks):
     width, deep, lanes = frame.shape
-    chan, wire = wires[0].shape[-2:]
+    chan = wires[0].shape[-2]
     own = deep - 2 * chan
+    wire = round_up(own // chan * (width // blocks) * views, 128)
+    parts = len(g_weights)
     size = round_up(2 * chan + 8 + 9 * chan // 2, 32) // 2
     vmem = pl.BlockSpec(memory_space=pltpu.VMEM)
     return pl.pallas_call(
-        functools.partial(weight_kernel, views, len(wires)),
+        functools.partial(weight_kernel, views, len(wires), parts),
         out_shape=(
             held(blocks, (width, chan, lanes), BF16),
             held(blocks, (width, chan, lanes), BF16),
@@ -283,7 +313,7 @@
             held(blocks, (size, 2 * chan), F32),
             held(blocks, (size, 2 * chan), F32),
         ),
-        in_specs=[vmem] * (len(wires) + 3),
+        in_specs=[vmem] * (len(wires) + 1 + 2 * parts),
         out_specs=(vmem,) * 5,
         scratch_shapes=[
             pltpu.VMEM((blocks, chan, wire), F32),
@@ -292,7 +322,7 @@
         ],
         name="weights",
         compiler_params=grant(blocks),
-    )(*here(blocks, *wires, frame, g_weights, g_gain))
+    )(*here(blocks, *wires, frame, *g_weights, *g_gain))
 
 
 def input_kernel(own_ref, near_ref, far_ref, w_ref, out_ref, frame_s, acc_s):
@@ -393,6 +423,7 @@
 def angular_kernel(
     scale,
     lag,
+    first,
     pieces,
     *refs,
 ):
@@ -405,7 +436,8 @@
     held_s, give_s, bias_ref, gain_ref, wqkv_ref, wkv_ref, wot_ref, wkv2_ref, gain_s = refs[:9]
     scratch = refs[9:]
     blocks = held_s.shape[0]
-    pixels, chan, lanes = cot_ref.shape
+    _, chan, lanes = cot_ref.shape
+    pixels = out_ref.shape[0]
     used = keep_ref.shape[1]
     each = used // blocks
     rows = bias_ref.shape[0]
@@ -485,7 +517,7 @@
         v_aug = jnp.concatenate([v, jnp.ones((16, rows), BF16)], axis=0)
         att_aug = dot(v_aug, e_s[:, :lanes])
         yield
-        cot = cot_ref[p]
+        cot = cot_ref[first + p]
         d_att32 = dot(wo_ref[...], cot).astype(BF16).astype(F32)
         inv = 1.0 / att_aug[chan : chan + 1]
         att = att_aug[:chan] * inv
@@ -550,8 +582,10 @@
     give(wires_out, give_s)
 
 
-def angular(wires, cotangent, keep, gain, w_query, w_key, w_value, w_out, blocks):
-    pixels, chan, lanes = cotangent.shape
+def angular(
+    wires, first, pixels, cotangent, keep, gain, w_query, w_key, w_value, w_out, blocks
+):
+    _, chan, lanes = cotangent.shape
     used = keep.shape[0]
     rows = round_up(used, 16)
     wire = wires[0].shape[-1]
@@ -563,7 +597,7 @@
         held(blocks, (8, 2 * chan), F32),
     ]
     *out, output, g_weights, g_gain = pl.pallas_call(
-        functools.partial(angular_kernel, scale, 8, len(wires)),
+        functools.partial(angular_kernel, scale, 8, first, len(wires)),
         out_shape=shapes,
         in_specs=[vmem] * (len(wires) + 7),
         out_specs=[vmem] * len(shapes),
@@ -630,14 +664,22 @@
     near, far = halo_swap(jnp.where(odd, first, last), jnp.where(odd, last, first))
     w_conv = jnp.transpose(w_conv, (2, 3, 0, 1))
     wires, frame = convolve(x, near, far, w_conv, blocks)
-    wires = exchange(wires)
+    chunks = plan(pixels, view_dev, blocks)
+    pieces = len(wires) // len(chunks)
+    arrived = [exchange(wires[c * pieces : (c + 1) * pieces]) for c in range(len(chunks))]
     cot = jnp.transpose(cotangent, (2, 3, 0, 1)).reshape(pixels, chan, views)
     cot = jnp.pad(cot, ((0, 0), (0, 0), (0, lanes - views)))
-    wires, output, g_weights, g_gain = angular(
-        wires, cot, keep, gain, w_query, w_key, w_value, w_out, blocks
-    )
+    weights = (gain, w_query, w_key, w_value, w_out)
+    wires, output, g_weights, g_gain = [], [], [], []
+    for (first, count, _, _), got in zip(chunks, arrived):
+        out, result, g_part, gain_part = angular(got, first, count, cot, keep, *weights, blocks)
+        wires += exchange(out)
+        output.append(result)
+        g_weights.append(g_part)
+        g_gain.append(gain_part)
+    output = jnp.concatenate(output, axis=0) if len(output) > 1 else output[0]
     output = jnp.transpose(output.reshape(row_dev, breadth, chan, views), (2, 3, 0, 1))
-    wires, output = lax.optimization_barrier((exchange(wires), output))
+    wires, output = lax.optimization_barrier((wires, output))
     near, far, own, kept, sent = weight_grads(wires, frame, g_weights, g_gain, view_dev, blocks)
     other = swap(sent, "row", 1)
     other, near, far = lax.optimization_barrier((other, near, far))

time: 56.1 us -> 60.4 us (1.077)
  starting transfers between devices: 21.5 us -> 32 us
  waiting for transfers between devices: 19.6 us -> 12.2 us
  Pallas kernels: 10.4 us -> 11.5 us
    ppermute x12 -> x18, starting transfers between devices: 13.1 us -> 24.8 us  [swap(): return lax.ppermute(cells, axis, [(i, i ^ step) for i in range(count)])]
    ppermute x12 -> x18, waiting for transfers between devices: 14.9 us -> 5.86 us  [swap(): return lax.ppermute(cells, axis, [(i, i ^ step) for i in range(count)])]
    ppermute x2, waiting for transfers between devices: 4.69 us -> 6.36 us  [halo_swap(): got_far = lax.ppermute(far, 'row', pairs) if pairs else jnp.zeros_like(far)]
    ppermute x2, starting transfers between devices: 7.79 us -> 6.41 us  [halo_swap(): got_far = lax.ppermute(far, 'row', pairs) if pairs else jnp.zeros_like(far)]
    pallas_call x2 -> x3, Pallas kernels: 6.89 us -> 7.97 us  [the longest x2 7.02 us: angular(): pl.pallas_call(functools.partial(angular_kernel, scale, 8, first, len(wir...]
  transfers between devices with their start and end apart: 16 -> 22, of which waited for: 9 -> 7; matrix products, arithmetic and copies ran while one was open for 2% -> 2% of each run, Pallas kernels for 3% -> 15%
where the time goes in v6:
time: 60.4 us; the launch traced here: 59.8 us
  starting transfers between devices  32 us (53%)
  waiting for transfers between devices  12.2 us (20%)
  Pallas kernels  11.5 us (19%)
  local copies, waits for them, and re-layouts  3.07 us (5%)
  between operations  0.86 us (1%)
    ppermute x18, starting transfers between devices, swap(): return lax.ppermute(cells, axis, [(i, i ^ step) for i in range(count)])  24.8 us
    pallas_call x2, Pallas kernels, angular(): pl.pallas_call(functools.partial(angular_kernel, scale, 8, first, len(wir...  7.02 us
    ppermute x2, starting transfers between devices, halo_swap(): got_far = lax.ppermute(far, 'row', pairs) if pairs else jnp.zeros_like(far)  6.41 us
    ppermute x2, waiting for transfers between devices, halo_swap(): got_far = lax.ppermute(far, 'row', pairs) if pairs else jnp.zeros_like(far)  6.36 us
    ppermute x18, waiting for transfers between devices, swap(): return lax.ppermute(cells, axis, [(i, i ^ step) for i in range(count)])  5.86 us
    unnamed x17, local copies, waits for them, and re-layouts  1.92 us
    pallas_call x1, Pallas kernels, input_grad(): pl.pallas_call(input_kernel, out_shape=jax.ShapeDtypeStruct((chan, size /...  1.74 us
  transfers between devices with their start and end apart: 22, of which 7 were waited for; matrix products, arithmetic and copies ran while one was open for 2% of the time, Pallas kernels for 15%

profile of v6, /device:TPU:1, one launch (start us, length us, event | category | flops | bytes accessed | tf_op | source)
XLA Modules:
  0.0 59.8 jit_solution(15064186116570216341)
XLA Ops:
  0.6 1.2 %copy.22 = bf16[64,73,2,16]{1,0,3,2:T(8,128)(2,1)S(1)} copy(bf16[64,73,2,16]{1,3,2,0:T(8,128)(2,1)} %param.9) | data formatting | bytes 598016 | tf_op args[0]
  2.0 4.5 %collective-permute-start.1 = (bf16[16,64,73]{2,1,0:T(8,128)(2,1)S(1)}, bf16[16,64,73]{2,1,0:T(8,128)(2,1)S(1)}, u32[]{:S(2)}, u32[]{:S(2)}) collective-permute-start(bf16[16,64,73]{2,1,0:T(8,128)(2,1)S(1)} %get-tuple-element.108), channel_id=1, source_target_pairs={{1,2},{2,1},{5,6},{6,5},{9,10},{10,9},{13,14},{14,13},{17,18},{18,... | collective-permute-start | bytes 448520 | tf_op jit(solution)/shard_map/ppermute | solution.py:40
  6.5 4.0 %collective-permute-done.1.far_ref = bf16[16,64,73]{2,1,0:T(8,128)(2,1)S(1)} collective-permute-done((bf16[16,64,73]{2,1,0:T(8,128)(2,1)S(1)}, bf16[16,64,73]{2,1,0:T(8,128)(2,1)S(1)}, u32[]{:S(2)}, u32[]{:S(2)}) %collective-permute-start.1) | collective-permute-done | bytes 149536 | tf_op jit(solution)/shard_map/ppermute | solution.py:40
  11.5 1.4 %collective-permute-start.8 = (bf16[64,256]{1,0:T(8,128)(2,1)S(1)}, bf16[64,256]{1,0:T(8,128)(2,1)S(1)}, u32[]{:S(2)}, u32[]{:S(2)}) collective-permute-start(bf16[64,256]{1,0:T(8,128)(2,1)S(1)} %get-tuple-element.67), channel_id=1, source_target_pairs={{0,4},{4,0},{8,12},{12,8},{1,5},{5,1},{9,13},{13,9},{2,6},{6,2},{1... | collective-permute-start | bytes 98312 | tf_op jit(solution)/shard_map/ppermute | solution.py:31
  12.8 2.3 %collective-permute-start.9 = (bf16[64,256]{1,0:T(8,128)(2,1)S(1)}, bf16[64,256]{1,0:T(8,128)(2,1)S(1)}, u32[]{:S(2)}, u32[]{:S(2)}) collective-permute-start(bf16[64,256]{1,0:T(8,128)(2,1)S(1)} %get-tuple-element.68), channel_id=1, source_target_pairs={{0,8},{4,12},{8,0},{12,4},{1,9},{5,13},{9,1},{13,5},{2,10},{6,14},... | collective-permute-start | bytes 98312 | tf_op jit(solution)/shard_map/ppermute | solution.py:31
  15.5 3.2 %collective-permute-start.3 = (bf16[64,384]{1,0:T(8,128)(2,1)S(1)}, bf16[64,384]{1,0:T(8,128)(2,1)S(1)}, u32[]{:S(2)}, u32[]{:S(2)}) collective-permute-start(bf16[64,384]{1,0:T(8,128)(2,1)S(1)} %get-tuple-element.60), channel_id=1, source_target_pairs={{0,8},{4,12},{8,0},{12,4},{1,9},{5,13},{9,1},{13,5},{2,10},{6,14},... | collective-permute-start | bytes 147464 | tf_op jit(solution)/shard_map/ppermute | solution.py:31
  18.9 1.0 %collective-permute-done.10.refs_3_ = bf16[64,256]{1,0:T(8,128)(2,1)S(1)} collective-permute-done((bf16[64,256]{1,0:T(8,128)(2,1)S(1)}, bf16[64,256]{1,0:T(8,128)(2,1)S(1)}, u32[]{:S(2)}, u32[]{:S(2)}) %collective-permute-start.10) | collective-permute-done | bytes 32800 | tf_op jit(solution)/shard_map/ppermute | solution.py:31
  20.6 2.9 %angular.3 = (bf16[64,256]{1,0:T(8,128)(2,1)S(1)}, bf16[64,256]{1,0:T(8,128)(2,1)S(1)}, bf16[64,256]{1,0:T(8,128)(2,1)S(1)}, bf16[64,256]{1,0:T(8,128)(2,1)S(1)}...) custom-call(bf16[64,256]{1,0:T(8,128)(2,1)S(1)} %get-tuple-element.66.refs_0_, ...), custom_call_target="tpu_custom_call" | custom-call | tf_op jit(solution)/shard_map/angular/pallas_call | solution.py:599
  23.5 2.5 %collective-permute-start.12 = (bf16[64,256]{1,0:T(8,128)(2,1)S(1)}, bf16[64,256]{1,0:T(8,128)(2,1)S(1)}, u32[]{:S(2)}, u32[]{:S(2)}) collective-permute-start(bf16[64,256]{1,0:T(8,128)(2,1)S(1)} %get-tuple-element.72), channel_id=1, source_target_pairs={{0,8},{4,12},{8,0},{12,4},{1,9},{5,13},{9,1},{13,5},{2,10},{6,14},... | collective-permute-start | bytes 98312 | tf_op jit(solution)/shard_map/ppermute | solution.py:31
  26.0 1.0 %collective-permute-start.13 = (bf16[64,256]{1,0:T(8,128)(2,1)S(1)}, bf16[64,256]{1,0:T(8,128)(2,1)S(1)}, u32[]{:S(2)}, u32[]{:S(2)}) collective-permute-start(bf16[64,256]{1,0:T(8,128)(2,1)S(1)} %get-tuple-element.73), channel_id=1, source_target_pairs={{0,12},{4,8},{8,4},{12,0},{1,13},{5,9},{9,5},{13,1},{2,14},{6,10},... | collective-permute-start | bytes 98312 | tf_op jit(solution)/shard_map/ppermute | solution.py:31
  27.1 4.1 %angular.2 = (bf16[64,384]{1,0:T(8,128)(2,1)S(1)}, bf16[64,384]{1,0:T(8,128)(2,1)S(1)}, bf16[64,384]{1,0:T(8,128)(2,1)S(1)}, bf16[64,384]{1,0:T(8,128)(2,1)S(1)}...) custom-call(bf16[64,384]{1,0:T(8,128)(2,1)S(1)} %get-tuple-element.58.refs_0_, ...), custom_call_target="tpu_custom_call" | custom-call | tf_op jit(solution)/shard_map/angular/pallas_call | solution.py:599
  31.3 2.5 %collective-permute-start.6 = (bf16[64,384]{1,0:T(8,128)(2,1)S(1)}, bf16[64,384]{1,0:T(8,128)(2,1)S(1)}, u32[]{:S(2)}, u32[]{:S(2)}) collective-permute-start(bf16[64,384]{1,0:T(8,128)(2,1)S(1)} %get-tuple-element.64), channel_id=1, source_target_pairs={{0,8},{4,12},{8,0},{12,4},{1,9},{5,13},{9,1},{13,5},{2,10},{6,14},... | collective-permute-start | bytes 147464 | tf_op jit(solution)/shard_map/ppermute | solution.py:31
  33.8 1.0 %collective-permute-start.7 = (bf16[64,384]{1,0:T(8,128)(2,1)S(1)}, bf16[64,384]{1,0:T(8,128)(2,1)S(1)}, u32[]{:S(2)}, u32[]{:S(2)}) collective-permute-start(bf16[64,384]{1,0:T(8,128)(2,1)S(1)} %get-tuple-element.65), channel_id=1, source_target_pairs={{0,12},{4,8},{8,4},{12,0},{1,13},{5,9},{9,5},{13,1},{2,14},{6,10},... | collective-permute-start | bytes 147464 | tf_op jit(solution)/shard_map/ppermute | solution.py:31
  34.9 1.1 %copy.23 = bf16[2,4,64,292]{3,1,0,2:T(4,128)(2,1)} copy(bf16[2,4,64,292]{3,2,1,0:T(8,128)(2,1)S(1)} %bitcast.24) | data formatting | bytes 598016 | tf_op jit(solution)/shard_map/reshape | solution.py:681
  36.0 2.6 %collective-permute-done.7.refs_3_ = bf16[64,384]{1,0:T(8,128)(2,1)S(1)} collective-permute-done((bf16[64,384]{1,0:T(8,128)(2,1)S(1)}, bf16[64,384]{1,0:T(8,128)(2,1)S(1)}, u32[]{:S(2)}, u32[]{:S(2)}) %collective-permute-start.7) | collective-permute-done | bytes 49184 | tf_op jit(solution)/shard_map/ppermute | solution.py:31
  38.6 1.0 %weights.1 = (bf16[16,64,128]{2,1,0:T(8,128)(2,1)S(1)}, bf16[16,64,128]{2,1,0:T(8,128)(2,1)S(1)}, bf16[16,128,128]{2,1,0:T(8,128)(2,1)S(1)}, f32[224,128]{1,0:T(8,128)S(1)}, f32[224,128]{1,0:T(8,128)S(1)}) custom-call(bf16[64,384]{1,0:T(8,128)(2,1)S(1)} %get-tuple-element.77.refs_0_, bf16[64,384]{1,0:T(8,128)(2,1)S(1)} %collective-permute-done.5.refs_1_, ...), custom_call_target="tpu_custom_call" | custom-call | tf_op jit(solution)/shard_map/weights/pallas_call | solution.py:307
  39.5 1.9 %collective-permute-start.14 = (f32[224,128]{1,0:T(8,128)S(1)}, f32[224,128]{1,0:T(8,128)S(1)}, u32[]{:S(2)}, u32[]{:S(2)}) collective-permute-start(f32[224,128]{1,0:T(8,128)S(1)} %get-tuple-element.91), channel_id=1, source_target_pairs={{0,1},{1,0},{2,3},{3,2},{4,5},{5,4},{6,7},{7,6},{8,9},{9,8},{10,11... | collective-permute-start | bytes 344072 | tf_op jit(solution)/shard_map/ppermute | solution.py:31
  41.5 1.0 %collective-permute-done.14 = f32[224,128]{1,0:T(8,128)S(1)} collective-permute-done((f32[224,128]{1,0:T(8,128)S(1)}, f32[224,128]{1,0:T(8,128)S(1)}, u32[]{:S(2)}, u32[]{:S(2)}) %collective-permute-start.14) | collective-permute-done | bytes 114720 | tf_op jit(solution)/shard_map/ppermute | solution.py:31
  42.5 4.2 %collective-permute-start.15 = (bf16[224,128]{1,0:T(8,128)(2,1)S(1)}, bf16[224,128]{1,0:T(8,128)(2,1)S(1)}, u32[]{:S(2)}, u32[]{:S(2)}) collective-permute-start(bf16[224,128]{1,0:T(8,128)(2,1)S(1)} %add_convert_fusion.1), channel_id=1, source_target_pairs={{0,2},{1,3},{2,0},{3,1},{4,6},{5,7},{6,4},{7,5},{8,10},{9,11},{10,... | collective-permute-start | bytes 172040 | tf_op jit(solution)/shard_map/ppermute | solution.py:31
  47.3 1.9 %collective-permute-start.20 = (bf16[16,64,128]{2,1,0:T(8,128)(2,1)S(1)}, bf16[16,64,128]{2,1,0:T(8,128)(2,1)S(1)}, u32[]{:S(2)}, u32[]{:S(2)}) collective-permute-start(bf16[16,64,128]{2,1,0:T(8,128)(2,1)S(1)} %get-tuple-element.97), channel_id=1, source_target_pairs={{1,2},{2,1},{5,6},{6,5},{9,10},{10,9},{13,14},{14,13},{17,18},{18,... | collective-permute-start | bytes 786440 | tf_op jit(solution)/shard_map/ppermute | solution.py:40
  50.2 2.7 %collective-permute-start.16 = (bf16[224,128]{1,0:T(8,128)(2,1)S(1)}, bf16[224,128]{1,0:T(8,128)(2,1)S(1)}, u32[]{:S(2)}, u32[]{:S(2)}) collective-permute-start(bf16[224,128]{1,0:T(8,128)(2,1)S(1)} %add_convert_fusion), channel_id=1, source_target_pairs={{0,4},{4,0},{8,12},{12,8},{1,5},{5,1},{9,13},{13,9},{2,6},{6,2},{1... | collective-permute-start | bytes 172040 | tf_op jit(solution)/shard_map/ppermute | solution.py:31
  52.9 2.4 %collective-permute-done.20.far_ref = bf16[16,64,128]{2,1,0:T(8,128)(2,1)S(1)} collective-permute-done((bf16[16,64,128]{2,1,0:T(8,128)(2,1)S(1)}, bf16[16,64,128]{2,1,0:T(8,128)(2,1)S(1)}, u32[]{:S(2)}, u32[]{:S(2)}) %collective-permute-start.20) | collective-permute-done | bytes 262176 | tf_op jit(solution)/shard_map/ppermute | solution.py:40
  55.3 1.7 %input.1 = bf16[64,2,16,73]{3,2,1,0:T(8,128)(2,1)} custom-call(bf16[16,128,128]{2,1,0:T(8,128)(2,1)S(1)} %get-tuple-element.95.own_ref, bf16[16,64,128]{2,1,0:T(8,128)(2,1)S(1)} %collective-permute-done.19.near_ref, bf16[16,64,128]{2,1,0:T(8,128)(2,1)S(1)} %collective-permute-done.20.far_ref, bf16[3,3,64,64]{3,2,1,0:T(8,128)(2,1)S(1)} %bitcast.21), custom_call_target="tpu_custom_call" | custom-call | tf_op jit(solution)/shard_map/input/pallas_call | solution.py:362
  58.0 1.0 %collective-permute-done.21.other_ref = f32[224,128]{1,0:T(8,128)S(1)} collective-permute-done((f32[224,128]{1,0:T(8,128)S(1)}, f32[224,128]{1,0:T(8,128)S(1)}, u32[]{:S(2)}, u32[]{:S(2)}) %collective-permute-start.21) | collective-permute-done | bytes 114720 | tf_op jit(solution)/shard_map/ppermute | solution.py:31
  (52 shorter events, 5.8 us)
Async XLA Ops:
  1.9 8.6 %copy-start = (bf16[64,64,3,3]{1,0,3,2:T(8,128)(2,1)S(1)}, bf16[64,64,3,3]{1,0,3,2:T(8,128)(2,1)}, u32[]{:S(2)}) copy-start(bf16[64,64,3,3]{1,0,3,2:T(8,128)(2,1)} %param.12) | copy-start | bytes 221188
  2.0 8.5 %collective-permute-start.1 = (bf16[16,64,73]{2,1,0:T(8,128)(2,1)S(1)}, bf16[16,64,73]{2,1,0:T(8,128)(2,1)S(1)}, u32[]{:S(2)}, u32[]{:S(2)}) collective-permute-start(bf16[16,64,73]{2,1,0:T(8,128)(2,1)S(1)} %get-tuple-element.108), channel_id=1, source_target_pairs={{1,2},{2,1},{5,6},{6,5},{9,10},{10,9},{13,14},{14,13},{17,18},{18,... | collective-permute-start | bytes 448520 | tf_op jit(solution)/shard_map/ppermute | solution.py:40
  6.5 4.0 %collective-permute-start = (bf16[16,64,73]{2,1,0:T(8,128)(2,1)S(1)}, bf16[16,64,73]{2,1,0:T(8,128)(2,1)S(1)}, u32[]{:S(2)}, u32[]{:S(2)}) collective-permute-start(bf16[16,64,73]{2,1,0:T(8,128)(2,1)S(1)} %get-tuple-element.109), channel_id=1, source_target_pairs={{0,1},{1,0},{2,3},{3,2},{4,5},{5,4},{6,7},{7,6},{8,9},{9,8},{10,11... | collective-permute-start | bytes 448520 | tf_op jit(solution)/shard_map/ppermute | solution.py:39
  10.5 8.2 %copy-start.6 = (bf16[64,292,2,4]{1,3,2,0:T(4,128)(2,1)S(1)}, bf16[64,292,2,4]{1,3,2,0:T(4,128)(2,1)}, u32[]{:S(2)}) copy-start(bf16[64,292,2,4]{1,3,2,0:T(4,128)(2,1)} %param.10) | copy-start | bytes 897028
  11.5 7.2 %collective-permute-start.8 = (bf16[64,256]{1,0:T(8,128)(2,1)S(1)}, bf16[64,256]{1,0:T(8,128)(2,1)S(1)}, u32[]{:S(2)}, u32[]{:S(2)}) collective-permute-start(bf16[64,256]{1,0:T(8,128)(2,1)S(1)} %get-tuple-element.67), channel_id=1, source_target_pairs={{0,4},{4,0},{8,12},{12,8},{1,5},{5,1},{9,13},{13,9},{2,6},{6,2},{1... | collective-permute-start | bytes 98312 | tf_op jit(solution)/shard_map/ppermute | solution.py:31
  12.8 6.1 %collective-permute-start.9 = (bf16[64,256]{1,0:T(8,128)(2,1)S(1)}, bf16[64,256]{1,0:T(8,128)(2,1)S(1)}, u32[]{:S(2)}, u32[]{:S(2)}) collective-permute-start(bf16[64,256]{1,0:T(8,128)(2,1)S(1)} %get-tuple-element.68), channel_id=1, source_target_pairs={{0,8},{4,12},{8,0},{12,4},{1,9},{5,13},{9,1},{13,5},{2,10},{6,14},... | collective-permute-start | bytes 98312 | tf_op jit(solution)/shard_map/ppermute | solution.py:31
  15.1 4.8 %collective-permute-start.10 = (bf16[64,256]{1,0:T(8,128)(2,1)S(1)}, bf16[64,256]{1,0:T(8,128)(2,1)S(1)}, u32[]{:S(2)}, u32[]{:S(2)}) collective-permute-start(bf16[64,256]{1,0:T(8,128)(2,1)S(1)} %get-tuple-element.69), channel_id=1, source_target_pairs={{0,12},{4,8},{8,4},{12,0},{1,13},{5,9},{9,5},{13,1},{2,14},{6,10},... | collective-permute-start | bytes 98312 | tf_op jit(solution)/shard_map/ppermute | solution.py:31
  15.1 10.9 %collective-permute-start.2 = (bf16[64,384]{1,0:T(8,128)(2,1)S(1)}, bf16[64,384]{1,0:T(8,128)(2,1)S(1)}, u32[]{:S(2)}, u32[]{:S(2)}) collective-permute-start(bf16[64,384]{1,0:T(8,128)(2,1)S(1)} %get-tuple-element.59), channel_id=1, source_target_pairs={{0,4},{4,0},{8,12},{12,8},{1,5},{5,1},{9,13},{13,9},{2,6},{6,2},{1... | collective-permute-start | bytes 147464 | tf_op jit(solution)/shard_map/ppermute | solution.py:31
  15.5 11.6 %collective-permute-start.3 = (bf16[64,384]{1,0:T(8,128)(2,1)S(1)}, bf16[64,384]{1,0:T(8,128)(2,1)S(1)}, u32[]{:S(2)}, u32[]{:S(2)}) collective-permute-start(bf16[64,384]{1,0:T(8,128)(2,1)S(1)} %get-tuple-element.60), channel_id=1, source_target_pairs={{0,8},{4,12},{8,0},{12,4},{1,9},{5,13},{9,1},{13,5},{2,10},{6,14},... | collective-permute-start | bytes 147464 | tf_op jit(solution)/shard_map/ppermute | solution.py:31
  18.7 8.4 %collective-permute-start.4 = (bf16[64,384]{1,0:T(8,128)(2,1)S(1)}, bf16[64,384]{1,0:T(8,128)(2,1)S(1)}, u32[]{:S(2)}, u32[]{:S(2)}) collective-permute-start(bf16[64,384]{1,0:T(8,128)(2,1)S(1)} %get-tuple-element.61), channel_id=1, source_target_pairs={{0,12},{4,8},{8,4},{12,0},{1,13},{5,9},{9,5},{13,1},{2,14},{6,10},... | collective-permute-start | bytes 147464 | tf_op jit(solution)/shard_map/ppermute | solution.py:31
  23.5 10.3 %collective-permute-start.11 = (bf16[64,256]{1,0:T(8,128)(2,1)S(1)}, bf16[64,256]{1,0:T(8,128)(2,1)S(1)}, u32[]{:S(2)}, u32[]{:S(2)}) collective-permute-start(bf16[64,256]{1,0:T(8,128)(2,1)S(1)} %get-tuple-element.71), channel_id=1, source_target_pairs={{0,4},{4,0},{8,12},{12,8},{1,5},{5,1},{9,13},{13,9},{2,6},{6,2},{1... | collective-permute-start | bytes 98312 | tf_op jit(solution)/shard_map/ppermute | solution.py:31
  23.5 12.4 %collective-permute-start.12 = (bf16[64,256]{1,0:T(8,128)(2,1)S(1)}, bf16[64,256]{1,0:T(8,128)(2,1)S(1)}, u32[]{:S(2)}, u32[]{:S(2)}) collective-permute-start(bf16[64,256]{1,0:T(8,128)(2,1)S(1)} %get-tuple-element.72), channel_id=1, source_target_pairs={{0,8},{4,12},{8,0},{12,4},{1,9},{5,13},{9,1},{13,5},{2,10},{6,14},... | collective-permute-start | bytes 98312 | tf_op jit(solution)/shard_map/ppermute | solution.py:31
  26.0 9.9 %collective-permute-start.13 = (bf16[64,256]{1,0:T(8,128)(2,1)S(1)}, bf16[64,256]{1,0:T(8,128)(2,1)S(1)}, u32[]{:S(2)}, u32[]{:S(2)}) collective-permute-start(bf16[64,256]{1,0:T(8,128)(2,1)S(1)} %get-tuple-element.73), channel_id=1, source_target_pairs={{0,12},{4,8},{8,4},{12,0},{1,13},{5,9},{9,5},{13,1},{2,14},{6,10},... | collective-permute-start | bytes 98312 | tf_op jit(solution)/shard_map/ppermute | solution.py:31
  31.2 4.8 %collective-permute-start.5 = (bf16[64,384]{1,0:T(8,128)(2,1)S(1)}, bf16[64,384]{1,0:T(8,128)(2,1)S(1)}, u32[]{:S(2)}, u32[]{:S(2)}) collective-permute-start(bf16[64,384]{1,0:T(8,128)(2,1)S(1)} %get-tuple-element.63), channel_id=1, source_target_pairs={{0,4},{4,0},{8,12},{12,8},{1,5},{5,1},{9,13},{13,9},{2,6},{6,2},{1... | collective-permute-start | bytes 147464 | tf_op jit(solution)/shard_map/ppermute | solution.py:31
  31.3 4.7 %collective-permute-start.6 = (bf16[64,384]{1,0:T(8,128)(2,1)S(1)}, bf16[64,384]{1,0:T(8,128)(2,1)S(1)}, u32[]{:S(2)}, u32[]{:S(2)}) collective-permute-start(bf16[64,384]{1,0:T(8,128)(2,1)S(1)} %get-tuple-element.64), channel_id=1, source_target_pairs={{0,8},{4,12},{8,0},{12,4},{1,9},{5,13},{9,1},{13,5},{2,10},{6,14},... | collective-permute-start | bytes 147464 | tf_op jit(solution)/shard_map/ppermute | solution.py:31
  33.8 4.8 %collective-permute-start.7 = (bf16[64,384]{1,0:T(8,128)(2,1)S(1)}, bf16[64,384]{1,0:T(8,128)(2,1)S(1)}, u32[]{:S(2)}, u32[]{:S(2)}) collective-permute-start(bf16[64,384]{1,0:T(8,128)(2,1)S(1)} %get-tuple-element.65), channel_id=1, source_target_pairs={{0,12},{4,8},{8,4},{12,0},{1,13},{5,9},{9,5},{13,1},{2,14},{6,10},... | collective-permute-start | bytes 147464 | tf_op jit(solution)/shard_map/ppermute | solution.py:31
  39.5 2.9 %collective-permute-start.14 = (f32[224,128]{1,0:T(8,128)S(1)}, f32[224,128]{1,0:T(8,128)S(1)}, u32[]{:S(2)}, u32[]{:S(2)}) collective-permute-start(f32[224,128]{1,0:T(8,128)S(1)} %get-tuple-element.91), channel_id=1, source_target_pairs={{0,1},{1,0},{2,3},{3,2},{4,5},{5,4},{6,7},{7,6},{8,9},{9,8},{10,11... | collective-permute-start | bytes 344072 | tf_op jit(solution)/shard_map/ppermute | solution.py:31
  42.5 6.8 %collective-permute-start.15 = (bf16[224,128]{1,0:T(8,128)(2,1)S(1)}, bf16[224,128]{1,0:T(8,128)(2,1)S(1)}, u32[]{:S(2)}, u32[]{:S(2)}) collective-permute-start(bf16[224,128]{1,0:T(8,128)(2,1)S(1)} %add_convert_fusion.1), channel_id=1, source_target_pairs={{0,2},{1,3},{2,0},{3,1},{4,6},{5,7},{6,4},{7,5},{8,10},{9,11},{10,... | collective-permute-start | bytes 172040 | tf_op jit(solution)/shard_map/ppermute | solution.py:31
  46.7 6.2 %collective-permute-start.19 = (bf16[16,64,128]{2,1,0:T(8,128)(2,1)S(1)}, bf16[16,64,128]{2,1,0:T(8,128)(2,1)S(1)}, u32[]{:S(2)}, u32[]{:S(2)}) collective-permute-start(bf16[16,64,128]{2,1,0:T(8,128)(2,1)S(1)} %get-tuple-element.96), channel_id=1, source_target_pairs={{0,1},{1,0},{2,3},{3,2},{4,5},{5,4},{6,7},{7,6},{8,9},{9,8},{10,11... | collective-permute-start | bytes 786440 | tf_op jit(solution)/shard_map/ppermute | solution.py:39
  47.3 8.0 %collective-permute-start.20 = (bf16[16,64,128]{2,1,0:T(8,128)(2,1)S(1)}, bf16[16,64,128]{2,1,0:T(8,128)(2,1)S(1)}, u32[]{:S(2)}, u32[]{:S(2)}) collective-permute-start(bf16[16,64,128]{2,1,0:T(8,128)(2,1)S(1)} %get-tuple-element.97), channel_id=1, source_target_pairs={{1,2},{2,1},{5,6},{6,5},{9,10},{10,9},{13,14},{14,13},{17,18},{18,... | collective-permute-start | bytes 786440 | tf_op jit(solution)/shard_map/ppermute | solution.py:40
  49.3 7.8 %collective-permute-start.18 = (bf16[224,128]{1,0:T(8,128)(2,1)S(1)}, bf16[224,128]{1,0:T(8,128)(2,1)S(1)}, u32[]{:S(2)}, u32[]{:S(2)}) collective-permute-start(bf16[224,128]{1,0:T(8,128)(2,1)S(1)} %add_convert_fusion), channel_id=1, source_target_pairs={{0,12},{4,8},{8,4},{12,0},{1,13},{5,9},{9,5},{13,1},{2,14},{6,10},... | collective-permute-start | bytes 172040 | tf_op jit(solution)/shard_map/ppermute | solution.py:31
  50.2 7.1 %collective-permute-start.17 = (bf16[224,128]{1,0:T(8,128)(2,1)S(1)}, bf16[224,128]{1,0:T(8,128)(2,1)S(1)}, u32[]{:S(2)}, u32[]{:S(2)}) collective-permute-start(bf16[224,128]{1,0:T(8,128)(2,1)S(1)} %add_convert_fusion), channel_id=1, source_target_pairs={{0,8},{4,12},{8,0},{12,4},{1,9},{5,13},{9,1},{13,5},{2,10},{6,14},... | collective-permute-start | bytes 172040 | tf_op jit(solution)/shard_map/ppermute | solution.py:31
  50.2 7.1 %collective-permute-start.16 = (bf16[224,128]{1,0:T(8,128)(2,1)S(1)}, bf16[224,128]{1,0:T(8,128)(2,1)S(1)}, u32[]{:S(2)}, u32[]{:S(2)}) collective-permute-start(bf16[224,128]{1,0:T(8,128)(2,1)S(1)} %add_convert_fusion), channel_id=1, source_target_pairs={{0,4},{4,0},{8,12},{12,8},{1,5},{5,1},{9,13},{13,9},{2,6},{6,2},{1... | collective-permute-start | bytes 172040 | tf_op jit(solution)/shard_map/ppermute | solution.py:31
  57.4 1.6 %collective-permute-start.21 = (f32[224,128]{1,0:T(8,128)S(1)}, f32[224,128]{1,0:T(8,128)S(1)}, u32[]{:S(2)}, u32[]{:S(2)}) collective-permute-start(f32[224,128]{1,0:T(8,128)S(1)} %convert_add_fusion.mine_ref), channel_id=1, source_target_pairs={{0,1},{1,0},{2,3},{3,2},{4,5},{5,4},{6,7},{7,6},{8,9},{9,8},{10,11... | collective-permute-start | bytes 344072 | tf_op jit(solution)/shard_map/ppermute | solution.py:31
  (6 other events, 8.7 us)

commit v7 on v5

--- a/solution.py
+++ b/solution.py
@@ -191,7 +191,7 @@
 def weight_kernel(count, pieces, *refs):
     wires = refs[:pieces]
     frame_ref, g_ref, gain_ref = refs[pieces : pieces + 3]
-    near_ref, far_ref, own_ref, keep_ref, send_ref, held_s, col_s, pack_s = refs[pieces + 3 :]
+    near_ref, far_ref, own_ref, *part_refs, held_s, col_s, pack_s = refs[pieces + 3 :]
     width, own, lanes = own_ref.shape
     blocks, chan, wire = held_s.shape
     rows = own // chan
@@ -263,16 +263,19 @@
     pack_s[at + 3 * chan : at + 3 * chan + half] = jnp.concatenate(
         [rest[:half], rest[half:]], axis=1
     )
-    size = keep_ref.shape[0]
-    keep_ref[...] = pack_s[pl.ds(pl.multiple_of(odd * size, 8), size)]
-    send_ref[...] = pack_s[pl.ds(pl.multiple_of((1 - odd) * size, 8), size)]
+    size = part_refs[0].shape[0]
+    for step, ref in enumerate(part_refs):
+        turn = lax.axis_index("row") ^ step if len(part_refs) > 1 else 0
+        ref[...] = pack_s[pl.ds(pl.multiple_of(turn * size, 16), size)].astype(ref.dtype)
 
 
 def weight_grads(wires, frame, g_weights, g_gain, views, blocks):
     width, deep, lanes = frame.shape
     chan, wire = wires[0].shape[-2:]
     own = deep - 2 * chan
-    size = round_up(2 * chan + 8 + 9 * chan // 2, 32) // 2
+    count = lax.axis_size("row")
+    parts = count if pairwise(count) else 1
+    size = round_up(2 * chan + 8 + 9 * chan // 2, 16 * parts) // parts
     vmem = pl.BlockSpec(memory_space=pltpu.VMEM)
     return pl.pallas_call(
         functools.partial(weight_kernel, views, len(wires)),
@@ -280,15 +283,14 @@
             held(blocks, (width, chan, lanes), BF16),
             held(blocks, (width, chan, lanes), BF16),
             held(blocks, (width, own, lanes), BF16),
-            held(blocks, (size, 2 * chan), F32),
-            held(blocks, (size, 2 * chan), F32),
-        ),
+        )
+        + (held(blocks, (size, 2 * chan), BF16 if parts > 1 else F32),) * parts,
         in_specs=[vmem] * (len(wires) + 3),
-        out_specs=(vmem,) * 5,
+        out_specs=(vmem,) * (3 + parts),
         scratch_shapes=[
             pltpu.VMEM((blocks, chan, wire), F32),
             pltpu.VMEM((width + 2, own, lanes), BF16),
-            pltpu.VMEM((2 * size, 2 * chan), F32),
+            pltpu.VMEM((parts * size, 2 * chan), F32),
         ],
         name="weights",
         compiler_params=grant(blocks),
@@ -343,12 +345,13 @@
     )(*here(blocks, own, near, far), w_conv)
 
 
-def unpack_kernel(mine_ref, other_ref, conv_ref, q_ref, k_ref, v_ref, o_ref, gain_ref, pack_s):
-    size = mine_ref.shape[0]
+def unpack_kernel(parts, *refs):
+    conv_ref, q_ref, k_ref, v_ref, o_ref, gain_ref, pack_s = refs[parts:]
+    size = refs[0].shape[0]
     chan = q_ref.shape[0]
-    odd = row_is_odd()
-    pack_s[pl.ds(pl.multiple_of(odd * size, 8), size)] = mine_ref[...]
-    pack_s[pl.ds(pl.multiple_of((1 - odd) * size, 8), size)] = other_ref[...]
+    for step in range(parts):
+        turn = lax.axis_index("row") ^ step if parts > 1 else 0
+        pack_s[pl.ds(pl.multiple_of(turn * size, 16), size)] = refs[step][...].astype(F32)
     k_ref[...] = pack_s[:chan, :chan]
     v_ref[...] = pack_s[:chan, chan:]
     q_ref[...] = pack_s[chan : 2 * chan, :chan]
@@ -369,11 +372,11 @@
             ]
 
 
-def unpack(mine, other, chan, blocks):
+def unpack(parts, chan, blocks):
     vmem = pl.BlockSpec(memory_space=pltpu.VMEM)
     square = jax.ShapeDtypeStruct((chan, chan), F32)
     return pl.pallas_call(
-        unpack_kernel,
+        functools.partial(unpack_kernel, len(parts)),
         out_shape=(
             jax.ShapeDtypeStruct((3, 3, chan, chan), F32),
             square,
@@ -382,12 +385,12 @@
             square,
             jax.ShapeDtypeStruct((1, chan), F32),
         ),
-        in_specs=[vmem] * 2,
+        in_specs=[vmem] * len(parts),
         out_specs=(vmem,) * 6,
-        scratch_shapes=[pltpu.VMEM((2 * mine.shape[0], 2 * chan), F32)],
+        scratch_shapes=[pltpu.VMEM((len(parts) * parts[0].shape[0], 2 * chan), F32)],
         name="unpack",
         compiler_params=grant(blocks),
-    )(*here(blocks, mine, other))
+    )(*here(blocks, *parts))
 
 
 def angular_kernel(
@@ -594,6 +597,13 @@
     return out, output, g_weights, g_gain
 
 
+def sum_parts(parts):
+    total = parts[0].astype(F32)
+    for part in parts[1:]:
+        total = total + part.astype(F32)
+    return total
+
+
 def reduce_views(own, beside):
     count = lax.axis_size("view")
     if not pairwise(count):
@@ -601,20 +611,22 @@
     own = own.astype(BF16)
     parts = [swap(own, "view", step) for step in range(1, count)]
     parts, beside = lax.optimization_barrier((parts, beside))
-    total = own.astype(F32)
-    for part in parts:
-        total = total + part.astype(F32)
-    return total, beside
-
-
-def reduce_rows(own):
-    count = lax.axis_size("row")
-    step = 2
-    while step < count:
-        own = own.astype(BF16)
-        own = own.astype(F32) + swap(own, "row", step).astype(F32)
-        step *= 2
-    return own
+    return sum_parts([own] + parts), beside
+
+
+def scatter_rows(parts):
+    if len(parts) == 1:
+        return lax.psum(parts[0], "row")
+    return sum_parts(
+        [parts[0]] + [swap(parts[step], "row", step) for step in range(1, len(parts))]
+    )
+
+
+def gather_rows(own, count):
+    if count == 1:
+        return [own]
+    own = own.astype(BF16)
+    return [own] + [swap(own, "row", step) for step in range(1, count)]
 
 
 def body(inputs, cotangent, keep, w_conv, gain, w_query, w_key, w_value, w_out):
@@ -638,15 +650,13 @@
     )
     output = jnp.transpose(output.reshape(row_dev, breadth, chan, views), (2, 3, 0, 1))
     wires, output = lax.optimization_barrier((exchange(wires), output))
-    near, far, own, kept, sent = weight_grads(wires, frame, g_weights, g_gain, view_dev, blocks)
-    other = swap(sent, "row", 1)
-    other, near, far = lax.optimization_barrier((other, near, far))
-    part = reduce_rows(kept + other)
+    near, far, own, *parts = weight_grads(wires, frame, g_weights, g_gain, view_dev, blocks)
+    part = scatter_rows(parts)
     near, far = halo_swap(near, far)
     d_input = input_grad(own, near, far, w_conv, view_dev, blocks)
     part, d_input = reduce_views(part, d_input)
-    other = swap(part, "row", 1)
-    g_conv, g_query, g_key, g_value, g_out, g_gain = unpack(part, other, chan, blocks)
+    parts = gather_rows(part, len(parts))
+    g_conv, g_query, g_key, g_value, g_out, g_gain = unpack(parts, chan, blocks)
     d_input = jnp.transpose(d_input, (0, 3, 1, 2))
     g_conv = jnp.transpose(g_conv, (2, 3, 0, 1))
     return (output, d_input, g_conv, g_gain[0], g_query, g_key, g_value, g_out)

time: 56.1 us -> 56.1 us (level)
  starting transfers between devices: 21.5 us -> 22.9 us
  waiting for transfers between devices: 19.6 us -> 18.5 us
    ppermute x12 -> x15, starting transfers between devices: 13.1 us -> 16.1 us  [swap(): return lax.ppermute(cells, axis, [(i, i ^ step) for i in range(count)])]
    ppermute x12 -> x15, waiting for transfers between devices: 14.9 us -> 12.6 us  [swap(): return lax.ppermute(cells, axis, [(i, i ^ step) for i in range(count)])]
    ppermute x2, starting transfers between devices: 7.79 us -> 6.6 us  [halo_swap(): got_far = lax.ppermute(far, 'row', pairs) if pairs else jnp.zeros_like(far)]
    ppermute x2, waiting for transfers between devices: 4.69 us -> 5.85 us  [halo_swap(): got_far = lax.ppermute(far, 'row', pairs) if pairs else jnp.zeros_like(far)]
  transfers between devices with their start and end apart: 16 -> 19, of which waited for: 9 -> 8; matrix products, arithmetic and copies ran while one was open for 2% -> 2% of each run, Pallas kernels for 3% -> 3%
where the time goes in v7:
time: 56.1 us; the launch traced here: 55.8 us
  starting transfers between devices  22.9 us (41%)
  waiting for transfers between devices  18.5 us (33%)
  Pallas kernels  10.4 us (19%)
  local copies, waits for them, and re-layouts  3.06 us (5%)
  between operations  0.85 us (2%)
    ppermute x15, starting transfers between devices, swap(): return lax.ppermute(cells, axis, [(i, i ^ step) for i in range(count)])  16.1 us
    ppermute x15, waiting for transfers between devices, swap(): return lax.ppermute(cells, axis, [(i, i ^ step) for i in range(count)])  12.6 us
    ppermute x2, starting transfers between devices, halo_swap(): got_far = lax.ppermute(far, 'row', pairs) if pairs else jnp.zeros_like(far)  6.6 us
    pallas_call x1, Pallas kernels, angular(): pl.pallas_call(functools.partial(angular_kernel, scale, 8, len(wires)), o...  5.92 us
    ppermute x2, waiting for transfers between devices, halo_swap(): got_far = lax.ppermute(far, 'row', pairs) if pairs else jnp.zeros_like(far)  5.85 us
    unnamed x17, local copies, waits for them, and re-layouts  1.91 us
    pallas_call x1, Pallas kernels, input_grad(): pl.pallas_call(input_kernel, out_shape=jax.ShapeDtypeStruct((chan, size /...  1.74 us
  transfers between devices with their start and end apart: 19, of which 8 were waited for; matrix products, arithmetic and copies ran while one was open for 2% of the time, Pallas kernels for 3%

profile of v7, /device:TPU:1, one launch (start us, length us, event | category | flops | bytes accessed | tf_op | source)
XLA Modules:
  0.0 55.8 jit_solution(152677294479212725)
XLA Ops:
  0.6 1.2 %copy.22 = bf16[64,73,2,16]{1,0,3,2:T(8,128)(2,1)S(1)} copy(bf16[64,73,2,16]{1,3,2,0:T(8,128)(2,1)} %param.9) | data formatting | bytes 598016 | tf_op args[0]
  2.0 4.5 %collective-permute-start.1 = (bf16[16,64,73]{2,1,0:T(8,128)(2,1)S(1)}, bf16[16,64,73]{2,1,0:T(8,128)(2,1)S(1)}, u32[]{:S(2)}, u32[]{:S(2)}) collective-permute-start(bf16[16,64,73]{2,1,0:T(8,128)(2,1)S(1)} %get-tuple-element.76), channel_id=1, source_target_pairs={{1,2},{2,1},{5,6},{6,5},{9,10},{10,9},{13,14},{14,13},{17,18},{18,... | collective-permute-start | bytes 448520 | tf_op jit(solution)/shard_map/ppermute | solution.py:40
  6.5 4.0 %collective-permute-done.1.far_ref = bf16[16,64,73]{2,1,0:T(8,128)(2,1)S(1)} collective-permute-done((bf16[16,64,73]{2,1,0:T(8,128)(2,1)S(1)}, bf16[16,64,73]{2,1,0:T(8,128)(2,1)S(1)}, u32[]{:S(2)}, u32[]{:S(2)}) %collective-permute-start.1) | collective-permute-done | bytes 149536 | tf_op jit(solution)/shard_map/ppermute | solution.py:40
  10.5 0.9 %conv.1 = (bf16[64,640]{1,0:T(8,128)(2,1)S(1)}, bf16[64,640]{1,0:T(8,128)(2,1)S(1)}, bf16[64,640]{1,0:T(8,128)(2,1)S(1)}, bf16[64,640]{1,0:T(8,128)(2,1)S(1)}, bf16[16,256,128]{2,1,0:T(8,128)(2,1)S(1)}) custom-call(bf16[2,16,64,73]{3,2,1,0:T(8,128)(2,1)S(1)} %bitcast.19, bf16[16,64,73]{2,1,0:T(8,128)(2,1)S(1)} %collective-permute-done.near_ref, ...), custom_call_target="tpu_custom_call" | custom-call | tf_op jit(solution)/shard_map/conv/pallas_call | solution.py:176
  11.5 1.4 %collective-permute-start.2 = (bf16[64,640]{1,0:T(8,128)(2,1)S(1)}, bf16[64,640]{1,0:T(8,128)(2,1)S(1)}, u32[]{:S(2)}, u32[]{:S(2)}) collective-permute-start(bf16[64,640]{1,0:T(8,128)(2,1)S(1)} %get-tuple-element.43), channel_id=1, source_target_pairs={{0,4},{4,0},{8,12},{12,8},{1,5},{5,1},{9,13},{13,9},{2,6},{6,2},{1... | collective-permute-start | bytes 245768 | tf_op jit(solution)/shard_map/ppermute | solution.py:31
  12.8 2.3 %collective-permute-start.3 = (bf16[64,640]{1,0:T(8,128)(2,1)S(1)}, bf16[64,640]{1,0:T(8,128)(2,1)S(1)}, u32[]{:S(2)}, u32[]{:S(2)}) collective-permute-start(bf16[64,640]{1,0:T(8,128)(2,1)S(1)} %get-tuple-element.44), channel_id=1, source_target_pairs={{0,8},{4,12},{8,0},{12,4},{1,9},{5,13},{9,1},{13,5},{2,10},{6,14},... | collective-permute-start | bytes 245768 | tf_op jit(solution)/shard_map/ppermute | solution.py:31
  15.6 4.9 %collective-permute-done.3.refs_2_ = bf16[64,640]{1,0:T(8,128)(2,1)S(1)} collective-permute-done((bf16[64,640]{1,0:T(8,128)(2,1)S(1)}, bf16[64,640]{1,0:T(8,128)(2,1)S(1)}, u32[]{:S(2)}, u32[]{:S(2)}) %collective-permute-start.3) | collective-permute-done | bytes 81952 | tf_op jit(solution)/shard_map/ppermute | solution.py:31
  21.2 5.9 %angular.1 = (bf16[64,640]{1,0:T(8,128)(2,1)S(1)}, bf16[64,640]{1,0:T(8,128)(2,1)S(1)}, bf16[64,640]{1,0:T(8,128)(2,1)S(1)}, bf16[64,640]{1,0:T(8,128)(2,1)S(1)}...) custom-call(bf16[64,640]{1,0:T(8,128)(2,1)S(1)} %get-tuple-element.42.refs_0_, ...), custom_call_target="tpu_custom_call" | custom-call | tf_op jit(solution)/shard_map/angular/pallas_call | solution.py:568
  27.1 1.4 %collective-permute-start.5 = (bf16[64,640]{1,0:T(8,128)(2,1)S(1)}, bf16[64,640]{1,0:T(8,128)(2,1)S(1)}, u32[]{:S(2)}, u32[]{:S(2)}) collective-permute-start(bf16[64,640]{1,0:T(8,128)(2,1)S(1)} %get-tuple-element.47), channel_id=1, source_target_pairs={{0,4},{4,0},{8,12},{12,8},{1,5},{5,1},{9,13},{13,9},{2,6},{6,2},{1... | collective-permute-start | bytes 245768 | tf_op jit(solution)/shard_map/ppermute | solution.py:31
  28.5 1.3 %collective-permute-start.6 = (bf16[64,640]{1,0:T(8,128)(2,1)S(1)}, bf16[64,640]{1,0:T(8,128)(2,1)S(1)}, u32[]{:S(2)}, u32[]{:S(2)}) collective-permute-start(bf16[64,640]{1,0:T(8,128)(2,1)S(1)} %get-tuple-element.48), channel_id=1, source_target_pairs={{0,8},{4,12},{8,0},{12,4},{1,9},{5,13},{9,1},{13,5},{2,10},{6,14},... | collective-permute-start | bytes 245768 | tf_op jit(solution)/shard_map/ppermute | solution.py:31
  29.9 0.9 %collective-permute-start.7 = (bf16[64,640]{1,0:T(8,128)(2,1)S(1)}, bf16[64,640]{1,0:T(8,128)(2,1)S(1)}, u32[]{:S(2)}, u32[]{:S(2)}) collective-permute-start(bf16[64,640]{1,0:T(8,128)(2,1)S(1)} %get-tuple-element.49), channel_id=1, source_target_pairs={{0,12},{4,8},{8,4},{12,0},{1,13},{5,9},{9,5},{13,1},{2,14},{6,10},... | collective-permute-start | bytes 245768 | tf_op jit(solution)/shard_map/ppermute | solution.py:31
  30.7 1.1 %copy.23 = bf16[2,4,64,292]{3,1,0,2:T(4,128)(2,1)} copy(bf16[2,4,64,292]{3,2,1,0:T(8,128)(2,1)S(1)} %bitcast.22) | data formatting | bytes 598016 | tf_op jit(solution)/shard_map/reshape | solution.py:651
  31.8 1.4 %collective-permute-done.6.refs_2_ = bf16[64,640]{1,0:T(8,128)(2,1)S(1)} collective-permute-done((bf16[64,640]{1,0:T(8,128)(2,1)S(1)}, bf16[64,640]{1,0:T(8,128)(2,1)S(1)}, u32[]{:S(2)}, u32[]{:S(2)}) %collective-permute-start.6) | collective-permute-done | bytes 81952 | tf_op jit(solution)/shard_map/ppermute | solution.py:31
  33.2 3.9 %collective-permute-done.7.refs_3_ = bf16[64,640]{1,0:T(8,128)(2,1)S(1)} collective-permute-done((bf16[64,640]{1,0:T(8,128)(2,1)S(1)}, bf16[64,640]{1,0:T(8,128)(2,1)S(1)}, u32[]{:S(2)}, u32[]{:S(2)}) %collective-permute-start.7) | collective-permute-done | bytes 81952 | tf_op jit(solution)/shard_map/ppermute | solution.py:31
  37.1 0.9 %weights.1 = (bf16[16,64,128]{2,1,0:T(8,128)(2,1)S(1)}, bf16[16,64,128]{2,1,0:T(8,128)(2,1)S(1)}, bf16[16,128,128]{2,1,0:T(8,128)(2,1)S(1)}, bf16[112,128]{1,0:T...) custom-call(bf16[64,640]{1,0:T(8,128)(2,1)S(1)} %get-tuple-element.52.ref, ...), custom_call_target="tpu_custom_call" | custom-call | tf_op jit(solution)/shard_map/weights/pallas_call | solution.py:280
  38.0 1.2 %collective-permute-start.8 = (bf16[112,128]{1,0:T(8,128)(2,1)S(1)}, bf16[112,128]{1,0:T(8,128)(2,1)S(1)}, u32[]{:S(2)}, u32[]{:S(2)}) collective-permute-start(bf16[112,128]{1,0:T(8,128)(2,1)S(1)} %get-tuple-element.60), channel_id=1, source_target_pairs={{0,1},{1,0},{2,3},{3,2},{4,5},{5,4},{6,7},{7,6},{8,9},{9,8},{10,11... | collective-permute-start | bytes 86024 | tf_op jit(solution)/shard_map/ppermute | solution.py:31
  39.3 1.7 %collective-permute-start.10 = (bf16[112,128]{1,0:T(8,128)(2,1)S(1)}, bf16[112,128]{1,0:T(8,128)(2,1)S(1)}, u32[]{:S(2)}, u32[]{:S(2)}) collective-permute-start(bf16[112,128]{1,0:T(8,128)(2,1)S(1)} %get-tuple-element.62), channel_id=1, source_target_pairs={{0,3},{1,2},{2,1},{3,0},{4,7},{5,6},{6,5},{7,4},{8,11},{9,10},{10,... | collective-permute-start | bytes 86024 | tf_op jit(solution)/shard_map/ppermute | solution.py:31
  41.1 2.1 %collective-permute-start.15 = (bf16[16,64,128]{2,1,0:T(8,128)(2,1)S(1)}, bf16[16,64,128]{2,1,0:T(8,128)(2,1)S(1)}, u32[]{:S(2)}, u32[]{:S(2)}) collective-permute-start(bf16[16,64,128]{2,1,0:T(8,128)(2,1)S(1)} %get-tuple-element.65), channel_id=1, source_target_pairs={{1,2},{2,1},{5,6},{6,5},{9,10},{10,9},{13,14},{14,13},{17,18},{18,... | collective-permute-start | bytes 786440 | tf_op jit(solution)/shard_map/ppermute | solution.py:40
  43.3 2.6 %collective-permute-start.13 = (bf16[112,128]{1,0:T(8,128)(2,1)S(1)}, bf16[112,128]{1,0:T(8,128)(2,1)S(1)}, u32[]{:S(2)}, u32[]{:S(2)}) collective-permute-start(bf16[112,128]{1,0:T(8,128)(2,1)S(1)} %add_convert_fusion.1), channel_id=1, source_target_pairs={{0,12},{4,8},{8,4},{12,0},{1,13},{5,9},{9,5},{13,1},{2,14},{6,10},... | collective-permute-start | bytes 86024 | tf_op jit(solution)/shard_map/ppermute | solution.py:31
  46.0 0.9 %collective-permute-start.11 = (bf16[112,128]{1,0:T(8,128)(2,1)S(1)}, bf16[112,128]{1,0:T(8,128)(2,1)S(1)}, u32[]{:S(2)}, u32[]{:S(2)}) collective-permute-start(bf16[112,128]{1,0:T(8,128)(2,1)S(1)} %add_convert_fusion.1), channel_id=1, source_target_pairs={{0,4},{4,0},{8,12},{12,8},{1,5},{5,1},{9,13},{13,9},{2,6},{6,2},{1... | collective-permute-start | bytes 86024 | tf_op jit(solution)/shard_map/ppermute | solution.py:31
  46.9 1.9 %collective-permute-done.15.far_ref = bf16[16,64,128]{2,1,0:T(8,128)(2,1)S(1)} collective-permute-done((bf16[16,64,128]{2,1,0:T(8,128)(2,1)S(1)}, bf16[16,64,128]{2,1,0:T(8,128)(2,1)S(1)}, u32[]{:S(2)}, u32[]{:S(2)}) %collective-permute-start.15) | collective-permute-done | bytes 262176 | tf_op jit(solution)/shard_map/ppermute | solution.py:40
  48.8 1.7 %input.1 = bf16[64,2,16,73]{3,2,1,0:T(8,128)(2,1)} custom-call(bf16[16,128,128]{2,1,0:T(8,128)(2,1)S(1)} %get-tuple-element.63.own_ref, bf16[16,64,128]{2,1,0:T(8,128)(2,1)S(1)} %collective-permute-done.14.near_ref, bf16[16,64,128]{2,1,0:T(8,128)(2,1)S(1)} %collective-permute-done.15.far_ref, bf16[3,3,64,64]{3,2,1,0:T(8,128)(2,1)S(1)} %bitcast.21), custom_call_target="tpu_custom_call" | custom-call | tf_op jit(solution)/shard_map/input/pallas_call | solution.py:334
  50.6 1.6 %collective-permute-start.18 = (bf16[112,128]{1,0:T(8,128)(2,1)S(1)}, bf16[112,128]{1,0:T(8,128)(2,1)S(1)}, u32[]{:S(2)}, u32[]{:S(2)}) collective-permute-start(bf16[112,128]{1,0:T(8,128)(2,1)S(1)} %add_convert_fusion.refs_0_), channel_id=1, source_target_pairs={{0,3},{1,2},{2,1},{3,0},{4,7},{5,6},{6,5},{7,4},{8,11},{9,10},{10,... | collective-permute-start | bytes 86024 | tf_op jit(solution)/shard_map/ppermute | solution.py:31
  52.8 1.3 %collective-permute-done.18.refs_3_ = bf16[112,128]{1,0:T(8,128)(2,1)S(1)} collective-permute-done((bf16[112,128]{1,0:T(8,128)(2,1)S(1)}, bf16[112,128]{1,0:T(8,128)(2,1)S(1)}, u32[]{:S(2)}, u32[]{:S(2)}) %collective-permute-start.18) | collective-permute-done | bytes 28704 | tf_op jit(solution)/shard_map/ppermute | solution.py:31
  (43 shorter events, 3.7 us)
Async XLA Ops:
  1.9 8.6 %copy-start = (bf16[64,64,3,3]{1,0,3,2:T(8,128)(2,1)S(1)}, bf16[64,64,3,3]{1,0,3,2:T(8,128)(2,1)}, u32[]{:S(2)}) copy-start(bf16[64,64,3,3]{1,0,3,2:T(8,128)(2,1)} %param.12) | copy-start | bytes 221188
  2.0 8.5 %collective-permute-start.1 = (bf16[16,64,73]{2,1,0:T(8,128)(2,1)S(1)}, bf16[16,64,73]{2,1,0:T(8,128)(2,1)S(1)}, u32[]{:S(2)}, u32[]{:S(2)}) collective-permute-start(bf16[16,64,73]{2,1,0:T(8,128)(2,1)S(1)} %get-tuple-element.76), channel_id=1, source_target_pairs={{1,2},{2,1},{5,6},{6,5},{9,10},{10,9},{13,14},{14,13},{17,18},{18,... | collective-permute-start | bytes 448520 | tf_op jit(solution)/shard_map/ppermute | solution.py:40
  6.5 4.0 %collective-permute-start = (bf16[16,64,73]{2,1,0:T(8,128)(2,1)S(1)}, bf16[16,64,73]{2,1,0:T(8,128)(2,1)S(1)}, u32[]{:S(2)}, u32[]{:S(2)}) collective-permute-start(bf16[16,64,73]{2,1,0:T(8,128)(2,1)S(1)} %get-tuple-element.77), channel_id=1, source_target_pairs={{0,1},{1,0},{2,3},{3,2},{4,5},{5,4},{6,7},{7,6},{8,9},{9,8},{10,11... | collective-permute-start | bytes 448520 | tf_op jit(solution)/shard_map/ppermute | solution.py:39
  11.5 4.2 %collective-permute-start.2 = (bf16[64,640]{1,0:T(8,128)(2,1)S(1)}, bf16[64,640]{1,0:T(8,128)(2,1)S(1)}, u32[]{:S(2)}, u32[]{:S(2)}) collective-permute-start(bf16[64,640]{1,0:T(8,128)(2,1)S(1)} %get-tuple-element.43), channel_id=1, source_target_pairs={{0,4},{4,0},{8,12},{12,8},{1,5},{5,1},{9,13},{13,9},{2,6},{6,2},{1... | collective-permute-start | bytes 245768 | tf_op jit(solution)/shard_map/ppermute | solution.py:31
  12.8 7.7 %collective-permute-start.3 = (bf16[64,640]{1,0:T(8,128)(2,1)S(1)}, bf16[64,640]{1,0:T(8,128)(2,1)S(1)}, u32[]{:S(2)}, u32[]{:S(2)}) collective-permute-start(bf16[64,640]{1,0:T(8,128)(2,1)S(1)} %get-tuple-element.44), channel_id=1, source_target_pairs={{0,8},{4,12},{8,0},{12,4},{1,9},{5,13},{9,1},{13,5},{2,10},{6,14},... | collective-permute-start | bytes 245768 | tf_op jit(solution)/shard_map/ppermute | solution.py:31
  15.2 5.4 %collective-permute-start.4 = (bf16[64,640]{1,0:T(8,128)(2,1)S(1)}, bf16[64,640]{1,0:T(8,128)(2,1)S(1)}, u32[]{:S(2)}, u32[]{:S(2)}) collective-permute-start(bf16[64,640]{1,0:T(8,128)(2,1)S(1)} %get-tuple-element.45), channel_id=1, source_target_pairs={{0,12},{4,8},{8,4},{12,0},{1,13},{5,9},{9,5},{13,1},{2,14},{6,10},... | collective-permute-start | bytes 245768 | tf_op jit(solution)/shard_map/ppermute | solution.py:31
  15.2 5.3 %copy-start.1 = (bf16[64,64]{1,0:T(8,128)(2,1)S(1)}, bf16[64,64]{1,0:T(8,128)(2,1)}, u32[]{:S(2)}) copy-start(bf16[64,64]{1,0:T(8,128)(2,1)} %refs_7_.1) | copy-start | bytes 24580
  15.2 5.3 %copy-start.2 = (bf16[64,64]{1,0:T(8,128)(2,1)S(1)}, bf16[64,64]{1,0:T(8,128)(2,1)}, u32[]{:S(2)}) copy-start(bf16[64,64]{1,0:T(8,128)(2,1)} %refs_8_.1) | copy-start | bytes 24580
  15.3 5.3 %copy-start.3 = (bf16[64,64]{1,0:T(8,128)(2,1)S(1)}, bf16[64,64]{1,0:T(8,128)(2,1)}, u32[]{:S(2)}) copy-start(bf16[64,64]{1,0:T(8,128)(2,1)} %refs_9_.1) | copy-start | bytes 24580
  15.3 5.3 %copy-start.4 = (bf16[64,64]{1,0:T(8,128)(2,1)S(1)}, bf16[64,64]{1,0:T(8,128)(2,1)}, u32[]{:S(2)}) copy-start(bf16[64,64]{1,0:T(8,128)(2,1)} %refs_10_.1) | copy-start | bytes 24580
  27.1 4.7 %collective-permute-start.5 = (bf16[64,640]{1,0:T(8,128)(2,1)S(1)}, bf16[64,640]{1,0:T(8,128)(2,1)S(1)}, u32[]{:S(2)}, u32[]{:S(2)}) collective-permute-start(bf16[64,640]{1,0:T(8,128)(2,1)S(1)} %get-tuple-element.47), channel_id=1, source_target_pairs={{0,4},{4,0},{8,12},{12,8},{1,5},{5,1},{9,13},{13,9},{2,6},{6,2},{1... | collective-permute-start | bytes 245768 | tf_op jit(solution)/shard_map/ppermute | solution.py:31
  28.5 4.6 %collective-permute-start.6 = (bf16[64,640]{1,0:T(8,128)(2,1)S(1)}, bf16[64,640]{1,0:T(8,128)(2,1)S(1)}, u32[]{:S(2)}, u32[]{:S(2)}) collective-permute-start(bf16[64,640]{1,0:T(8,128)(2,1)S(1)} %get-tuple-element.48), channel_id=1, source_target_pairs={{0,8},{4,12},{8,0},{12,4},{1,9},{5,13},{9,1},{13,5},{2,10},{6,14},... | collective-permute-start | bytes 245768 | tf_op jit(solution)/shard_map/ppermute | solution.py:31
  29.9 7.2 %collective-permute-start.7 = (bf16[64,640]{1,0:T(8,128)(2,1)S(1)}, bf16[64,640]{1,0:T(8,128)(2,1)S(1)}, u32[]{:S(2)}, u32[]{:S(2)}) collective-permute-start(bf16[64,640]{1,0:T(8,128)(2,1)S(1)} %get-tuple-element.49), channel_id=1, source_target_pairs={{0,12},{4,8},{8,4},{12,0},{1,13},{5,9},{9,5},{13,1},{2,14},{6,10},... | collective-permute-start | bytes 245768 | tf_op jit(solution)/shard_map/ppermute | solution.py:31
  38.0 5.2 %collective-permute-start.8 = (bf16[112,128]{1,0:T(8,128)(2,1)S(1)}, bf16[112,128]{1,0:T(8,128)(2,1)S(1)}, u32[]{:S(2)}, u32[]{:S(2)}) collective-permute-start(bf16[112,128]{1,0:T(8,128)(2,1)S(1)} %get-tuple-element.60), channel_id=1, source_target_pairs={{0,1},{1,0},{2,3},{3,2},{4,5},{5,4},{6,7},{7,6},{8,9},{9,8},{10,11... | collective-permute-start | bytes 86024 | tf_op jit(solution)/shard_map/ppermute | solution.py:31
  39.3 4.0 %collective-permute-start.9 = (bf16[112,128]{1,0:T(8,128)(2,1)S(1)}, bf16[112,128]{1,0:T(8,128)(2,1)S(1)}, u32[]{:S(2)}, u32[]{:S(2)}) collective-permute-start(bf16[112,128]{1,0:T(8,128)(2,1)S(1)} %get-tuple-element.61), channel_id=1, source_target_pairs={{0,2},{1,3},{2,0},{3,1},{4,6},{5,7},{6,4},{7,5},{8,10},{9,11},{10,... | collective-permute-start | bytes 86024 | tf_op jit(solution)/shard_map/ppermute | solution.py:31
  39.3 4.0 %collective-permute-start.10 = (bf16[112,128]{1,0:T(8,128)(2,1)S(1)}, bf16[112,128]{1,0:T(8,128)(2,1)S(1)}, u32[]{:S(2)}, u32[]{:S(2)}) collective-permute-start(bf16[112,128]{1,0:T(8,128)(2,1)S(1)} %get-tuple-element.62), channel_id=1, source_target_pairs={{0,3},{1,2},{2,1},{3,0},{4,7},{5,6},{6,5},{7,4},{8,11},{9,10},{10,... | collective-permute-start | bytes 86024 | tf_op jit(solution)/shard_map/ppermute | solution.py:31
  41.0 5.9 %collective-permute-start.14 = (bf16[16,64,128]{2,1,0:T(8,128)(2,1)S(1)}, bf16[16,64,128]{2,1,0:T(8,128)(2,1)S(1)}, u32[]{:S(2)}, u32[]{:S(2)}) collective-permute-start(bf16[16,64,128]{2,1,0:T(8,128)(2,1)S(1)} %get-tuple-element.64), channel_id=1, source_target_pairs={{0,1},{1,0},{2,3},{3,2},{4,5},{5,4},{6,7},{7,6},{8,9},{9,8},{10,11... | collective-permute-start | bytes 786440 | tf_op jit(solution)/shard_map/ppermute | solution.py:39
  41.1 7.7 %collective-permute-start.15 = (bf16[16,64,128]{2,1,0:T(8,128)(2,1)S(1)}, bf16[16,64,128]{2,1,0:T(8,128)(2,1)S(1)}, u32[]{:S(2)}, u32[]{:S(2)}) collective-permute-start(bf16[16,64,128]{2,1,0:T(8,128)(2,1)S(1)} %get-tuple-element.65), channel_id=1, source_target_pairs={{1,2},{2,1},{5,6},{6,5},{9,10},{10,9},{13,14},{14,13},{17,18},{18,... | collective-permute-start | bytes 786440 | tf_op jit(solution)/shard_map/ppermute | solution.py:40
  43.3 7.2 %collective-permute-start.13 = (bf16[112,128]{1,0:T(8,128)(2,1)S(1)}, bf16[112,128]{1,0:T(8,128)(2,1)S(1)}, u32[]{:S(2)}, u32[]{:S(2)}) collective-permute-start(bf16[112,128]{1,0:T(8,128)(2,1)S(1)} %add_convert_fusion.1), channel_id=1, source_target_pairs={{0,12},{4,8},{8,4},{12,0},{1,13},{5,9},{9,5},{13,1},{2,14},{6,10},... | collective-permute-start | bytes 86024 | tf_op jit(solution)/shard_map/ppermute | solution.py:31
  45.9 4.6 %collective-permute-start.12 = (bf16[112,128]{1,0:T(8,128)(2,1)S(1)}, bf16[112,128]{1,0:T(8,128)(2,1)S(1)}, u32[]{:S(2)}, u32[]{:S(2)}) collective-permute-start(bf16[112,128]{1,0:T(8,128)(2,1)S(1)} %add_convert_fusion.1), channel_id=1, source_target_pairs={{0,8},{4,12},{8,0},{12,4},{1,9},{5,13},{9,1},{13,5},{2,10},{6,14},... | collective-permute-start | bytes 86024 | tf_op jit(solution)/shard_map/ppermute | solution.py:31
  46.0 4.6 %collective-permute-start.11 = (bf16[112,128]{1,0:T(8,128)(2,1)S(1)}, bf16[112,128]{1,0:T(8,128)(2,1)S(1)}, u32[]{:S(2)}, u32[]{:S(2)}) collective-permute-start(bf16[112,128]{1,0:T(8,128)(2,1)S(1)} %add_convert_fusion.1), channel_id=1, source_target_pairs={{0,4},{4,0},{8,12},{12,8},{1,5},{5,1},{9,13},{13,9},{2,6},{6,2},{1... | collective-permute-start | bytes 86024 | tf_op jit(solution)/shard_map/ppermute | solution.py:31
  50.6 3.5 %collective-permute-start.18 = (bf16[112,128]{1,0:T(8,128)(2,1)S(1)}, bf16[112,128]{1,0:T(8,128)(2,1)S(1)}, u32[]{:S(2)}, u32[]{:S(2)}) collective-permute-start(bf16[112,128]{1,0:T(8,128)(2,1)S(1)} %add_convert_fusion.refs_0_), channel_id=1, source_target_pairs={{0,3},{1,2},{2,1},{3,0},{4,7},{5,6},{6,5},{7,4},{8,11},{9,10},{10,... | collective-permute-start | bytes 86024 | tf_op jit(solution)/shard_map/ppermute | solution.py:31
  52.2 2.7 %collective-permute-start.17 = (bf16[112,128]{1,0:T(8,128)(2,1)S(1)}, bf16[112,128]{1,0:T(8,128)(2,1)S(1)}, u32[]{:S(2)}, u32[]{:S(2)}) collective-permute-start(bf16[112,128]{1,0:T(8,128)(2,1)S(1)} %add_convert_fusion.refs_0_), channel_id=1, source_target_pairs={{0,2},{1,3},{2,0},{3,1},{4,6},{5,7},{6,4},{7,5},{8,10},{9,11},{10,... | collective-permute-start | bytes 86024 | tf_op jit(solution)/shard_map/ppermute | solution.py:31
  52.5 2.5 %collective-permute-start.16 = (bf16[112,128]{1,0:T(8,128)(2,1)S(1)}, bf16[112,128]{1,0:T(8,128)(2,1)S(1)}, u32[]{:S(2)}, u32[]{:S(2)}) collective-permute-start(bf16[112,128]{1,0:T(8,128)(2,1)S(1)} %add_convert_fusion.refs_0_), channel_id=1, source_target_pairs={{0,1},{1,0},{2,3},{3,2},{4,5},{5,4},{6,7},{7,6},{8,9},{9,8},{10,11... | collective-permute-start | bytes 86024 | tf_op jit(solution)/shard_map/ppermute | solution.py:31
  (3 other events, 9.0 us)

commit v8 on v7

--- a/solution.py
+++ b/solution.py
@@ -210,22 +210,28 @@
                 value = cells[:, at : at + views]
                 if lanes > views:
                     value = jnp.concatenate(
-                        [value, jnp.zeros((chan, lanes - views), F32)], axis=1
+                        [value, jnp.zeros((chan, lanes - views), BF16)], axis=1
                     )
-                col_s[b * breadth + k + 1, r * chan : (r + 1) * chan] = value.astype(BF16)
+                col_s[b * breadth + k + 1, r * chan : (r + 1) * chan] = value
         return carry
 
     lax.fori_loop(0, blocks, block, 0, unroll=blocks <= 4)
 
     def copy(w, carry):
-        cells = col_s[w + 1]
-        own_ref[w] = cells
-        first, last = cells[:chan], cells[own - chan :]
-        near_ref[w] = jnp.where(odd > 0, first, last)
-        far_ref[w] = jnp.where(odd > 0, last, first)
+        own_ref[w] = col_s[w + 1]
         return carry
 
     lax.fori_loop(0, width, copy, 0, unroll=width <= 16)
+    edges = []
+    for r in (0, rows - 1):
+        span = breadth * views
+        edges.append(
+            jnp.concatenate(
+                [held_s[b, :, r * span : (r + 1) * span] for b in range(blocks)], axis=1
+            )
+        )
+    near_ref[:, : width * views] = jnp.where(odd > 0, edges[0], edges[1])
+    far_ref[:, : width * views] = jnp.where(odd > 0, edges[1], edges[0])
 
     def pair(q, total):
         left, right = [], []
@@ -280,15 +286,15 @@
     return pl.pallas_call(
         functools.partial(weight_kernel, views, len(wires)),
         out_shape=(
-            held(blocks, (width, chan, lanes), BF16),
-            held(blocks, (width, chan, lanes), BF16),
+            held(blocks, (chan, round_up(width * views, 128)), BF16),
+            held(blocks, (chan, round_up(width * views, 128)), BF16),
             held(blocks, (width, own, lanes), BF16),
         )
         + (held(blocks, (size, 2 * chan), BF16 if parts > 1 else F32),) * parts,
         in_specs=[vmem] * (len(wires) + 3),
         out_specs=(vmem,) * (3 + parts),
         scratch_shapes=[
-            pltpu.VMEM((blocks, chan, wire), F32),
+            pltpu.VMEM((blocks, chan, wire), BF16),
             pltpu.VMEM((width + 2, own, lanes), BF16),
             pltpu.VMEM((parts * size, 2 * chan), F32),
         ],
@@ -299,16 +305,18 @@
 
 def input_kernel(own_ref, near_ref, far_ref, w_ref, out_ref, frame_s, acc_s):
     width, own, lanes = own_ref.shape
-    chan = near_ref.shape[1]
+    chan = near_ref.shape[0]
     rows = own // chan
     views = out_ref.shape[3]
     odd = row_is_odd() > 0
+    for w in range(width):
+        near = near_ref[:, w * views : (w + 1) * views]
+        far = far_ref[:, w * views : (w + 1) * views]
+        frame_s[w, :chan, :views] = jnp.where(odd, near, far)
+        frame_s[w, chan + own :, :views] = jnp.where(odd, far, near)
 
     def fill(w, carry):
-        near, far = near_ref[w], far_ref[w]
-        frame_s[w, :chan] = jnp.where(odd, near, far)
         frame_s[w, chan : chan + own] = own_ref[w]
-        frame_s[w, chan + own :] = jnp.where(odd, far, near)
         return carry
 
     lax.fori_loop(0, width, fill, 0, unroll=width <= 16)
@@ -329,7 +337,7 @@
 
 def input_grad(own, near, far, w_conv, views, blocks):
     width, size, lanes = own.shape
-    chan = near.shape[1]
+    chan = near.shape[0]
     vmem = pl.BlockSpec(memory_space=pltpu.VMEM)
     return pl.pallas_call(
         input_kernel,
@@ -604,14 +612,13 @@
     return total
 
 
-def reduce_views(own, beside):
+def reduce_views(own):
     count = lax.axis_size("view")
     if not pairwise(count):
-        return lax.psum(own, "view"), beside
+        return lax.psum(own, "view")
     own = own.astype(BF16)
     parts = [swap(own, "view", step) for step in range(1, count)]
-    parts, beside = lax.optimization_barrier((parts, beside))
-    return sum_parts([own] + parts), beside
+    return sum_parts([own] + parts).astype(BF16)
 
 
 def scatter_rows(parts):
@@ -625,7 +632,6 @@
 def gather_rows(own, count):
     if count == 1:
         return [own]
-    own = own.astype(BF16)
     return [own] + [swap(own, "row", step) for step in range(1, count)]
 
 
@@ -653,9 +659,10 @@
     near, far, own, *parts = weight_grads(wires, frame, g_weights, g_gain, view_dev, blocks)
     part = scatter_rows(parts)
     near, far = halo_swap(near, far)
+    part, near, far = lax.optimization_barrier((reduce_views(part), near, far))
+    parts = gather_rows(part, len(parts))
     d_input = input_grad(own, near, far, w_conv, view_dev, blocks)
-    part, d_input = reduce_views(part, d_input)
-    parts = gather_rows(part, len(parts))
+    parts, d_input = lax.optimization_barrier((parts, d_input))
     g_conv, g_query, g_key, g_value, g_out, g_gain = unpack(parts, chan, blocks)
     d_input = jnp.transpose(d_input, (0, 3, 1, 2))
     g_conv = jnp.transpose(g_conv, (2, 3, 0, 1))

time: 56.1 us -> 59.1 us (1.053)
  starting transfers between devices: 22.9 us -> 27 us
  waiting for transfers between devices: 18.5 us -> 16.5 us
  local copies, waits for them, and re-layouts: 3.06 us -> 3.68 us
    ppermute x15, waiting for transfers between devices: 12.6 us -> 9.19 us  [swap(): return lax.ppermute(cells, axis, [(i, i ^ step) for i in range(count)])]
    ppermute x15, starting transfers between devices: 16.1 us -> 18.5 us  [swap(): return lax.ppermute(cells, axis, [(i, i ^ step) for i in range(count)])]
    ppermute x2, waiting for transfers between devices: 5.85 us -> 7.28 us  [halo_swap(): got_far = lax.ppermute(far, 'row', pairs) if pairs else jnp.zeros_like(far)]
    ppermute x2, starting transfers between devices: 6.6 us -> 7.79 us  [halo_swap(): got_far = lax.ppermute(far, 'row', pairs) if pairs else jnp.zeros_like(far)]
    unnamed x17, local copies, waits for them, and re-layouts: 1.91 us -> 2.54 us
where the time goes in v8:
time: 59.1 us; the launch traced here: 58.6 us
  starting transfers between devices  27 us (46%)
  waiting for transfers between devices  16.5 us (28%)
  Pallas kernels  10.5 us (18%)
  local copies, waits for them, and re-layouts  3.68 us (6%)
  between operations  0.81 us (1%)
    ppermute x15, starting transfers between devices, swap(): return lax.ppermute(cells, axis, [(i, i ^ step) for i in range(count)])  18.5 us
    ppermute x15, waiting for transfers between devices, swap(): return lax.ppermute(cells, axis, [(i, i ^ step) for i in range(count)])  9.19 us
    ppermute x2, starting transfers between devices, halo_swap(): got_far = lax.ppermute(far, 'row', pairs) if pairs else jnp.zeros_like(far)  7.79 us
    ppermute x2, waiting for transfers between devices, halo_swap(): got_far = lax.ppermute(far, 'row', pairs) if pairs else jnp.zeros_like(far)  7.28 us
    pallas_call x1, Pallas kernels, angular(): pl.pallas_call(functools.partial(angular_kernel, scale, 8, len(wires)), o...  5.92 us
    unnamed x17, local copies, waits for them, and re-layouts  2.54 us
    pallas_call x1, Pallas kernels, input_grad(): pl.pallas_call(input_kernel, out_shape=jax.ShapeDtypeStruct((chan, size /...  1.8 us
  transfers between devices with their start and end apart: 19, of which 8 were waited for; matrix products, arithmetic and copies ran while one was open for 2% of the time, Pallas kernels for 3%

profile of v8, /device:TPU:1, one launch (start us, length us, event | category | flops | bytes accessed | tf_op | source)
XLA Modules:
  0.0 58.6 jit_solution(11370385466538843493)
XLA Ops:
  0.6 1.2 %copy.22 = bf16[64,73,2,16]{1,0,3,2:T(8,128)(2,1)S(1)} copy(bf16[64,73,2,16]{1,3,2,0:T(8,128)(2,1)} %param.9) | data formatting | bytes 598016 | tf_op args[0]
  2.0 4.5 %collective-permute-start.1 = (bf16[16,64,73]{2,1,0:T(8,128)(2,1)S(1)}, bf16[16,64,73]{2,1,0:T(8,128)(2,1)S(1)}, u32[]{:S(2)}, u32[]{:S(2)}) collective-permute-start(bf16[16,64,73]{2,1,0:T(8,128)(2,1)S(1)} %get-tuple-element.84), channel_id=1, source_target_pairs={{1,2},{2,1},{5,6},{6,5},{9,10},{10,9},{13,14},{14,13},{17,18},{18,... | collective-permute-start | bytes 448520 | tf_op jit(solution)/shard_map/ppermute | solution.py:40
  6.5 4.0 %collective-permute-done.1.far_ref = bf16[16,64,73]{2,1,0:T(8,128)(2,1)S(1)} collective-permute-done((bf16[16,64,73]{2,1,0:T(8,128)(2,1)S(1)}, bf16[16,64,73]{2,1,0:T(8,128)(2,1)S(1)}, u32[]{:S(2)}, u32[]{:S(2)}) %collective-permute-start.1) | collective-permute-done | bytes 149536 | tf_op jit(solution)/shard_map/ppermute | solution.py:40
  10.6 1.0 %conv.1 = (bf16[64,640]{1,0:T(8,128)(2,1)S(1)}, bf16[64,640]{1,0:T(8,128)(2,1)S(1)}, bf16[64,640]{1,0:T(8,128)(2,1)S(1)}, bf16[64,640]{1,0:T(8,128)(2,1)S(1)}, bf16[16,256,128]{2,1,0:T(8,128)(2,1)S(1)}) custom-call(bf16[2,16,64,73]{3,2,1,0:T(8,128)(2,1)S(1)} %bitcast.19, bf16[16,64,73]{2,1,0:T(8,128)(2,1)S(1)} %collective-permute-done.near_ref, ...), custom_call_target="tpu_custom_call" | custom-call | tf_op jit(solution)/shard_map/conv/pallas_call | solution.py:176
  11.6 2.3 %collective-permute-start.2 = (bf16[64,640]{1,0:T(8,128)(2,1)S(1)}, bf16[64,640]{1,0:T(8,128)(2,1)S(1)}, u32[]{:S(2)}, u32[]{:S(2)}) collective-permute-start(bf16[64,640]{1,0:T(8,128)(2,1)S(1)} %get-tuple-element.47), channel_id=1, source_target_pairs={{0,4},{4,0},{8,12},{12,8},{1,5},{5,1},{9,13},{13,9},{2,6},{6,2},{1... | collective-permute-start | bytes 245768 | tf_op jit(solution)/shard_map/ppermute | solution.py:31
  13.9 2.3 %collective-permute-start.3 = (bf16[64,640]{1,0:T(8,128)(2,1)S(1)}, bf16[64,640]{1,0:T(8,128)(2,1)S(1)}, u32[]{:S(2)}, u32[]{:S(2)}) collective-permute-start(bf16[64,640]{1,0:T(8,128)(2,1)S(1)} %get-tuple-element.48), channel_id=1, source_target_pairs={{0,8},{4,12},{8,0},{12,4},{1,9},{5,13},{9,1},{13,5},{2,10},{6,14},... | collective-permute-start | bytes 245768 | tf_op jit(solution)/shard_map/ppermute | solution.py:31
  16.9 2.0 %collective-permute-done.3.refs_2_ = bf16[64,640]{1,0:T(8,128)(2,1)S(1)} collective-permute-done((bf16[64,640]{1,0:T(8,128)(2,1)S(1)}, bf16[64,640]{1,0:T(8,128)(2,1)S(1)}, u32[]{:S(2)}, u32[]{:S(2)}) %collective-permute-start.3) | collective-permute-done | bytes 81952 | tf_op jit(solution)/shard_map/ppermute | solution.py:31
  18.9 2.3 %collective-permute-done.4.refs_3_ = bf16[64,640]{1,0:T(8,128)(2,1)S(1)} collective-permute-done((bf16[64,640]{1,0:T(8,128)(2,1)S(1)}, bf16[64,640]{1,0:T(8,128)(2,1)S(1)}, u32[]{:S(2)}, u32[]{:S(2)}) %collective-permute-start.4) | collective-permute-done | bytes 81952 | tf_op jit(solution)/shard_map/ppermute | solution.py:31
  21.9 5.9 %angular.1 = (bf16[64,640]{1,0:T(8,128)(2,1)S(1)}, bf16[64,640]{1,0:T(8,128)(2,1)S(1)}, bf16[64,640]{1,0:T(8,128)(2,1)S(1)}, bf16[64,640]{1,0:T(8,128)(2,1)S(1)}...) custom-call(bf16[64,640]{1,0:T(8,128)(2,1)S(1)} %get-tuple-element.46.refs_0_, ...), custom_call_target="tpu_custom_call" | custom-call | tf_op jit(solution)/shard_map/angular/pallas_call | solution.py:576
  27.9 1.2 %collective-permute-start.6 = (bf16[64,640]{1,0:T(8,128)(2,1)S(1)}, bf16[64,640]{1,0:T(8,128)(2,1)S(1)}, u32[]{:S(2)}, u32[]{:S(2)}) collective-permute-start(bf16[64,640]{1,0:T(8,128)(2,1)S(1)} %get-tuple-element.52), channel_id=1, source_target_pairs={{0,8},{4,12},{8,0},{12,4},{1,9},{5,13},{9,1},{13,5},{2,10},{6,14},... | collective-permute-start | bytes 245768 | tf_op jit(solution)/shard_map/ppermute | solution.py:31
  29.2 2.3 %collective-permute-start.7 = (bf16[64,640]{1,0:T(8,128)(2,1)S(1)}, bf16[64,640]{1,0:T(8,128)(2,1)S(1)}, u32[]{:S(2)}, u32[]{:S(2)}) collective-permute-start(bf16[64,640]{1,0:T(8,128)(2,1)S(1)} %get-tuple-element.53), channel_id=1, source_target_pairs={{0,12},{4,8},{8,4},{12,0},{1,13},{5,9},{9,5},{13,1},{2,14},{6,10},... | collective-permute-start | bytes 245768 | tf_op jit(solution)/shard_map/ppermute | solution.py:31
  31.5 1.1 %copy.23 = bf16[2,4,64,292]{3,1,0,2:T(4,128)(2,1)} copy(bf16[2,4,64,292]{3,2,1,0:T(8,128)(2,1)S(1)} %bitcast.22) | data formatting | bytes 598016 | tf_op jit(solution)/shard_map/reshape | solution.py:657
  32.5 1.7 %collective-permute-done.7.refs_3_ = bf16[64,640]{1,0:T(8,128)(2,1)S(1)} collective-permute-done((bf16[64,640]{1,0:T(8,128)(2,1)S(1)}, bf16[64,640]{1,0:T(8,128)(2,1)S(1)}, u32[]{:S(2)}, u32[]{:S(2)}) %collective-permute-start.7) | collective-permute-done | bytes 81952 | tf_op jit(solution)/shard_map/ppermute | solution.py:31
  34.3 0.9 %weights.1 = (bf16[64,1280]{1,0:T(8,128)(2,1)S(1)}, bf16[64,1280]{1,0:T(8,128)(2,1)S(1)}, bf16[16,128,128]{2,1,0:T(8,128)(2,1)S(1)}, bf16[112,128]{1,0:T(8,128)(...) custom-call(bf16[64,640]{1,0:T(8,128)(2,1)S(1)} %get-tuple-element.56.refs_0_, ...), custom_call_target="tpu_custom_call" | custom-call | tf_op jit(solution)/shard_map/weights/pallas_call | solution.py:286
  35.2 4.0 %collective-permute-start.10 = (bf16[112,128]{1,0:T(8,128)(2,1)S(1)}, bf16[112,128]{1,0:T(8,128)(2,1)S(1)}, u32[]{:S(2)}, u32[]{:S(2)}) collective-permute-start(bf16[112,128]{1,0:T(8,128)(2,1)S(1)} %get-tuple-element.66), channel_id=1, source_target_pairs={{0,3},{1,2},{2,1},{3,0},{4,7},{5,6},{6,5},{7,4},{8,11},{9,10},{10,... | collective-permute-start | bytes 86024 | tf_op jit(solution)/shard_map/ppermute | solution.py:31
  39.7 1.1 %collective-permute-done.10 = bf16[112,128]{1,0:T(8,128)(2,1)S(1)} collective-permute-done((bf16[112,128]{1,0:T(8,128)(2,1)S(1)}, bf16[112,128]{1,0:T(8,128)(2,1)S(1)}, u32[]{:S(2)}, u32[]{:S(2)}) %collective-permute-start.10) | collective-permute-done | bytes 28704 | tf_op jit(solution)/shard_map/ppermute | solution.py:31
  40.8 1.2 %collective-permute-done.9 = bf16[112,128]{1,0:T(8,128)(2,1)S(1)} collective-permute-done((bf16[112,128]{1,0:T(8,128)(2,1)S(1)}, bf16[112,128]{1,0:T(8,128)(2,1)S(1)}, u32[]{:S(2)}, u32[]{:S(2)}) %collective-permute-start.9) | collective-permute-done | bytes 28704 | tf_op jit(solution)/shard_map/ppermute | solution.py:31
  42.0 2.6 %collective-permute-start.13 = (bf16[112,128]{1,0:T(8,128)(2,1)S(1)}, bf16[112,128]{1,0:T(8,128)(2,1)S(1)}, u32[]{:S(2)}, u32[]{:S(2)}) collective-permute-start(bf16[112,128]{1,0:T(8,128)(2,1)S(1)} %add_convert_fusion.1), channel_id=1, source_target_pairs={{0,12},{4,8},{8,4},{12,0},{1,13},{5,9},{9,5},{13,1},{2,14},{6,10},... | collective-permute-start | bytes 86024 | tf_op jit(solution)/shard_map/ppermute | solution.py:31
  44.6 1.0 %collective-permute-start.11 = (bf16[112,128]{1,0:T(8,128)(2,1)S(1)}, bf16[112,128]{1,0:T(8,128)(2,1)S(1)}, u32[]{:S(2)}, u32[]{:S(2)}) collective-permute-start(bf16[112,128]{1,0:T(8,128)(2,1)S(1)} %add_convert_fusion.1), channel_id=1, source_target_pairs={{0,4},{4,0},{8,12},{12,8},{1,5},{5,1},{9,13},{13,9},{2,6},{6,2},{1... | collective-permute-start | bytes 86024 | tf_op jit(solution)/shard_map/ppermute | solution.py:31
  46.3 3.3 %collective-permute-start.15 = (bf16[64,1280]{1,0:T(8,128)(2,1)S(1)}, bf16[64,1280]{1,0:T(8,128)(2,1)S(1)}, u32[]{:S(2)}, u32[]{:S(2)}) collective-permute-start(bf16[64,1280]{1,0:T(8,128)(2,1)S(1)} %get-tuple-element.68), channel_id=1, source_target_pairs={{1,2},{2,1},{5,6},{6,5},{9,10},{10,9},{13,14},{14,13},{17,18},{18,... | collective-permute-start | bytes 491528 | tf_op jit(solution)/shard_map/ppermute | solution.py:40
  49.6 3.3 %collective-permute-done.15.far_ref = bf16[64,1280]{1,0:T(8,128)(2,1)S(1)} collective-permute-done((bf16[64,1280]{1,0:T(8,128)(2,1)S(1)}, bf16[64,1280]{1,0:T(8,128)(2,1)S(1)}, u32[]{:S(2)}, u32[]{:S(2)}) %collective-permute-start.15) | collective-permute-done | bytes 163872 | tf_op jit(solution)/shard_map/ppermute | solution.py:40
  52.9 1.5 %collective-permute-start.17 = (bf16[112,128]{1,0:T(8,128)(2,1)S(1)}, bf16[112,128]{1,0:T(8,128)(2,1)S(1)}, u32[]{:S(2)}, u32[]{:S(2)}) collective-permute-start(bf16[112,128]{1,0:T(8,128)(2,1)S(1)} %add_convert_fusion.refs_0_), channel_id=1, source_target_pairs={{0,2},{1,3},{2,0},{3,1},{4,6},{5,7},{6,4},{7,5},{8,10},{9,11},{10,... | collective-permute-start | bytes 86024 | tf_op jit(solution)/shard_map/ppermute | solution.py:31
  55.0 1.8 %input.1 = bf16[64,2,16,73]{3,2,1,0:T(8,128)(2,1)} custom-call(bf16[16,128,128]{2,1,0:T(8,128)(2,1)S(1)} %get-tuple-element.70.own_ref, bf16[64,1280]{1,0:T(8,128)(2,1)S(1)} %collective-permute-done.14.near_ref, bf16[64,1280]{1,0:T(8,128)(2,1)S(1)} %collective-permute-done.15.far_ref, bf16[3,3,64,64]{3,2,1,0:T(8,128)(2,1)S(1)} %bitcast.21), custom_call_target="tpu_custom_call" | custom-call | tf_op jit(solution)/shard_map/input/pallas_call | solution.py:342
  57.7 0.9 %unpack.1 = (f32[3,3,64,64]{3,2,1,0:T(8,128)}, f32[64,64]{1,0:T(8,128)}, f32[64,64]{1,0:T(8,128)}, f32[64,64]{1,0:T(8,128)}, f32[64,64]{1,0:T(8,128)}, /*index=5*/f32[1,64]{1,0:T(1,128)}) custom-call(bf16[112,128]{1,0:T(8,128)(2,1)S(1)} %add_convert_fusion.refs_0_, bf16[112,128]{1,0:T(8,128)(2,1)S(1)} %collective-permute-done.16.refs_1_, ...), custom_call_target="tpu_custom_call" | custom-call | tf_op jit(solution)/shard_map/unpack/pallas_call | solution.py:386
  (43 shorter events, 4.3 us)
Async XLA Ops:
  1.9 8.7 %copy-start = (bf16[64,64,3,3]{1,0,3,2:T(8,128)(2,1)S(1)}, bf16[64,64,3,3]{1,0,3,2:T(8,128)(2,1)}, u32[]{:S(2)}) copy-start(bf16[64,64,3,3]{1,0,3,2:T(8,128)(2,1)} %param.12) | copy-start | bytes 221188
  2.0 4.6 %collective-permute-start = (bf16[16,64,73]{2,1,0:T(8,128)(2,1)S(1)}, bf16[16,64,73]{2,1,0:T(8,128)(2,1)S(1)}, u32[]{:S(2)}, u32[]{:S(2)}) collective-permute-start(bf16[16,64,73]{2,1,0:T(8,128)(2,1)S(1)} %get-tuple-element.85), channel_id=1, source_target_pairs={{0,1},{1,0},{2,3},{3,2},{4,5},{5,4},{6,7},{7,6},{8,9},{9,8},{10,11... | collective-permute-start | bytes 448520 | tf_op jit(solution)/shard_map/ppermute | solution.py:39
  2.0 8.5 %collective-permute-start.1 = (bf16[16,64,73]{2,1,0:T(8,128)(2,1)S(1)}, bf16[16,64,73]{2,1,0:T(8,128)(2,1)S(1)}, u32[]{:S(2)}, u32[]{:S(2)}) collective-permute-start(bf16[16,64,73]{2,1,0:T(8,128)(2,1)S(1)} %get-tuple-element.84), channel_id=1, source_target_pairs={{1,2},{2,1},{5,6},{6,5},{9,10},{10,9},{13,14},{14,13},{17,18},{18,... | collective-permute-start | bytes 448520 | tf_op jit(solution)/shard_map/ppermute | solution.py:40
  10.6 5.6 %copy-start.6 = (bf16[64,292,2,4]{1,3,2,0:T(4,128)(2,1)S(1)}, bf16[64,292,2,4]{1,3,2,0:T(4,128)(2,1)}, u32[]{:S(2)}) copy-start(bf16[64,292,2,4]{1,3,2,0:T(4,128)(2,1)} %param.10) | copy-start | bytes 897028
  11.6 5.4 %collective-permute-start.2 = (bf16[64,640]{1,0:T(8,128)(2,1)S(1)}, bf16[64,640]{1,0:T(8,128)(2,1)S(1)}, u32[]{:S(2)}, u32[]{:S(2)}) collective-permute-start(bf16[64,640]{1,0:T(8,128)(2,1)S(1)} %get-tuple-element.47), channel_id=1, source_target_pairs={{0,4},{4,0},{8,12},{12,8},{1,5},{5,1},{9,13},{13,9},{2,6},{6,2},{1... | collective-permute-start | bytes 245768 | tf_op jit(solution)/shard_map/ppermute | solution.py:31
  13.9 5.1 %collective-permute-start.3 = (bf16[64,640]{1,0:T(8,128)(2,1)S(1)}, bf16[64,640]{1,0:T(8,128)(2,1)S(1)}, u32[]{:S(2)}, u32[]{:S(2)}) collective-permute-start(bf16[64,640]{1,0:T(8,128)(2,1)S(1)} %get-tuple-element.48), channel_id=1, source_target_pairs={{0,8},{4,12},{8,0},{12,4},{1,9},{5,13},{9,1},{13,5},{2,10},{6,14},... | collective-permute-start | bytes 245768 | tf_op jit(solution)/shard_map/ppermute | solution.py:31
  16.2 5.1 %collective-permute-start.4 = (bf16[64,640]{1,0:T(8,128)(2,1)S(1)}, bf16[64,640]{1,0:T(8,128)(2,1)S(1)}, u32[]{:S(2)}, u32[]{:S(2)}) collective-permute-start(bf16[64,640]{1,0:T(8,128)(2,1)S(1)} %get-tuple-element.49), channel_id=1, source_target_pairs={{0,12},{4,8},{8,4},{12,0},{1,13},{5,9},{9,5},{13,1},{2,14},{6,10},... | collective-permute-start | bytes 245768 | tf_op jit(solution)/shard_map/ppermute | solution.py:31
  16.9 4.4 %copy-start.2 = (bf16[64,64]{1,0:T(8,128)(2,1)S(1)}, bf16[64,64]{1,0:T(8,128)(2,1)}, u32[]{:S(2)}) copy-start(bf16[64,64]{1,0:T(8,128)(2,1)} %refs_8_.1) | copy-start | bytes 24580
  16.9 4.4 %copy-start.3 = (bf16[64,64]{1,0:T(8,128)(2,1)S(1)}, bf16[64,64]{1,0:T(8,128)(2,1)}, u32[]{:S(2)}) copy-start(bf16[64,64]{1,0:T(8,128)(2,1)} %refs_9_.1) | copy-start | bytes 24580
  16.9 4.4 %copy-start.4 = (bf16[64,64]{1,0:T(8,128)(2,1)S(1)}, bf16[64,64]{1,0:T(8,128)(2,1)}, u32[]{:S(2)}) copy-start(bf16[64,64]{1,0:T(8,128)(2,1)} %refs_10_.1) | copy-start | bytes 24580
  27.8 4.7 %collective-permute-start.5 = (bf16[64,640]{1,0:T(8,128)(2,1)S(1)}, bf16[64,640]{1,0:T(8,128)(2,1)S(1)}, u32[]{:S(2)}, u32[]{:S(2)}) collective-permute-start(bf16[64,640]{1,0:T(8,128)(2,1)S(1)} %get-tuple-element.51), channel_id=1, source_target_pairs={{0,4},{4,0},{8,12},{12,8},{1,5},{5,1},{9,13},{13,9},{2,6},{6,2},{1... | collective-permute-start | bytes 245768 | tf_op jit(solution)/shard_map/ppermute | solution.py:31
  27.9 4.6 %collective-permute-start.6 = (bf16[64,640]{1,0:T(8,128)(2,1)S(1)}, bf16[64,640]{1,0:T(8,128)(2,1)S(1)}, u32[]{:S(2)}, u32[]{:S(2)}) collective-permute-start(bf16[64,640]{1,0:T(8,128)(2,1)S(1)} %get-tuple-element.52), channel_id=1, source_target_pairs={{0,8},{4,12},{8,0},{12,4},{1,9},{5,13},{9,1},{13,5},{2,10},{6,14},... | collective-permute-start | bytes 245768 | tf_op jit(solution)/shard_map/ppermute | solution.py:31
  29.2 5.1 %collective-permute-start.7 = (bf16[64,640]{1,0:T(8,128)(2,1)S(1)}, bf16[64,640]{1,0:T(8,128)(2,1)S(1)}, u32[]{:S(2)}, u32[]{:S(2)}) collective-permute-start(bf16[64,640]{1,0:T(8,128)(2,1)S(1)} %get-tuple-element.53), channel_id=1, source_target_pairs={{0,12},{4,8},{8,4},{12,0},{1,13},{5,9},{9,5},{13,1},{2,14},{6,10},... | collective-permute-start | bytes 245768 | tf_op jit(solution)/shard_map/ppermute | solution.py:31
  35.2 5.6 %collective-permute-start.10 = (bf16[112,128]{1,0:T(8,128)(2,1)S(1)}, bf16[112,128]{1,0:T(8,128)(2,1)S(1)}, u32[]{:S(2)}, u32[]{:S(2)}) collective-permute-start(bf16[112,128]{1,0:T(8,128)(2,1)S(1)} %get-tuple-element.66), channel_id=1, source_target_pairs={{0,3},{1,2},{2,1},{3,0},{4,7},{5,6},{6,5},{7,4},{8,11},{9,10},{10,... | collective-permute-start | bytes 86024 | tf_op jit(solution)/shard_map/ppermute | solution.py:31
  39.2 2.7 %collective-permute-start.9 = (bf16[112,128]{1,0:T(8,128)(2,1)S(1)}, bf16[112,128]{1,0:T(8,128)(2,1)S(1)}, u32[]{:S(2)}, u32[]{:S(2)}) collective-permute-start(bf16[112,128]{1,0:T(8,128)(2,1)S(1)} %get-tuple-element.65), channel_id=1, source_target_pairs={{0,2},{1,3},{2,0},{3,1},{4,6},{5,7},{6,4},{7,5},{8,10},{9,11},{10,... | collective-permute-start | bytes 86024 | tf_op jit(solution)/shard_map/ppermute | solution.py:31
  39.2 2.7 %collective-permute-start.8 = (bf16[112,128]{1,0:T(8,128)(2,1)S(1)}, bf16[112,128]{1,0:T(8,128)(2,1)S(1)}, u32[]{:S(2)}, u32[]{:S(2)}) collective-permute-start(bf16[112,128]{1,0:T(8,128)(2,1)S(1)} %get-tuple-element.64), channel_id=1, source_target_pairs={{0,1},{1,0},{2,3},{3,2},{4,5},{5,4},{6,7},{7,6},{8,9},{9,8},{10,11... | collective-permute-start | bytes 86024 | tf_op jit(solution)/shard_map/ppermute | solution.py:31
  42.0 7.6 %collective-permute-start.13 = (bf16[112,128]{1,0:T(8,128)(2,1)S(1)}, bf16[112,128]{1,0:T(8,128)(2,1)S(1)}, u32[]{:S(2)}, u32[]{:S(2)}) collective-permute-start(bf16[112,128]{1,0:T(8,128)(2,1)S(1)} %add_convert_fusion.1), channel_id=1, source_target_pairs={{0,12},{4,8},{8,4},{12,0},{1,13},{5,9},{9,5},{13,1},{2,14},{6,10},... | collective-permute-start | bytes 86024 | tf_op jit(solution)/shard_map/ppermute | solution.py:31
  44.6 5.0 %collective-permute-start.12 = (bf16[112,128]{1,0:T(8,128)(2,1)S(1)}, bf16[112,128]{1,0:T(8,128)(2,1)S(1)}, u32[]{:S(2)}, u32[]{:S(2)}) collective-permute-start(bf16[112,128]{1,0:T(8,128)(2,1)S(1)} %add_convert_fusion.1), channel_id=1, source_target_pairs={{0,8},{4,12},{8,0},{12,4},{1,9},{5,13},{9,1},{13,5},{2,10},{6,14},... | collective-permute-start | bytes 86024 | tf_op jit(solution)/shard_map/ppermute | solution.py:31
  44.6 5.0 %collective-permute-start.11 = (bf16[112,128]{1,0:T(8,128)(2,1)S(1)}, bf16[112,128]{1,0:T(8,128)(2,1)S(1)}, u32[]{:S(2)}, u32[]{:S(2)}) collective-permute-start(bf16[112,128]{1,0:T(8,128)(2,1)S(1)} %add_convert_fusion.1), channel_id=1, source_target_pairs={{0,4},{4,0},{8,12},{12,8},{1,5},{5,1},{9,13},{13,9},{2,6},{6,2},{1... | collective-permute-start | bytes 86024 | tf_op jit(solution)/shard_map/ppermute | solution.py:31
  45.6 4.0 %collective-permute-start.14 = (bf16[64,1280]{1,0:T(8,128)(2,1)S(1)}, bf16[64,1280]{1,0:T(8,128)(2,1)S(1)}, u32[]{:S(2)}, u32[]{:S(2)}) collective-permute-start(bf16[64,1280]{1,0:T(8,128)(2,1)S(1)} %get-tuple-element.67), channel_id=1, source_target_pairs={{0,1},{1,0},{2,3},{3,2},{4,5},{5,4},{6,7},{7,6},{8,9},{9,8},{10,11... | collective-permute-start | bytes 491528 | tf_op jit(solution)/shard_map/ppermute | solution.py:39
  46.3 6.6 %collective-permute-start.15 = (bf16[64,1280]{1,0:T(8,128)(2,1)S(1)}, bf16[64,1280]{1,0:T(8,128)(2,1)S(1)}, u32[]{:S(2)}, u32[]{:S(2)}) collective-permute-start(bf16[64,1280]{1,0:T(8,128)(2,1)S(1)} %get-tuple-element.68), channel_id=1, source_target_pairs={{1,2},{2,1},{5,6},{6,5},{9,10},{10,9},{13,14},{14,13},{17,18},{18,... | collective-permute-start | bytes 491528 | tf_op jit(solution)/shard_map/ppermute | solution.py:40
  52.9 3.9 %collective-permute-start.16 = (bf16[112,128]{1,0:T(8,128)(2,1)S(1)}, bf16[112,128]{1,0:T(8,128)(2,1)S(1)}, u32[]{:S(2)}, u32[]{:S(2)}) collective-permute-start(bf16[112,128]{1,0:T(8,128)(2,1)S(1)} %add_convert_fusion.refs_0_), channel_id=1, source_target_pairs={{0,1},{1,0},{2,3},{3,2},{4,5},{5,4},{6,7},{7,6},{8,9},{9,8},{10,11... | collective-permute-start | bytes 86024 | tf_op jit(solution)/shard_map/ppermute | solution.py:31
  52.9 3.9 %collective-permute-start.17 = (bf16[112,128]{1,0:T(8,128)(2,1)S(1)}, bf16[112,128]{1,0:T(8,128)(2,1)S(1)}, u32[]{:S(2)}, u32[]{:S(2)}) collective-permute-start(bf16[112,128]{1,0:T(8,128)(2,1)S(1)} %add_convert_fusion.refs_0_), channel_id=1, source_target_pairs={{0,2},{1,3},{2,0},{3,1},{4,6},{5,7},{6,4},{7,5},{8,10},{9,11},{10,... | collective-permute-start | bytes 86024 | tf_op jit(solution)/shard_map/ppermute | solution.py:31
  54.4 3.3 %collective-permute-start.18 = (bf16[112,128]{1,0:T(8,128)(2,1)S(1)}, bf16[112,128]{1,0:T(8,128)(2,1)S(1)}, u32[]{:S(2)}, u32[]{:S(2)}) collective-permute-start(bf16[112,128]{1,0:T(8,128)(2,1)S(1)} %add_convert_fusion.refs_0_), channel_id=1, source_target_pairs={{0,3},{1,2},{2,1},{3,0},{4,7},{5,6},{6,5},{7,4},{8,11},{9,10},{10,... | collective-permute-start | bytes 86024 | tf_op jit(solution)/shard_map/ppermute | solution.py:31
  (3 other events, 5.7 us)

commit v9 on v7

--- a/solution.py
+++ b/solution.py
@@ -604,14 +604,13 @@
     return total
 
 
-def reduce_views(own, beside):
+def reduce_views(own):
     count = lax.axis_size("view")
     if not pairwise(count):
-        return lax.psum(own, "view"), beside
+        return lax.psum(own, "view")
     own = own.astype(BF16)
     parts = [swap(own, "view", step) for step in range(1, count)]
-    parts, beside = lax.optimization_barrier((parts, beside))
-    return sum_parts([own] + parts), beside
+    return sum_parts([own] + parts).astype(BF16)
 
 
 def scatter_rows(parts):
@@ -625,7 +624,6 @@
 def gather_rows(own, count):
     if count == 1:
         return [own]
-    own = own.astype(BF16)
     return [own] + [swap(own, "row", step) for step in range(1, count)]
 
 
@@ -653,9 +651,10 @@
     near, far, own, *parts = weight_grads(wires, frame, g_weights, g_gain, view_dev, blocks)
     part = scatter_rows(parts)
     near, far = halo_swap(near, far)
+    part, near, far = lax.optimization_barrier((reduce_views(part), near, far))
+    parts = gather_rows(part, len(parts))
     d_input = input_grad(own, near, far, w_conv, view_dev, blocks)
-    part, d_input = reduce_views(part, d_input)
-    parts = gather_rows(part, len(parts))
+    parts, d_input = lax.optimization_barrier((parts, d_input))
     g_conv, g_query, g_key, g_value, g_out, g_gain = unpack(parts, chan, blocks)
     d_input = jnp.transpose(d_input, (0, 3, 1, 2))
     g_conv = jnp.transpose(g_conv, (2, 3, 0, 1))

time: 56.1 us -> 56.1 us (level)
    ppermute x2, waiting for transfers between devices: 5.85 us -> 3.96 us  [halo_swap(): got_far = lax.ppermute(far, 'row', pairs) if pairs else jnp.zeros_like(far)]
    ppermute x15, waiting for transfers between devices: 12.6 us -> 14.3 us  [swap(): return lax.ppermute(cells, axis, [(i, i ^ step) for i in range(count)])]
where the time goes in v9:
time: 56.1 us; the launch traced here: 55.8 us
  starting transfers between devices  23.2 us (41%)
  waiting for transfers between devices  18.2 us (32%)
  Pallas kernels  10.4 us (19%)
  local copies, waits for them, and re-layouts  3.06 us (5%)
  between operations  0.86 us (2%)
    ppermute x15, starting transfers between devices, swap(): return lax.ppermute(cells, axis, [(i, i ^ step) for i in range(count)])  16.4 us
    ppermute x15, waiting for transfers between devices, swap(): return lax.ppermute(cells, axis, [(i, i ^ step) for i in range(count)])  14.3 us
    ppermute x2, starting transfers between devices, halo_swap(): got_far = lax.ppermute(far, 'row', pairs) if pairs else jnp.zeros_like(far)  6.6 us
    pallas_call x1, Pallas kernels, angular(): pl.pallas_call(functools.partial(angular_kernel, scale, 8, len(wires)), o...  5.92 us
    ppermute x2, waiting for transfers between devices, halo_swap(): got_far = lax.ppermute(far, 'row', pairs) if pairs else jnp.zeros_like(far)  3.96 us
    unnamed x17, local copies, waits for them, and re-layouts  1.91 us
    pallas_call x1, Pallas kernels, input_grad(): pl.pallas_call(input_kernel, out_shape=jax.ShapeDtypeStruct((chan, size /...  1.74 us
  transfers between devices with their start and end apart: 19, of which 8 were waited for; matrix products, arithmetic and copies ran while one was open for 2% of the time, Pallas kernels for 3%

profile of v9, /device:TPU:1, one launch (start us, length us, event | category | flops | bytes accessed | tf_op | source)
XLA Modules:
  0.0 55.8 jit_solution(15187778789833876663)
XLA Ops:
  0.6 1.2 %copy.22 = bf16[64,73,2,16]{1,0,3,2:T(8,128)(2,1)S(1)} copy(bf16[64,73,2,16]{1,3,2,0:T(8,128)(2,1)} %param.9) | data formatting | bytes 598016 | tf_op args[0]
  2.0 4.5 %collective-permute-start.1 = (bf16[16,64,73]{2,1,0:T(8,128)(2,1)S(1)}, bf16[16,64,73]{2,1,0:T(8,128)(2,1)S(1)}, u32[]{:S(2)}, u32[]{:S(2)}) collective-permute-start(bf16[16,64,73]{2,1,0:T(8,128)(2,1)S(1)} %get-tuple-element.84), channel_id=1, source_target_pairs={{1,2},{2,1},{5,6},{6,5},{9,10},{10,9},{13,14},{14,13},{17,18},{18,... | collective-permute-start | bytes 448520 | tf_op jit(solution)/shard_map/ppermute | solution.py:40
  6.5 4.0 %collective-permute-done.1.far_ref = bf16[16,64,73]{2,1,0:T(8,128)(2,1)S(1)} collective-permute-done((bf16[16,64,73]{2,1,0:T(8,128)(2,1)S(1)}, bf16[16,64,73]{2,1,0:T(8,128)(2,1)S(1)}, u32[]{:S(2)}, u32[]{:S(2)}) %collective-permute-start.1) | collective-permute-done | bytes 149536 | tf_op jit(solution)/shard_map/ppermute | solution.py:40
  10.5 0.9 %conv.1 = (bf16[64,640]{1,0:T(8,128)(2,1)S(1)}, bf16[64,640]{1,0:T(8,128)(2,1)S(1)}, bf16[64,640]{1,0:T(8,128)(2,1)S(1)}, bf16[64,640]{1,0:T(8,128)(2,1)S(1)}, bf16[16,256,128]{2,1,0:T(8,128)(2,1)S(1)}) custom-call(bf16[2,16,64,73]{3,2,1,0:T(8,128)(2,1)S(1)} %bitcast.19, bf16[16,64,73]{2,1,0:T(8,128)(2,1)S(1)} %collective-permute-done.near_ref, ...), custom_call_target="tpu_custom_call" | custom-call | tf_op jit(solution)/shard_map/conv/pallas_call | solution.py:176
  11.5 1.4 %collective-permute-start.2 = (bf16[64,640]{1,0:T(8,128)(2,1)S(1)}, bf16[64,640]{1,0:T(8,128)(2,1)S(1)}, u32[]{:S(2)}, u32[]{:S(2)}) collective-permute-start(bf16[64,640]{1,0:T(8,128)(2,1)S(1)} %get-tuple-element.47), channel_id=1, source_target_pairs={{0,4},{4,0},{8,12},{12,8},{1,5},{5,1},{9,13},{13,9},{2,6},{6,2},{1... | collective-permute-start | bytes 245768 | tf_op jit(solution)/shard_map/ppermute | solution.py:31
  12.8 2.3 %collective-permute-start.3 = (bf16[64,640]{1,0:T(8,128)(2,1)S(1)}, bf16[64,640]{1,0:T(8,128)(2,1)S(1)}, u32[]{:S(2)}, u32[]{:S(2)}) collective-permute-start(bf16[64,640]{1,0:T(8,128)(2,1)S(1)} %get-tuple-element.48), channel_id=1, source_target_pairs={{0,8},{4,12},{8,0},{12,4},{1,9},{5,13},{9,1},{13,5},{2,10},{6,14},... | collective-permute-start | bytes 245768 | tf_op jit(solution)/shard_map/ppermute | solution.py:31
  15.6 4.9 %collective-permute-done.3.refs_2_ = bf16[64,640]{1,0:T(8,128)(2,1)S(1)} collective-permute-done((bf16[64,640]{1,0:T(8,128)(2,1)S(1)}, bf16[64,640]{1,0:T(8,128)(2,1)S(1)}, u32[]{:S(2)}, u32[]{:S(2)}) %collective-permute-start.3) | collective-permute-done | bytes 81952 | tf_op jit(solution)/shard_map/ppermute | solution.py:31
  21.2 5.9 %angular.1 = (bf16[64,640]{1,0:T(8,128)(2,1)S(1)}, bf16[64,640]{1,0:T(8,128)(2,1)S(1)}, bf16[64,640]{1,0:T(8,128)(2,1)S(1)}, bf16[64,640]{1,0:T(8,128)(2,1)S(1)}...) custom-call(bf16[64,640]{1,0:T(8,128)(2,1)S(1)} %get-tuple-element.46.refs_0_, ...), custom_call_target="tpu_custom_call" | custom-call | tf_op jit(solution)/shard_map/angular/pallas_call | solution.py:568
  27.1 1.4 %collective-permute-start.5 = (bf16[64,640]{1,0:T(8,128)(2,1)S(1)}, bf16[64,640]{1,0:T(8,128)(2,1)S(1)}, u32[]{:S(2)}, u32[]{:S(2)}) collective-permute-start(bf16[64,640]{1,0:T(8,128)(2,1)S(1)} %get-tuple-element.51), channel_id=1, source_target_pairs={{0,4},{4,0},{8,12},{12,8},{1,5},{5,1},{9,13},{13,9},{2,6},{6,2},{1... | collective-permute-start | bytes 245768 | tf_op jit(solution)/shard_map/ppermute | solution.py:31
  28.5 1.3 %collective-permute-start.6 = (bf16[64,640]{1,0:T(8,128)(2,1)S(1)}, bf16[64,640]{1,0:T(8,128)(2,1)S(1)}, u32[]{:S(2)}, u32[]{:S(2)}) collective-permute-start(bf16[64,640]{1,0:T(8,128)(2,1)S(1)} %get-tuple-element.52), channel_id=1, source_target_pairs={{0,8},{4,12},{8,0},{12,4},{1,9},{5,13},{9,1},{13,5},{2,10},{6,14},... | collective-permute-start | bytes 245768 | tf_op jit(solution)/shard_map/ppermute | solution.py:31
  29.9 0.9 %collective-permute-start.7 = (bf16[64,640]{1,0:T(8,128)(2,1)S(1)}, bf16[64,640]{1,0:T(8,128)(2,1)S(1)}, u32[]{:S(2)}, u32[]{:S(2)}) collective-permute-start(bf16[64,640]{1,0:T(8,128)(2,1)S(1)} %get-tuple-element.53), channel_id=1, source_target_pairs={{0,12},{4,8},{8,4},{12,0},{1,13},{5,9},{9,5},{13,1},{2,14},{6,10},... | collective-permute-start | bytes 245768 | tf_op jit(solution)/shard_map/ppermute | solution.py:31
  30.7 1.1 %copy.23 = bf16[2,4,64,292]{3,1,0,2:T(4,128)(2,1)} copy(bf16[2,4,64,292]{3,2,1,0:T(8,128)(2,1)S(1)} %bitcast.22) | data formatting | bytes 598016 | tf_op jit(solution)/shard_map/reshape | solution.py:649
  31.8 1.4 %collective-permute-done.6.refs_2_ = bf16[64,640]{1,0:T(8,128)(2,1)S(1)} collective-permute-done((bf16[64,640]{1,0:T(8,128)(2,1)S(1)}, bf16[64,640]{1,0:T(8,128)(2,1)S(1)}, u32[]{:S(2)}, u32[]{:S(2)}) %collective-permute-start.6) | collective-permute-done | bytes 81952 | tf_op jit(solution)/shard_map/ppermute | solution.py:31
  33.2 3.9 %collective-permute-done.7.refs_3_ = bf16[64,640]{1,0:T(8,128)(2,1)S(1)} collective-permute-done((bf16[64,640]{1,0:T(8,128)(2,1)S(1)}, bf16[64,640]{1,0:T(8,128)(2,1)S(1)}, u32[]{:S(2)}, u32[]{:S(2)}) %collective-permute-start.7) | collective-permute-done | bytes 81952 | tf_op jit(solution)/shard_map/ppermute | solution.py:31
  37.1 0.9 %weights.1 = (bf16[16,64,128]{2,1,0:T(8,128)(2,1)S(1)}, bf16[16,64,128]{2,1,0:T(8,128)(2,1)S(1)}, bf16[16,128,128]{2,1,0:T(8,128)(2,1)S(1)}, bf16[112,128]{1,0:T...) custom-call(bf16[64,640]{1,0:T(8,128)(2,1)S(1)} %get-tuple-element.56.ref, ...), custom_call_target="tpu_custom_call" | custom-call | tf_op jit(solution)/shard_map/weights/pallas_call | solution.py:280
  38.0 1.2 %collective-permute-start.8 = (bf16[112,128]{1,0:T(8,128)(2,1)S(1)}, bf16[112,128]{1,0:T(8,128)(2,1)S(1)}, u32[]{:S(2)}, u32[]{:S(2)}) collective-permute-start(bf16[112,128]{1,0:T(8,128)(2,1)S(1)} %get-tuple-element.64), channel_id=1, source_target_pairs={{0,1},{1,0},{2,3},{3,2},{4,5},{5,4},{6,7},{7,6},{8,9},{9,8},{10,11... | collective-permute-start | bytes 86024 | tf_op jit(solution)/shard_map/ppermute | solution.py:31
  39.3 1.7 %collective-permute-start.10 = (bf16[112,128]{1,0:T(8,128)(2,1)S(1)}, bf16[112,128]{1,0:T(8,128)(2,1)S(1)}, u32[]{:S(2)}, u32[]{:S(2)}) collective-permute-start(bf16[112,128]{1,0:T(8,128)(2,1)S(1)} %get-tuple-element.66), channel_id=1, source_target_pairs={{0,3},{1,2},{2,1},{3,0},{4,7},{5,6},{6,5},{7,4},{8,11},{9,10},{10,... | collective-permute-start | bytes 86024 | tf_op jit(solution)/shard_map/ppermute | solution.py:31
  41.1 2.1 %collective-permute-start.15 = (bf16[16,64,128]{2,1,0:T(8,128)(2,1)S(1)}, bf16[16,64,128]{2,1,0:T(8,128)(2,1)S(1)}, u32[]{:S(2)}, u32[]{:S(2)}) collective-permute-start(bf16[16,64,128]{2,1,0:T(8,128)(2,1)S(1)} %get-tuple-element.68), channel_id=1, source_target_pairs={{1,2},{2,1},{5,6},{6,5},{9,10},{10,9},{13,14},{14,13},{17,18},{18,... | collective-permute-start | bytes 786440 | tf_op jit(solution)/shard_map/ppermute | solution.py:40
  43.3 2.6 %collective-permute-start.13 = (bf16[112,128]{1,0:T(8,128)(2,1)S(1)}, bf16[112,128]{1,0:T(8,128)(2,1)S(1)}, u32[]{:S(2)}, u32[]{:S(2)}) collective-permute-start(bf16[112,128]{1,0:T(8,128)(2,1)S(1)} %add_convert_fusion.1), channel_id=1, source_target_pairs={{0,12},{4,8},{8,4},{12,0},{1,13},{5,9},{9,5},{13,1},{2,14},{6,10},... | collective-permute-start | bytes 86024 | tf_op jit(solution)/shard_map/ppermute | solution.py:31
  46.0 0.9 %collective-permute-start.11 = (bf16[112,128]{1,0:T(8,128)(2,1)S(1)}, bf16[112,128]{1,0:T(8,128)(2,1)S(1)}, u32[]{:S(2)}, u32[]{:S(2)}) collective-permute-start(bf16[112,128]{1,0:T(8,128)(2,1)S(1)} %add_convert_fusion.1), channel_id=1, source_target_pairs={{0,4},{4,0},{8,12},{12,8},{1,5},{5,1},{9,13},{13,9},{2,6},{6,2},{1... | collective-permute-start | bytes 86024 | tf_op jit(solution)/shard_map/ppermute | solution.py:31
  46.9 1.1 %collective-permute-done.13 = bf16[112,128]{1,0:T(8,128)(2,1)S(1)} collective-permute-done((bf16[112,128]{1,0:T(8,128)(2,1)S(1)}, bf16[112,128]{1,0:T(8,128)(2,1)S(1)}, u32[]{:S(2)}, u32[]{:S(2)}) %collective-permute-start.13) | collective-permute-done | bytes 28704 | tf_op jit(solution)/shard_map/ppermute | solution.py:31
  48.0 2.2 %collective-permute-done.12 = bf16[112,128]{1,0:T(8,128)(2,1)S(1)} collective-permute-done((bf16[112,128]{1,0:T(8,128)(2,1)S(1)}, bf16[112,128]{1,0:T(8,128)(2,1)S(1)}, u32[]{:S(2)}, u32[]{:S(2)}) %collective-permute-start.12) | collective-permute-done | bytes 28704 | tf_op jit(solution)/shard_map/ppermute | solution.py:31
  50.2 2.0 %collective-permute-start.18 = (bf16[112,128]{1,0:T(8,128)(2,1)S(1)}, bf16[112,128]{1,0:T(8,128)(2,1)S(1)}, u32[]{:S(2)}, u32[]{:S(2)}) collective-permute-start(bf16[112,128]{1,0:T(8,128)(2,1)S(1)} %add_convert_fusion.refs_0_), channel_id=1, source_target_pairs={{0,3},{1,2},{2,1},{3,0},{4,7},{5,6},{6,5},{7,4},{8,11},{9,10},{10,... | collective-permute-start | bytes 86024 | tf_op jit(solution)/shard_map/ppermute | solution.py:31
  52.7 1.7 %input.1 = bf16[64,2,16,73]{3,2,1,0:T(8,128)(2,1)} custom-call(bf16[16,128,128]{2,1,0:T(8,128)(2,1)S(1)} %get-tuple-element.70.own_ref, bf16[16,64,128]{2,1,0:T(8,128)(2,1)S(1)} %collective-permute-done.14.near_ref, bf16[16,64,128]{2,1,0:T(8,128)(2,1)S(1)} %collective-permute-done.15.far_ref, bf16[3,3,64,64]{3,2,1,0:T(8,128)(2,1)S(1)} %bitcast.21), custom_call_target="tpu_custom_call" | custom-call | tf_op jit(solution)/shard_map/input/pallas_call | solution.py:334
  (43 shorter events, 3.3 us)
Async XLA Ops:
  1.9 8.6 %copy-start = (bf16[64,64,3,3]{1,0,3,2:T(8,128)(2,1)S(1)}, bf16[64,64,3,3]{1,0,3,2:T(8,128)(2,1)}, u32[]{:S(2)}) copy-start(bf16[64,64,3,3]{1,0,3,2:T(8,128)(2,1)} %param.12) | copy-start | bytes 221188
  2.0 8.5 %collective-permute-start.1 = (bf16[16,64,73]{2,1,0:T(8,128)(2,1)S(1)}, bf16[16,64,73]{2,1,0:T(8,128)(2,1)S(1)}, u32[]{:S(2)}, u32[]{:S(2)}) collective-permute-start(bf16[16,64,73]{2,1,0:T(8,128)(2,1)S(1)} %get-tuple-element.84), channel_id=1, source_target_pairs={{1,2},{2,1},{5,6},{6,5},{9,10},{10,9},{13,14},{14,13},{17,18},{18,... | collective-permute-start | bytes 448520 | tf_op jit(solution)/shard_map/ppermute | solution.py:40
  6.5 4.0 %collective-permute-start = (bf16[16,64,73]{2,1,0:T(8,128)(2,1)S(1)}, bf16[16,64,73]{2,1,0:T(8,128)(2,1)S(1)}, u32[]{:S(2)}, u32[]{:S(2)}) collective-permute-start(bf16[16,64,73]{2,1,0:T(8,128)(2,1)S(1)} %get-tuple-element.85), channel_id=1, source_target_pairs={{0,1},{1,0},{2,3},{3,2},{4,5},{5,4},{6,7},{7,6},{8,9},{9,8},{10,11... | collective-permute-start | bytes 448520 | tf_op jit(solution)/shard_map/ppermute | solution.py:39
  11.5 4.2 %collective-permute-start.2 = (bf16[64,640]{1,0:T(8,128)(2,1)S(1)}, bf16[64,640]{1,0:T(8,128)(2,1)S(1)}, u32[]{:S(2)}, u32[]{:S(2)}) collective-permute-start(bf16[64,640]{1,0:T(8,128)(2,1)S(1)} %get-tuple-element.47), channel_id=1, source_target_pairs={{0,4},{4,0},{8,12},{12,8},{1,5},{5,1},{9,13},{13,9},{2,6},{6,2},{1... | collective-permute-start | bytes 245768 | tf_op jit(solution)/shard_map/ppermute | solution.py:31
  12.8 7.7 %collective-permute-start.3 = (bf16[64,640]{1,0:T(8,128)(2,1)S(1)}, bf16[64,640]{1,0:T(8,128)(2,1)S(1)}, u32[]{:S(2)}, u32[]{:S(2)}) collective-permute-start(bf16[64,640]{1,0:T(8,128)(2,1)S(1)} %get-tuple-element.48), channel_id=1, source_target_pairs={{0,8},{4,12},{8,0},{12,4},{1,9},{5,13},{9,1},{13,5},{2,10},{6,14},... | collective-permute-start | bytes 245768 | tf_op jit(solution)/shard_map/ppermute | solution.py:31
  15.2 5.4 %collective-permute-start.4 = (bf16[64,640]{1,0:T(8,128)(2,1)S(1)}, bf16[64,640]{1,0:T(8,128)(2,1)S(1)}, u32[]{:S(2)}, u32[]{:S(2)}) collective-permute-start(bf16[64,640]{1,0:T(8,128)(2,1)S(1)} %get-tuple-element.49), channel_id=1, source_target_pairs={{0,12},{4,8},{8,4},{12,0},{1,13},{5,9},{9,5},{13,1},{2,14},{6,10},... | collective-permute-start | bytes 245768 | tf_op jit(solution)/shard_map/ppermute | solution.py:31
  15.2 5.3 %copy-start.1 = (bf16[64,64]{1,0:T(8,128)(2,1)S(1)}, bf16[64,64]{1,0:T(8,128)(2,1)}, u32[]{:S(2)}) copy-start(bf16[64,64]{1,0:T(8,128)(2,1)} %refs_7_.1) | copy-start | bytes 24580
  15.2 5.3 %copy-start.2 = (bf16[64,64]{1,0:T(8,128)(2,1)S(1)}, bf16[64,64]{1,0:T(8,128)(2,1)}, u32[]{:S(2)}) copy-start(bf16[64,64]{1,0:T(8,128)(2,1)} %refs_8_.1) | copy-start | bytes 24580
  15.3 5.3 %copy-start.3 = (bf16[64,64]{1,0:T(8,128)(2,1)S(1)}, bf16[64,64]{1,0:T(8,128)(2,1)}, u32[]{:S(2)}) copy-start(bf16[64,64]{1,0:T(8,128)(2,1)} %refs_9_.1) | copy-start | bytes 24580
  15.3 5.3 %copy-start.4 = (bf16[64,64]{1,0:T(8,128)(2,1)S(1)}, bf16[64,64]{1,0:T(8,128)(2,1)}, u32[]{:S(2)}) copy-start(bf16[64,64]{1,0:T(8,128)(2,1)} %refs_10_.1) | copy-start | bytes 24580
  27.1 4.7 %collective-permute-start.5 = (bf16[64,640]{1,0:T(8,128)(2,1)S(1)}, bf16[64,640]{1,0:T(8,128)(2,1)S(1)}, u32[]{:S(2)}, u32[]{:S(2)}) collective-permute-start(bf16[64,640]{1,0:T(8,128)(2,1)S(1)} %get-tuple-element.51), channel_id=1, source_target_pairs={{0,4},{4,0},{8,12},{12,8},{1,5},{5,1},{9,13},{13,9},{2,6},{6,2},{1... | collective-permute-start | bytes 245768 | tf_op jit(solution)/shard_map/ppermute | solution.py:31
  28.5 4.6 %collective-permute-start.6 = (bf16[64,640]{1,0:T(8,128)(2,1)S(1)}, bf16[64,640]{1,0:T(8,128)(2,1)S(1)}, u32[]{:S(2)}, u32[]{:S(2)}) collective-permute-start(bf16[64,640]{1,0:T(8,128)(2,1)S(1)} %get-tuple-element.52), channel_id=1, source_target_pairs={{0,8},{4,12},{8,0},{12,4},{1,9},{5,13},{9,1},{13,5},{2,10},{6,14},... | collective-permute-start | bytes 245768 | tf_op jit(solution)/shard_map/ppermute | solution.py:31
  29.9 7.2 %collective-permute-start.7 = (bf16[64,640]{1,0:T(8,128)(2,1)S(1)}, bf16[64,640]{1,0:T(8,128)(2,1)S(1)}, u32[]{:S(2)}, u32[]{:S(2)}) collective-permute-start(bf16[64,640]{1,0:T(8,128)(2,1)S(1)} %get-tuple-element.53), channel_id=1, source_target_pairs={{0,12},{4,8},{8,4},{12,0},{1,13},{5,9},{9,5},{13,1},{2,14},{6,10},... | collective-permute-start | bytes 245768 | tf_op jit(solution)/shard_map/ppermute | solution.py:31
  38.0 5.2 %collective-permute-start.8 = (bf16[112,128]{1,0:T(8,128)(2,1)S(1)}, bf16[112,128]{1,0:T(8,128)(2,1)S(1)}, u32[]{:S(2)}, u32[]{:S(2)}) collective-permute-start(bf16[112,128]{1,0:T(8,128)(2,1)S(1)} %get-tuple-element.64), channel_id=1, source_target_pairs={{0,1},{1,0},{2,3},{3,2},{4,5},{5,4},{6,7},{7,6},{8,9},{9,8},{10,11... | collective-permute-start | bytes 86024 | tf_op jit(solution)/shard_map/ppermute | solution.py:31
  39.3 4.0 %collective-permute-start.9 = (bf16[112,128]{1,0:T(8,128)(2,1)S(1)}, bf16[112,128]{1,0:T(8,128)(2,1)S(1)}, u32[]{:S(2)}, u32[]{:S(2)}) collective-permute-start(bf16[112,128]{1,0:T(8,128)(2,1)S(1)} %get-tuple-element.65), channel_id=1, source_target_pairs={{0,2},{1,3},{2,0},{3,1},{4,6},{5,7},{6,4},{7,5},{8,10},{9,11},{10,... | collective-permute-start | bytes 86024 | tf_op jit(solution)/shard_map/ppermute | solution.py:31
  39.3 4.0 %collective-permute-start.10 = (bf16[112,128]{1,0:T(8,128)(2,1)S(1)}, bf16[112,128]{1,0:T(8,128)(2,1)S(1)}, u32[]{:S(2)}, u32[]{:S(2)}) collective-permute-start(bf16[112,128]{1,0:T(8,128)(2,1)S(1)} %get-tuple-element.66), channel_id=1, source_target_pairs={{0,3},{1,2},{2,1},{3,0},{4,7},{5,6},{6,5},{7,4},{8,11},{9,10},{10,... | collective-permute-start | bytes 86024 | tf_op jit(solution)/shard_map/ppermute | solution.py:31
  41.0 9.2 %collective-permute-start.14 = (bf16[16,64,128]{2,1,0:T(8,128)(2,1)S(1)}, bf16[16,64,128]{2,1,0:T(8,128)(2,1)S(1)}, u32[]{:S(2)}, u32[]{:S(2)}) collective-permute-start(bf16[16,64,128]{2,1,0:T(8,128)(2,1)S(1)} %get-tuple-element.67), channel_id=1, source_target_pairs={{0,1},{1,0},{2,3},{3,2},{4,5},{5,4},{6,7},{7,6},{8,9},{9,8},{10,11... | collective-permute-start | bytes 786440 | tf_op jit(solution)/shard_map/ppermute | solution.py:39
  41.1 9.1 %collective-permute-start.15 = (bf16[16,64,128]{2,1,0:T(8,128)(2,1)S(1)}, bf16[16,64,128]{2,1,0:T(8,128)(2,1)S(1)}, u32[]{:S(2)}, u32[]{:S(2)}) collective-permute-start(bf16[16,64,128]{2,1,0:T(8,128)(2,1)S(1)} %get-tuple-element.68), channel_id=1, source_target_pairs={{1,2},{2,1},{5,6},{6,5},{9,10},{10,9},{13,14},{14,13},{17,18},{18,... | collective-permute-start | bytes 786440 | tf_op jit(solution)/shard_map/ppermute | solution.py:40
  43.3 4.7 %collective-permute-start.13 = (bf16[112,128]{1,0:T(8,128)(2,1)S(1)}, bf16[112,128]{1,0:T(8,128)(2,1)S(1)}, u32[]{:S(2)}, u32[]{:S(2)}) collective-permute-start(bf16[112,128]{1,0:T(8,128)(2,1)S(1)} %add_convert_fusion.1), channel_id=1, source_target_pairs={{0,12},{4,8},{8,4},{12,0},{1,13},{5,9},{9,5},{13,1},{2,14},{6,10},... | collective-permute-start | bytes 86024 | tf_op jit(solution)/shard_map/ppermute | solution.py:31
  45.9 4.2 %collective-permute-start.12 = (bf16[112,128]{1,0:T(8,128)(2,1)S(1)}, bf16[112,128]{1,0:T(8,128)(2,1)S(1)}, u32[]{:S(2)}, u32[]{:S(2)}) collective-permute-start(bf16[112,128]{1,0:T(8,128)(2,1)S(1)} %add_convert_fusion.1), channel_id=1, source_target_pairs={{0,8},{4,12},{8,0},{12,4},{1,9},{5,13},{9,1},{13,5},{2,10},{6,14},... | collective-permute-start | bytes 86024 | tf_op jit(solution)/shard_map/ppermute | solution.py:31
  46.0 4.2 %collective-permute-start.11 = (bf16[112,128]{1,0:T(8,128)(2,1)S(1)}, bf16[112,128]{1,0:T(8,128)(2,1)S(1)}, u32[]{:S(2)}, u32[]{:S(2)}) collective-permute-start(bf16[112,128]{1,0:T(8,128)(2,1)S(1)} %add_convert_fusion.1), channel_id=1, source_target_pairs={{0,4},{4,0},{8,12},{12,8},{1,5},{5,1},{9,13},{13,9},{2,6},{6,2},{1... | collective-permute-start | bytes 86024 | tf_op jit(solution)/shard_map/ppermute | solution.py:31
  50.2 4.2 %collective-permute-start.18 = (bf16[112,128]{1,0:T(8,128)(2,1)S(1)}, bf16[112,128]{1,0:T(8,128)(2,1)S(1)}, u32[]{:S(2)}, u32[]{:S(2)}) collective-permute-start(bf16[112,128]{1,0:T(8,128)(2,1)S(1)} %add_convert_fusion.refs_0_), channel_id=1, source_target_pairs={{0,3},{1,2},{2,1},{3,0},{4,7},{5,6},{6,5},{7,4},{8,11},{9,10},{10,... | collective-permute-start | bytes 86024 | tf_op jit(solution)/shard_map/ppermute | solution.py:31
  52.2 2.7 %collective-permute-start.17 = (bf16[112,128]{1,0:T(8,128)(2,1)S(1)}, bf16[112,128]{1,0:T(8,128)(2,1)S(1)}, u32[]{:S(2)}, u32[]{:S(2)}) collective-permute-start(bf16[112,128]{1,0:T(8,128)(2,1)S(1)} %add_convert_fusion.refs_0_), channel_id=1, source_target_pairs={{0,2},{1,3},{2,0},{3,1},{4,6},{5,7},{6,4},{7,5},{8,10},{9,11},{10,... | collective-permute-start | bytes 86024 | tf_op jit(solution)/shard_map/ppermute | solution.py:31
  52.5 2.5 %collective-permute-start.16 = (bf16[112,128]{1,0:T(8,128)(2,1)S(1)}, bf16[112,128]{1,0:T(8,128)(2,1)S(1)}, u32[]{:S(2)}, u32[]{:S(2)}) collective-permute-start(bf16[112,128]{1,0:T(8,128)(2,1)S(1)} %add_convert_fusion.refs_0_), channel_id=1, source_target_pairs={{0,1},{1,0},{2,3},{3,2},{4,5},{5,4},{6,7},{7,6},{8,9},{9,8},{10,11... | collective-permute-start | bytes 86024 | tf_op jit(solution)/shard_map/ppermute | solution.py:31
  (3 other events, 9.0 us)

commit v10 on v9

--- a/solution.py
+++ b/solution.py
@@ -189,7 +189,7 @@
 
 
 def weight_kernel(count, pieces, *refs):
-    wires = refs[:pieces]
+    wires = refs[:pieces][::-1]
     frame_ref, g_ref, gain_ref = refs[pieces : pieces + 3]
     near_ref, far_ref, own_ref, *part_refs, held_s, col_s, pack_s = refs[pieces + 3 :]
     width, own, lanes = own_ref.shape
@@ -294,7 +294,7 @@
         ],
         name="weights",
         compiler_params=grant(blocks),
-    )(*here(blocks, *wires, frame, g_weights, g_gain))
+    )(*here(blocks, *wires[::-1], frame, g_weights, g_gain))
 
 
 def input_kernel(own_ref, near_ref, far_ref, w_ref, out_ref, frame_s, acc_s):
@@ -399,7 +399,7 @@
     pieces,
     *refs,
 ):
-    wires_in = refs[:pieces]
+    wires_in = refs[:pieces][::-1]
     cot_ref, keep_ref, gain_row, wq_ref, wkey_ref, wv_ref, wo_ref = refs[pieces : pieces + 7]
     refs = refs[pieces + 7 :]
     wires_out = refs[:pieces]
@@ -593,7 +593,7 @@
         * 6,
         name="angular",
         compiler_params=grant(blocks),
-    )(*here(blocks, *wires, cotangent), keep[None, :], gain[None, :], w_query, w_key, w_value, w_out)
+    )(*here(blocks, *wires[::-1], cotangent), keep[None, :], gain[None, :], w_query, w_key, w_value, w_out)
     return out, output, g_weights, g_gain
 
 
@@ -647,7 +647,8 @@
         wires, cot, keep, gain, w_query, w_key, w_value, w_out, blocks
     )
     output = jnp.transpose(output.reshape(row_dev, breadth, chan, views), (2, 3, 0, 1))
-    wires, output = lax.optimization_barrier((exchange(wires), output))
+    wires, output = lax.optimization_barrier((exchange(wires)[::-1], output))
+    wires = wires[::-1]
     near, far, own, *parts = weight_grads(wires, frame, g_weights, g_gain, view_dev, blocks)
     part = scatter_rows(parts)
     near, far = halo_swap(near, far)

time: 56.1 us -> 54.4 us (0.970)
  waiting for transfers between devices: 18.2 us -> 17.1 us
    ppermute x15, waiting for transfers between devices: 14.3 us -> 13.1 us  [swap(): return lax.ppermute(cells, axis, [(i, i ^ step) for i in range(count)])]
where the time goes in v10:
time: 54.4 us; the launch traced here: 54.2 us
  starting transfers between devices  22.7 us (42%)
  waiting for transfers between devices  17.1 us (31%)
  Pallas kernels  10.4 us (19%)
  local copies, waits for them, and re-layouts  3.06 us (6%)
  between operations  0.85 us (2%)
    ppermute x15, starting transfers between devices, swap(): return lax.ppermute(cells, axis, [(i, i ^ step) for i in range(count)])  15.8 us
    ppermute x15, waiting for transfers between devices, swap(): return lax.ppermute(cells, axis, [(i, i ^ step) for i in range(count)])  13.1 us
    ppermute x2, starting transfers between devices, halo_swap(): got_far = lax.ppermute(far, 'row', pairs) if pairs else jnp.zeros_like(far)  6.72 us
    pallas_call x1, Pallas kernels, angular(): pl.pallas_call(functools.partial(angular_kernel, scale, 8, len(wires)), o...  5.92 us
    ppermute x2, waiting for transfers between devices, halo_swap(): got_far = lax.ppermute(far, 'row', pairs) if pairs else jnp.zeros_like(far)  3.96 us
    unnamed x17, local copies, waits for them, and re-layouts  1.91 us
    pallas_call x1, Pallas kernels, input_grad(): pl.pallas_call(input_kernel, out_shape=jax.ShapeDtypeStruct((chan, size /...  1.74 us
  transfers between devices with their start and end apart: 19, of which 8 were waited for; matrix products, arithmetic and copies ran while one was open for 2% of the time, Pallas kernels for 3%

profile of v10, /device:TPU:1, one launch (start us, length us, event | category | flops | bytes accessed | tf_op | source)
XLA Modules:
  0.0 54.2 jit_solution(12261782754698606018)
XLA Ops:
  0.6 1.2 %copy.22 = bf16[64,73,2,16]{1,0,3,2:T(8,128)(2,1)S(1)} copy(bf16[64,73,2,16]{1,3,2,0:T(8,128)(2,1)} %param.9) | data formatting | bytes 598016 | tf_op args[0]
  2.0 4.5 %collective-permute-start.1 = (bf16[16,64,73]{2,1,0:T(8,128)(2,1)S(1)}, bf16[16,64,73]{2,1,0:T(8,128)(2,1)S(1)}, u32[]{:S(2)}, u32[]{:S(2)}) collective-permute-start(bf16[16,64,73]{2,1,0:T(8,128)(2,1)S(1)} %get-tuple-element.84), channel_id=1, source_target_pairs={{1,2},{2,1},{5,6},{6,5},{9,10},{10,9},{13,14},{14,13},{17,18},{18,... | collective-permute-start | bytes 448520 | tf_op jit(solution)/shard_map/ppermute | solution.py:40
  6.5 4.0 %collective-permute-done.1.far_ref = bf16[16,64,73]{2,1,0:T(8,128)(2,1)S(1)} collective-permute-done((bf16[16,64,73]{2,1,0:T(8,128)(2,1)S(1)}, bf16[16,64,73]{2,1,0:T(8,128)(2,1)S(1)}, u32[]{:S(2)}, u32[]{:S(2)}) %collective-permute-start.1) | collective-permute-done | bytes 149536 | tf_op jit(solution)/shard_map/ppermute | solution.py:40
  10.5 0.9 %conv.1 = (bf16[64,640]{1,0:T(8,128)(2,1)S(1)}, bf16[64,640]{1,0:T(8,128)(2,1)S(1)}, bf16[64,640]{1,0:T(8,128)(2,1)S(1)}, bf16[64,640]{1,0:T(8,128)(2,1)S(1)}, bf16[16,256,128]{2,1,0:T(8,128)(2,1)S(1)}) custom-call(bf16[2,16,64,73]{3,2,1,0:T(8,128)(2,1)S(1)} %bitcast.19, bf16[16,64,73]{2,1,0:T(8,128)(2,1)S(1)} %collective-permute-done.near_ref, ...), custom_call_target="tpu_custom_call" | custom-call | tf_op jit(solution)/shard_map/conv/pallas_call | solution.py:176
  11.5 3.4 %collective-permute-start.2 = (bf16[64,640]{1,0:T(8,128)(2,1)S(1)}, bf16[64,640]{1,0:T(8,128)(2,1)S(1)}, u32[]{:S(2)}, u32[]{:S(2)}) collective-permute-start(bf16[64,640]{1,0:T(8,128)(2,1)S(1)} %get-tuple-element.46), channel_id=1, source_target_pairs={{0,12},{4,8},{8,4},{12,0},{1,13},{5,9},{9,5},{13,1},{2,14},{6,10},... | collective-permute-start | bytes 245768 | tf_op jit(solution)/shard_map/ppermute | solution.py:31
  15.4 2.1 %collective-permute-done.2.refs_0_ = bf16[64,640]{1,0:T(8,128)(2,1)S(1)} collective-permute-done((bf16[64,640]{1,0:T(8,128)(2,1)S(1)}, bf16[64,640]{1,0:T(8,128)(2,1)S(1)}, u32[]{:S(2)}, u32[]{:S(2)}) %collective-permute-start.2) | collective-permute-done | bytes 81952 | tf_op jit(solution)/shard_map/ppermute | solution.py:31
  17.5 2.9 %collective-permute-done.3.refs_1_ = bf16[64,640]{1,0:T(8,128)(2,1)S(1)} collective-permute-done((bf16[64,640]{1,0:T(8,128)(2,1)S(1)}, bf16[64,640]{1,0:T(8,128)(2,1)S(1)}, u32[]{:S(2)}, u32[]{:S(2)}) %collective-permute-start.3) | collective-permute-done | bytes 81952 | tf_op jit(solution)/shard_map/ppermute | solution.py:31
  20.4 0.6 %copy-done.5 = f32[64]{0:T(128)S(1)} copy-done((f32[64]{0:T(128)S(1)}, f32[64]{0:T(128)}, u32[]{:S(2)}) %copy-start.5) | copy-done | bytes 280
  21.0 5.9 %angular.1 = (bf16[64,640]{1,0:T(8,128)(2,1)S(1)}, bf16[64,640]{1,0:T(8,128)(2,1)S(1)}, bf16[64,640]{1,0:T(8,128)(2,1)S(1)}, bf16[64,640]{1,0:T(8,128)(2,1)S(1)}...) custom-call(bf16[64,640]{1,0:T(8,128)(2,1)S(1)} %collective-permute-done.2.refs_0_, ...), custom_call_target="tpu_custom_call" | custom-call | tf_op jit(solution)/shard_map/angular/pallas_call | solution.py:568
  27.0 2.4 %collective-permute-start.5 = (bf16[64,640]{1,0:T(8,128)(2,1)S(1)}, bf16[64,640]{1,0:T(8,128)(2,1)S(1)}, u32[]{:S(2)}, u32[]{:S(2)}) collective-permute-start(bf16[64,640]{1,0:T(8,128)(2,1)S(1)} %get-tuple-element.50), channel_id=1, source_target_pairs={{0,12},{4,8},{8,4},{12,0},{1,13},{5,9},{9,5},{13,1},{2,14},{6,10},... | collective-permute-start | bytes 245768 | tf_op jit(solution)/shard_map/ppermute | solution.py:31
  29.3 1.2 %collective-permute-start.7 = (bf16[64,640]{1,0:T(8,128)(2,1)S(1)}, bf16[64,640]{1,0:T(8,128)(2,1)S(1)}, u32[]{:S(2)}, u32[]{:S(2)}) collective-permute-start(bf16[64,640]{1,0:T(8,128)(2,1)S(1)} %get-tuple-element.52), channel_id=1, source_target_pairs={{0,4},{4,0},{8,12},{12,8},{1,5},{5,1},{9,13},{13,9},{2,6},{6,2},{1... | collective-permute-start | bytes 245768 | tf_op jit(solution)/shard_map/ppermute | solution.py:31
  30.6 1.1 %copy.23 = bf16[2,4,64,292]{3,1,0,2:T(4,128)(2,1)} copy(bf16[2,4,64,292]{3,2,1,0:T(8,128)(2,1)S(1)} %bitcast.22) | data formatting | bytes 598016 | tf_op jit(solution)/shard_map/reshape | solution.py:649
  31.6 0.8 %collective-permute-done.5.refs_0_ = bf16[64,640]{1,0:T(8,128)(2,1)S(1)} collective-permute-done((bf16[64,640]{1,0:T(8,128)(2,1)S(1)}, bf16[64,640]{1,0:T(8,128)(2,1)S(1)}, u32[]{:S(2)}, u32[]{:S(2)}) %collective-permute-start.5) | collective-permute-done | bytes 81952 | tf_op jit(solution)/shard_map/ppermute | solution.py:31
  32.4 4.3 %collective-permute-done.6.refs_1_ = bf16[64,640]{1,0:T(8,128)(2,1)S(1)} collective-permute-done((bf16[64,640]{1,0:T(8,128)(2,1)S(1)}, bf16[64,640]{1,0:T(8,128)(2,1)S(1)}, u32[]{:S(2)}, u32[]{:S(2)}) %collective-permute-start.6) | collective-permute-done | bytes 81952 | tf_op jit(solution)/shard_map/ppermute | solution.py:31
  36.7 0.9 %weights.1 = (bf16[16,64,128]{2,1,0:T(8,128)(2,1)S(1)}, bf16[16,64,128]{2,1,0:T(8,128)(2,1)S(1)}, bf16[16,128,128]{2,1,0:T(8,128)(2,1)S(1)}, bf16[112,128]{1,0:T...) custom-call(bf16[64,640]{1,0:T(8,128)(2,1)S(1)} %collective-permute-done., ...), custom_call_target="tpu_custom_call" | custom-call | tf_op jit(solution)/shard_map/weights/pallas_call | solution.py:280
  38.2 1.7 %collective-permute-start.10 = (bf16[112,128]{1,0:T(8,128)(2,1)S(1)}, bf16[112,128]{1,0:T(8,128)(2,1)S(1)}, u32[]{:S(2)}, u32[]{:S(2)}) collective-permute-start(bf16[112,128]{1,0:T(8,128)(2,1)S(1)} %get-tuple-element.66), channel_id=1, source_target_pairs={{0,3},{1,2},{2,1},{3,0},{4,7},{5,6},{6,5},{7,4},{8,11},{9,10},{10,... | collective-permute-start | bytes 86024 | tf_op jit(solution)/shard_map/ppermute | solution.py:31
  40.0 2.2 %collective-permute-start.15 = (bf16[16,64,128]{2,1,0:T(8,128)(2,1)S(1)}, bf16[16,64,128]{2,1,0:T(8,128)(2,1)S(1)}, u32[]{:S(2)}, u32[]{:S(2)}) collective-permute-start(bf16[16,64,128]{2,1,0:T(8,128)(2,1)S(1)} %get-tuple-element.68), channel_id=1, source_target_pairs={{1,2},{2,1},{5,6},{6,5},{9,10},{10,9},{13,14},{14,13},{17,18},{18,... | collective-permute-start | bytes 786440 | tf_op jit(solution)/shard_map/ppermute | solution.py:40
  42.3 1.8 %collective-permute-start.13 = (bf16[112,128]{1,0:T(8,128)(2,1)S(1)}, bf16[112,128]{1,0:T(8,128)(2,1)S(1)}, u32[]{:S(2)}, u32[]{:S(2)}) collective-permute-start(bf16[112,128]{1,0:T(8,128)(2,1)S(1)} %add_convert_fusion.1), channel_id=1, source_target_pairs={{0,12},{4,8},{8,4},{12,0},{1,13},{5,9},{9,5},{13,1},{2,14},{6,10},... | collective-permute-start | bytes 86024 | tf_op jit(solution)/shard_map/ppermute | solution.py:31
  44.1 1.8 %collective-permute-start.11 = (bf16[112,128]{1,0:T(8,128)(2,1)S(1)}, bf16[112,128]{1,0:T(8,128)(2,1)S(1)}, u32[]{:S(2)}, u32[]{:S(2)}) collective-permute-start(bf16[112,128]{1,0:T(8,128)(2,1)S(1)} %add_convert_fusion.1), channel_id=1, source_target_pairs={{0,4},{4,0},{8,12},{12,8},{1,5},{5,1},{9,13},{13,9},{2,6},{6,2},{1... | collective-permute-start | bytes 86024 | tf_op jit(solution)/shard_map/ppermute | solution.py:31
  45.9 1.0 %collective-permute-done.13 = bf16[112,128]{1,0:T(8,128)(2,1)S(1)} collective-permute-done((bf16[112,128]{1,0:T(8,128)(2,1)S(1)}, bf16[112,128]{1,0:T(8,128)(2,1)S(1)}, u32[]{:S(2)}, u32[]{:S(2)}) %collective-permute-start.13) | collective-permute-done | bytes 28704 | tf_op jit(solution)/shard_map/ppermute | solution.py:31
  46.9 1.5 %collective-permute-done.12 = bf16[112,128]{1,0:T(8,128)(2,1)S(1)} collective-permute-done((bf16[112,128]{1,0:T(8,128)(2,1)S(1)}, bf16[112,128]{1,0:T(8,128)(2,1)S(1)}, u32[]{:S(2)}, u32[]{:S(2)}) %collective-permute-start.12) | collective-permute-done | bytes 28704 | tf_op jit(solution)/shard_map/ppermute | solution.py:31
  48.4 2.1 %collective-permute-start.18 = (bf16[112,128]{1,0:T(8,128)(2,1)S(1)}, bf16[112,128]{1,0:T(8,128)(2,1)S(1)}, u32[]{:S(2)}, u32[]{:S(2)}) collective-permute-start(bf16[112,128]{1,0:T(8,128)(2,1)S(1)} %add_convert_fusion.refs_0_), channel_id=1, source_target_pairs={{0,3},{1,2},{2,1},{3,0},{4,7},{5,6},{6,5},{7,4},{8,11},{9,10},{10,... | collective-permute-start | bytes 86024 | tf_op jit(solution)/shard_map/ppermute | solution.py:31
  51.1 1.7 %input.1 = bf16[64,2,16,73]{3,2,1,0:T(8,128)(2,1)} custom-call(bf16[16,128,128]{2,1,0:T(8,128)(2,1)S(1)} %get-tuple-element.70.own_ref, bf16[16,64,128]{2,1,0:T(8,128)(2,1)S(1)} %collective-permute-done.14.near_ref, bf16[16,64,128]{2,1,0:T(8,128)(2,1)S(1)} %collective-permute-done.15.far_ref, bf16[3,3,64,64]{3,2,1,0:T(8,128)(2,1)S(1)} %bitcast.21), custom_call_target="tpu_custom_call" | custom-call | tf_op jit(solution)/shard_map/input/pallas_call | solution.py:334
  53.3 0.9 %unpack.1 = (f32[3,3,64,64]{3,2,1,0:T(8,128)}, f32[64,64]{1,0:T(8,128)}, f32[64,64]{1,0:T(8,128)}, f32[64,64]{1,0:T(8,128)}, f32[64,64]{1,0:T(8,128)}, /*index=5*/f32[1,64]{1,0:T(1,128)}) custom-call(bf16[112,128]{1,0:T(8,128)(2,1)S(1)} %add_convert_fusion.refs_0_, bf16[112,128]{1,0:T(8,128)(2,1)S(1)} %collective-permute-done.16.refs_1_, ...), custom_call_target="tpu_custom_call" | custom-call | tf_op jit(solution)/shard_map/unpack/pallas_call | solution.py:378
  (43 shorter events, 2.3 us)
Async XLA Ops:
  1.9 8.6 %copy-start = (bf16[64,64,3,3]{1,0,3,2:T(8,128)(2,1)S(1)}, bf16[64,64,3,3]{1,0,3,2:T(8,128)(2,1)}, u32[]{:S(2)}) copy-start(bf16[64,64,3,3]{1,0,3,2:T(8,128)(2,1)} %param.12) | copy-start | bytes 221188
  2.0 8.5 %collective-permute-start.1 = (bf16[16,64,73]{2,1,0:T(8,128)(2,1)S(1)}, bf16[16,64,73]{2,1,0:T(8,128)(2,1)S(1)}, u32[]{:S(2)}, u32[]{:S(2)}) collective-permute-start(bf16[16,64,73]{2,1,0:T(8,128)(2,1)S(1)} %get-tuple-element.84), channel_id=1, source_target_pairs={{1,2},{2,1},{5,6},{6,5},{9,10},{10,9},{13,14},{14,13},{17,18},{18,... | collective-permute-start | bytes 448520 | tf_op jit(solution)/shard_map/ppermute | solution.py:40
  6.5 4.0 %collective-permute-start = (bf16[16,64,73]{2,1,0:T(8,128)(2,1)S(1)}, bf16[16,64,73]{2,1,0:T(8,128)(2,1)S(1)}, u32[]{:S(2)}, u32[]{:S(2)}) collective-permute-start(bf16[16,64,73]{2,1,0:T(8,128)(2,1)S(1)} %get-tuple-element.85), channel_id=1, source_target_pairs={{0,1},{1,0},{2,3},{3,2},{4,5},{5,4},{6,7},{7,6},{8,9},{9,8},{10,11... | collective-permute-start | bytes 448520 | tf_op jit(solution)/shard_map/ppermute | solution.py:39
  11.5 6.0 %collective-permute-start.2 = (bf16[64,640]{1,0:T(8,128)(2,1)S(1)}, bf16[64,640]{1,0:T(8,128)(2,1)S(1)}, u32[]{:S(2)}, u32[]{:S(2)}) collective-permute-start(bf16[64,640]{1,0:T(8,128)(2,1)S(1)} %get-tuple-element.46), channel_id=1, source_target_pairs={{0,12},{4,8},{8,4},{12,0},{1,13},{5,9},{9,5},{13,1},{2,14},{6,10},... | collective-permute-start | bytes 245768 | tf_op jit(solution)/shard_map/ppermute | solution.py:31
  14.9 5.5 %collective-permute-start.3 = (bf16[64,640]{1,0:T(8,128)(2,1)S(1)}, bf16[64,640]{1,0:T(8,128)(2,1)S(1)}, u32[]{:S(2)}, u32[]{:S(2)}) collective-permute-start(bf16[64,640]{1,0:T(8,128)(2,1)S(1)} %get-tuple-element.47), channel_id=1, source_target_pairs={{0,8},{4,12},{8,0},{12,4},{1,9},{5,13},{9,1},{13,5},{2,10},{6,14},... | collective-permute-start | bytes 245768 | tf_op jit(solution)/shard_map/ppermute | solution.py:31
  14.9 5.5 %collective-permute-start.4 = (bf16[64,640]{1,0:T(8,128)(2,1)S(1)}, bf16[64,640]{1,0:T(8,128)(2,1)S(1)}, u32[]{:S(2)}, u32[]{:S(2)}) collective-permute-start(bf16[64,640]{1,0:T(8,128)(2,1)S(1)} %get-tuple-element.48), channel_id=1, source_target_pairs={{0,4},{4,0},{8,12},{12,8},{1,5},{5,1},{9,13},{13,9},{2,6},{6,2},{1... | collective-permute-start | bytes 245768 | tf_op jit(solution)/shard_map/ppermute | solution.py:31
  15.3 5.1 %copy-start.1 = (bf16[64,64]{1,0:T(8,128)(2,1)S(1)}, bf16[64,64]{1,0:T(8,128)(2,1)}, u32[]{:S(2)}) copy-start(bf16[64,64]{1,0:T(8,128)(2,1)} %refs_7_.1) | copy-start | bytes 24580
  15.3 5.1 %copy-start.2 = (bf16[64,64]{1,0:T(8,128)(2,1)S(1)}, bf16[64,64]{1,0:T(8,128)(2,1)}, u32[]{:S(2)}) copy-start(bf16[64,64]{1,0:T(8,128)(2,1)} %refs_8_.1) | copy-start | bytes 24580
  15.3 5.1 %copy-start.3 = (bf16[64,64]{1,0:T(8,128)(2,1)S(1)}, bf16[64,64]{1,0:T(8,128)(2,1)}, u32[]{:S(2)}) copy-start(bf16[64,64]{1,0:T(8,128)(2,1)} %refs_9_.1) | copy-start | bytes 24580
  15.3 5.1 %copy-start.4 = (bf16[64,64]{1,0:T(8,128)(2,1)S(1)}, bf16[64,64]{1,0:T(8,128)(2,1)}, u32[]{:S(2)}) copy-start(bf16[64,64]{1,0:T(8,128)(2,1)} %refs_10_.1) | copy-start | bytes 24580
  27.0 5.5 %collective-permute-start.5 = (bf16[64,640]{1,0:T(8,128)(2,1)S(1)}, bf16[64,640]{1,0:T(8,128)(2,1)S(1)}, u32[]{:S(2)}, u32[]{:S(2)}) collective-permute-start(bf16[64,640]{1,0:T(8,128)(2,1)S(1)} %get-tuple-element.50), channel_id=1, source_target_pairs={{0,12},{4,8},{8,4},{12,0},{1,13},{5,9},{9,5},{13,1},{2,14},{6,10},... | collective-permute-start | bytes 245768 | tf_op jit(solution)/shard_map/ppermute | solution.py:31
  29.3 7.4 %collective-permute-start.6 = (bf16[64,640]{1,0:T(8,128)(2,1)S(1)}, bf16[64,640]{1,0:T(8,128)(2,1)S(1)}, u32[]{:S(2)}, u32[]{:S(2)}) collective-permute-start(bf16[64,640]{1,0:T(8,128)(2,1)S(1)} %get-tuple-element.51), channel_id=1, source_target_pairs={{0,8},{4,12},{8,0},{12,4},{1,9},{5,13},{9,1},{13,5},{2,10},{6,14},... | collective-permute-start | bytes 245768 | tf_op jit(solution)/shard_map/ppermute | solution.py:31
  29.3 7.4 %collective-permute-start.7 = (bf16[64,640]{1,0:T(8,128)(2,1)S(1)}, bf16[64,640]{1,0:T(8,128)(2,1)S(1)}, u32[]{:S(2)}, u32[]{:S(2)}) collective-permute-start(bf16[64,640]{1,0:T(8,128)(2,1)S(1)} %get-tuple-element.52), channel_id=1, source_target_pairs={{0,4},{4,0},{8,12},{12,8},{1,5},{5,1},{9,13},{13,9},{2,6},{6,2},{1... | collective-permute-start | bytes 245768 | tf_op jit(solution)/shard_map/ppermute | solution.py:31
  37.7 4.6 %collective-permute-start.8 = (bf16[112,128]{1,0:T(8,128)(2,1)S(1)}, bf16[112,128]{1,0:T(8,128)(2,1)S(1)}, u32[]{:S(2)}, u32[]{:S(2)}) collective-permute-start(bf16[112,128]{1,0:T(8,128)(2,1)S(1)} %get-tuple-element.64), channel_id=1, source_target_pairs={{0,1},{1,0},{2,3},{3,2},{4,5},{5,4},{6,7},{7,6},{8,9},{9,8},{10,11... | collective-permute-start | bytes 86024 | tf_op jit(solution)/shard_map/ppermute | solution.py:31
  38.1 4.1 %collective-permute-start.9 = (bf16[112,128]{1,0:T(8,128)(2,1)S(1)}, bf16[112,128]{1,0:T(8,128)(2,1)S(1)}, u32[]{:S(2)}, u32[]{:S(2)}) collective-permute-start(bf16[112,128]{1,0:T(8,128)(2,1)S(1)} %get-tuple-element.65), channel_id=1, source_target_pairs={{0,2},{1,3},{2,0},{3,1},{4,6},{5,7},{6,4},{7,5},{8,10},{9,11},{10,... | collective-permute-start | bytes 86024 | tf_op jit(solution)/shard_map/ppermute | solution.py:31
  38.2 4.0 %collective-permute-start.10 = (bf16[112,128]{1,0:T(8,128)(2,1)S(1)}, bf16[112,128]{1,0:T(8,128)(2,1)S(1)}, u32[]{:S(2)}, u32[]{:S(2)}) collective-permute-start(bf16[112,128]{1,0:T(8,128)(2,1)S(1)} %get-tuple-element.66), channel_id=1, source_target_pairs={{0,3},{1,2},{2,1},{3,0},{4,7},{5,6},{6,5},{7,4},{8,11},{9,10},{10,... | collective-permute-start | bytes 86024 | tf_op jit(solution)/shard_map/ppermute | solution.py:31
  39.9 8.6 %collective-permute-start.14 = (bf16[16,64,128]{2,1,0:T(8,128)(2,1)S(1)}, bf16[16,64,128]{2,1,0:T(8,128)(2,1)S(1)}, u32[]{:S(2)}, u32[]{:S(2)}) collective-permute-start(bf16[16,64,128]{2,1,0:T(8,128)(2,1)S(1)} %get-tuple-element.67), channel_id=1, source_target_pairs={{0,1},{1,0},{2,3},{3,2},{4,5},{5,4},{6,7},{7,6},{8,9},{9,8},{10,11... | collective-permute-start | bytes 786440 | tf_op jit(solution)/shard_map/ppermute | solution.py:39
  40.0 8.5 %collective-permute-start.15 = (bf16[16,64,128]{2,1,0:T(8,128)(2,1)S(1)}, bf16[16,64,128]{2,1,0:T(8,128)(2,1)S(1)}, u32[]{:S(2)}, u32[]{:S(2)}) collective-permute-start(bf16[16,64,128]{2,1,0:T(8,128)(2,1)S(1)} %get-tuple-element.68), channel_id=1, source_target_pairs={{1,2},{2,1},{5,6},{6,5},{9,10},{10,9},{13,14},{14,13},{17,18},{18,... | collective-permute-start | bytes 786440 | tf_op jit(solution)/shard_map/ppermute | solution.py:40
  42.3 4.6 %collective-permute-start.13 = (bf16[112,128]{1,0:T(8,128)(2,1)S(1)}, bf16[112,128]{1,0:T(8,128)(2,1)S(1)}, u32[]{:S(2)}, u32[]{:S(2)}) collective-permute-start(bf16[112,128]{1,0:T(8,128)(2,1)S(1)} %add_convert_fusion.1), channel_id=1, source_target_pairs={{0,12},{4,8},{8,4},{12,0},{1,13},{5,9},{9,5},{13,1},{2,14},{6,10},... | collective-permute-start | bytes 86024 | tf_op jit(solution)/shard_map/ppermute | solution.py:31
  44.1 4.3 %collective-permute-start.12 = (bf16[112,128]{1,0:T(8,128)(2,1)S(1)}, bf16[112,128]{1,0:T(8,128)(2,1)S(1)}, u32[]{:S(2)}, u32[]{:S(2)}) collective-permute-start(bf16[112,128]{1,0:T(8,128)(2,1)S(1)} %add_convert_fusion.1), channel_id=1, source_target_pairs={{0,8},{4,12},{8,0},{12,4},{1,9},{5,13},{9,1},{13,5},{2,10},{6,14},... | collective-permute-start | bytes 86024 | tf_op jit(solution)/shard_map/ppermute | solution.py:31
  44.1 4.3 %collective-permute-start.11 = (bf16[112,128]{1,0:T(8,128)(2,1)S(1)}, bf16[112,128]{1,0:T(8,128)(2,1)S(1)}, u32[]{:S(2)}, u32[]{:S(2)}) collective-permute-start(bf16[112,128]{1,0:T(8,128)(2,1)S(1)} %add_convert_fusion.1), channel_id=1, source_target_pairs={{0,4},{4,0},{8,12},{12,8},{1,5},{5,1},{9,13},{13,9},{2,6},{6,2},{1... | collective-permute-start | bytes 86024 | tf_op jit(solution)/shard_map/ppermute | solution.py:31
  48.4 4.4 %collective-permute-start.18 = (bf16[112,128]{1,0:T(8,128)(2,1)S(1)}, bf16[112,128]{1,0:T(8,128)(2,1)S(1)}, u32[]{:S(2)}, u32[]{:S(2)}) collective-permute-start(bf16[112,128]{1,0:T(8,128)(2,1)S(1)} %add_convert_fusion.refs_0_), channel_id=1, source_target_pairs={{0,3},{1,2},{2,1},{3,0},{4,7},{5,6},{6,5},{7,4},{8,11},{9,10},{10,... | collective-permute-start | bytes 86024 | tf_op jit(solution)/shard_map/ppermute | solution.py:31
  50.6 2.7 %collective-permute-start.17 = (bf16[112,128]{1,0:T(8,128)(2,1)S(1)}, bf16[112,128]{1,0:T(8,128)(2,1)S(1)}, u32[]{:S(2)}, u32[]{:S(2)}) collective-permute-start(bf16[112,128]{1,0:T(8,128)(2,1)S(1)} %add_convert_fusion.refs_0_), channel_id=1, source_target_pairs={{0,2},{1,3},{2,0},{3,1},{4,6},{5,7},{6,4},{7,5},{8,10},{9,11},{10,... | collective-permute-start | bytes 86024 | tf_op jit(solution)/shard_map/ppermute | solution.py:31
  50.6 2.7 %collective-permute-start.16 = (bf16[112,128]{1,0:T(8,128)(2,1)S(1)}, bf16[112,128]{1,0:T(8,128)(2,1)S(1)}, u32[]{:S(2)}, u32[]{:S(2)}) collective-permute-start(bf16[112,128]{1,0:T(8,128)(2,1)S(1)} %add_convert_fusion.refs_0_), channel_id=1, source_target_pairs={{0,1},{1,0},{2,3},{3,2},{4,5},{5,4},{6,7},{7,6},{8,9},{9,8},{10,11... | collective-permute-start | bytes 86024 | tf_op jit(solution)/shard_map/ppermute | solution.py:31
  (3 other events, 9.2 us)

commit v11 on v10

--- a/solution.py
+++ b/solution.py
@@ -128,8 +128,10 @@
     lax.fori_loop(0, width // 2, pair, 0, unroll=width <= 16)
 
 
-def conv_kernel(blocks, x_ref, near_ref, far_ref, w_ref, *refs):
-    *wires, frame_ref, acc_s, held_s = refs
+def conv_kernel(blocks, x_ref, near_ref, far_ref, w_ref, gain_in, *refs):
+    *wires, frame_ref, gain_out, acc_s, held_s, sem = refs
+    fetch = pltpu.make_async_copy(gain_in, gain_out, sem)
+    fetch.start()
     rows, width, chan, views = x_ref.shape
     own = rows * chan
     lanes = frame_ref.shape[2]
@@ -163,29 +165,38 @@
 
     lax.fori_loop(0, blocks, block, 0, unroll=blocks <= 4)
     give(wires, held_s)
-
-
-def convolve(x, near, far, w_conv, blocks):
+    fetch.wait()
+
+
+def convolve(x, near, far, w_conv, gain, blocks):
     rows, width, chan, views = x.shape
     own = rows * chan
     lanes = round_up(views, 128)
     wire = round_up(rows * (width // blocks) * views, 128)
     vmem = pl.BlockSpec(memory_space=pltpu.VMEM)
     shapes = wire_shapes(blocks, chan, wire)
-    shapes = shapes + [held(blocks, (width, own + 2 * chan, lanes), BF16)]
-    *wires, frame = pl.pallas_call(
+    shapes = shapes + [
+        held(blocks, (width, own + 2 * chan, lanes), BF16),
+        held(blocks, (1, chan), F32),
+    ]
+    *wires, frame, gain = pl.pallas_call(
         functools.partial(conv_kernel, blocks),
         out_shape=shapes,
-        in_specs=[vmem] * 4,
+        in_specs=[vmem] * 4 + [pl.BlockSpec(memory_space=pltpu.HBM)],
         out_specs=[vmem] * len(shapes),
         scratch_shapes=[
             pltpu.VMEM((width + 2, own, lanes), F32),
             pltpu.VMEM((blocks, chan, wire), F32),
+            pltpu.SemaphoreType.DMA,
         ],
         name="conv",
         compiler_params=grant(blocks),
-    )(*here(blocks, x, near, far), w_conv)
-    return wires, frame
+    )(
+        *here(blocks, x, near, far),
+        w_conv,
+        pltpu.with_memory_space_constraint(gain[None, :], pltpu.HBM),
+    )
+    return wires, frame, gain
 
 
 def weight_kernel(count, pieces, *refs):
@@ -593,7 +604,7 @@
         * 6,
         name="angular",
         compiler_params=grant(blocks),
-    )(*here(blocks, *wires[::-1], cotangent), keep[None, :], gain[None, :], w_query, w_key, w_value, w_out)
+    )(*here(blocks, *wires[::-1], cotangent), keep[None, :], *here(blocks, gain), w_query, w_key, w_value, w_out)
     return out, output, g_weights, g_gain
 
 
@@ -639,7 +650,7 @@
     first, last = x[0], x[row_dev - 1]
     near, far = halo_swap(jnp.where(odd, first, last), jnp.where(odd, last, first))
     w_conv = jnp.transpose(w_conv, (2, 3, 0, 1))
-    wires, frame = convolve(x, near, far, w_conv, blocks)
+    wires, frame, gain = convolve(x, near, far, w_conv, gain, blocks)
     wires = exchange(wires)
     cot = jnp.transpose(cotangent, (2, 3, 0, 1)).reshape(pixels, chan, views)
     cot = jnp.pad(cot, ((0, 0), (0, 0), (0, lanes - views)))

time: 54.4 us -> 54.4 us (level)
  Pallas kernels: 10.4 us -> 11.1 us
  local copies, waits for them, and re-layouts: 3.06 us -> 2.44 us
    unnamed x17 -> x15, local copies, waits for them, and re-layouts: 1.91 us -> 1.29 us
    pallas_call x1, Pallas kernels: 0.94 us -> 1.56 us  [convolve(): pl.pallas_call(functools.partial(conv_kernel, blocks), out_shape=shapes,...]
where the time goes in v11:
time: 54.4 us; the launch traced here: 54.2 us
  starting transfers between devices  22.7 us (42%)
  waiting for transfers between devices  17.1 us (31%)
  Pallas kernels  11.1 us (20%)
  local copies, waits for them, and re-layouts  2.44 us (4%)
  between operations  0.84 us (2%)
    ppermute x15, starting transfers between devices, swap(): return lax.ppermute(cells, axis, [(i, i ^ step) for i in range(count)])  15.8 us
    ppermute x15, waiting for transfers between devices, swap(): return lax.ppermute(cells, axis, [(i, i ^ step) for i in range(count)])  13.1 us
    ppermute x2, starting transfers between devices, halo_swap(): got_far = lax.ppermute(far, 'row', pairs) if pairs else jnp.zeros_like(far)  6.73 us
    pallas_call x1, Pallas kernels, angular(): pl.pallas_call(functools.partial(angular_kernel, scale, 8, len(wires)), o...  5.94 us
    ppermute x2, waiting for transfers between devices, halo_swap(): got_far = lax.ppermute(far, 'row', pairs) if pairs else jnp.zeros_like(far)  3.96 us
    pallas_call x1, Pallas kernels, input_grad(): pl.pallas_call(input_kernel, out_shape=jax.ShapeDtypeStruct((chan, size /...  1.74 us
    pallas_call x1, Pallas kernels, convolve(): pl.pallas_call(functools.partial(conv_kernel, blocks), out_shape=shapes,...  1.56 us
    unnamed x15, local copies, waits for them, and re-layouts  1.29 us
  transfers between devices with their start and end apart: 19, of which 8 were waited for; matrix products, arithmetic and copies ran while one was open for 2% of the time, Pallas kernels for 3%

profile of v11, /device:TPU:1, one launch (start us, length us, event | category | flops | bytes accessed | tf_op | source)
XLA Modules:
  0.0 54.2 jit_solution(12332120424812841290)
XLA Ops:
  0.6 1.2 %copy.22 = bf16[64,73,2,16]{1,0,3,2:T(8,128)(2,1)S(1)} copy(bf16[64,73,2,16]{1,3,2,0:T(8,128)(2,1)} %param.9) | data formatting | bytes 598016 | tf_op args[0]
  2.0 4.5 %collective-permute-start.1 = (bf16[16,64,73]{2,1,0:T(8,128)(2,1)S(1)}, bf16[16,64,73]{2,1,0:T(8,128)(2,1)S(1)}, u32[]{:S(2)}, u32[]{:S(2)}) collective-permute-start(bf16[16,64,73]{2,1,0:T(8,128)(2,1)S(1)} %get-tuple-element.86), channel_id=1, source_target_pairs={{1,2},{2,1},{5,6},{6,5},{9,10},{10,9},{13,14},{14,13},{17,18},{18,... | collective-permute-start | bytes 448520 | tf_op jit(solution)/shard_map/ppermute | solution.py:40
  6.5 4.0 %collective-permute-done.1.far_ref = bf16[16,64,73]{2,1,0:T(8,128)(2,1)S(1)} collective-permute-done((bf16[16,64,73]{2,1,0:T(8,128)(2,1)S(1)}, bf16[16,64,73]{2,1,0:T(8,128)(2,1)S(1)}, u32[]{:S(2)}, u32[]{:S(2)}) %collective-permute-start.1) | collective-permute-done | bytes 149536 | tf_op jit(solution)/shard_map/ppermute | solution.py:40
  10.5 1.6 %conv.1 = (bf16[64,640]{1,0:T(8,128)(2,1)S(1)}, bf16[64,640]{1,0:T(8,128)(2,1)S(1)}, bf16[64,640]{1,0:T(8,128)(2,1)S(1)}, bf16[64,640]{1,0:T(8,128)(2,1)S(1)}, b...) custom-call(bf16[2,16,64,73]{3,2,1,0:T(8,128)(2,1)S(1)} %bitcast.19, ...), custom_call_target="tpu_custom_call" | custom-call | tf_op jit(solution)/shard_map/conv/pallas_call | solution.py:182
  12.1 3.4 %collective-permute-start.2 = (bf16[64,640]{1,0:T(8,128)(2,1)S(1)}, bf16[64,640]{1,0:T(8,128)(2,1)S(1)}, u32[]{:S(2)}, u32[]{:S(2)}) collective-permute-start(bf16[64,640]{1,0:T(8,128)(2,1)S(1)} %get-tuple-element.47), channel_id=1, source_target_pairs={{0,12},{4,8},{8,4},{12,0},{1,13},{5,9},{9,5},{13,1},{2,14},{6,10},... | collective-permute-start | bytes 245768 | tf_op jit(solution)/shard_map/ppermute | solution.py:31
  16.0 2.1 %collective-permute-done.2.refs_0_ = bf16[64,640]{1,0:T(8,128)(2,1)S(1)} collective-permute-done((bf16[64,640]{1,0:T(8,128)(2,1)S(1)}, bf16[64,640]{1,0:T(8,128)(2,1)S(1)}, u32[]{:S(2)}, u32[]{:S(2)}) %collective-permute-start.2) | collective-permute-done | bytes 81952 | tf_op jit(solution)/shard_map/ppermute | solution.py:31
  18.1 2.9 %collective-permute-done.3.refs_1_ = bf16[64,640]{1,0:T(8,128)(2,1)S(1)} collective-permute-done((bf16[64,640]{1,0:T(8,128)(2,1)S(1)}, bf16[64,640]{1,0:T(8,128)(2,1)S(1)}, u32[]{:S(2)}, u32[]{:S(2)}) %collective-permute-start.3) | collective-permute-done | bytes 81952 | tf_op jit(solution)/shard_map/ppermute | solution.py:31
  21.0 5.9 %angular.1 = (bf16[64,640]{1,0:T(8,128)(2,1)S(1)}, bf16[64,640]{1,0:T(8,128)(2,1)S(1)}, bf16[64,640]{1,0:T(8,128)(2,1)S(1)}, bf16[64,640]{1,0:T(8,128)(2,1)S(1)}...) custom-call(bf16[64,640]{1,0:T(8,128)(2,1)S(1)} %collective-permute-done.2.refs_0_, ...), custom_call_target="tpu_custom_call" | custom-call | tf_op jit(solution)/shard_map/angular/pallas_call | solution.py:579
  27.0 2.4 %collective-permute-start.5 = (bf16[64,640]{1,0:T(8,128)(2,1)S(1)}, bf16[64,640]{1,0:T(8,128)(2,1)S(1)}, u32[]{:S(2)}, u32[]{:S(2)}) collective-permute-start(bf16[64,640]{1,0:T(8,128)(2,1)S(1)} %get-tuple-element.52), channel_id=1, source_target_pairs={{0,12},{4,8},{8,4},{12,0},{1,13},{5,9},{9,5},{13,1},{2,14},{6,10},... | collective-permute-start | bytes 245768 | tf_op jit(solution)/shard_map/ppermute | solution.py:31
  29.3 1.2 %collective-permute-start.7 = (bf16[64,640]{1,0:T(8,128)(2,1)S(1)}, bf16[64,640]{1,0:T(8,128)(2,1)S(1)}, u32[]{:S(2)}, u32[]{:S(2)}) collective-permute-start(bf16[64,640]{1,0:T(8,128)(2,1)S(1)} %get-tuple-element.54), channel_id=1, source_target_pairs={{0,4},{4,0},{8,12},{12,8},{1,5},{5,1},{9,13},{13,9},{2,6},{6,2},{1... | collective-permute-start | bytes 245768 | tf_op jit(solution)/shard_map/ppermute | solution.py:31
  30.6 1.1 %copy.23 = bf16[2,4,64,292]{3,1,0,2:T(4,128)(2,1)} copy(bf16[2,4,64,292]{3,2,1,0:T(8,128)(2,1)S(1)} %bitcast.22) | data formatting | bytes 598016 | tf_op jit(solution)/shard_map/reshape | solution.py:660
  31.6 0.8 %collective-permute-done.5.refs_0_ = bf16[64,640]{1,0:T(8,128)(2,1)S(1)} collective-permute-done((bf16[64,640]{1,0:T(8,128)(2,1)S(1)}, bf16[64,640]{1,0:T(8,128)(2,1)S(1)}, u32[]{:S(2)}, u32[]{:S(2)}) %collective-permute-start.5) | collective-permute-done | bytes 81952 | tf_op jit(solution)/shard_map/ppermute | solution.py:31
  32.4 4.3 %collective-permute-done.6.refs_1_ = bf16[64,640]{1,0:T(8,128)(2,1)S(1)} collective-permute-done((bf16[64,640]{1,0:T(8,128)(2,1)S(1)}, bf16[64,640]{1,0:T(8,128)(2,1)S(1)}, u32[]{:S(2)}, u32[]{:S(2)}) %collective-permute-start.6) | collective-permute-done | bytes 81952 | tf_op jit(solution)/shard_map/ppermute | solution.py:31
  36.7 1.0 %weights.1 = (bf16[16,64,128]{2,1,0:T(8,128)(2,1)S(1)}, bf16[16,64,128]{2,1,0:T(8,128)(2,1)S(1)}, bf16[16,128,128]{2,1,0:T(8,128)(2,1)S(1)}, bf16[112,128]{1,0:T...) custom-call(bf16[64,640]{1,0:T(8,128)(2,1)S(1)} %collective-permute-done., ...), custom_call_target="tpu_custom_call" | custom-call | tf_op jit(solution)/shard_map/weights/pallas_call | solution.py:291
  38.2 1.7 %collective-permute-start.10 = (bf16[112,128]{1,0:T(8,128)(2,1)S(1)}, bf16[112,128]{1,0:T(8,128)(2,1)S(1)}, u32[]{:S(2)}, u32[]{:S(2)}) collective-permute-start(bf16[112,128]{1,0:T(8,128)(2,1)S(1)} %get-tuple-element.68), channel_id=1, source_target_pairs={{0,3},{1,2},{2,1},{3,0},{4,7},{5,6},{6,5},{7,4},{8,11},{9,10},{10,... | collective-permute-start | bytes 86024 | tf_op jit(solution)/shard_map/ppermute | solution.py:31
  40.0 2.2 %collective-permute-start.15 = (bf16[16,64,128]{2,1,0:T(8,128)(2,1)S(1)}, bf16[16,64,128]{2,1,0:T(8,128)(2,1)S(1)}, u32[]{:S(2)}, u32[]{:S(2)}) collective-permute-start(bf16[16,64,128]{2,1,0:T(8,128)(2,1)S(1)} %get-tuple-element.70), channel_id=1, source_target_pairs={{1,2},{2,1},{5,6},{6,5},{9,10},{10,9},{13,14},{14,13},{17,18},{18,... | collective-permute-start | bytes 786440 | tf_op jit(solution)/shard_map/ppermute | solution.py:40
  42.3 1.8 %collective-permute-start.13 = (bf16[112,128]{1,0:T(8,128)(2,1)S(1)}, bf16[112,128]{1,0:T(8,128)(2,1)S(1)}, u32[]{:S(2)}, u32[]{:S(2)}) collective-permute-start(bf16[112,128]{1,0:T(8,128)(2,1)S(1)} %add_convert_fusion.1), channel_id=1, source_target_pairs={{0,12},{4,8},{8,4},{12,0},{1,13},{5,9},{9,5},{13,1},{2,14},{6,10},... | collective-permute-start | bytes 86024 | tf_op jit(solution)/shard_map/ppermute | solution.py:31
  44.1 1.8 %collective-permute-start.11 = (bf16[112,128]{1,0:T(8,128)(2,1)S(1)}, bf16[112,128]{1,0:T(8,128)(2,1)S(1)}, u32[]{:S(2)}, u32[]{:S(2)}) collective-permute-start(bf16[112,128]{1,0:T(8,128)(2,1)S(1)} %add_convert_fusion.1), channel_id=1, source_target_pairs={{0,4},{4,0},{8,12},{12,8},{1,5},{5,1},{9,13},{13,9},{2,6},{6,2},{1... | collective-permute-start | bytes 86024 | tf_op jit(solution)/shard_map/ppermute | solution.py:31
  45.9 1.0 %collective-permute-done.13 = bf16[112,128]{1,0:T(8,128)(2,1)S(1)} collective-permute-done((bf16[112,128]{1,0:T(8,128)(2,1)S(1)}, bf16[112,128]{1,0:T(8,128)(2,1)S(1)}, u32[]{:S(2)}, u32[]{:S(2)}) %collective-permute-start.13) | collective-permute-done | bytes 28704 | tf_op jit(solution)/shard_map/ppermute | solution.py:31
  46.9 1.5 %collective-permute-done.12 = bf16[112,128]{1,0:T(8,128)(2,1)S(1)} collective-permute-done((bf16[112,128]{1,0:T(8,128)(2,1)S(1)}, bf16[112,128]{1,0:T(8,128)(2,1)S(1)}, u32[]{:S(2)}, u32[]{:S(2)}) %collective-permute-start.12) | collective-permute-done | bytes 28704 | tf_op jit(solution)/shard_map/ppermute | solution.py:31
  48.4 2.1 %collective-permute-start.18 = (bf16[112,128]{1,0:T(8,128)(2,1)S(1)}, bf16[112,128]{1,0:T(8,128)(2,1)S(1)}, u32[]{:S(2)}, u32[]{:S(2)}) collective-permute-start(bf16[112,128]{1,0:T(8,128)(2,1)S(1)} %add_convert_fusion.refs_0_), channel_id=1, source_target_pairs={{0,3},{1,2},{2,1},{3,0},{4,7},{5,6},{6,5},{7,4},{8,11},{9,10},{10,... | collective-permute-start | bytes 86024 | tf_op jit(solution)/shard_map/ppermute | solution.py:31
  51.0 1.7 %input.1 = bf16[64,2,16,73]{3,2,1,0:T(8,128)(2,1)} custom-call(bf16[16,128,128]{2,1,0:T(8,128)(2,1)S(1)} %get-tuple-element.72.own_ref, bf16[16,64,128]{2,1,0:T(8,128)(2,1)S(1)} %collective-permute-done.14.near_ref, bf16[16,64,128]{2,1,0:T(8,128)(2,1)S(1)} %collective-permute-done.15.far_ref, bf16[3,3,64,64]{3,2,1,0:T(8,128)(2,1)S(1)} %bitcast.21), custom_call_target="tpu_custom_call" | custom-call | tf_op jit(solution)/shard_map/input/pallas_call | solution.py:345
  52.8 0.5 collective-permute-done.17.refs_2_
  53.3 0.9 %unpack.1 = (f32[3,3,64,64]{3,2,1,0:T(8,128)}, f32[64,64]{1,0:T(8,128)}, f32[64,64]{1,0:T(8,128)}, f32[64,64]{1,0:T(8,128)}, f32[64,64]{1,0:T(8,128)}, /*index=5*/f32[1,64]{1,0:T(1,128)}) custom-call(bf16[112,128]{1,0:T(8,128)(2,1)S(1)} %add_convert_fusion.refs_0_, bf16[112,128]{1,0:T(8,128)(2,1)S(1)} %collective-permute-done.16.refs_1_, ...), custom_call_target="tpu_custom_call" | custom-call | tf_op jit(solution)/shard_map/unpack/pallas_call | solution.py:389
  (41 shorter events, 1.8 us)
Async XLA Ops:
  1.9 8.6 %copy-start = (bf16[64,64,3,3]{1,0,3,2:T(8,128)(2,1)S(1)}, bf16[64,64,3,3]{1,0,3,2:T(8,128)(2,1)}, u32[]{:S(2)}) copy-start(bf16[64,64,3,3]{1,0,3,2:T(8,128)(2,1)} %param.12) | copy-start | bytes 221188
  2.0 8.5 %collective-permute-start.1 = (bf16[16,64,73]{2,1,0:T(8,128)(2,1)S(1)}, bf16[16,64,73]{2,1,0:T(8,128)(2,1)S(1)}, u32[]{:S(2)}, u32[]{:S(2)}) collective-permute-start(bf16[16,64,73]{2,1,0:T(8,128)(2,1)S(1)} %get-tuple-element.86), channel_id=1, source_target_pairs={{1,2},{2,1},{5,6},{6,5},{9,10},{10,9},{13,14},{14,13},{17,18},{18,... | collective-permute-start | bytes 448520 | tf_op jit(solution)/shard_map/ppermute | solution.py:40
  6.5 4.0 %collective-permute-start = (bf16[16,64,73]{2,1,0:T(8,128)(2,1)S(1)}, bf16[16,64,73]{2,1,0:T(8,128)(2,1)S(1)}, u32[]{:S(2)}, u32[]{:S(2)}) collective-permute-start(bf16[16,64,73]{2,1,0:T(8,128)(2,1)S(1)} %get-tuple-element.87), channel_id=1, source_target_pairs={{0,1},{1,0},{2,3},{3,2},{4,5},{5,4},{6,7},{7,6},{8,9},{9,8},{10,11... | collective-permute-start | bytes 448520 | tf_op jit(solution)/shard_map/ppermute | solution.py:39
  10.5 5.3 %copy-start.5 = (bf16[64,292,2,4]{1,3,2,0:T(4,128)(2,1)S(1)}, bf16[64,292,2,4]{1,3,2,0:T(4,128)(2,1)}, u32[]{:S(2)}) copy-start(bf16[64,292,2,4]{1,3,2,0:T(4,128)(2,1)} %param.10) | copy-start | bytes 897028
  12.1 6.0 %collective-permute-start.2 = (bf16[64,640]{1,0:T(8,128)(2,1)S(1)}, bf16[64,640]{1,0:T(8,128)(2,1)S(1)}, u32[]{:S(2)}, u32[]{:S(2)}) collective-permute-start(bf16[64,640]{1,0:T(8,128)(2,1)S(1)} %get-tuple-element.47), channel_id=1, source_target_pairs={{0,12},{4,8},{8,4},{12,0},{1,13},{5,9},{9,5},{13,1},{2,14},{6,10},... | collective-permute-start | bytes 245768 | tf_op jit(solution)/shard_map/ppermute | solution.py:31
  15.5 5.5 %collective-permute-start.3 = (bf16[64,640]{1,0:T(8,128)(2,1)S(1)}, bf16[64,640]{1,0:T(8,128)(2,1)S(1)}, u32[]{:S(2)}, u32[]{:S(2)}) collective-permute-start(bf16[64,640]{1,0:T(8,128)(2,1)S(1)} %get-tuple-element.48), channel_id=1, source_target_pairs={{0,8},{4,12},{8,0},{12,4},{1,9},{5,13},{9,1},{13,5},{2,10},{6,14},... | collective-permute-start | bytes 245768 | tf_op jit(solution)/shard_map/ppermute | solution.py:31
  15.5 5.5 %collective-permute-start.4 = (bf16[64,640]{1,0:T(8,128)(2,1)S(1)}, bf16[64,640]{1,0:T(8,128)(2,1)S(1)}, u32[]{:S(2)}, u32[]{:S(2)}) collective-permute-start(bf16[64,640]{1,0:T(8,128)(2,1)S(1)} %get-tuple-element.49), channel_id=1, source_target_pairs={{0,4},{4,0},{8,12},{12,8},{1,5},{5,1},{9,13},{13,9},{2,6},{6,2},{1... | collective-permute-start | bytes 245768 | tf_op jit(solution)/shard_map/ppermute | solution.py:31
  15.9 5.1 %copy-start.1 = (bf16[64,64]{1,0:T(8,128)(2,1)S(1)}, bf16[64,64]{1,0:T(8,128)(2,1)}, u32[]{:S(2)}) copy-start(bf16[64,64]{1,0:T(8,128)(2,1)} %refs_7_.1) | copy-start | bytes 24580
  15.9 5.1 %copy-start.2 = (bf16[64,64]{1,0:T(8,128)(2,1)S(1)}, bf16[64,64]{1,0:T(8,128)(2,1)}, u32[]{:S(2)}) copy-start(bf16[64,64]{1,0:T(8,128)(2,1)} %refs_8_.1) | copy-start | bytes 24580
  15.9 5.1 %copy-start.3 = (bf16[64,64]{1,0:T(8,128)(2,1)S(1)}, bf16[64,64]{1,0:T(8,128)(2,1)}, u32[]{:S(2)}) copy-start(bf16[64,64]{1,0:T(8,128)(2,1)} %refs_9_.1) | copy-start | bytes 24580
  27.0 5.5 %collective-permute-start.5 = (bf16[64,640]{1,0:T(8,128)(2,1)S(1)}, bf16[64,640]{1,0:T(8,128)(2,1)S(1)}, u32[]{:S(2)}, u32[]{:S(2)}) collective-permute-start(bf16[64,640]{1,0:T(8,128)(2,1)S(1)} %get-tuple-element.52), channel_id=1, source_target_pairs={{0,12},{4,8},{8,4},{12,0},{1,13},{5,9},{9,5},{13,1},{2,14},{6,10},... | collective-permute-start | bytes 245768 | tf_op jit(solution)/shard_map/ppermute | solution.py:31
  29.3 7.4 %collective-permute-start.6 = (bf16[64,640]{1,0:T(8,128)(2,1)S(1)}, bf16[64,640]{1,0:T(8,128)(2,1)S(1)}, u32[]{:S(2)}, u32[]{:S(2)}) collective-permute-start(bf16[64,640]{1,0:T(8,128)(2,1)S(1)} %get-tuple-element.53), channel_id=1, source_target_pairs={{0,8},{4,12},{8,0},{12,4},{1,9},{5,13},{9,1},{13,5},{2,10},{6,14},... | collective-permute-start | bytes 245768 | tf_op jit(solution)/shard_map/ppermute | solution.py:31
  29.3 7.4 %collective-permute-start.7 = (bf16[64,640]{1,0:T(8,128)(2,1)S(1)}, bf16[64,640]{1,0:T(8,128)(2,1)S(1)}, u32[]{:S(2)}, u32[]{:S(2)}) collective-permute-start(bf16[64,640]{1,0:T(8,128)(2,1)S(1)} %get-tuple-element.54), channel_id=1, source_target_pairs={{0,4},{4,0},{8,12},{12,8},{1,5},{5,1},{9,13},{13,9},{2,6},{6,2},{1... | collective-permute-start | bytes 245768 | tf_op jit(solution)/shard_map/ppermute | solution.py:31
  37.7 4.6 %collective-permute-start.8 = (bf16[112,128]{1,0:T(8,128)(2,1)S(1)}, bf16[112,128]{1,0:T(8,128)(2,1)S(1)}, u32[]{:S(2)}, u32[]{:S(2)}) collective-permute-start(bf16[112,128]{1,0:T(8,128)(2,1)S(1)} %get-tuple-element.66), channel_id=1, source_target_pairs={{0,1},{1,0},{2,3},{3,2},{4,5},{5,4},{6,7},{7,6},{8,9},{9,8},{10,11... | collective-permute-start | bytes 86024 | tf_op jit(solution)/shard_map/ppermute | solution.py:31
  38.1 4.1 %collective-permute-start.9 = (bf16[112,128]{1,0:T(8,128)(2,1)S(1)}, bf16[112,128]{1,0:T(8,128)(2,1)S(1)}, u32[]{:S(2)}, u32[]{:S(2)}) collective-permute-start(bf16[112,128]{1,0:T(8,128)(2,1)S(1)} %get-tuple-element.67), channel_id=1, source_target_pairs={{0,2},{1,3},{2,0},{3,1},{4,6},{5,7},{6,4},{7,5},{8,10},{9,11},{10,... | collective-permute-start | bytes 86024 | tf_op jit(solution)/shard_map/ppermute | solution.py:31
  38.2 4.0 %collective-permute-start.10 = (bf16[112,128]{1,0:T(8,128)(2,1)S(1)}, bf16[112,128]{1,0:T(8,128)(2,1)S(1)}, u32[]{:S(2)}, u32[]{:S(2)}) collective-permute-start(bf16[112,128]{1,0:T(8,128)(2,1)S(1)} %get-tuple-element.68), channel_id=1, source_target_pairs={{0,3},{1,2},{2,1},{3,0},{4,7},{5,6},{6,5},{7,4},{8,11},{9,10},{10,... | collective-permute-start | bytes 86024 | tf_op jit(solution)/shard_map/ppermute | solution.py:31
  39.9 8.6 %collective-permute-start.14 = (bf16[16,64,128]{2,1,0:T(8,128)(2,1)S(1)}, bf16[16,64,128]{2,1,0:T(8,128)(2,1)S(1)}, u32[]{:S(2)}, u32[]{:S(2)}) collective-permute-start(bf16[16,64,128]{2,1,0:T(8,128)(2,1)S(1)} %get-tuple-element.69), channel_id=1, source_target_pairs={{0,1},{1,0},{2,3},{3,2},{4,5},{5,4},{6,7},{7,6},{8,9},{9,8},{10,11... | collective-permute-start | bytes 786440 | tf_op jit(solution)/shard_map/ppermute | solution.py:39
  40.0 8.5 %collective-permute-start.15 = (bf16[16,64,128]{2,1,0:T(8,128)(2,1)S(1)}, bf16[16,64,128]{2,1,0:T(8,128)(2,1)S(1)}, u32[]{:S(2)}, u32[]{:S(2)}) collective-permute-start(bf16[16,64,128]{2,1,0:T(8,128)(2,1)S(1)} %get-tuple-element.70), channel_id=1, source_target_pairs={{1,2},{2,1},{5,6},{6,5},{9,10},{10,9},{13,14},{14,13},{17,18},{18,... | collective-permute-start | bytes 786440 | tf_op jit(solution)/shard_map/ppermute | solution.py:40
  42.3 4.6 %collective-permute-start.13 = (bf16[112,128]{1,0:T(8,128)(2,1)S(1)}, bf16[112,128]{1,0:T(8,128)(2,1)S(1)}, u32[]{:S(2)}, u32[]{:S(2)}) collective-permute-start(bf16[112,128]{1,0:T(8,128)(2,1)S(1)} %add_convert_fusion.1), channel_id=1, source_target_pairs={{0,12},{4,8},{8,4},{12,0},{1,13},{5,9},{9,5},{13,1},{2,14},{6,10},... | collective-permute-start | bytes 86024 | tf_op jit(solution)/shard_map/ppermute | solution.py:31
  44.1 4.3 %collective-permute-start.12 = (bf16[112,128]{1,0:T(8,128)(2,1)S(1)}, bf16[112,128]{1,0:T(8,128)(2,1)S(1)}, u32[]{:S(2)}, u32[]{:S(2)}) collective-permute-start(bf16[112,128]{1,0:T(8,128)(2,1)S(1)} %add_convert_fusion.1), channel_id=1, source_target_pairs={{0,8},{4,12},{8,0},{12,4},{1,9},{5,13},{9,1},{13,5},{2,10},{6,14},... | collective-permute-start | bytes 86024 | tf_op jit(solution)/shard_map/ppermute | solution.py:31
  44.1 4.3 %collective-permute-start.11 = (bf16[112,128]{1,0:T(8,128)(2,1)S(1)}, bf16[112,128]{1,0:T(8,128)(2,1)S(1)}, u32[]{:S(2)}, u32[]{:S(2)}) collective-permute-start(bf16[112,128]{1,0:T(8,128)(2,1)S(1)} %add_convert_fusion.1), channel_id=1, source_target_pairs={{0,4},{4,0},{8,12},{12,8},{1,5},{5,1},{9,13},{13,9},{2,6},{6,2},{1... | collective-permute-start | bytes 86024 | tf_op jit(solution)/shard_map/ppermute | solution.py:31
  48.4 4.3 %collective-permute-start.18 = (bf16[112,128]{1,0:T(8,128)(2,1)S(1)}, bf16[112,128]{1,0:T(8,128)(2,1)S(1)}, u32[]{:S(2)}, u32[]{:S(2)}) collective-permute-start(bf16[112,128]{1,0:T(8,128)(2,1)S(1)} %add_convert_fusion.refs_0_), channel_id=1, source_target_pairs={{0,3},{1,2},{2,1},{3,0},{4,7},{5,6},{6,5},{7,4},{8,11},{9,10},{10,... | collective-permute-start | bytes 86024 | tf_op jit(solution)/shard_map/ppermute | solution.py:31
  50.6 2.7 %collective-permute-start.17 = (bf16[112,128]{1,0:T(8,128)(2,1)S(1)}, bf16[112,128]{1,0:T(8,128)(2,1)S(1)}, u32[]{:S(2)}, u32[]{:S(2)}) collective-permute-start(bf16[112,128]{1,0:T(8,128)(2,1)S(1)} %add_convert_fusion.refs_0_), channel_id=1, source_target_pairs={{0,2},{1,3},{2,0},{3,1},{4,6},{5,7},{6,4},{7,5},{8,10},{9,11},{10,... | collective-permute-start | bytes 86024 | tf_op jit(solution)/shard_map/ppermute | solution.py:31
  50.6 2.7 %collective-permute-start.16 = (bf16[112,128]{1,0:T(8,128)(2,1)S(1)}, bf16[112,128]{1,0:T(8,128)(2,1)S(1)}, u32[]{:S(2)}, u32[]{:S(2)}) collective-permute-start(bf16[112,128]{1,0:T(8,128)(2,1)S(1)} %add_convert_fusion.refs_0_), channel_id=1, source_target_pairs={{0,1},{1,0},{2,3},{3,2},{4,5},{5,4},{6,7},{7,6},{8,9},{9,8},{10,11... | collective-permute-start | bytes 86024 | tf_op jit(solution)/shard_map/ppermute | solution.py:31
  (2 other events, 8.8 us)
